TPU v7x, 32 devices: a whole 2x2x4 slice. The times are simulated.
32 devices in a mesh: parts: 32 (over z, y, x, core).
Axes of the slice: x: 2, y: 2, z: 4, core: 2. Of those that a mesh axis runs over, the one named last changes fastest.
Arguments:
- basis: float32 [16, 32768], P(None, 'parts'), may hold values from -8000 to 8000, as said below
- k_tiles: float32 [256, 5, 128, 128], P('parts'), may hold values from -3 to 11, as said below
- m_tiles: float32 [256, 5, 128, 128], P('parts'), may hold values from -2 to 4, as said below
- tile_part: int32 [256, 5], P('parts'), may hold values from 0 to 31, as said below
- tile_slot: int32 [256, 5], P('parts'), may hold values from 0 to 7, as said below
- iface_rows: int32 [64], P('parts'), may hold values from 0 to 7
Outputs:
- corrections: float32 [16, 32768], P(None, 'parts')
- theta: float32 [16], replicated
Inputs may be any that keep to these rules, and one draw needn't show every extreme that they name: `basis`: the rows form a full-rank set. `k_tiles`: block 0 of every row tile has a positive diagonal well above its other entries. `m_tiles`: block 0 of every row tile has a positive diagonal. `tile_part`: block 0 of a row tile lies in its own partition; every other block lies in its own partition, in the partition 1 away on either side, or in the partition 16 away, counted modulo the number of partitions. `tile_slot`: where the block lies in the own partition this is a row tile of it (for block 0 the row tile itself); elsewhere an interface slot below 2.
All inputs are finite; a program needn't handle non-finite values.
Results may differ from a plain program's by a relative error of at most 0.0003.
Values sent between devices are 32-bit elements; how exact they have to be, the bound alone decides.
No kernel may reach another device: no remote copies, remote signals or barrier semaphores. Data moves between devices by JAX's collectives and lax.ppermute only.
A program may use at most 64 MiB of HBM per device.

v0:
```python
import jax
import jax.numpy as jnp
from jax import lax
from jax.sharding import PartitionSpec as P

STEPS = 4


relax = 0.4


def shifted(value, axis, steps):
    count = lax.axis_size(axis)
    pairs = [(source, (source + steps) % count) for source in range(count)]
    return lax.ppermute(value, axis, pairs)


def product(left, right):
    return jnp.dot(left, right, precision=lax.Precision.HIGHEST, preferred_element_type=jnp.float32)


def inverse_lower(chol):
    eye = jnp.eye(chol.shape[0], dtype=chol.dtype)
    return jax.scipy.linalg.solve_triangular(chol, eye, lower=True)


def shards(basis, k_tiles, m_tiles, tile_part, tile_slot, iface_rows):
    pairs = basis.shape[0]
    tiles = k_tiles.shape[0]
    width = k_tiles.shape[2]
    count = iface_rows.shape[0]
    parts = lax.axis_size("parts")
    me = lax.axis_index("parts")
    scale = 1.0 / (basis.shape[1] * parts)
    far_step = parts // 2
    neighbours = (1, -1, far_step, -far_step)
    direction = jnp.full_like(tile_part, 3)
    for number in (2, 1, 0):
        target = (me + neighbours[number] + parts) % parts
        direction = jnp.where(tile_part == target, number, direction)
    remote = tiles + direction * count + tile_slot
    columns = jnp.where(tile_part == me, tile_slot, remote)

    def apply_pair(vectors):
        blocks = vectors.reshape(pairs, tiles, width)
        outgoing = jnp.take(blocks, iface_rows, axis=1)
        received = []
        for offset in neighbours:
            received.append(shifted(outgoing, "parts", -offset))
        incoming = jnp.concatenate(received, axis=1)
        sources = jnp.concatenate([blocks, incoming], axis=1)
        picked = jnp.take(sources, columns, axis=1)
        stiff = jnp.einsum("ptbc,tbrc->ptr", picked, k_tiles, precision=lax.Precision.HIGHEST)
        mass = jnp.einsum("ptbc,tbrc->ptr", picked, m_tiles, precision=lax.Precision.HIGHEST)
        return (stiff.reshape(pairs, -1), mass.reshape(pairs, -1))

    gram = lax.psum(product(basis, basis.T) * scale, "parts")
    inv_v = inverse_lower(jnp.linalg.cholesky(gram))
    ortho = product(inv_v, basis)
    k_ortho, m_ortho = apply_pair(ortho)
    mass_gram, stiff_cross = lax.psum(
        (product(m_ortho, m_ortho.T) * scale, product(m_ortho, k_ortho.T) * scale), "parts"
    )
    chol_b = jnp.linalg.cholesky(mass_gram)
    inv_b = inverse_lower(chol_b)
    test_basis = product(inv_b, m_ortho)
    projected_k = product(inv_b, stiff_cross)
    theta = jnp.diagonal(projected_k) / jnp.diagonal(chol_b)
    resid = k_ortho - theta[:, None] * m_ortho
    diag_k = jnp.diagonal(k_tiles[:, 0], axis1=1, axis2=2).reshape(-1)
    correct = -relax * resid / diag_k
    for step in range(STEPS):
        right = lax.psum(product(correct, ortho.T) * scale, "parts")
        moved = correct - product(right, ortho)
        k_moved, m_moved = apply_pair(moved)
        image = k_moved - theta[:, None] * m_moved
        left = lax.psum(product(image, test_basis.T) * scale, "parts")
        image = image - product(left, test_basis)
        correct = correct - relax * (resid + image) / diag_k
    final = lax.psum(product(correct, ortho.T) * scale, "parts")
    correct = correct - product(final, ortho)
    return (correct, theta)


def solution(mesh):
    placed = (
        P(None, "parts"),
        P("parts", None, None, None),
        P("parts", None, None, None),
        P("parts", None),
        P("parts", None),
        P("parts"),
    )
    return jax.shard_map(
        shards, mesh=mesh, in_specs=placed, out_specs=(P(None, "parts"), P()), check_vma=False
    )
```

profile of v0, /device:TPU:0, one launch (start us, length us, event | category | flops | bytes accessed | tf_op | source)
XLA Modules:
  0.0 536.0 jit_solution(4131112549924731336)
XLA Ops:
  0.6 0.8 compare_select_fusion.1
  1.5 0.7 compare_and_fusion.1
  2.1 1.1 convolution_multiply_fusion.9
  3.2 42.1 %psum.84 = f32[16,16]{0,1:T(8,128)S(1)} all-reduce(f32[16,16]{0,1:T(8,128)S(1)} %convolution_multiply_fusion.9), channel_id=1, replica_groups=mesh['parts'=32] {'parts'}, use_global_device_ids=true, to_apply=%region_0.1 | all-reduce | flops 256 | bytes 2048 | tf_op jit(solution)/shard_map/psum | solution.py:57
  45.3 1.5 cholesky.44
  46.8 0.6 compare_reduce_fusion.1
  47.5 0.6 fusion.79
  48.1 1.2 custom-call.12
  49.6 1.0 fusion.99
  50.6 0.5 gather_fusion.3
  51.3 2.5 collective-permute-start
  53.8 0.8 collective-permute-start.2
  54.6 0.7 compare_and_fusion
  55.4 1.1 slice.11
  56.5 4.6 copy.65
  61.1 1.8 gather_fusion.2
  63.0 0.6 gather_fusion.4
  63.6 4.3 fusion.32
  68.0 2.6 fusion.30
  71.0 40.2 %all-reduce = (f32[16,16]{0,1:T(8,128)S(1)}, f32[16,16]{0,1:T(8,128)S(1)}) all-reduce(f32[16,16]{0,1:T(8,128)S(1)} %fusion.21, f32[16,16]{0,1:T(8,128)S(1)} %fusion.20), channel_id=1, replica_groups=mesh['parts'=32] {'parts'}, use_global_device_ids=true, to_apply=%region_3.8 | all-reduce | flops 512 | bytes 4096 | tf_op jit(solution)/shard_map/psum | solution.py:61
  111.3 1.5 cholesky.55
  112.8 0.6 compare_reduce_fusion
  113.5 0.6 select_bitcast_fusion.5
  114.1 1.2 custom-call.13
  115.9 0.7 gather_fusion
  116.6 0.7 gather_fusion.1
  117.5 39.9 %psum.87 = f32[16,16]{0,1:T(8,128)S(1)} all-reduce(f32[16,16]{0,1:T(8,128)S(1)} %convolution_multiply_fusion.8), channel_id=1, replica_groups=mesh['parts'=32] {'parts'}, use_global_device_ids=true, to_apply=%region_5.10 | all-reduce | flops 256 | bytes 2048 | tf_op jit(solution)/shard_map/psum | solution.py:73
  157.7 0.5 gather_fusion.5
  158.3 2.2 collective-permute-start.3
  160.7 1.8 collective-permute-start.5
  162.5 5.0 collective-permute-done.4
  167.5 0.6 gather_fusion.6
  168.1 2.6 convolution_bitcast_fusion.6
  170.8 2.6 convolution_bitcast_fusion.7
  173.7 36.9 %psum.88 = f32[16,16]{0,1:T(8,128)S(1)} all-reduce(f32[16,16]{0,1:T(8,128)S(1)} %convolution_multiply_fusion.7), channel_id=1, replica_groups=mesh['parts'=32] {'parts'}, use_global_device_ids=true, to_apply=%region_6.11 | all-reduce | flops 256 | bytes 2048 | tf_op jit(solution)/shard_map/psum | solution.py:77
  211.0 41.0 %psum.89 = f32[16,16]{0,1:T(8,128)S(1)} all-reduce(f32[16,16]{0,1:T(8,128)S(1)} %convolution_multiply_fusion.6), channel_id=1, replica_groups=mesh['parts'=32] {'parts'}, use_global_device_ids=true, to_apply=%region_7.12 | all-reduce | flops 256 | bytes 2048 | tf_op jit(solution)/shard_map/psum | solution.py:73
  252.3 0.5 gather_fusion.7
  252.9 1.8 collective-permute-start.6
  255.2 1.0 collective-permute-done.6
  256.2 5.3 collective-permute-done.7
  261.6 0.6 gather_fusion.8
  262.2 2.6 convolution_bitcast_fusion.4
  264.8 2.6 convolution_bitcast_fusion.5
  267.7 37.4 %psum.90 = f32[16,16]{0,1:T(8,128)S(1)} all-reduce(f32[16,16]{0,1:T(8,128)S(1)} %convolution_multiply_fusion.5), channel_id=1, replica_groups=mesh['parts'=32] {'parts'}, use_global_device_ids=true, to_apply=%region_8.13 | all-reduce | flops 256 | bytes 2048 | tf_op jit(solution)/shard_map/psum | solution.py:77
  305.5 41.0 %psum.91 = f32[16,16]{0,1:T(8,128)S(1)} all-reduce(f32[16,16]{0,1:T(8,128)S(1)} %convolution_multiply_fusion.4), channel_id=1, replica_groups=mesh['parts'=32] {'parts'}, use_global_device_ids=true, to_apply=%region_9.14 | all-reduce | flops 256 | bytes 2048 | tf_op jit(solution)/shard_map/psum | solution.py:73
  346.9 0.5 gather_fusion.9
  347.5 1.9 collective-permute-start.9
  349.5 1.4 collective-permute-done.9
  350.8 5.3 collective-permute-done.10
  356.2 0.6 gather_fusion.10
  356.8 2.6 convolution_bitcast_fusion.2
  359.4 2.6 convolution_bitcast_fusion.3
  362.3 36.9 %psum.92 = f32[16,16]{0,1:T(8,128)S(1)} all-reduce(f32[16,16]{0,1:T(8,128)S(1)} %convolution_multiply_fusion.3), channel_id=1, replica_groups=mesh['parts'=32] {'parts'}, use_global_device_ids=true, to_apply=%region_10.15 | all-reduce | flops 256 | bytes 2048 | tf_op jit(solution)/shard_map/psum | solution.py:77
  399.7 41.0 %psum.93 = f32[16,16]{0,1:T(8,128)S(1)} all-reduce(f32[16,16]{0,1:T(8,128)S(1)} %convolution_multiply_fusion.2), channel_id=1, replica_groups=mesh['parts'=32] {'parts'}, use_global_device_ids=true, to_apply=%region_11.16 | all-reduce | flops 256 | bytes 2048 | tf_op jit(solution)/shard_map/psum | solution.py:73
  441.0 0.5 gather_fusion.11
  441.6 1.9 collective-permute-start.12
  443.7 1.2 collective-permute-done.12
  444.9 5.5 %collective-permute-done.13 = f32[16,2,128]{2,0,1:T(8,128)S(1)} collective-permute-done((f32[16,2,128]{2,0,1:T(8,128)S(1)}, f32[16,2,128]{2,0,1:T(8,128)S(1)}, u32[]{:S(2)}, u32[]{:S(2)}) %collective-permute-start.13) | collective-permute-done | bytes 16416 | tf_op jit(solution)/shard_map/ppermute | solution.py:15
  450.4 0.6 gather_fusion.12
  451.0 2.6 convolution_bitcast_fusion
  453.7 2.6 convolution_bitcast_fusion.1
  456.6 36.9 %psum.94 = f32[16,16]{0,1:T(8,128)S(1)} all-reduce(f32[16,16]{0,1:T(8,128)S(1)} %convolution_multiply_fusion.1), channel_id=1, replica_groups=mesh['parts'=32] {'parts'}, use_global_device_ids=true, to_apply=%region_12.17 | all-reduce | flops 256 | bytes 2048 | tf_op jit(solution)/shard_map/psum | solution.py:77
  493.9 41.0 %psum.95 = f32[16,16]{0,1:T(8,128)S(1)} all-reduce(f32[16,16]{0,1:T(8,128)S(1)} %convolution_multiply_fusion), channel_id=1, replica_groups=mesh['parts'=32] {'parts'}, use_global_device_ids=true, to_apply=%region_13.18 | all-reduce | flops 256 | bytes 2048 | tf_op jit(solution)/shard_map/psum | solution.py:80
  535.0 0.9 convolution_subtract_fusion
  (100 shorter events, 7.2 us)
Async XLA Ops:
  0.6 67.4 %copy-start = (f32[8,5,128,128]{3,2,1,0:T(8,128)S(1)}, f32[8,5,128,128]{3,2,1,0:T(8,128)}, u32[]{:S(2)}) copy-start(f32[8,5,128,128]{3,2,1,0:T(8,128)} %param.15) | copy-start | bytes 7864324
  51.3 11.7 %collective-permute-start = (f32[16,2,128]{2,0,1:T(8,128)S(1)}, f32[16,2,128]{2,0,1:T(8,128)S(1)}, u32[]{:S(2)}, u32[]{:S(2)}) collective-permute-start(f32[16,2,128]{2,0,1:T(8,128)S(1)} %select_bitcast_fusion.4), channel_id=1, source_target_pairs={{0,31},{1,0},{2,1},{3,2},{4,3},{5,4},{6,5},{7,6},{8,7},{9,8},{10,9... | collective-permute-start | bytes 49160 | tf_op jit(solution)/shard_map/ppermute | solution.py:15
  53.8 9.2 %collective-permute-start.1 = (f32[16,2,128]{2,0,1:T(8,128)S(1)}, f32[16,2,128]{2,0,1:T(8,128)S(1)}, u32[]{:S(2)}, u32[]{:S(2)}) collective-permute-start(f32[16,2,128]{2,0,1:T(8,128)S(1)} %select_bitcast_fusion.4), channel_id=1, source_target_pairs={{0,1},{1,2},{2,3},{3,4},{4,5},{5,6},{6,7},{7,8},{8,9},{9,10},{10,1... | collective-permute-start | bytes 49160 | tf_op jit(solution)/shard_map/ppermute | solution.py:15
  53.8 9.2 %collective-permute-start.2 = (f32[16,2,128]{2,0,1:T(8,128)S(1)}, f32[16,2,128]{2,0,1:T(8,128)S(1)}, u32[]{:S(2)}, u32[]{:S(2)}) collective-permute-start(f32[16,2,128]{2,0,1:T(8,128)S(1)} %select_bitcast_fusion.4), channel_id=1, source_target_pairs={{0,16},{1,17},{2,18},{3,19},{4,20},{5,21},{6,22},{7,23},{8,24},{9,... | collective-permute-start | bytes 49160 | tf_op jit(solution)/shard_map/ppermute | solution.py:15
  117.2 376.2 %copy-start.5 = (f32[16]{0:T(128)}, f32[16]{0:T(128)S(1)}, u32[]{:S(2)}) copy-start(f32[16]{0:T(128)S(1)} %div.47) | copy-start | bytes 196
  158.3 4.2 collective-permute-start.3
  160.5 7.0 %collective-permute-start.4 = (f32[16,2,128]{2,0,1:T(8,128)S(1)}, f32[16,2,128]{2,0,1:T(8,128)S(1)}, u32[]{:S(2)}, u32[]{:S(2)}) collective-permute-start(f32[16,2,128]{2,0,1:T(8,128)S(1)} %select_bitcast_fusion.3), channel_id=1, source_target_pairs={{0,1},{1,2},{2,3},{3,4},{4,5},{5,6},{6,7},{7,8},{8,9},{9,10},{10,1... | collective-permute-start | bytes 49160 | tf_op jit(solution)/shard_map/ppermute | solution.py:15
  160.7 6.8 %collective-permute-start.5 = (f32[16,2,128]{2,0,1:T(8,128)S(1)}, f32[16,2,128]{2,0,1:T(8,128)S(1)}, u32[]{:S(2)}, u32[]{:S(2)}) collective-permute-start(f32[16,2,128]{2,0,1:T(8,128)S(1)} %select_bitcast_fusion.3), channel_id=1, source_target_pairs={{0,16},{1,17},{2,18},{3,19},{4,20},{5,21},{6,22},{7,23},{8,24},{9,... | collective-permute-start | bytes 49160 | tf_op jit(solution)/shard_map/ppermute | solution.py:15
  168.1 2.6 copy-start.1
  252.9 3.3 collective-permute-start.6
  254.8 6.8 %collective-permute-start.7 = (f32[16,2,128]{2,0,1:T(8,128)S(1)}, f32[16,2,128]{2,0,1:T(8,128)S(1)}, u32[]{:S(2)}, u32[]{:S(2)}) collective-permute-start(f32[16,2,128]{2,0,1:T(8,128)S(1)} %select_bitcast_fusion.2), channel_id=1, source_target_pairs={{0,1},{1,2},{2,3},{3,4},{4,5},{5,6},{6,7},{7,8},{8,9},{9,10},{10,1... | collective-permute-start | bytes 49160 | tf_op jit(solution)/shard_map/ppermute | solution.py:15
  254.8 6.8 %collective-permute-start.8 = (f32[16,2,128]{2,0,1:T(8,128)S(1)}, f32[16,2,128]{2,0,1:T(8,128)S(1)}, u32[]{:S(2)}, u32[]{:S(2)}) collective-permute-start(f32[16,2,128]{2,0,1:T(8,128)S(1)} %select_bitcast_fusion.2), channel_id=1, source_target_pairs={{0,16},{1,17},{2,18},{3,19},{4,20},{5,21},{6,22},{7,23},{8,24},{9,... | collective-permute-start | bytes 49160 | tf_op jit(solution)/shard_map/ppermute | solution.py:15
  262.2 2.6 copy-start.2
  347.5 3.3 collective-permute-start.9
  349.4 6.8 %collective-permute-start.10 = (f32[16,2,128]{2,0,1:T(8,128)S(1)}, f32[16,2,128]{2,0,1:T(8,128)S(1)}, u32[]{:S(2)}, u32[]{:S(2)}) collective-permute-start(f32[16,2,128]{2,0,1:T(8,128)S(1)} %select_bitcast_fusion.1), channel_id=1, source_target_pairs={{0,1},{1,2},{2,3},{3,4},{4,5},{5,6},{6,7},{7,8},{8,9},{9,10},{10,1... | collective-permute-start | bytes 49160 | tf_op jit(solution)/shard_map/ppermute | solution.py:15
  349.4 6.8 %collective-permute-start.11 = (f32[16,2,128]{2,0,1:T(8,128)S(1)}, f32[16,2,128]{2,0,1:T(8,128)S(1)}, u32[]{:S(2)}, u32[]{:S(2)}) collective-permute-start(f32[16,2,128]{2,0,1:T(8,128)S(1)} %select_bitcast_fusion.1), channel_id=1, source_target_pairs={{0,16},{1,17},{2,18},{3,19},{4,20},{5,21},{6,22},{7,23},{8,24},{9,... | collective-permute-start | bytes 49160 | tf_op jit(solution)/shard_map/ppermute | solution.py:15
  356.8 2.6 copy-start.3
  441.6 3.3 collective-permute-start.12
  443.5 6.9 %collective-permute-start.13 = (f32[16,2,128]{2,0,1:T(8,128)S(1)}, f32[16,2,128]{2,0,1:T(8,128)S(1)}, u32[]{:S(2)}, u32[]{:S(2)}) collective-permute-start(f32[16,2,128]{2,0,1:T(8,128)S(1)} %select_bitcast_fusion), channel_id=1, source_target_pairs={{0,1},{1,2},{2,3},{3,4},{4,5},{5,6},{6,7},{7,8},{8,9},{9,10},{10,1... | collective-permute-start | bytes 49160 | tf_op jit(solution)/shard_map/ppermute | solution.py:15
  443.7 6.8 %collective-permute-start.14 = (f32[16,2,128]{2,0,1:T(8,128)S(1)}, f32[16,2,128]{2,0,1:T(8,128)S(1)}, u32[]{:S(2)}, u32[]{:S(2)}) collective-permute-start(f32[16,2,128]{2,0,1:T(8,128)S(1)} %select_bitcast_fusion), channel_id=1, source_target_pairs={{0,16},{1,17},{2,18},{3,19},{4,20},{5,21},{6,22},{7,23},{8,24},{9,... | collective-permute-start | bytes 49160 | tf_op jit(solution)/shard_map/ppermute | solution.py:15
  451.0 2.6 copy-start.4
where the time goes:
time: 545 us; the launch traced here: 536 us
  blocking collectives  434 us (80%)
  matrix products  36.2 us (7%)
  waiting for transfers between devices  24.7 us (5%)
  local copies, waits for them, and re-layouts  15 us (3%)
  starting transfers between devices  13.8 us (3%)
  other arithmetic  10.7 us (2%)
    psum x4, blocking collectives, shards(): right = lax.psum(product(correct, ortho.T) * scale, 'parts')  163 us
    psum x4, blocking collectives, shards(): left = lax.psum(product(image, test_basis.T) * scale, 'parts')  148 us
    psum x1, blocking collectives, shards(): gram = lax.psum(product(basis, basis.T) * scale, 'parts')  42.1 us
    psum x1, blocking collectives, shards(): final = lax.psum(product(correct, ortho.T) * scale, 'parts')  41 us
    psum x1, blocking collectives, shards(): lax.psum((product(m_ortho, m_ortho.T) * scale, product(m_ortho, k_ortho.T...  40.2 us
    ppermute x15, waiting for transfers between devices, shifted(): return lax.ppermute(value, axis, pairs)  24.7 us
    dot_general x5, matrix products, apply_pair(): jnp.einsum('ptbc,tbrc->ptr', picked, k_tiles, precision=lax.Precision.HIG...  14.9 us
    ppermute x15, starting transfers between devices, shifted(): return lax.ppermute(value, axis, pairs)  13.8 us
  transfers between devices with their start and end apart: 15, of which 7 were waited for; matrix products, arithmetic and copies ran while one was open for 2% of the time, Pallas kernels for 0%

commit v1 on v0

v1 whole, which is shorter than its diff:
```python
import jax
import jax.numpy as jnp
from jax import lax
from jax.experimental import pallas as pl
from jax.experimental.pallas import tpu as pltpu
from jax.sharding import PartitionSpec as P

relax = 0.4

F32 = jnp.float32
BF16 = jnp.bfloat16
VM = pl.BlockSpec(memory_space=pltpu.VMEM)
SM = pl.BlockSpec(memory_space=pltpu.SMEM)
MAT = 128


def call(kernel, name, outs, specs, scratch=()):
    return pl.pallas_call(
        kernel,
        name=name,
        in_specs=specs,
        out_specs=[VM] * len(outs),
        out_shape=[jax.ShapeDtypeStruct(shape, dtype) for shape, dtype in outs],
        scratch_shapes=list(scratch),
        compiler_params=pltpu.CompilerParams(vmem_limit_bytes=24 << 20),
    )


def mm(left, right):
    return jnp.dot(left, right, precision=lax.Precision.HIGHEST, preferred_element_type=F32)


def nt(left, right):
    return lax.dot_general(
        left, right, (((1,), (1,)), ((), ())), precision=lax.Precision.HIGHEST, preferred_element_type=F32
    )


def split(value):
    high = value.astype(BF16)
    return high, (value - high.astype(F32)).astype(BF16)


def rows(parts):
    return jnp.concatenate(parts, axis=0)


def lanes(parts):
    return jnp.concatenate(parts, axis=1)


def halo_lanes(refs, first, last):
    return lanes([ref[slot, first:last] for ref in refs for slot in range(ref.shape[0])])


def put_sources(xs, at, value):
    n, width = value.shape[0], xs.shape[2]
    for t in range(value.shape[1] // width):
        high, low = split(value[:, t * width : (t + 1) * width])
        xs[at + t, :n] = high
        xs[at + t, n:] = low


def apply_pair(xs, cols, w_high, w_low, k_out, m_out):
    tiles, blocks = cols.shape
    width = xs.shape[2]
    n = xs.shape[1] // 2
    for i in range(tiles):
        lhs = lanes([xs[cols[i, b]] for b in range(blocks)])
        dims = (((1,), (1,)), ((), ()))
        both = lax.dot_general(lhs, w_high[i], dims, preferred_element_type=F32)
        low = lax.dot_general(lhs[:n], w_low[i], dims, preferred_element_type=F32)
        result = both[:n] + both[n:] + low
        k_out[:, i * width : (i + 1) * width] = result[:, :width]
        m_out[:, i * width : (i + 1) * width] = result[:, width:]


def send_tiles(iface, outgoing, at, ref):
    width = outgoing.shape[2]
    n = ref.shape[0]
    for slot in range(outgoing.shape[0]):
        start = pl.multiple_of(iface[slot] * width, width)
        outgoing[slot, at : at + n] = ref[:, pl.ds(start, width)]


def lane_row(shape):
    return lax.broadcasted_iota(jnp.int32, shape, 1), lax.broadcasted_iota(jnp.int32, shape, 0)


def blocks_of(summed, n):
    square = rows([summed, jnp.zeros((MAT - n, MAT), F32)])
    turned = square.T
    return [turned[k * n : (k + 1) * n] for k in range(MAT // n)]


def inverse_chols(grams):
    n = grams[0].shape[0]
    lane, row = lane_row(grams[0].shape)
    states = [g + jnp.where(lane == row + n, 1.0, 0.0) for g in grams]
    for k in range(n - 1):
        for index, a in enumerate(states):
            pivot_row = a[k : k + 1, :]
            factor = a[:, k : k + 1] * (1.0 / a[k : k + 1, k : k + 1])
            states[index] = a - jnp.where(row > k, factor, 0.0) * pivot_row
    out = []
    for a in states:
        pivots = jnp.sum(jnp.where(lane == row, a, 0.0), axis=1, keepdims=True)
        moved = pltpu.roll(a, MAT - n, 1)
        out.append(jnp.where(lane < n, moved, 0.0) * lax.rsqrt(pivots))
    return out


def diagonal(a):
    lane, row = lane_row(a.shape)
    return jnp.sum(jnp.where(lane == row, a, 0.0), axis=1, keepdims=True)


def k_first(iface, basis, outgoing):
    send_tiles(iface, outgoing, 0, basis)


def k_prep(k, m, w_high, w_low, inv_d):
    tiles, blocks, width, _ = k.shape
    row = lax.broadcasted_iota(jnp.int32, (width, width), 0)
    lane = lax.broadcasted_iota(jnp.int32, (width, width), 1)
    for i in range(tiles):
        for b in range(blocks):
            high, low = split(k[i, b])
            w_high[i, :width, b * width : (b + 1) * width] = high
            w_low[i, :width, b * width : (b + 1) * width] = low
            high, low = split(m[i, b])
            w_high[i, width:, b * width : (b + 1) * width] = high
            w_low[i, width:, b * width : (b + 1) * width] = low
        diag = jnp.sum(jnp.where(row == lane, k[i, 0], 0.0), axis=0, keepdims=True)
        inv_d[:, i * width : (i + 1) * width] = 1.0 / diag


def fill_blocks(out, value):
    for device in range(out.shape[0]):
        out[device] = value


def total(ref):
    value = ref[0]
    for device in range(1, ref.shape[0]):
        value = value + ref[device]
    return value


def fold(value):
    half = value.shape[0] // 2
    return value[:half] + pltpu.roll(value[half:], MAT // 2, 1)


def unfold(value):
    lane, _ = lane_row(value.shape)
    keep = lane < MAT // 2
    return rows([jnp.where(keep, value, 0.0), jnp.where(keep, pltpu.roll(value, MAT // 2, 1), 0.0)])


def make_kernels(n, scale):
    def k_a(cols, iface, basis, h_a, h_b, h_f, w_high, w_low, inv_d, kb, mb, u, outgoing, grams, xs):
        put_sources(xs, 0, basis[...])
        put_sources(xs, basis.shape[1] // xs.shape[2], halo_lanes((h_a, h_b, h_f), 0, n))
        apply_pair(xs, cols, w_high, w_low, kb, mb)
        d = inv_d[...]
        u[:n] = kb[...] * d
        u[n:] = mb[...] * d
        send_tiles(iface, outgoing, 0, u)
        right = rows([basis[...], u[...], mb[...], kb[...], jnp.zeros((MAT - 5 * n, basis.shape[1]), F32)])
        both = nt(rows([basis[...], mb[...]]), right) * scale
        lane, _ = lane_row((n, MAT))
        fill_blocks(grams, jnp.where(lane < 3 * n, both[:n], both[n:]))

    def k_b(
        cols, iface, red, basis, kb, mb, u, h_a, h_b, h_f, w_high, w_low, inv_d,
        p_out, image_out, v_out, t_out, ko_out, mo_out, c0_out, words, words_halo, kf_out, small, outgoing,
        theta_out, xs, res,
    ):
        g_bb, g_u1b, g_u2b, g_mm, g_km = blocks_of(total(red), n)[:5]
        inv_v, inv_c = inverse_chols([g_bb, g_mm])
        lv, lc = inv_v[:, :n], inv_c[:, :n]
        cross = nt(mm(lv, g_km[:, :n]), lc)
        mass = nt(mm(lv, g_mm[:, :n]), lc)
        theta = diagonal(cross) * diagonal(inv_c) / diagonal(inv_v)
        e1 = nt(mm(lv, g_u1b[:, :n]), lv)
        e2 = nt(mm(lv, g_u2b[:, :n]), lv)
        ef = nt(mm(lc, g_u2b[:, :n]), lv)
        right = -relax * (e1 - theta * e2)
        pad = jnp.zeros((n, MAT - n), F32)
        for k, value in enumerate((cross, mass, e1, e2, ef)):
            small[k * n : (k + 1) * n] = lanes([value, pad])
        small[5 * n : 6 * n] = jnp.broadcast_to(theta, (n, MAT))
        lane, row = lane_row((n, MAT))
        theta_out[...] = jnp.sum(jnp.where(lane == row, theta, 0.0), axis=0, keepdims=True)[:, :n]
        local = basis.shape[1]
        tiles = local // xs.shape[2]
        u1 = lanes([u[:n], halo_lanes((h_a, h_b, h_f), 0, n)])
        u2 = lanes([u[n:], halo_lanes((h_a, h_b, h_f), n, 2 * n)])
        g1 = mm(lv, u1)
        both = mm(rows([lv, lc]), u2)
        g2, f1 = both[:n], both[n:]
        c0 = -relax * (g1 - theta * g2)
        put_sources(xs, 0, rows([c0, f1]))
        apply_pair(xs, cols, w_high, w_low, res.at[0], res.at[1])
        for k, value in ((0, f1), (3, g1), (4, g2)):
            words[k * n : (k + 1) * n] = value[:, :local]
        for k, value in ((0, f1), (1, g1), (2, g2)):
            words_halo[k * n : (k + 1) * n] = value[:, local:]
        c0_out[...] = c0[:, :local]
        ko = mm(lv, kb[...])
        both = mm(rows([lv, lc]), mb[...])
        mo = both[:n]
        t_out[...] = both[n:]
        ko_out[...] = ko
        mo_out[...] = mo
        v_out[...] = mm(lv, basis[...])
        d = inv_d[...]
        image = res[0, :n] - theta * res[1, :n] - mm(lanes([right, -theta * right]), rows([ko, mo]))
        image_out[...] = image
        kf_out[:n] = res[0, n:]
        kf_out[n:] = res[1, n:]
        words[n : 2 * n] = res[0, n:] * d
        words[2 * n : 3 * n] = res[1, n:] * d
        p_out[...] = 2.0 * c0[:, :local] - relax * d * image
        send_tiles(iface, outgoing, 0, p_out)
        send_tiles(iface, outgoing, n, words.at[n : 3 * n])

    def half(cols, p, halo, small, c0, w_high, w_low, inv_d, xs, res):
        put_sources(xs, 0, p)
        put_sources(xs, p.shape[1] // xs.shape[2], halo)
        apply_pair(xs, cols, w_high, w_low, res.at[0], res.at[1])
        theta = small[5 * n : 6 * n, :1]
        image = res[0] - theta * res[1]
        return image, p + c0[...] - relax * inv_d[...] * image

    def k_c(
        cols, iface, p, h_a, h_b, h_f, image0, v, t, c0, words, kf, small, w_high, w_low, inv_d,
        p_out, outgoing, grams, xs, res,
    ):
        image, fresh = half(
            cols, p[...], halo_lanes((h_a, h_b, h_f), 0, n), small, c0, w_high, w_low, inv_d, xs, res
        )
        p_out[...] = fresh
        send_tiles(iface, outgoing, 0, p_out)
        right = rows([image0[...], kf[...], image, p[...], words[n : 3 * n], fresh])
        both = nt(rows([t[...], v[...]]), right) * scale
        lane, _ = lane_row((n, MAT))
        fill_blocks(grams, jnp.where(lane < 4 * n, both[:n], both[n:]))

    def solve(small, g_left, g_kf, g_mf, g_a, g_p, g_h1, g_h2, g_fresh):
        cross, mass, e1, e2, ef = (small[k * n : (k + 1) * n, :n] for k in range(5))
        theta = small[5 * n : 6 * n, :1]
        right = g_p + relax * mm(g_left, ef)
        left = (
            g_a
            + mm(lanes([relax * g_left, -relax * theta * g_left]), rows([g_kf, g_mf]))
            + mm(lanes([-right, theta * right]), rows([cross, mass]))
        )
        coef = lanes(
            [
                relax * (g_left + left),
                -relax * relax * g_left,
                relax * relax * theta * g_left,
                relax * right,
                -relax * theta * right,
            ]
        )
        after = g_fresh + mm(coef, rows([ef, g_h1, g_h2, e1, e2]))
        return coef, after

    def k_d(
        cols, iface, red, p, h_a, h_b, h_f, q_a, q_b, q_f, ko, mo, c0, words, words_halo, small,
        w_high, w_low, inv_d, p_out, image_out, words_grams, outgoing, xs, res,
    ):
        g = [value[:, :n] for value in blocks_of(total(red), n)]
        g_left, g_kf, g_mf, g_a, g_p, g_h1, g_h2, g_fresh = g
        pad = jnp.zeros((n, MAT - n), F32)
        for k, value in enumerate((g_kf, g_mf, g_h1, g_h2)):
            words_grams[k * n : (k + 1) * n] = lanes([value, pad])
        coef, right = solve(small, *g)
        theta = small[5 * n : 6 * n, :1]
        local = p.shape[1]
        c_local = p[...] + mm(coef, words[...])
        around = rows([words_halo[:n], halo_lanes((q_a, q_b, q_f), n, 3 * n), words_halo[n:]])
        c_halo = halo_lanes((h_a, h_b, h_f), 0, n) + mm(coef, around)
        put_sources(xs, 0, c_local)
        put_sources(xs, local // xs.shape[2], c_halo)
        apply_pair(xs, cols, w_high, w_low, res.at[0], res.at[1])
        image = res[0] - theta * res[1] - mm(lanes([right, -theta * right]), rows([ko[...], mo[...]]))
        image_out[...] = image
        p_out[...] = c_local + c0[...] - relax * inv_d[...] * image
        send_tiles(iface, outgoing, 0, p_out)

    def k_e(
        cols, p, h_a, h_b, h_f, image2, v, t, c0, small, w_high, w_low, inv_d, p_out, grams, xs, res
    ):
        image, fresh = half(
            cols, p[...], halo_lanes((h_a, h_b, h_f), 0, n), small, c0, w_high, w_low, inv_d, xs, res
        )
        p_out[...] = fresh
        right = rows([image2[...], image, p[...], fresh, jnp.zeros((MAT - 4 * n, p.shape[1]), F32)])
        both = nt(rows([t[...], v[...]]), right) * scale
        lane, _ = lane_row((n, MAT))
        fill_blocks(grams, fold(jnp.where(lane < 2 * n, both[:n], both[n:])))

    def k_f(red, p, v, words, small, words_grams, out):
        g_left, g_a, g_p, g_fresh = (value[:, :n] for value in blocks_of(unfold(total(red)), n)[:4])
        g_kf, g_mf, g_h1, g_h2 = (words_grams[k * n : (k + 1) * n, :n] for k in range(4))
        coef, right = solve(small, g_left, g_kf, g_mf, g_a, g_p, g_h1, g_h2, g_fresh)
        out[...] = p[...] + mm(lanes([coef, -right]), rows([words[...], v[...]]))

    return k_a, k_b, k_c, k_d, k_e, k_f


def shards(basis, k_tiles, m_tiles, tile_part, tile_slot, iface):
    n, local = basis.shape
    tiles, blocks, width, _ = k_tiles.shape
    count = iface.shape[0]
    parts = lax.axis_size("parts")
    me = lax.axis_index("parts")
    half_way = parts // 2
    scale = 1.0 / (local * parts)
    chip = [(source, source ^ 1) for source in range(parts)]
    other = [(source, (source + 1 if source % 2 else source - 1) % parts) for source in range(parts)]
    far = [(source, (source + half_way) % parts) for source in range(parts)]

    remote = jnp.where(
        tile_part == me ^ 1, 0, jnp.where(tile_part == (me + half_way) % parts, 2 * count, count)
    )
    cols = jnp.where(tile_part == me, tile_slot, tiles + remote + tile_slot)

    def halo(outgoing):
        return [lax.ppermute(outgoing, "parts", pairs) for pairs in (chip, other, far)]

    def reduced(blocks_out):
        return lax.all_to_all(blocks_out, "parts", 0, 0, tiled=True)

    k_a, k_b, k_c, k_d, k_e, k_f = make_kernels(n, scale)
    sources = tiles + 3 * count
    xs = lambda m: pltpu.VMEM((sources, 2 * m, width), BF16)
    vec = ((n, local), F32)
    out = lambda m: ((count, m, width), F32)
    grams16 = ((parts, n, MAT), F32)
    grams8 = ((parts, n // 2, MAT), F32)

    (outgoing,) = call(k_first, "first", [out(n)], [SM, VM])(iface, basis)
    h0 = halo(outgoing)
    w_high, w_low, inv_d = call(
        k_prep,
        "prep",
        [((tiles, 2 * width, blocks * width), BF16)] * 2 + [((1, local), F32)],
        [VM, VM],
    )(k_tiles, m_tiles)
    w = (w_high, w_low, inv_d)
    kb, mb, u, outgoing, grams = call(
        k_a, "level0", [vec, vec, ((2 * n, local), F32), out(2 * n), grams16], [SM, SM] + [VM] * 7, [xs(n)]
    )(cols, iface, basis, *h0, *w)
    red = reduced(grams)
    h1 = halo(outgoing)
    p1, image0, v, t, ko, mo, c0, words, words_halo, kf, small, outgoing, theta = call(
        k_b,
        "level1",
        [vec] * 7
        + [((5 * n, local), F32), ((3 * n, 3 * count * width), F32), ((2 * n, local), F32)]
        + [((6 * n, MAT), F32), out(3 * n), ((1, n), F32)],
        [SM, SM] + [VM] * 11,
        [xs(2 * n), pltpu.VMEM((2, 2 * n, local), F32)],
    )(cols, iface, red, basis, kb, mb, u, *h1, *w)
    h2 = halo(outgoing)
    res = pltpu.VMEM((2, n, local), F32)
    p2, outgoing, grams = call(k_c, "level2", [vec, out(n), grams16], [SM, SM] + [VM] * 14, [xs(n), res])(
        cols, iface, p1, *h2, image0, v, t, c0, words, kf, small, *w
    )
    red = reduced(grams)
    h3 = halo(outgoing)
    p3, image2, words_grams, outgoing = call(
        k_d, "level3", [vec, vec, ((4 * n, MAT), F32), out(n)], [SM, SM] + [VM] * 17, [xs(n), res]
    )(cols, iface, red, p2, *h3, *h2, ko, mo, c0, words, words_halo, small, *w)
    h4 = halo(outgoing)
    p4, grams = call(k_e, "level4", [vec, grams8], [SM] + [VM] * 12, [xs(n), res])(
        cols, p3, *h4, image2, v, t, c0, small, *w
    )
    red = reduced(grams)
    (correct,) = call(k_f, "last", [vec], [VM] * 6)(red, p4, v, words, small, words_grams)
    return (correct, theta.reshape(-1))


def solution(mesh):
    placed = (
        P(None, "parts"),
        P("parts", None, None, None),
        P("parts", None, None, None),
        P("parts", None),
        P("parts", None),
        P("parts"),
    )
    return jax.shard_map(
        shards, mesh=mesh, in_specs=placed, out_specs=(P(None, "parts"), P()), check_vma=False
    )
```

time: 545 us -> 116 us (0.21); the launches traced: 536 us -> 115 us
  blocking collectives: 434 us -> 9.97 us
  matrix products: 36.2 us -> 0 us
  Pallas kernels: 0 us -> 20.4 us
  starting transfers between devices: 13.8 us -> 30.3 us
  local copies, waits for them, and re-layouts: 15 us -> 31.1 us
  other arithmetic: 10.7 us -> 0.71 us
    psum x11 -> x0, blocking collectives: 434 us -> none  [the longest x4 163 us: shards(): right = lax.psum(product(correct, ortho.T) * scale, 'parts')]
    dot_general x34 -> x0, matrix products: 35.8 us -> none  [the longest x5 14.9 us: apply_pair(): jnp.einsum('ptbc,tbrc->ptr', picked, k_tiles, precision=lax.Precision.HIG...]
    unnamed x33 -> x96, local copies, waits for them, and re-layouts: 4.76 us -> 31.1 us
    pallas_call x0 -> x8, Pallas kernels: none -> 20.4 us  [the longest x1 5.39 us: shards(): call(k_b, 'level1', [vec] * 7 + [((5 * n, local), F32), ((3 * n, 3 * coun...]
    ppermute x15, starting transfers between devices: 13.8 us -> 24.1 us  [halo(): lax.ppermute(outgoing, 'parts', pairs)]
    all_to_all x0 -> x1, blocking collectives: none -> 9.97 us  [reduced(): return lax.all_to_all(blocks_out, 'parts', 0, 0, tiled=True)]
    gather x14 -> x0, local copies, waits for them, and re-layouts: 8.89 us -> none  [the longest x5 2.98 us: apply_pair(): picked = jnp.take(sources, columns, axis=1)]
    another operation x10 -> x0, other arithmetic: 8.01 us -> none  [the longest x4 3.75 us: inverse_lower(): return jax.scipy.linalg.solve_triangular(chol, eye, lower=True)]
  transfers between devices with their start and end apart: 15 -> 17, of which waited for: 7 -> 8; matrix products, arithmetic and copies ran while one was open for 2% -> 1% of each run, Pallas kernels for 0% -> 1%
where the time goes in v1:
time: 116 us; the launch traced here: 115 us
  local copies, waits for them, and re-layouts  31.1 us (27%)
  starting transfers between devices  30.3 us (26%)
  waiting for transfers between devices  21.2 us (18%)
  Pallas kernels  20.4 us (18%)
  blocking collectives  9.97 us (9%)
    unnamed x96, local copies, waits for them, and re-layouts  31.1 us
    ppermute x15, starting transfers between devices, halo(): lax.ppermute(outgoing, 'parts', pairs)  24.1 us
    ppermute x15, waiting for transfers between devices, halo(): lax.ppermute(outgoing, 'parts', pairs)  21.2 us
    all_to_all x1, blocking collectives, reduced(): return lax.all_to_all(blocks_out, 'parts', 0, 0, tiled=True)  9.97 us
    all_to_all x2, starting transfers between devices, reduced(): return lax.all_to_all(blocks_out, 'parts', 0, 0, tiled=True)  6.27 us
    pallas_call x1, Pallas kernels, shards(): call(k_b, 'level1', [vec] * 7 + [((5 * n, local), F32), ((3 * n, 3 * coun...  5.39 us
    pallas_call x1, Pallas kernels, shards(): call(k_a, 'level0', [vec, vec, ((2 * n, local), F32), out(2 * n), grams16...  3.34 us
    pallas_call x1, Pallas kernels, shards(): call(k_d, 'level3', [vec, vec, ((4 * n, MAT), F32), out(n)], [SM, SM] + [...  3.09 us
  transfers between devices with their start and end apart: 17, of which 8 were waited for; matrix products, arithmetic and copies ran while one was open for 1% of the time, Pallas kernels for 1%

profile of v1, /device:TPU:0, one launch (start us, length us, event | category | flops | bytes accessed | tf_op | source)
XLA Modules:
  0.0 114.6 jit_solution(14794395752222555471)
XLA Ops:
  0.6 0.8 copy-done.5
  1.5 0.7 copy-done.42
  2.7 4.1 %collective-permute-start.2 = (f32[2,16,128]{2,1,0:T(8,128)S(1)}, f32[2,16,128]{2,1,0:T(8,128)S(1)}, u32[]{:S(2)}, u32[]{:S(2)}) collective-permute-start(f32[2,16,128]{2,1,0:T(8,128)S(1)} %first.1), channel_id=1, source_target_pairs={{0,16},{1,17},{2,18},{3,19},{4,20},{5,21},{6,22},{7,23},{8,24},{9,... | collective-permute-start | bytes 49160 | tf_op jit(solution)/shard_map/ppermute | solution.py:334
  6.8 2.4 %collective-permute-start.1 = (f32[2,16,128]{2,1,0:T(8,128)S(1)}, f32[2,16,128]{2,1,0:T(8,128)S(1)}, u32[]{:S(2)}, u32[]{:S(2)}) collective-permute-start(f32[2,16,128]{2,1,0:T(8,128)S(1)} %first.1), channel_id=1, source_target_pairs={{0,31},{1,2},{2,1},{3,4},{4,3},{5,6},{6,5},{7,8},{8,7},{9,10},{10,... | collective-permute-start | bytes 49160 | tf_op jit(solution)/shard_map/ppermute | solution.py:334
  9.2 0.7 add_select_fusion.cols
  9.9 1.7 %copy-done.3 = f32[8,5,128,128]{3,2,1,0:T(8,128)S(1)} copy-done((f32[8,5,128,128]{3,2,1,0:T(8,128)S(1)}, f32[8,5,128,128]{3,2,1,0:T(8,128)}, u32[]{:S(2)}) %copy-start.3) | copy-done | bytes 2621464
  11.7 1.7 %copy-done.4 = f32[8,5,128,128]{3,2,1,0:T(8,128)S(1)} copy-done((f32[8,5,128,128]{3,2,1,0:T(8,128)S(1)}, f32[8,5,128,128]{3,2,1,0:T(8,128)}, u32[]{:S(2)}) %copy-start.4) | copy-done | bytes 2621464
  13.4 0.9 prep.1
  14.4 3.3 %level0.1 = (f32[16,1024]{1,0:T(8,128)S(1)}, f32[16,1024]{1,0:T(8,128)S(1)}, f32[32,1024]{1,0:T(8,128)S(1)}, f32[2,32,128]{2,1,0:T(8,128)S(1)}, f32[32,16,128]{2,1,0:T(8,128)}) custom-call(s32[8,5]{1,0:T(8,128)S(1)} %add_select_fusion.cols, s32[2]{0:T(128)S(1)} %copy-done.43, f32[16,1024]{1,0:T(8,128)S(1)} %copy-done.6, ...), custom_call_target="tpu_custom_call" | custom-call | tf_op jit(solution)/shard_map/level0/pallas_call | solution.py:356
  17.7 0.6 copy-done.46
  18.4 3.7 %all-to-all-start = ((f32[32,16,128]{2,1,0:T(8,128)}), f32[32,16,128]{2,1,0:T(8,128)S(1)}, u32[]{:S(2)}, u32[]{:S(2)}) async-start(f32[32,16,128]{2,1,0:T(8,128)} %get-tuple-element.35), calls=%async_computation | async-start | bytes 524288 | tf_op jit(solution)/shard_map/all_to_all | solution.py:337
  22.0 2.7 %collective-permute-start.5 = (f32[2,32,128]{2,1,0:T(8,128)}, f32[2,32,128]{2,1,0:T(8,128)S(1)}, u32[]{:S(2)}, u32[]{:S(2)}) collective-permute-start(f32[2,32,128]{2,1,0:T(8,128)} %copy-done.46), channel_id=1, source_target_pairs={{0,16},{1,17},{2,18},{3,19},{4,20},{5,21},{6,22},{7,23},{8,24},{9,... | collective-permute-start | bytes 98312 | tf_op jit(solution)/shard_map/ppermute | solution.py:334
  24.8 2.7 %collective-permute-start.4 = (f32[2,32,128]{2,1,0:T(8,128)}, f32[2,32,128]{2,1,0:T(8,128)S(1)}, u32[]{:S(2)}, u32[]{:S(2)}) collective-permute-start(f32[2,32,128]{2,1,0:T(8,128)} %copy-done.46), channel_id=1, source_target_pairs={{0,31},{1,2},{2,1},{3,4},{4,3},{5,6},{6,5},{7,8},{8,7},{9,10},{10,... | collective-permute-start | bytes 98312 | tf_op jit(solution)/shard_map/ppermute | solution.py:334
  27.5 5.3 %collective-permute-done.5.h_f = f32[2,32,128]{2,1,0:T(8,128)S(1)} collective-permute-done((f32[2,32,128]{2,1,0:T(8,128)}, f32[2,32,128]{2,1,0:T(8,128)S(1)}, u32[]{:S(2)}, u32[]{:S(2)}) %collective-permute-start.5) | collective-permute-done | bytes 32800 | tf_op jit(solution)/shard_map/ppermute | solution.py:334
  32.8 0.6 copy-done.30
  33.6 0.6 copy-done.32
  34.3 0.6 copy-done.34
  34.9 1.7 %copy-done.1 = bf16[8,256,640]{2,1,0:T(8,128)(2,1)S(1)} copy-done((bf16[8,256,640]{2,1,0:T(8,128)(2,1)S(1)}, bf16[8,256,640]{2,1,0:T(8,128)(2,1)}, u32[]{:S(2)}) %copy-start.1) | copy-done | bytes 2621464
  36.6 0.9 copy-done.16
  37.5 0.8 copy-done.25
  38.4 0.8 copy-done.27
  39.2 0.8 copy-done.31
  40.0 0.8 copy-done.33
  40.7 0.8 copy-done.35
  41.5 5.4 %level1.1 = (f32[16,1024]{1,0:T(8,128)S(1)}, f32[16,1024]{1,0:T(8,128)S(1)}, f32[16,1024]{1,0:T(8,128)S(1)}, f32[16,1024]{1,0:T(8,128)S(1)}, f32[16,1024]{1,0:T(...) custom-call(s32[8,5]{1,0:T(8,128)S(1)} %add_select_fusion.cols, ...), custom_call_target="tpu_custom_call" | custom-call | tf_op jit(solution)/shard_map/level1/pallas_call | solution.py:361
  46.9 0.7 copy-done.10
  47.6 0.6 copy-done.20
  48.2 0.6 copy-done.22
  48.8 1.9 %collective-permute-start.8 = (f32[2,48,128]{2,1,0:T(8,128)S(1)}, f32[2,48,128]{2,1,0:T(8,128)S(1)}, u32[]{:S(2)}, u32[]{:S(2)}) collective-permute-start(f32[2,48,128]{2,1,0:T(8,128)S(1)} %get-tuple-element.41), channel_id=1, source_target_pairs={{0,16},{1,17},{2,18},{3,19},{4,20},{5,21},{6,22},{7,23},{8,24},{9,... | collective-permute-start | bytes 147464 | tf_op jit(solution)/shard_map/ppermute | solution.py:334
  50.7 1.5 %collective-permute-start.7 = (f32[2,48,128]{2,1,0:T(8,128)S(1)}, f32[2,48,128]{2,1,0:T(8,128)S(1)}, u32[]{:S(2)}, u32[]{:S(2)}) collective-permute-start(f32[2,48,128]{2,1,0:T(8,128)S(1)} %get-tuple-element.41), channel_id=1, source_target_pairs={{0,31},{1,2},{2,1},{3,4},{4,3},{5,6},{6,5},{7,8},{8,7},{9,10},{10,... | collective-permute-start | bytes 147464 | tf_op jit(solution)/shard_map/ppermute | solution.py:334
  52.2 1.7 %collective-permute-done.8.h_f.q_f = f32[2,48,128]{2,1,0:T(8,128)S(1)} collective-permute-done((f32[2,48,128]{2,1,0:T(8,128)S(1)}, f32[2,48,128]{2,1,0:T(8,128)S(1)}, u32[]{:S(2)}, u32[]{:S(2)}) %collective-permute-start.8) | collective-permute-done | bytes 49184 | tf_op jit(solution)/shard_map/ppermute | solution.py:334
  53.9 3.9 %collective-permute-done.7.h_b.q_b = f32[2,48,128]{2,1,0:T(8,128)S(1)} collective-permute-done((f32[2,48,128]{2,1,0:T(8,128)S(1)}, f32[2,48,128]{2,1,0:T(8,128)S(1)}, u32[]{:S(2)}, u32[]{:S(2)}) %collective-permute-start.7) | collective-permute-done | bytes 49184 | tf_op jit(solution)/shard_map/ppermute | solution.py:334
  57.8 0.7 copy-done.13
  58.5 0.7 copy-done.18
  59.2 2.9 %level2.1 = (f32[16,1024]{1,0:T(8,128)S(1)}, f32[2,16,128]{2,1,0:T(8,128)S(1)}, f32[32,16,128]{2,1,0:T(8,128)S(1)}) custom-call(s32[8,5]{1,0:T(8,128)S(1)} %copy-done.13, s32[2]{0:T(128)S(1)} %copy-done.44, f32[16,1024]{1,0:T(8,128)S(1)} %get-tuple-element.40.p, f32[2,48,128]{2,1,0:T(8,128)S(1)} %collective-permute-done.6.h_a.q_a, ...), custom_call_target="tpu_custom_call" | custom-call | tf_op jit(solution)/shard_map/level2/pallas_call | solution.py:372
  62.0 0.7 copy-done.7
  62.7 0.6 copy-done.28
  63.4 0.6 copy-done.47
  64.0 2.6 %all-to-all-start.1 = ((f32[32,16,128]{2,1,0:T(8,128)}), f32[32,16,128]{2,1,0:T(8,128)S(1)}, u32[]{:S(2)}, u32[]{:S(2)}) async-start(f32[32,16,128]{2,1,0:T(8,128)} %copy-done.7), calls=%async_computation.1 | async-start | bytes 524288 | tf_op jit(solution)/shard_map/all_to_all | solution.py:337
  66.6 2.7 %collective-permute-start.11 = (f32[2,16,128]{2,1,0:T(8,128)}, f32[2,16,128]{2,1,0:T(8,128)S(1)}, u32[]{:S(2)}, u32[]{:S(2)}) collective-permute-start(f32[2,16,128]{2,1,0:T(8,128)} %copy-done.47), channel_id=1, source_target_pairs={{0,16},{1,17},{2,18},{3,19},{4,20},{5,21},{6,22},{7,23},{8,24},{9,... | collective-permute-start | bytes 49160 | tf_op jit(solution)/shard_map/ppermute | solution.py:334
  69.3 2.7 %collective-permute-start.10 = (f32[2,16,128]{2,1,0:T(8,128)}, f32[2,16,128]{2,1,0:T(8,128)S(1)}, u32[]{:S(2)}, u32[]{:S(2)}) collective-permute-start(f32[2,16,128]{2,1,0:T(8,128)} %copy-done.47), channel_id=1, source_target_pairs={{0,31},{1,2},{2,1},{3,4},{4,3},{5,6},{6,5},{7,8},{8,7},{9,10},{10,... | collective-permute-start | bytes 49160 | tf_op jit(solution)/shard_map/ppermute | solution.py:334
  72.0 4.6 %collective-permute-done.11.h_f = f32[2,16,128]{2,1,0:T(8,128)S(1)} collective-permute-done((f32[2,16,128]{2,1,0:T(8,128)}, f32[2,16,128]{2,1,0:T(8,128)S(1)}, u32[]{:S(2)}, u32[]{:S(2)}) %collective-permute-start.11) | collective-permute-done | bytes 16416 | tf_op jit(solution)/shard_map/ppermute | solution.py:334
  76.6 0.6 copy-done.36
  78.0 0.6 copy-done.40
  78.6 1.7 %copy-done.2 = bf16[8,256,640]{2,1,0:T(8,128)(2,1)S(1)} copy-done((bf16[8,256,640]{2,1,0:T(8,128)(2,1)S(1)}, bf16[8,256,640]{2,1,0:T(8,128)(2,1)}, u32[]{:S(2)}) %copy-start.2) | copy-done | bytes 2621464
  80.4 0.8 copy-done.9
  81.2 0.9 copy-done.11
  82.1 0.7 copy-done.14
  82.8 0.7 copy-done.19
  83.5 0.8 copy-done.21
  84.3 0.8 copy-done.23
  85.1 0.8 copy-done.29
  86.0 0.7 copy-done.37
  86.7 0.7 copy-done.39
  87.4 0.7 copy-done.41
  88.1 0.7 copy-done.45
  88.8 3.1 %level3.1 = (f32[16,1024]{1,0:T(8,128)S(1)}, f32[16,1024]{1,0:T(8,128)S(1)}, f32[64,128]{1,0:T(8,128)S(1)}, f32[2,16,128]{2,1,0:T(8,128)S(1)}) custom-call(s32[8,5]{1,0:T(8,128)S(1)} %copy-done.14, s32[2]{0:T(128)S(1)} %copy-done.45, f32[32,16,128]{2,1,0:T(8,128)S(1)} %all-to-all-done.1.red, f32[16,1024]{1,0:T(8,128)S(1)} %copy-done.29, ...), custom_call_target="tpu_custom_call" | custom-call | tf_op jit(solution)/shard_map/level3/pallas_call | solution.py:377
  91.9 1.7 %collective-permute-start.14 = (f32[2,16,128]{2,1,0:T(8,128)S(1)}, f32[2,16,128]{2,1,0:T(8,128)S(1)}, u32[]{:S(2)}, u32[]{:S(2)}) collective-permute-start(f32[2,16,128]{2,1,0:T(8,128)S(1)} %get-tuple-element.56), channel_id=1, source_target_pairs={{0,16},{1,17},{2,18},{3,19},{4,20},{5,21},{6,22},{7,23},{8,24},{9,... | collective-permute-start | bytes 49160 | tf_op jit(solution)/shard_map/ppermute | solution.py:334
  93.6 1.6 %collective-permute-start.13 = (f32[2,16,128]{2,1,0:T(8,128)S(1)}, f32[2,16,128]{2,1,0:T(8,128)S(1)}, u32[]{:S(2)}, u32[]{:S(2)}) collective-permute-start(f32[2,16,128]{2,1,0:T(8,128)S(1)} %get-tuple-element.56), channel_id=1, source_target_pairs={{0,31},{1,2},{2,1},{3,4},{4,3},{5,6},{6,5},{7,8},{8,7},{9,10},{10,... | collective-permute-start | bytes 49160 | tf_op jit(solution)/shard_map/ppermute | solution.py:334
  95.1 1.5 %collective-permute-done.14.h_f = f32[2,16,128]{2,1,0:T(8,128)S(1)} collective-permute-done((f32[2,16,128]{2,1,0:T(8,128)S(1)}, f32[2,16,128]{2,1,0:T(8,128)S(1)}, u32[]{:S(2)}, u32[]{:S(2)}) %collective-permute-start.14) | collective-permute-done | bytes 16416 | tf_op jit(solution)/shard_map/ppermute | solution.py:334
  96.7 3.6 %collective-permute-done.13.h_b = f32[2,16,128]{2,1,0:T(8,128)S(1)} collective-permute-done((f32[2,16,128]{2,1,0:T(8,128)S(1)}, f32[2,16,128]{2,1,0:T(8,128)S(1)}, u32[]{:S(2)}, u32[]{:S(2)}) %collective-permute-start.13) | collective-permute-done | bytes 16416 | tf_op jit(solution)/shard_map/ppermute | solution.py:334
  100.3 2.6 %level4.1 = (f32[16,1024]{1,0:T(8,128)S(1)}, f32[32,8,128]{2,1,0:T(8,128)S(1)}) custom-call(s32[8,5]{1,0:T(8,128)S(1)} %copy-done.14, f32[16,1024]{1,0:T(8,128)S(1)} %get-tuple-element.55.p, f32[2,16,128]{2,1,0:T(8,128)S(1)} %collective-permute-done.12.h_a, f32[2,16,128]{2,1,0:T(8,128)S(1)} %collective-permute-done.13.h_b, ...), custom_call_target="tpu_custom_call" | custom-call | tf_op jit(solution)/shard_map/level4/pallas_call | solution.py:381
  102.9 10.0 %all_to_all.15.red = f32[32,8,128]{2,1,0:T(8,128)S(1)} all-to-all(f32[32,8,128]{2,1,0:T(8,128)S(1)} %get-tuple-element.58), channel_id=1, replica_groups=mesh['parts'=32] {'parts'}, dimensions={0} | all-to-all | bytes 262144 | tf_op jit(solution)/shard_map/all_to_all | solution.py:337
  112.9 1.7 %last.1 = f32[16,1024]{1,0:T(8,128)} custom-call(f32[32,8,128]{2,1,0:T(8,128)S(1)} %all_to_all.15.red, f32[16,1024]{1,0:T(8,128)S(1)} %get-tuple-element.59.p, f32[16,1024]{1,0:T(8,128)S(1)} %get-tuple-element.43.v, f32[80,1024]{1,0:T(8,128)S(1)} %get-tuple-element.46.words, f32[96,128]{1,0:T(8,128)S(1)} %get-tuple-element.48.small, ...), custom_call_target="tpu_custom_call" | custom-call | tf_op jit(solution)/shard_map/last/pallas_call | solution.py:385
  (76 shorter events, 1.7 us)
Async XLA Ops:
  0.6 0.8 copy-start.5
  1.5 0.7 copy-start.42
  2.7 11.7 %collective-permute-start.2 = (f32[2,16,128]{2,1,0:T(8,128)S(1)}, f32[2,16,128]{2,1,0:T(8,128)S(1)}, u32[]{:S(2)}, u32[]{:S(2)}) collective-permute-start(f32[2,16,128]{2,1,0:T(8,128)S(1)} %first.1), channel_id=1, source_target_pairs={{0,16},{1,17},{2,18},{3,19},{4,20},{5,21},{6,22},{7,23},{8,24},{9,... | collective-permute-start | bytes 49160 | tf_op jit(solution)/shard_map/ppermute | solution.py:334
  6.8 7.5 %collective-permute-start.1 = (f32[2,16,128]{2,1,0:T(8,128)S(1)}, f32[2,16,128]{2,1,0:T(8,128)S(1)}, u32[]{:S(2)}, u32[]{:S(2)}) collective-permute-start(f32[2,16,128]{2,1,0:T(8,128)S(1)} %first.1), channel_id=1, source_target_pairs={{0,31},{1,2},{2,1},{3,4},{4,3},{5,6},{6,5},{7,8},{8,7},{9,10},{10,... | collective-permute-start | bytes 49160 | tf_op jit(solution)/shard_map/ppermute | solution.py:334
  9.2 5.1 %collective-permute-start = (f32[2,16,128]{2,1,0:T(8,128)S(1)}, f32[2,16,128]{2,1,0:T(8,128)S(1)}, u32[]{:S(2)}, u32[]{:S(2)}) collective-permute-start(f32[2,16,128]{2,1,0:T(8,128)S(1)} %first.1), channel_id=1, source_target_pairs={{0,1},{1,0},{2,3},{3,2},{4,5},{5,4},{6,7},{7,6},{8,9},{9,8},{10,11... | collective-permute-start | bytes 49160 | tf_op jit(solution)/shard_map/ppermute | solution.py:334
  9.9 1.7 %copy-start.3 = (f32[8,5,128,128]{3,2,1,0:T(8,128)S(1)}, f32[8,5,128,128]{3,2,1,0:T(8,128)}, u32[]{:S(2)}) copy-start(f32[8,5,128,128]{3,2,1,0:T(8,128)} %k.1) | copy-start | bytes 7864324
  11.7 1.7 %copy-start.4 = (f32[8,5,128,128]{3,2,1,0:T(8,128)S(1)}, f32[8,5,128,128]{3,2,1,0:T(8,128)}, u32[]{:S(2)}) copy-start(f32[8,5,128,128]{3,2,1,0:T(8,128)} %m.1) | copy-start | bytes 7864324
  13.4 21.5 %copy-start.12 = (s32[8,5]{1,0:T(8,128)}, s32[8,5]{1,0:T(8,128)S(1)}, u32[]{:S(2)}) copy-start(s32[8,5]{1,0:T(8,128)S(1)} %add_select_fusion.cols) | copy-start | bytes 484
  13.4 1.0 copy-start.6
  13.4 1.0 copy-start.43
  14.3 3.4 %copy-start = (bf16[8,256,640]{2,1,0:T(8,128)(2,1)}, bf16[8,256,640]{2,1,0:T(8,128)(2,1)S(1)}, u32[]{:S(2)}) copy-start(bf16[8,256,640]{2,1,0:T(8,128)(2,1)S(1)} %get-tuple-element.33.w_low) | copy-start | bytes 7864324
  14.3 20.6 %copy-start.17 = (f32[1,1024]{1,0:T(1,128)}, f32[1,1024]{1,0:T(1,128)S(1)}, u32[]{:S(2)}) copy-start(f32[1,1024]{1,0:T(1,128)S(1)} %get-tuple-element.34.inv_d) | copy-start | bytes 12292
  17.7 0.6 copy-start.46
  18.4 16.5 %copy-start.15 = (f32[32,1024]{1,0:T(8,128)}, f32[32,1024]{1,0:T(8,128)S(1)}, u32[]{:S(2)}) copy-start(f32[32,1024]{1,0:T(8,128)S(1)} %get-tuple-element.38.u) | copy-start | bytes 393220
  18.4 16.5 %copy-start.24 = (f32[16,1024]{1,0:T(8,128)}, f32[16,1024]{1,0:T(8,128)S(1)}, u32[]{:S(2)}) copy-start(f32[16,1024]{1,0:T(8,128)S(1)} %get-tuple-element.36.kb) | copy-start | bytes 196612
  18.4 16.5 %copy-start.26 = (f32[16,1024]{1,0:T(8,128)}, f32[16,1024]{1,0:T(8,128)S(1)}, u32[]{:S(2)}) copy-start(f32[16,1024]{1,0:T(8,128)S(1)} %get-tuple-element.37.mb) | copy-start | bytes 196612
  18.4 16.5 %all-to-all-start = ((f32[32,16,128]{2,1,0:T(8,128)}), f32[32,16,128]{2,1,0:T(8,128)S(1)}, u32[]{:S(2)}, u32[]{:S(2)}) async-start(f32[32,16,128]{2,1,0:T(8,128)} %get-tuple-element.35), calls=%async_computation | async-start | bytes 524288 | tf_op jit(solution)/shard_map/all_to_all | solution.py:337
  22.0 10.8 %collective-permute-start.5 = (f32[2,32,128]{2,1,0:T(8,128)}, f32[2,32,128]{2,1,0:T(8,128)S(1)}, u32[]{:S(2)}, u32[]{:S(2)}) collective-permute-start(f32[2,32,128]{2,1,0:T(8,128)} %copy-done.46), channel_id=1, source_target_pairs={{0,16},{1,17},{2,18},{3,19},{4,20},{5,21},{6,22},{7,23},{8,24},{9,... | collective-permute-start | bytes 98312 | tf_op jit(solution)/shard_map/ppermute | solution.py:334
  24.8 8.8 %collective-permute-start.4 = (f32[2,32,128]{2,1,0:T(8,128)}, f32[2,32,128]{2,1,0:T(8,128)S(1)}, u32[]{:S(2)}, u32[]{:S(2)}) collective-permute-start(f32[2,32,128]{2,1,0:T(8,128)} %copy-done.46), channel_id=1, source_target_pairs={{0,31},{1,2},{2,1},{3,4},{4,3},{5,6},{6,5},{7,8},{8,7},{9,10},{10,... | collective-permute-start | bytes 98312 | tf_op jit(solution)/shard_map/ppermute | solution.py:334
  27.5 6.8 %collective-permute-start.3 = (f32[2,32,128]{2,1,0:T(8,128)}, f32[2,32,128]{2,1,0:T(8,128)S(1)}, u32[]{:S(2)}, u32[]{:S(2)}) collective-permute-start(f32[2,32,128]{2,1,0:T(8,128)} %copy-done.46), channel_id=1, source_target_pairs={{0,1},{1,0},{2,3},{3,2},{4,5},{5,4},{6,7},{7,6},{8,9},{9,8},{10,11... | collective-permute-start | bytes 98312 | tf_op jit(solution)/shard_map/ppermute | solution.py:334
  32.8 0.6 copy-start.30
  33.6 0.6 copy-start.32
  34.3 0.6 copy-start.34
  34.9 1.7 %copy-start.1 = (bf16[8,256,640]{2,1,0:T(8,128)(2,1)S(1)}, bf16[8,256,640]{2,1,0:T(8,128)(2,1)}, u32[]{:S(2)}) copy-start(bf16[8,256,640]{2,1,0:T(8,128)(2,1)} %copy-done) | copy-start | bytes 7864324
  36.6 0.9 copy-start.16
  37.5 0.8 copy-start.25
  38.4 0.8 copy-start.27
  39.2 0.8 copy-start.31
  40.0 0.8 copy-start.33
  40.7 0.8 copy-start.35
  41.5 16.3 %copy-start.44 = (s32[2]{0:T(128)S(1)}, s32[2]{0:T(128)}, u32[]{:S(2)}) copy-start(s32[2]{0:T(128)} %iface.9) | copy-start | bytes 28
  46.9 0.7 copy-start.10
  47.6 0.6 copy-start.20
  48.2 0.6 copy-start.22
  48.8 5.1 %collective-permute-start.8 = (f32[2,48,128]{2,1,0:T(8,128)S(1)}, f32[2,48,128]{2,1,0:T(8,128)S(1)}, u32[]{:S(2)}, u32[]{:S(2)}) collective-permute-start(f32[2,48,128]{2,1,0:T(8,128)S(1)} %get-tuple-element.41), channel_id=1, source_target_pairs={{0,16},{1,17},{2,18},{3,19},{4,20},{5,21},{6,22},{7,23},{8,24},{9,... | collective-permute-start | bytes 147464 | tf_op jit(solution)/shard_map/ppermute | solution.py:334
  50.7 7.1 %collective-permute-start.7 = (f32[2,48,128]{2,1,0:T(8,128)S(1)}, f32[2,48,128]{2,1,0:T(8,128)S(1)}, u32[]{:S(2)}, u32[]{:S(2)}) collective-permute-start(f32[2,48,128]{2,1,0:T(8,128)S(1)} %get-tuple-element.41), channel_id=1, source_target_pairs={{0,31},{1,2},{2,1},{3,4},{4,3},{5,6},{6,5},{7,8},{8,7},{9,10},{10,... | collective-permute-start | bytes 147464 | tf_op jit(solution)/shard_map/ppermute | solution.py:334
  52.2 5.6 %collective-permute-start.6 = (f32[2,48,128]{2,1,0:T(8,128)S(1)}, f32[2,48,128]{2,1,0:T(8,128)S(1)}, u32[]{:S(2)}, u32[]{:S(2)}) collective-permute-start(f32[2,48,128]{2,1,0:T(8,128)S(1)} %get-tuple-element.41), channel_id=1, source_target_pairs={{0,1},{1,0},{2,3},{3,2},{4,5},{5,4},{6,7},{7,6},{8,9},{9,8},{10,11... | collective-permute-start | bytes 147464 | tf_op jit(solution)/shard_map/ppermute | solution.py:334
  57.8 4.2 %copy-start.8 = (f32[2,48,128]{2,1,0:T(8,128)}, f32[2,48,128]{2,1,0:T(8,128)S(1)}, u32[]{:S(2)}) copy-start(f32[2,48,128]{2,1,0:T(8,128)S(1)} %collective-permute-done.6.h_a.q_a) | copy-start | bytes 147460
  57.8 0.7 copy-start.13
  58.5 0.7 copy-start.18
  62.0 0.7 copy-start.7
  62.7 0.6 copy-start.28
  63.4 0.6 copy-start.47
  64.0 14.7 %all-to-all-start.1 = ((f32[32,16,128]{2,1,0:T(8,128)}), f32[32,16,128]{2,1,0:T(8,128)S(1)}, u32[]{:S(2)}, u32[]{:S(2)}) async-start(f32[32,16,128]{2,1,0:T(8,128)} %copy-done.7), calls=%async_computation.1 | async-start | bytes 524288 | tf_op jit(solution)/shard_map/all_to_all | solution.py:337
  66.6 10.0 %collective-permute-start.11 = (f32[2,16,128]{2,1,0:T(8,128)}, f32[2,16,128]{2,1,0:T(8,128)S(1)}, u32[]{:S(2)}, u32[]{:S(2)}) collective-permute-start(f32[2,16,128]{2,1,0:T(8,128)} %copy-done.47), channel_id=1, source_target_pairs={{0,16},{1,17},{2,18},{3,19},{4,20},{5,21},{6,22},{7,23},{8,24},{9,... | collective-permute-start | bytes 49160 | tf_op jit(solution)/shard_map/ppermute | solution.py:334
  69.3 8.2 %collective-permute-start.10 = (f32[2,16,128]{2,1,0:T(8,128)}, f32[2,16,128]{2,1,0:T(8,128)S(1)}, u32[]{:S(2)}, u32[]{:S(2)}) collective-permute-start(f32[2,16,128]{2,1,0:T(8,128)} %copy-done.47), channel_id=1, source_target_pairs={{0,31},{1,2},{2,1},{3,4},{4,3},{5,6},{6,5},{7,8},{8,7},{9,10},{10,... | collective-permute-start | bytes 49160 | tf_op jit(solution)/shard_map/ppermute | solution.py:334
  72.0 6.1 %collective-permute-start.9 = (f32[2,16,128]{2,1,0:T(8,128)}, f32[2,16,128]{2,1,0:T(8,128)S(1)}, u32[]{:S(2)}, u32[]{:S(2)}) collective-permute-start(f32[2,16,128]{2,1,0:T(8,128)} %copy-done.47), channel_id=1, source_target_pairs={{0,1},{1,0},{2,3},{3,2},{4,5},{5,4},{6,7},{7,6},{8,9},{9,8},{10,11... | collective-permute-start | bytes 49160 | tf_op jit(solution)/shard_map/ppermute | solution.py:334
  76.6 0.6 copy-start.36
  78.0 0.6 copy-start.40
  78.6 1.7 %copy-start.2 = (bf16[8,256,640]{2,1,0:T(8,128)(2,1)S(1)}, bf16[8,256,640]{2,1,0:T(8,128)(2,1)}, u32[]{:S(2)}) copy-start(bf16[8,256,640]{2,1,0:T(8,128)(2,1)} %copy-done) | copy-start | bytes 7864324
  80.4 0.8 copy-start.9
  81.2 0.9 copy-start.11
  82.1 0.7 copy-start.14
  82.8 0.7 copy-start.19
  83.4 0.8 copy-start.21
  84.3 0.8 copy-start.23
  85.1 0.8 copy-start.29
  86.0 0.7 copy-start.37
  86.7 0.7 copy-start.39
  87.4 0.7 copy-start.41
  88.1 0.7 copy-start.45
  91.9 4.8 %collective-permute-start.14 = (f32[2,16,128]{2,1,0:T(8,128)S(1)}, f32[2,16,128]{2,1,0:T(8,128)S(1)}, u32[]{:S(2)}, u32[]{:S(2)}) collective-permute-start(f32[2,16,128]{2,1,0:T(8,128)S(1)} %get-tuple-element.56), channel_id=1, source_target_pairs={{0,16},{1,17},{2,18},{3,19},{4,20},{5,21},{6,22},{7,23},{8,24},{9,... | collective-permute-start | bytes 49160 | tf_op jit(solution)/shard_map/ppermute | solution.py:334
  93.6 6.8 %collective-permute-start.13 = (f32[2,16,128]{2,1,0:T(8,128)S(1)}, f32[2,16,128]{2,1,0:T(8,128)S(1)}, u32[]{:S(2)}, u32[]{:S(2)}) collective-permute-start(f32[2,16,128]{2,1,0:T(8,128)S(1)} %get-tuple-element.56), channel_id=1, source_target_pairs={{0,31},{1,2},{2,1},{3,4},{4,3},{5,6},{6,5},{7,8},{8,7},{9,10},{10,... | collective-permute-start | bytes 49160 | tf_op jit(solution)/shard_map/ppermute | solution.py:334
  95.1 5.2 %collective-permute-start.12 = (f32[2,16,128]{2,1,0:T(8,128)S(1)}, f32[2,16,128]{2,1,0:T(8,128)S(1)}, u32[]{:S(2)}, u32[]{:S(2)}) collective-permute-start(f32[2,16,128]{2,1,0:T(8,128)S(1)} %get-tuple-element.56), channel_id=1, source_target_pairs={{0,1},{1,0},{2,3},{3,2},{4,5},{5,4},{6,7},{7,6},{8,9},{9,8},{10,11... | collective-permute-start | bytes 49160 | tf_op jit(solution)/shard_map/ppermute | solution.py:334
  (1 other events, 0.6 us)

commit v2 on v1

v2 whole, which is shorter than its diff:
```python
import jax
import jax.numpy as jnp
from jax import lax
from jax.experimental import pallas as pl
from jax.experimental.pallas import tpu as pltpu
from jax.sharding import PartitionSpec as P

relax = 0.4

F32 = jnp.float32
BF16 = jnp.bfloat16
VM = pl.BlockSpec(memory_space=pltpu.VMEM)
SM = pl.BlockSpec(memory_space=pltpu.SMEM)
HBM = pl.BlockSpec(memory_space=pltpu.MemorySpace.HBM)
MAT = 128


def call(kernel, outs, specs, scratch=()):
    return pl.pallas_call(
        kernel,
        in_specs=specs,
        out_specs=[VM] * len(outs),
        out_shape=[jax.ShapeDtypeStruct(shape, dtype) for shape, dtype in outs],
        scratch_shapes=list(scratch),
        compiler_params=pltpu.CompilerParams(vmem_limit_bytes=24 << 20),
    )


def in_hbm(value):
    return pltpu.with_memory_space_constraint(value, pltpu.MemorySpace.HBM)


def mm(left, right):
    return jnp.dot(left, right, precision=lax.Precision.HIGHEST, preferred_element_type=F32)


def nt(left, right):
    return lax.dot_general(
        left, right, (((1,), (1,)), ((), ())), precision=lax.Precision.HIGHEST, preferred_element_type=F32
    )


def split(value):
    high = value.astype(BF16)
    return high, (value - high.astype(F32)).astype(BF16)


def rows(parts):
    return jnp.concatenate(parts, axis=0)


def lanes(parts):
    return jnp.concatenate(parts, axis=1)


def halo_lanes(refs, first, last):
    return lanes([ref[slot, first:last] for ref in refs for slot in range(ref.shape[0])])


def put_sources(xs, at, value):
    n, width = value.shape[0], xs.shape[2]
    for t in range(value.shape[1] // width):
        high, low = split(value[:, t * width : (t + 1) * width])
        xs[at + t, :n] = high
        xs[at + t, n:] = low


def apply_pair(xs, cols, w_high, w_low, k_out, m_out):
    tiles, blocks = cols.shape
    width = xs.shape[2]
    n = xs.shape[1] // 2
    for i in range(tiles):
        lhs = lanes([xs[cols[i, b]] for b in range(blocks)])
        both = jnp.dot(lhs, w_high[i], preferred_element_type=F32)
        low = jnp.dot(lhs[:n], w_low[i], preferred_element_type=F32)
        result = both[:n] + both[n:] + low
        k_out[:, i * width : (i + 1) * width] = result[:, :width]
        m_out[:, i * width : (i + 1) * width] = result[:, width:]


def send_tiles(iface, outgoing, at, ref):
    width = outgoing.shape[2]
    n = ref.shape[0]
    for slot in range(outgoing.shape[0]):
        start = pl.multiple_of(iface[slot] * width, width)
        outgoing[slot, at : at + n] = ref[:, pl.ds(start, width)]


def lane_row(shape):
    return lax.broadcasted_iota(jnp.int32, shape, 1), lax.broadcasted_iota(jnp.int32, shape, 0)


def blocks_of(summed, n):
    square = rows([summed, jnp.zeros((MAT - n, MAT), F32)])
    turned = square.T
    return [turned[k * n : (k + 1) * n] for k in range(MAT // n)]


def inverse_chols(grams):
    n = grams[0].shape[0]
    lane, row = lane_row(grams[0].shape)
    states = [g + jnp.where(lane == row + n, 1.0, 0.0) for g in grams]
    for k in range(n - 1):
        for index, a in enumerate(states):
            pivot_row = a[k : k + 1, :]
            factor = a[:, k : k + 1] * (1.0 / a[k : k + 1, k : k + 1])
            states[index] = a - jnp.where(row > k, factor, 0.0) * pivot_row
    out = []
    for a in states:
        pivots = jnp.sum(jnp.where(lane == row, a, 0.0), axis=1, keepdims=True)
        moved = pltpu.roll(a, MAT - n, 1)
        out.append(jnp.where(lane < n, moved, 0.0) * lax.rsqrt(pivots))
    return out


def diagonal(a):
    lane, row = lane_row(a.shape)
    return jnp.sum(jnp.where(lane == row, a, 0.0), axis=1, keepdims=True)


def k_first(iface_hbm, basis, outgoing, iface, sems):
    copy = pltpu.make_async_copy(iface_hbm, iface, sems.at[0])
    copy.start()
    copy.wait()
    width = outgoing.shape[2]
    copies = []
    for slot in range(outgoing.shape[0]):
        start = pl.multiple_of(iface[slot] * width, width)
        copy = pltpu.make_async_copy(basis.at[:, pl.ds(start, width)], outgoing.at[slot], sems.at[slot])
        copy.start()
        copies.append(copy)
    for copy in copies:
        copy.wait()


def make_prep(count):
    def k_prep(part_hbm, slot_hbm, k_hbm, m_hbm, w_high, w_low, inv_d, cols, k, m, part_in, slot_in, sems):
        tiles, blocks, width, _ = k.shape
        pattern = [
            pltpu.make_async_copy(source, target, sems.at[which, tiles])
            for which, (source, target) in enumerate(((part_hbm, part_in), (slot_hbm, slot_in)))
        ]
        for copy in pattern:
            copy.start()
        copies = []
        for i in range(tiles):
            pair = [
                pltpu.make_async_copy(source.at[i], target.at[i], sems.at[which, i])
                for which, (source, target) in enumerate(((k_hbm, k), (m_hbm, m)))
            ]
            for copy in pair:
                copy.start()
            copies.append(pair)
        parts = lax.axis_size("parts")
        me = lax.axis_index("parts")
        for copy in pattern:
            copy.wait()
        part, slot = part_in[...], slot_in[...]
        remote = jnp.where(part == me ^ 1, 0, jnp.where(part == (me + parts // 2) % parts, count, 2 * count))
        cols[...] = jnp.where(part == me, slot, tiles + remote + slot)
        row = lax.broadcasted_iota(jnp.int32, (width, width), 0)
        lane = lax.broadcasted_iota(jnp.int32, (width, width), 1)
        for i in range(tiles):
            for which, source in enumerate((k, m)):
                copies[i][which].wait()
                for b in range(blocks):
                    high, low = split(source[i, b].T)
                    w_high[i, b * width : (b + 1) * width, which * width : (which + 1) * width] = high
                    w_low[i, b * width : (b + 1) * width, which * width : (which + 1) * width] = low
            diag = jnp.sum(jnp.where(row == lane, k[i, 0], 0.0), axis=0, keepdims=True)
            inv_d[:, i * width : (i + 1) * width] = 1.0 / diag

    return k_prep


def fill_blocks(out, value):
    for device in range(out.shape[0]):
        out[device] = value


def total(ref):
    value = ref[0]
    for device in range(1, ref.shape[0]):
        value = value + ref[device]
    return value


def fold(value):
    half = value.shape[0] // 2
    return value[:half] + pltpu.roll(value[half:], MAT // 2, 1)


def unfold(value):
    lane, _ = lane_row(value.shape)
    keep = lane < MAT // 2
    return rows([jnp.where(keep, value, 0.0), jnp.where(keep, pltpu.roll(value, MAT // 2, 1), 0.0)])


def make_kernels(n, scale):
    def put_small(ref, k, value):
        ref[k * n : (k + 1) * n] = jnp.broadcast_to(value, (n, MAT)) if value.shape[1] == 1 else lanes(
            [value, jnp.zeros((n, MAT - n), F32)]
        )

    def get_small(ref, k):
        return ref[k * n : (k + 1) * n, :n]

    def k_a(cols, iface, basis, h_a, h_f, h_b, w_high, w_low, inv_d, kb, mb, u, outgoing, grams, xs):
        put_sources(xs, 0, basis[...])
        put_sources(xs, basis.shape[1] // xs.shape[2], halo_lanes((h_a, h_f, h_b), 0, n))
        apply_pair(xs, cols, w_high, w_low, kb, mb)
        d = inv_d[...]
        u[:n] = kb[...] * d
        u[n:] = mb[...] * d
        send_tiles(iface, outgoing, 0, u)
        right = rows([basis[...], u[...], mb[...], kb[...], jnp.zeros((MAT - 5 * n, basis.shape[1]), F32)])
        both = nt(rows([basis[...], mb[...]]), right) * scale
        lane, _ = lane_row((n, MAT))
        fill_blocks(grams, jnp.where(lane < 3 * n, both[:n], both[n:]))

    def k_b0(red, basis, kb, mb, u, v_out, t_out, ko_out, mo_out, c0_out, words, small, theta_out):
        g_bb, g_u1b, g_u2b, g_mm, g_km = blocks_of(total(red), n)[:5]
        inv_v, inv_c = inverse_chols([g_bb, g_mm])
        lv, lc = inv_v[:, :n], inv_c[:, :n]
        cross = nt(mm(lv, g_km[:, :n]), lc)
        theta = diagonal(cross) * diagonal(inv_c) / diagonal(inv_v)
        g1 = mm(lv, u[:n])
        both = mm(rows([lv, lc]), u[n:])
        g2, f1 = both[:n], both[n:]
        for k, value in ((0, f1), (3, g1), (4, g2)):
            words[k * n : (k + 1) * n] = value
        c0_out[...] = -relax * (g1 - theta * g2)
        ko_out[...] = mm(lv, kb[...])
        both = mm(rows([lv, lc]), mb[...])
        mo_out[...] = both[:n]
        t_out[...] = both[n:]
        v_out[...] = mm(lv, basis[...])
        mass = nt(mm(lv, g_mm[:, :n]), lc)
        e1 = nt(mm(lv, g_u1b[:, :n]), lv)
        e2 = nt(mm(lv, g_u2b[:, :n]), lv)
        ef = nt(mm(lc, g_u2b[:, :n]), lv)
        right = -relax * (e1 - theta * e2)
        for k, value in enumerate((cross, mass, e1, e2, ef, theta, lv, lc, right)):
            put_small(small, k, value)
        lane, row = lane_row((n, MAT))
        theta_out[...] = jnp.sum(jnp.where(lane == row, theta, 0.0), axis=0, keepdims=True)[:, :n]

    def k_b1(
        cols, iface, h_a, h_f, h_b, w_high, w_low, inv_d, ko, mo, c0, words_in, small,
        p_out, image_out, words, words_halo, kf_out, outgoing, xs, res,
    ):
        lv, lc, right = (get_small(small, k) for k in (6, 7, 8))
        theta = small[5 * n : 6 * n, :1]
        g1 = mm(lv, halo_lanes((h_a, h_f, h_b), 0, n))
        both = mm(rows([lv, lc]), halo_lanes((h_a, h_f, h_b), n, 2 * n))
        g2, f1 = both[:n], both[n:]
        put_sources(xs, 0, rows([c0[...], words_in[:n]]))
        put_sources(xs, c0.shape[1] // xs.shape[2], rows([-relax * (g1 - theta * g2), f1]))
        apply_pair(xs, cols, w_high, w_low, res.at[0], res.at[1])
        for k, value in ((0, f1), (1, g1), (2, g2)):
            words_halo[k * n : (k + 1) * n] = value
        d = inv_d[...]
        image = res[0, :n] - theta * res[1, :n] - mm(lanes([right, -theta * right]), rows([ko[...], mo[...]]))
        image_out[...] = image
        kf_out[:n] = res[0, n:]
        kf_out[n:] = res[1, n:]
        words[:n] = words_in[:n]
        words[n : 2 * n] = res[0, n:] * d
        words[2 * n : 3 * n] = res[1, n:] * d
        words[3 * n :] = words_in[3 * n :]
        p_out[...] = 2.0 * c0[...] - relax * d * image
        send_tiles(iface, outgoing, 0, p_out)
        send_tiles(iface, outgoing, n, words.at[n : 3 * n])

    def half(cols, p, halo, small, c0, w_high, w_low, inv_d, xs, res):
        put_sources(xs, 0, p)
        put_sources(xs, p.shape[1] // xs.shape[2], halo)
        apply_pair(xs, cols, w_high, w_low, res.at[0], res.at[1])
        theta = small[5 * n : 6 * n, :1]
        image = res[0] - theta * res[1]
        return image, p + c0[...] - relax * inv_d[...] * image

    def k_c(
        cols, iface, p, h_a, h_f, h_b, image0, v, t, c0, words, kf, small, w_high, w_low, inv_d,
        p_out, outgoing, grams, xs, res,
    ):
        image, fresh = half(
            cols, p[...], halo_lanes((h_a, h_f, h_b), 0, n), small, c0, w_high, w_low, inv_d, xs, res
        )
        p_out[...] = fresh
        send_tiles(iface, outgoing, 0, p_out)
        right = rows([image0[...], kf[...], image, p[...], words[n : 3 * n], fresh])
        both = nt(rows([t[...], v[...]]), right) * scale
        lane, _ = lane_row((n, MAT))
        fill_blocks(grams, jnp.where(lane < 4 * n, both[:n], both[n:]))

    def solve(small, g_left, g_kf, g_mf, g_a, g_p, g_h1, g_h2, g_fresh):
        cross, mass, e1, e2, ef = (get_small(small, k) for k in range(5))
        theta = small[5 * n : 6 * n, :1]
        right = g_p + relax * mm(g_left, ef)
        left = (
            g_a
            + mm(lanes([relax * g_left, -relax * theta * g_left]), rows([g_kf, g_mf]))
            + mm(lanes([-right, theta * right]), rows([cross, mass]))
        )
        coef = lanes(
            [
                relax * (g_left + left),
                -relax * relax * g_left,
                relax * relax * theta * g_left,
                relax * right,
                -relax * theta * right,
            ]
        )
        after = g_fresh + mm(coef, rows([ef, g_h1, g_h2, e1, e2]))
        return coef, after

    def k_d0(red, p, words, small, c_out, words_grams, coefs):
        g = [value[:, :n] for value in blocks_of(total(red), n)]
        coef, right = solve(small, *g)
        for k, index in enumerate((1, 2, 5, 6)):
            put_small(words_grams, k, g[index])
        coefs[:n] = lanes([coef, jnp.zeros((n, MAT - 5 * n), F32)])
        put_small(coefs, 1, right)
        c_out[...] = p[...] + mm(coef, words[...])

    def k_d1(
        cols, iface, c_local, coefs, h_a, h_f, h_b, q_a, q_f, q_b, ko, mo, c0, words_halo, small,
        w_high, w_low, inv_d, p_out, image_out, outgoing, xs, res,
    ):
        coef, right = coefs[:n, : 5 * n], get_small(coefs, 1)
        theta = small[5 * n : 6 * n, :1]
        around = rows([words_halo[:n], halo_lanes((q_a, q_f, q_b), n, 3 * n), words_halo[n:]])
        c_halo = halo_lanes((h_a, h_f, h_b), 0, n) + mm(coef, around)
        put_sources(xs, 0, c_local[...])
        put_sources(xs, c_local.shape[1] // xs.shape[2], c_halo)
        apply_pair(xs, cols, w_high, w_low, res.at[0], res.at[1])
        image = res[0] - theta * res[1] - mm(lanes([right, -theta * right]), rows([ko[...], mo[...]]))
        image_out[...] = image
        p_out[...] = c_local[...] + c0[...] - relax * inv_d[...] * image
        send_tiles(iface, outgoing, 0, p_out)

    def k_e(
        cols, p, h_a, h_f, h_b, image2, v, t, c0, small, w_high, w_low, inv_d, p_out, grams, xs, res
    ):
        image, fresh = half(
            cols, p[...], halo_lanes((h_a, h_f, h_b), 0, n), small, c0, w_high, w_low, inv_d, xs, res
        )
        p_out[...] = fresh
        right = rows([image2[...], image, p[...], fresh, jnp.zeros((MAT - 4 * n, p.shape[1]), F32)])
        both = nt(rows([t[...], v[...]]), right) * scale
        lane, _ = lane_row((n, MAT))
        fill_blocks(grams, fold(jnp.where(lane < 2 * n, both[:n], both[n:])))

    def k_f(red, p, v, words, small, words_grams, out):
        g_left, g_a, g_p, g_fresh = (value[:, :n] for value in blocks_of(unfold(total(red)), n)[:4])
        g_kf, g_mf, g_h1, g_h2 = (get_small(words_grams, k) for k in range(4))
        coef, right = solve(small, g_left, g_kf, g_mf, g_a, g_p, g_h1, g_h2, g_fresh)
        out[...] = p[...] + mm(lanes([coef, -right]), rows([words[...], v[...]]))

    return k_a, k_b0, k_b1, k_c, k_d0, k_d1, k_e, k_f


def ordered(first, second):
    return lax.optimization_barrier((first, second))


def shards(basis, k_tiles, m_tiles, tile_part, tile_slot, iface):
    n, local = basis.shape
    tiles, blocks, width, _ = k_tiles.shape
    count = iface.shape[0]
    parts = lax.axis_size("parts")
    half_way = parts // 2
    scale = 1.0 / (local * parts)
    chip = [(source, source ^ 1) for source in range(parts)]
    other = [(source, (source + 1 if source % 2 else source - 1) % parts) for source in range(parts)]
    far = [(source, (source + half_way) % parts) for source in range(parts)]

    def halo(outgoing):
        return [lax.ppermute(outgoing, "parts", pairs) for pairs in (chip, far, other)]

    def reduced(blocks_out):
        return lax.all_to_all(blocks_out, "parts", 0, 0, tiled=True)

    k_a, k_b0, k_b1, k_c, k_d0, k_d1, k_e, k_f = make_kernels(n, scale)
    sources = tiles + 3 * count
    xs = lambda m: pltpu.VMEM((sources, 2 * m, width), BF16)
    vec = ((n, local), F32)
    vecs = lambda m: ((m * n, local), F32)
    mats = lambda m: ((m * n, MAT), F32)
    out = lambda m: ((count, m, width), F32)
    grams16 = ((parts, n, MAT), F32)
    grams8 = ((parts, n // 2, MAT), F32)
    res = pltpu.VMEM((2, n, local), F32)

    (outgoing,) = call(
        k_first, [out(n)], [HBM, HBM], [pltpu.SMEM((count,), jnp.int32), pltpu.SemaphoreType.DMA((count,))]
    )(in_hbm(iface), in_hbm(basis))
    h0 = halo(outgoing)
    w_high, w_low, inv_d, cols = call(
        make_prep(count),
        [((tiles, blocks * width, 2 * width), BF16)] * 2 + [((1, local), F32), ((tiles, blocks), jnp.int32)],
        [HBM] * 4,
        [pltpu.VMEM(k_tiles.shape, F32)] * 2
        + [pltpu.VMEM((tiles, blocks), jnp.int32)] * 2
        + [pltpu.SemaphoreType.DMA((2, tiles + 1))],
    )(*(in_hbm(value) for value in (tile_part, tile_slot, k_tiles, m_tiles)))
    w = (w_high, w_low, inv_d)
    kb, mb, u, outgoing, grams = call(
        k_a, [vec, vec, vecs(2), out(2 * n), grams16], [SM, SM] + [VM] * 7, [xs(n)]
    )(cols, iface, basis, *h0, *w)
    red, outgoing = ordered(reduced(grams), outgoing)
    h1 = halo(outgoing)
    v, t, ko, mo, c0, words, small, theta = call(
        k_b0, [vec] * 5 + [vecs(5), mats(9), ((1, n), F32)], [VM] * 5
    )(red, basis, kb, mb, u)
    p1, image0, words, words_halo, kf, outgoing = call(
        k_b1,
        [vec, vec, vecs(5), ((3 * n, 3 * count * width), F32), vecs(2), out(3 * n)],
        [SM, SM] + [VM] * 11,
        [xs(2 * n), pltpu.VMEM((2, 2 * n, local), F32)],
    )(cols, iface, *h1, *w, ko, mo, c0, words, small)
    h2 = halo(outgoing)
    p2, outgoing, grams = call(k_c, [vec, out(n), grams16], [SM, SM] + [VM] * 14, [xs(n), res])(
        cols, iface, p1, *h2, image0, v, t, c0, words, kf, small, *w
    )
    red, outgoing = ordered(reduced(grams), outgoing)
    h3 = halo(outgoing)
    c2, words_grams, coefs = call(k_d0, [vec, mats(4), mats(2)], [VM] * 4)(red, p2, words, small)
    p3, image2, outgoing = call(k_d1, [vec, vec, out(n)], [SM, SM] + [VM] * 16, [xs(n), res])(
        cols, iface, c2, coefs, *h3, *h2, ko, mo, c0, words_halo, small, *w
    )
    h4 = halo(outgoing)
    p4, grams = call(k_e, [vec, grams8], [SM] + [VM] * 12, [xs(n), res])(cols, p3, *h4, image2, v, t, c0, small, *w)
    red = reduced(grams)
    (correct,) = call(k_f, [vec], [VM] * 6)(red, p4, v, words, small, words_grams)
    return (correct, theta.reshape(-1))


def solution(mesh):
    placed = (
        P(None, "parts"),
        P("parts", None, None, None),
        P("parts", None, None, None),
        P("parts", None),
        P("parts", None),
        P("parts"),
    )
    return jax.shard_map(
        shards, mesh=mesh, in_specs=placed, out_specs=(P(None, "parts"), P()), check_vma=False
    )
```

time: 116 us -> 89.3 us (0.77); the launches traced: 115 us -> 89.1 us
  local copies, waits for them, and re-layouts: 31.1 us -> 0.01 us
  blocking collectives: 9.97 us -> 36.4 us
  starting transfers between devices: 30.3 us -> 15 us
  waiting for transfers between devices: 21.2 us -> 16.6 us
    unnamed x96 -> x4, local copies, waits for them, and re-layouts: 31.1 us -> 0.01 us
    all_to_all x1 -> x3, blocking collectives: 9.97 us -> 36.4 us  [reduced(): return lax.all_to_all(blocks_out, 'parts', 0, 0, tiled=True)]
    ppermute x15, starting transfers between devices: 24.1 us -> 15 us  [halo(): lax.ppermute(outgoing, 'parts', pairs)]
    all_to_all x2 -> x0, starting transfers between devices: 6.27 us -> none  [reduced(): return lax.all_to_all(blocks_out, 'parts', 0, 0, tiled=True)]
    ppermute x15, waiting for transfers between devices: 21.2 us -> 16.6 us  [halo(): lax.ppermute(outgoing, 'parts', pairs)]
    pallas_call x8 -> x10, Pallas kernels: 20.4 us -> 20.4 us  [the longest x1 3.94 us: shards(): call(make_prep(count), [((tiles, blocks * width, 2 * width), BF16)] * 2 +...]
  transfers between devices with their start and end apart: 17 -> 15, of which waited for: 8 -> 5; matrix products, arithmetic and copies ran while one was open for 1% -> 0% of each run, Pallas kernels for 1% -> 8%
where the time goes in v2:
time: 89.3 us; the launch traced here: 89.1 us
  blocking collectives  36.4 us (41%)
  Pallas kernels  20.4 us (23%)
  waiting for transfers between devices  16.6 us (19%)
  starting transfers between devices  15 us (17%)
    all_to_all x3, blocking collectives, reduced(): return lax.all_to_all(blocks_out, 'parts', 0, 0, tiled=True)  36.4 us
    ppermute x15, waiting for transfers between devices, halo(): lax.ppermute(outgoing, 'parts', pairs)  16.6 us
    ppermute x15, starting transfers between devices, halo(): lax.ppermute(outgoing, 'parts', pairs)  15 us
    pallas_call x1, Pallas kernels, shards(): call(make_prep(count), [((tiles, blocks * width, 2 * width), BF16)] * 2 +...  3.94 us
    pallas_call x1, Pallas kernels, shards(): call(k_b0, [vec] * 5 + [vecs(5), mats(9), ((1, n), F32)], [VM] * 5)  2.66 us
    pallas_call x1, Pallas kernels, shards(): call(k_c, [vec, out(n), grams16], [SM, SM] + [VM] * 14, [xs(n), res])  2.22 us
    pallas_call x1, Pallas kernels, shards(): call(k_b1, [vec, vec, vecs(5), ((3 * n, 3 * count * width), F32), vecs(2)...  2.02 us
    pallas_call x1, Pallas kernels, shards(): call(k_a, [vec, vec, vecs(2), out(2 * n), grams16], [SM, SM] + [VM] * 7,...  1.93 us
  transfers between devices with their start and end apart: 15, of which 5 were waited for; matrix products, arithmetic and copies ran while one was open for 0% of the time, Pallas kernels for 8%

profile of v2, /device:TPU:0, one launch (start us, length us, event | category | flops | bytes accessed | tf_op | source)
XLA Modules:
  0.0 89.1 jit_solution(16452573281744454033)
XLA Ops:
  0.6 1.4 %shard_map.78 = f32[2,16,128]{2,1,0:T(8,128)S(1)} custom-call(s32[2]{0:T(128)} %iface.7, f32[16,1024]{1,0:T(8,128)} %basis.5), custom_call_target="tpu_custom_call" | custom-call | tf_op jit(solution)/shard_map/pallas_call | solution.py:396
  2.0 0.0 copy-start
  2.1 0.0 copy-start.1
  2.1 6.5 %collective-permute-start.2 = (f32[2,16,128]{2,1,0:T(8,128)S(1)}, f32[2,16,128]{2,1,0:T(8,128)S(1)}, u32[]{:S(2)}, u32[]{:S(2)}) collective-permute-start(f32[2,16,128]{2,1,0:T(8,128)S(1)} %shard_map.78), channel_id=1, source_target_pairs={{0,31},{1,2},{2,1},{3,4},{4,3},{5,6},{6,5},{7,8},{8,7},{9,10},{10,... | collective-permute-start | bytes 49160 | tf_op jit(solution)/shard_map/ppermute | solution.py:380
  8.6 0.0 collective-permute-start.1
  8.6 0.0 collective-permute-start
  8.6 3.9 %shard_map.77 = (bf16[8,640,256]{2,1,0:T(8,128)(2,1)S(1)}, bf16[8,640,256]{2,1,0:T(8,128)(2,1)S(1)}, f32[1,1024]{1,0:T(1,128)S(1)}, s32[8,5]{1,0:T(8,128)S(1)}) custom-call(s32[8,5]{1,0:T(8,128)} %part_hbm.1, s32[8,5]{1,0:T(8,128)} %slot_hbm.1, f32[8,5,128,128]{3,2,1,0:T(8,128)} %k_hbm.1, f32[8,5,128,128]{3,2,1,0:T(8,128)} %m_hbm.1), custom_call_target="tpu_custom_call" | custom-call | tf_op jit(solution)/shard_map/pallas_call | solution.py:400
  12.5 0.0 collective-permute-done.2.h_b
  12.6 0.7 collective-permute-done.1.h_f
  13.2 0.0 collective-permute-done.h_a
  13.2 0.0 copy-done
  13.2 0.0 copy-done.1
  13.2 1.9 %shard_map.79 = (f32[16,1024]{1,0:T(8,128)S(1)}, f32[16,1024]{1,0:T(8,128)S(1)}, f32[32,1024]{1,0:T(8,128)S(1)}, f32[2,32,128]{2,1,0:T(8,128)S(1)}, f32[32,16,128]{2,1,0:T(8,128)S(1)}) custom-call(s32[8,5]{1,0:T(8,128)S(1)} %get-tuple-element.40.cols, s32[2]{0:T(128)S(1)} %copy-done.1, f32[16,1024]{1,0:T(8,128)S(1)} %copy-done, ...), custom_call_target="tpu_custom_call" | custom-call | tf_op jit(solution)/shard_map/pallas_call | solution.py:409
  15.2 13.1 %all_to_all.15.red = f32[32,16,128]{2,1,0:T(8,128)S(1)} all-to-all(f32[32,16,128]{2,1,0:T(8,128)S(1)} %get-tuple-element.44), channel_id=1, replica_groups=mesh['parts'=32] {'parts'}, dimensions={0} | all-to-all | bytes 524288 | tf_op jit(solution)/shard_map/all_to_all | solution.py:383
  28.3 1.4 %collective-permute-start.5 = (f32[2,32,128]{2,1,0:T(8,128)S(1)}, f32[2,32,128]{2,1,0:T(8,128)S(1)}, u32[]{:S(2)}, u32[]{:S(2)}) collective-permute-start(f32[2,32,128]{2,1,0:T(8,128)S(1)} %get-tuple-element.46), channel_id=1, source_target_pairs={{0,31},{1,2},{2,1},{3,4},{4,3},{5,6},{6,5},{7,8},{8,7},{9,10},{10,... | collective-permute-start | bytes 98312 | tf_op jit(solution)/shard_map/ppermute | solution.py:380
  29.7 0.4 collective-permute-start.4
  30.1 0.0 collective-permute-start.3
  30.1 2.7 %shard_map.80 = (f32[16,1024]{1,0:T(8,128)S(1)}, f32[16,1024]{1,0:T(8,128)S(1)}, f32[16,1024]{1,0:T(8,128)S(1)}, f32[16,1024]{1,0:T(8,128)S(1)}, f32[16,1024]{1,...) custom-call(f32[32,16,128]{2,1,0:T(8,128)S(1)} %all_to_all.15.red, ...), custom_call_target="tpu_custom_call" | custom-call | tf_op jit(solution)/shard_map/pallas_call | solution.py:414
  32.7 2.6 %collective-permute-done.5.h_b = f32[2,32,128]{2,1,0:T(8,128)S(1)} collective-permute-done((f32[2,32,128]{2,1,0:T(8,128)S(1)}, f32[2,32,128]{2,1,0:T(8,128)S(1)}, u32[]{:S(2)}, u32[]{:S(2)}) %collective-permute-start.5) | collective-permute-done | bytes 32800 | tf_op jit(solution)/shard_map/ppermute | solution.py:380
  35.3 0.0 collective-permute-done.4.h_f
  35.3 0.0 collective-permute-done.3.h_a
  35.3 2.0 %shard_map.81 = (f32[16,1024]{1,0:T(8,128)S(1)}, f32[16,1024]{1,0:T(8,128)S(1)}, f32[80,1024]{1,0:T(8,128)S(1)}, f32[48,768]{1,0:T(8,128)S(1)}, f32[32,1024]{1,0:T(8,128)S(1)}, /*index=5*/f32[2,48,128]{2,1,0:T(8,128)S(1)}) custom-call(s32[8,5]{1,0:T(8,128)S(1)} %get-tuple-element.40.cols, s32[2]{0:T(128)S(1)} %copy-done.1, ...), custom_call_target="tpu_custom_call" | custom-call | tf_op jit(solution)/shard_map/pallas_call | solution.py:417
  37.4 2.0 %collective-permute-start.8 = (f32[2,48,128]{2,1,0:T(8,128)S(1)}, f32[2,48,128]{2,1,0:T(8,128)S(1)}, u32[]{:S(2)}, u32[]{:S(2)}) collective-permute-start(f32[2,48,128]{2,1,0:T(8,128)S(1)} %get-tuple-element.57), channel_id=1, source_target_pairs={{0,31},{1,2},{2,1},{3,4},{4,3},{5,6},{6,5},{7,8},{8,7},{9,10},{10,... | collective-permute-start | bytes 147464 | tf_op jit(solution)/shard_map/ppermute | solution.py:380
  39.4 0.8 collective-permute-start.7
  40.2 0.0 collective-permute-start.6
  40.2 4.4 %collective-permute-done.8.h_b.q_b = f32[2,48,128]{2,1,0:T(8,128)S(1)} collective-permute-done((f32[2,48,128]{2,1,0:T(8,128)S(1)}, f32[2,48,128]{2,1,0:T(8,128)S(1)}, u32[]{:S(2)}, u32[]{:S(2)}) %collective-permute-start.8) | collective-permute-done | bytes 49184 | tf_op jit(solution)/shard_map/ppermute | solution.py:380
  44.5 0.0 collective-permute-done.7.h_f.q_f
  44.5 0.0 collective-permute-done.6.h_a.q_a
  44.5 2.2 %shard_map.82 = (f32[16,1024]{1,0:T(8,128)S(1)}, f32[2,16,128]{2,1,0:T(8,128)S(1)}, f32[32,16,128]{2,1,0:T(8,128)S(1)}) custom-call(s32[8,5]{1,0:T(8,128)S(1)} %get-tuple-element.40.cols, s32[2]{0:T(128)S(1)} %copy-done.1, f32[16,1024]{1,0:T(8,128)S(1)} %get-tuple-element.56.p, f32[2,48,128]{2,1,0:T(8,128)S(1)} %collective-permute-done.6.h_a.q_a, ...), custom_call_target="tpu_custom_call" | custom-call | tf_op jit(solution)/shard_map/pallas_call | solution.py:424
  46.8 12.8 %all_to_all.16.red = f32[32,16,128]{2,1,0:T(8,128)S(1)} all-to-all(f32[32,16,128]{2,1,0:T(8,128)S(1)} %get-tuple-element.63), channel_id=1, replica_groups=mesh['parts'=32] {'parts'}, dimensions={0} | all-to-all | bytes 524288 | tf_op jit(solution)/shard_map/all_to_all | solution.py:383
  59.6 1.4 %collective-permute-start.11 = (f32[2,16,128]{2,1,0:T(8,128)S(1)}, f32[2,16,128]{2,1,0:T(8,128)S(1)}, u32[]{:S(2)}, u32[]{:S(2)}) collective-permute-start(f32[2,16,128]{2,1,0:T(8,128)S(1)} %get-tuple-element.69), channel_id=1, source_target_pairs={{0,31},{1,2},{2,1},{3,4},{4,3},{5,6},{6,5},{7,8},{8,7},{9,10},{10,... | collective-permute-start | bytes 49160 | tf_op jit(solution)/shard_map/ppermute | solution.py:380
  61.0 0.4 collective-permute-start.10
  61.3 0.0 collective-permute-start.9
  61.3 0.7 shard_map.83
  62.1 4.2 %collective-permute-done.11.h_b = f32[2,16,128]{2,1,0:T(8,128)S(1)} collective-permute-done((f32[2,16,128]{2,1,0:T(8,128)S(1)}, f32[2,16,128]{2,1,0:T(8,128)S(1)}, u32[]{:S(2)}, u32[]{:S(2)}) %collective-permute-start.11) | collective-permute-done | bytes 16416 | tf_op jit(solution)/shard_map/ppermute | solution.py:380
  66.3 0.0 collective-permute-done.10.h_f
  66.3 0.0 collective-permute-done.9.h_a
  66.3 1.9 %shard_map.84 = (f32[16,1024]{1,0:T(8,128)S(1)}, f32[16,1024]{1,0:T(8,128)S(1)}, f32[2,16,128]{2,1,0:T(8,128)S(1)}) custom-call(s32[8,5]{1,0:T(8,128)S(1)} %get-tuple-element.40.cols, s32[2]{0:T(128)S(1)} %copy-done.1, f32[16,1024]{1,0:T(8,128)S(1)} %get-tuple-element.67.c_local, f32[32,128]{1,0:T(8,128)S(1)} %get-tuple-element.68.coefs, ...), custom_call_target="tpu_custom_call" | custom-call | tf_op jit(solution)/shard_map/pallas_call | solution.py:430
  68.2 2.1 %collective-permute-start.14 = (f32[2,16,128]{2,1,0:T(8,128)S(1)}, f32[2,16,128]{2,1,0:T(8,128)S(1)}, u32[]{:S(2)}, u32[]{:S(2)}) collective-permute-start(f32[2,16,128]{2,1,0:T(8,128)S(1)} %get-tuple-element.72), channel_id=1, source_target_pairs={{0,31},{1,2},{2,1},{3,4},{4,3},{5,6},{6,5},{7,8},{8,7},{9,10},{10,... | collective-permute-start | bytes 49160 | tf_op jit(solution)/shard_map/ppermute | solution.py:380
  70.3 0.0 collective-permute-start.13
  70.3 0.0 collective-permute-start.12
  70.3 4.7 %collective-permute-done.14.h_b = f32[2,16,128]{2,1,0:T(8,128)S(1)} collective-permute-done((f32[2,16,128]{2,1,0:T(8,128)S(1)}, f32[2,16,128]{2,1,0:T(8,128)S(1)}, u32[]{:S(2)}, u32[]{:S(2)}) %collective-permute-start.14) | collective-permute-done | bytes 16416 | tf_op jit(solution)/shard_map/ppermute | solution.py:380
  75.0 0.0 collective-permute-done.13.h_f
  75.0 0.0 collective-permute-done.12.h_a
  75.0 1.9 %shard_map.85 = (f32[16,1024]{1,0:T(8,128)S(1)}, f32[32,8,128]{2,1,0:T(8,128)S(1)}) custom-call(s32[8,5]{1,0:T(8,128)S(1)} %get-tuple-element.40.cols, f32[16,1024]{1,0:T(8,128)S(1)} %get-tuple-element.71.p, f32[2,16,128]{2,1,0:T(8,128)S(1)} %collective-permute-done.12.h_a, f32[2,16,128]{2,1,0:T(8,128)S(1)} %collective-permute-done.13.h_f, ...), custom_call_target="tpu_custom_call" | custom-call | tf_op jit(solution)/shard_map/pallas_call | solution.py:434
  76.9 10.4 %all_to_all.17.red = f32[32,8,128]{2,1,0:T(8,128)S(1)} all-to-all(f32[32,8,128]{2,1,0:T(8,128)S(1)} %get-tuple-element.74), channel_id=1, replica_groups=mesh['parts'=32] {'parts'}, dimensions={0} | all-to-all | bytes 262144 | tf_op jit(solution)/shard_map/all_to_all | solution.py:383
  87.4 1.7 %shard_map.86 = f32[16,1024]{1,0:T(8,128)} custom-call(f32[32,8,128]{2,1,0:T(8,128)S(1)} %all_to_all.17.red, f32[16,1024]{1,0:T(8,128)S(1)} %get-tuple-element.75.p, f32[16,1024]{1,0:T(8,128)S(1)} %get-tuple-element.59.v, f32[80,1024]{1,0:T(8,128)S(1)} %get-tuple-element.61.words, f32[144,128]{1,0:T(8,128)S(1)} %get-tuple-element.55.small, ...), custom_call_target="tpu_custom_call" | custom-call | tf_op jit(solution)/shard_map/pallas_call | solution.py:436
Async XLA Ops:
  2.0 11.2 %copy-start = (f32[16,1024]{1,0:T(8,128)S(1)}, f32[16,1024]{1,0:T(8,128)}, u32[]{:S(2)}) copy-start(f32[16,1024]{1,0:T(8,128)} %basis.5) | copy-start | bytes 196612
  2.1 11.2 %copy-start.1 = (s32[2]{0:T(128)S(1)}, s32[2]{0:T(128)}, u32[]{:S(2)}) copy-start(s32[2]{0:T(128)} %iface.7) | copy-start | bytes 28
  2.1 10.5 %collective-permute-start.2 = (f32[2,16,128]{2,1,0:T(8,128)S(1)}, f32[2,16,128]{2,1,0:T(8,128)S(1)}, u32[]{:S(2)}, u32[]{:S(2)}) collective-permute-start(f32[2,16,128]{2,1,0:T(8,128)S(1)} %shard_map.78), channel_id=1, source_target_pairs={{0,31},{1,2},{2,1},{3,4},{4,3},{5,6},{6,5},{7,8},{8,7},{9,10},{10,... | collective-permute-start | bytes 49160 | tf_op jit(solution)/shard_map/ppermute | solution.py:380
  8.6 4.6 %collective-permute-start.1 = (f32[2,16,128]{2,1,0:T(8,128)S(1)}, f32[2,16,128]{2,1,0:T(8,128)S(1)}, u32[]{:S(2)}, u32[]{:S(2)}) collective-permute-start(f32[2,16,128]{2,1,0:T(8,128)S(1)} %shard_map.78), channel_id=1, source_target_pairs={{0,16},{1,17},{2,18},{3,19},{4,20},{5,21},{6,22},{7,23},{8,24},{9,... | collective-permute-start | bytes 49160 | tf_op jit(solution)/shard_map/ppermute | solution.py:380
  8.6 4.6 %collective-permute-start = (f32[2,16,128]{2,1,0:T(8,128)S(1)}, f32[2,16,128]{2,1,0:T(8,128)S(1)}, u32[]{:S(2)}, u32[]{:S(2)}) collective-permute-start(f32[2,16,128]{2,1,0:T(8,128)S(1)} %shard_map.78), channel_id=1, source_target_pairs={{0,1},{1,0},{2,3},{3,2},{4,5},{5,4},{6,7},{7,6},{8,9},{9,8},{10,11... | collective-permute-start | bytes 49160 | tf_op jit(solution)/shard_map/ppermute | solution.py:380
  28.3 7.0 %collective-permute-start.5 = (f32[2,32,128]{2,1,0:T(8,128)S(1)}, f32[2,32,128]{2,1,0:T(8,128)S(1)}, u32[]{:S(2)}, u32[]{:S(2)}) collective-permute-start(f32[2,32,128]{2,1,0:T(8,128)S(1)} %get-tuple-element.46), channel_id=1, source_target_pairs={{0,31},{1,2},{2,1},{3,4},{4,3},{5,6},{6,5},{7,8},{8,7},{9,10},{10,... | collective-permute-start | bytes 98312 | tf_op jit(solution)/shard_map/ppermute | solution.py:380
  29.7 5.6 %collective-permute-start.4 = (f32[2,32,128]{2,1,0:T(8,128)S(1)}, f32[2,32,128]{2,1,0:T(8,128)S(1)}, u32[]{:S(2)}, u32[]{:S(2)}) collective-permute-start(f32[2,32,128]{2,1,0:T(8,128)S(1)} %get-tuple-element.46), channel_id=1, source_target_pairs={{0,16},{1,17},{2,18},{3,19},{4,20},{5,21},{6,22},{7,23},{8,24},{9,... | collective-permute-start | bytes 98312 | tf_op jit(solution)/shard_map/ppermute | solution.py:380
  30.1 5.3 %collective-permute-start.3 = (f32[2,32,128]{2,1,0:T(8,128)S(1)}, f32[2,32,128]{2,1,0:T(8,128)S(1)}, u32[]{:S(2)}, u32[]{:S(2)}) collective-permute-start(f32[2,32,128]{2,1,0:T(8,128)S(1)} %get-tuple-element.46), channel_id=1, source_target_pairs={{0,1},{1,0},{2,3},{3,2},{4,5},{5,4},{6,7},{7,6},{8,9},{9,8},{10,11... | collective-permute-start | bytes 98312 | tf_op jit(solution)/shard_map/ppermute | solution.py:380
  37.4 7.2 %collective-permute-start.8 = (f32[2,48,128]{2,1,0:T(8,128)S(1)}, f32[2,48,128]{2,1,0:T(8,128)S(1)}, u32[]{:S(2)}, u32[]{:S(2)}) collective-permute-start(f32[2,48,128]{2,1,0:T(8,128)S(1)} %get-tuple-element.57), channel_id=1, source_target_pairs={{0,31},{1,2},{2,1},{3,4},{4,3},{5,6},{6,5},{7,8},{8,7},{9,10},{10,... | collective-permute-start | bytes 147464 | tf_op jit(solution)/shard_map/ppermute | solution.py:380
  39.4 5.1 %collective-permute-start.7 = (f32[2,48,128]{2,1,0:T(8,128)S(1)}, f32[2,48,128]{2,1,0:T(8,128)S(1)}, u32[]{:S(2)}, u32[]{:S(2)}) collective-permute-start(f32[2,48,128]{2,1,0:T(8,128)S(1)} %get-tuple-element.57), channel_id=1, source_target_pairs={{0,16},{1,17},{2,18},{3,19},{4,20},{5,21},{6,22},{7,23},{8,24},{9,... | collective-permute-start | bytes 147464 | tf_op jit(solution)/shard_map/ppermute | solution.py:380
  40.2 4.4 %collective-permute-start.6 = (f32[2,48,128]{2,1,0:T(8,128)S(1)}, f32[2,48,128]{2,1,0:T(8,128)S(1)}, u32[]{:S(2)}, u32[]{:S(2)}) collective-permute-start(f32[2,48,128]{2,1,0:T(8,128)S(1)} %get-tuple-element.57), channel_id=1, source_target_pairs={{0,1},{1,0},{2,3},{3,2},{4,5},{5,4},{6,7},{7,6},{8,9},{9,8},{10,11... | collective-permute-start | bytes 147464 | tf_op jit(solution)/shard_map/ppermute | solution.py:380
  59.6 6.8 %collective-permute-start.11 = (f32[2,16,128]{2,1,0:T(8,128)S(1)}, f32[2,16,128]{2,1,0:T(8,128)S(1)}, u32[]{:S(2)}, u32[]{:S(2)}) collective-permute-start(f32[2,16,128]{2,1,0:T(8,128)S(1)} %get-tuple-element.69), channel_id=1, source_target_pairs={{0,31},{1,2},{2,1},{3,4},{4,3},{5,6},{6,5},{7,8},{8,7},{9,10},{10,... | collective-permute-start | bytes 49160 | tf_op jit(solution)/shard_map/ppermute | solution.py:380
  61.0 5.4 %collective-permute-start.10 = (f32[2,16,128]{2,1,0:T(8,128)S(1)}, f32[2,16,128]{2,1,0:T(8,128)S(1)}, u32[]{:S(2)}, u32[]{:S(2)}) collective-permute-start(f32[2,16,128]{2,1,0:T(8,128)S(1)} %get-tuple-element.69), channel_id=1, source_target_pairs={{0,16},{1,17},{2,18},{3,19},{4,20},{5,21},{6,22},{7,23},{8,24},{9,... | collective-permute-start | bytes 49160 | tf_op jit(solution)/shard_map/ppermute | solution.py:380
  61.3 5.0 %collective-permute-start.9 = (f32[2,16,128]{2,1,0:T(8,128)S(1)}, f32[2,16,128]{2,1,0:T(8,128)S(1)}, u32[]{:S(2)}, u32[]{:S(2)}) collective-permute-start(f32[2,16,128]{2,1,0:T(8,128)S(1)} %get-tuple-element.69), channel_id=1, source_target_pairs={{0,1},{1,0},{2,3},{3,2},{4,5},{5,4},{6,7},{7,6},{8,9},{9,8},{10,11... | collective-permute-start | bytes 49160 | tf_op jit(solution)/shard_map/ppermute | solution.py:380
  68.2 6.8 %collective-permute-start.14 = (f32[2,16,128]{2,1,0:T(8,128)S(1)}, f32[2,16,128]{2,1,0:T(8,128)S(1)}, u32[]{:S(2)}, u32[]{:S(2)}) collective-permute-start(f32[2,16,128]{2,1,0:T(8,128)S(1)} %get-tuple-element.72), channel_id=1, source_target_pairs={{0,31},{1,2},{2,1},{3,4},{4,3},{5,6},{6,5},{7,8},{8,7},{9,10},{10,... | collective-permute-start | bytes 49160 | tf_op jit(solution)/shard_map/ppermute | solution.py:380
  70.3 4.7 %collective-permute-start.13 = (f32[2,16,128]{2,1,0:T(8,128)S(1)}, f32[2,16,128]{2,1,0:T(8,128)S(1)}, u32[]{:S(2)}, u32[]{:S(2)}) collective-permute-start(f32[2,16,128]{2,1,0:T(8,128)S(1)} %get-tuple-element.72), channel_id=1, source_target_pairs={{0,16},{1,17},{2,18},{3,19},{4,20},{5,21},{6,22},{7,23},{8,24},{9,... | collective-permute-start | bytes 49160 | tf_op jit(solution)/shard_map/ppermute | solution.py:380
  70.3 4.7 %collective-permute-start.12 = (f32[2,16,128]{2,1,0:T(8,128)S(1)}, f32[2,16,128]{2,1,0:T(8,128)S(1)}, u32[]{:S(2)}, u32[]{:S(2)}) collective-permute-start(f32[2,16,128]{2,1,0:T(8,128)S(1)} %get-tuple-element.72), channel_id=1, source_target_pairs={{0,1},{1,0},{2,3},{3,2},{4,5},{5,4},{6,7},{7,6},{8,9},{9,8},{10,11... | collective-permute-start | bytes 49160 | tf_op jit(solution)/shard_map/ppermute | solution.py:380

commit v3 on v2

--- a/solution.py
+++ b/solution.py
@@ -4,6 +4,7 @@
 from jax.experimental import pallas as pl
 from jax.experimental.pallas import tpu as pltpu
 from jax.sharding import PartitionSpec as P
+
 
 relax = 0.4
 
@@ -43,6 +44,22 @@
 def split(value):
     high = value.astype(BF16)
     return high, (value - high.astype(F32)).astype(BF16)
+
+
+def mm3(left, right):
+    lh, ll = split(left)
+    rh, rl = split(right)
+    n = left.shape[0]
+    both = jnp.dot(jnp.concatenate([lh, ll], axis=0), rh, preferred_element_type=F32)
+    return both[:n] + both[n:] + jnp.dot(lh, rl, preferred_element_type=F32)
+
+
+def nt3(high, low, right):
+    dims = (((1,), (1,)), ((), ()))
+    rh, rl = split(right)
+    n = high.shape[0]
+    both = lax.dot_general(jnp.concatenate([high, low], axis=0), rh, dims, preferred_element_type=F32)
+    return both[:n] + both[n:] + lax.dot_general(high, rl, dims, preferred_element_type=F32)
 
 
 def rows(parts):
@@ -96,21 +113,32 @@
     return [turned[k * n : (k + 1) * n] for k in range(MAT // n)]
 
 
-def inverse_chols(grams):
-    n = grams[0].shape[0]
-    lane, row = lane_row(grams[0].shape)
-    states = [g + jnp.where(lane == row + n, 1.0, 0.0) for g in grams]
-    for k in range(n - 1):
-        for index, a in enumerate(states):
-            pivot_row = a[k : k + 1, :]
-            factor = a[:, k : k + 1] * (1.0 / a[k : k + 1, k : k + 1])
-            states[index] = a - jnp.where(row > k, factor, 0.0) * pivot_row
-    out = []
-    for a in states:
-        pivots = jnp.sum(jnp.where(lane == row, a, 0.0), axis=1, keepdims=True)
-        moved = pltpu.roll(a, MAT - n, 1)
-        out.append(jnp.where(lane < n, moved, 0.0) * lax.rsqrt(pivots))
-    return out
+def inverse_chols(first, second):
+    n = first.shape[0]
+    shape = first.shape
+    lane, row = lane_row(shape)
+    half = MAT // 2
+    columns = [
+        jnp.where(
+            lane < half,
+            jnp.broadcast_to(first[:, j : j + 1], shape),
+            jnp.broadcast_to(second[:, j : j + 1], shape),
+        )
+        for j in range(n)
+    ]
+    inverse = jnp.where(lane % half == row, 1.0, 0.0)
+    pivots = jnp.ones(shape, F32)
+    for k in range(n):
+        pivot = columns[k][k : k + 1, :]
+        pivots = jnp.where(row == k, pivot, pivots)
+        if k == n - 1:
+            break
+        factor = jnp.where(row > k, columns[k], 0.0) * (1.0 / pivot)
+        for j in range(k + 1, n):
+            columns[j] = columns[j] - factor * columns[j][k : k + 1, :]
+        inverse = inverse - factor * inverse[k : k + 1, :]
+    inverse = inverse * lax.rsqrt(pivots)
+    return [jnp.where(lane < n, value, 0.0) for value in (inverse, pltpu.roll(inverse, half, 1))]
 
 
 def diagonal(a):
@@ -213,36 +241,46 @@
         u[:n] = kb[...] * d
         u[n:] = mb[...] * d
         send_tiles(iface, outgoing, 0, u)
-        right = rows([basis[...], u[...], mb[...], kb[...], jnp.zeros((MAT - 5 * n, basis.shape[1]), F32)])
+        right = rows([basis[...], u[...], kb[...], mb[...], jnp.zeros((MAT - 5 * n, basis.shape[1]), F32)])
         both = nt(rows([basis[...], mb[...]]), right) * scale
-        lane, _ = lane_row((n, MAT))
-        fill_blocks(grams, jnp.where(lane < 3 * n, both[:n], both[n:]))
-
-    def k_b0(red, basis, kb, mb, u, v_out, t_out, ko_out, mo_out, c0_out, words, small, theta_out):
-        g_bb, g_u1b, g_u2b, g_mm, g_km = blocks_of(total(red), n)[:5]
-        inv_v, inv_c = inverse_chols([g_bb, g_mm])
+        lane, row = lane_row((n, MAT))
+        chosen = jnp.where(lane < 3 * n, both[:n], both[n:])
+        mass = pltpu.roll(chosen, MAT - 4 * n, 1)
+        packed = jnp.where((lane < n) & (lane > row), mass, jnp.where(lane < 4 * n, chosen, 0.0))
+        mass_diag = jnp.sum(jnp.where((lane == row) & (lane < n), mass, 0.0), axis=0, keepdims=True)
+        packed = fold(packed)
+        for device in range(grams.shape[0]):
+            grams[device, : n // 2, 0, :] = packed
+            grams[device, n // 2] = mass_diag
+
+    def k_b0(red, kb, mb, u, ko_out, mo_out, c0_out, words, small, theta_out):
+        packed, mass_diag = red[0, : n // 2, 0, :], red[0, n // 2]
+        for device in range(1, red.shape[0]):
+            packed = packed + red[device, : n // 2, 0, :]
+            mass_diag = mass_diag + red[device, n // 2]
+        packed = unfold(packed)
+        turned, g_u1b, g_u2b, g_km = blocks_of(packed, n)[:4]
+        lane, row = lane_row((n, MAT))
+        g_bb = jnp.where(lane < n, jnp.where(lane <= row, packed, turned), 0.0)
+        g_mm = jnp.where(lane == row, mass_diag, jnp.where(lane > row, packed, turned))
+        g_mm = jnp.where(lane < n, g_mm, 0.0)
+        inv_v, inv_c = inverse_chols(g_bb, g_mm)
         lv, lc = inv_v[:, :n], inv_c[:, :n]
         cross = nt(mm(lv, g_km[:, :n]), lc)
         theta = diagonal(cross) * diagonal(inv_c) / diagonal(inv_v)
-        g1 = mm(lv, u[:n])
-        both = mm(rows([lv, lc]), u[n:])
+        g1 = mm3(lv, u[:n])
+        both = mm3(rows([lv, lc]), u[n:])
         g2, f1 = both[:n], both[n:]
         for k, value in ((0, f1), (3, g1), (4, g2)):
             words[k * n : (k + 1) * n] = value
         c0_out[...] = -relax * (g1 - theta * g2)
-        ko_out[...] = mm(lv, kb[...])
-        both = mm(rows([lv, lc]), mb[...])
-        mo_out[...] = both[:n]
-        t_out[...] = both[n:]
-        v_out[...] = mm(lv, basis[...])
-        mass = nt(mm(lv, g_mm[:, :n]), lc)
+        ko_out[...] = mm3(lv, kb[...])
+        mo_out[...] = mm3(lv, mb[...])
         e1 = nt(mm(lv, g_u1b[:, :n]), lv)
         e2 = nt(mm(lv, g_u2b[:, :n]), lv)
-        ef = nt(mm(lc, g_u2b[:, :n]), lv)
         right = -relax * (e1 - theta * e2)
-        for k, value in enumerate((cross, mass, e1, e2, ef, theta, lv, lc, right)):
+        for k, value in enumerate((cross, g_mm[:, :n], e1, e2, g_u2b[:, :n], theta, lv, lc, right)):
             put_small(small, k, value)
-        lane, row = lane_row((n, MAT))
         theta_out[...] = jnp.sum(jnp.where(lane == row, theta, 0.0), axis=0, keepdims=True)[:, :n]
 
     def k_b1(
@@ -251,8 +289,8 @@
     ):
         lv, lc, right = (get_small(small, k) for k in (6, 7, 8))
         theta = small[5 * n : 6 * n, :1]
-        g1 = mm(lv, halo_lanes((h_a, h_f, h_b), 0, n))
-        both = mm(rows([lv, lc]), halo_lanes((h_a, h_f, h_b), n, 2 * n))
+        g1 = mm3(lv, halo_lanes((h_a, h_f, h_b), 0, n))
+        both = mm3(rows([lv, lc]), halo_lanes((h_a, h_f, h_b), n, 2 * n))
         g2, f1 = both[:n], both[n:]
         put_sources(xs, 0, rows([c0[...], words_in[:n]]))
         put_sources(xs, c0.shape[1] // xs.shape[2], rows([-relax * (g1 - theta * g2), f1]))
@@ -260,7 +298,7 @@
         for k, value in ((0, f1), (1, g1), (2, g2)):
             words_halo[k * n : (k + 1) * n] = value
         d = inv_d[...]
-        image = res[0, :n] - theta * res[1, :n] - mm(lanes([right, -theta * right]), rows([ko[...], mo[...]]))
+        image = res[0, :n] - theta * res[1, :n] - mm3(lanes([right, -theta * right]), rows([ko[...], mo[...]]))
         image_out[...] = image
         kf_out[:n] = res[0, n:]
         kf_out[n:] = res[1, n:]
@@ -272,30 +310,48 @@
         send_tiles(iface, outgoing, 0, p_out)
         send_tiles(iface, outgoing, n, words.at[n : 3 * n])
 
-    def half(cols, p, halo, small, c0, w_high, w_low, inv_d, xs, res):
+    def k_c0(small, basis, mb, image0, kf, p, words, v_out, tests_high, tests_low, small_b, part):
+        lv, lc = get_small(small, 6), get_small(small, 7)
+        v = mm3(lv, basis[...])
+        v_out[...] = v
+        high, low = split(rows([mm3(lc, mb[...]), v]))
+        tests_high[...] = high
+        tests_low[...] = low
+        put_small(small_b, 0, nt(mm(lv, get_small(small, 1)), lc))
+        put_small(small_b, 1, nt(mm(lc, get_small(small, 4)), lv))
+        right = rows([image0[...], kf[...], p[...], words[n : 3 * n], jnp.zeros((2 * n, p.shape[1]), F32)])
+        both = nt3(high, low, right) * scale
+        lane, _ = lane_row((n, MAT))
+        part[...] = jnp.where(lane < 3 * n, both[:n], both[n:])
+
+    def half(cols, p, halo, small, c0, w_high, w_low, inv_d, tests_high, tests_low, xs, res):
         put_sources(xs, 0, p)
         put_sources(xs, p.shape[1] // xs.shape[2], halo)
         apply_pair(xs, cols, w_high, w_low, res.at[0], res.at[1])
         theta = small[5 * n : 6 * n, :1]
         image = res[0] - theta * res[1]
-        return image, p + c0[...] - relax * inv_d[...] * image
-
-    def k_c(
-        cols, iface, p, h_a, h_f, h_b, image0, v, t, c0, words, kf, small, w_high, w_low, inv_d,
+        fresh = p + c0[...] - relax * inv_d[...] * image
+        both = nt3(tests_high[...], tests_low[...], rows([image, fresh])) * scale
+        both = lanes([both, jnp.zeros((2 * n, MAT - 2 * n), F32)])
+        lane, _ = lane_row((n, MAT))
+        return fresh, jnp.where(lane < n, both[:n], both[n:])
+
+    def k_c1(
+        cols, iface, p, h_a, h_f, h_b, c0, small, part, tests_high, tests_low, w_high, w_low, inv_d,
         p_out, outgoing, grams, xs, res,
     ):
-        image, fresh = half(
-            cols, p[...], halo_lanes((h_a, h_f, h_b), 0, n), small, c0, w_high, w_low, inv_d, xs, res
+        fresh, added = half(
+            cols, p[...], halo_lanes((h_a, h_f, h_b), 0, n), small, c0, w_high, w_low, inv_d,
+            tests_high, tests_low, xs, res,
         )
         p_out[...] = fresh
         send_tiles(iface, outgoing, 0, p_out)
-        right = rows([image0[...], kf[...], image, p[...], words[n : 3 * n], fresh])
-        both = nt(rows([t[...], v[...]]), right) * scale
         lane, _ = lane_row((n, MAT))
-        fill_blocks(grams, jnp.where(lane < 4 * n, both[:n], both[n:]))
-
-    def solve(small, g_left, g_kf, g_mf, g_a, g_p, g_h1, g_h2, g_fresh):
-        cross, mass, e1, e2, ef = (get_small(small, k) for k in range(5))
+        fill_blocks(grams, jnp.where(lane < 6 * n, part[...], pltpu.roll(added, 6 * n, 1)))
+
+    def solve(small, small_b, g_left, g_kf, g_mf, g_p, g_h1, g_h2, g_a, g_fresh):
+        cross, e1, e2 = (get_small(small, k) for k in (0, 2, 3))
+        mass, ef = (get_small(small_b, k) for k in range(2))
         theta = small[5 * n : 6 * n, :1]
         right = g_p + relax * mm(g_left, ef)
         left = (
@@ -315,14 +371,14 @@
         after = g_fresh + mm(coef, rows([ef, g_h1, g_h2, e1, e2]))
         return coef, after
 
-    def k_d0(red, p, words, small, c_out, words_grams, coefs):
+    def k_d0(red, p, words, small, small_b, c_out, words_grams, coefs):
         g = [value[:, :n] for value in blocks_of(total(red), n)]
-        coef, right = solve(small, *g)
-        for k, index in enumerate((1, 2, 5, 6)):
+        coef, right = solve(small, small_b, *g)
+        for k, index in enumerate((1, 2, 4, 5)):
             put_small(words_grams, k, g[index])
         coefs[:n] = lanes([coef, jnp.zeros((n, MAT - 5 * n), F32)])
         put_small(coefs, 1, right)
-        c_out[...] = p[...] + mm(coef, words[...])
+        c_out[...] = p[...] + mm3(coef, words[...])
 
     def k_d1(
         cols, iface, c_local, coefs, h_a, h_f, h_b, q_a, q_f, q_b, ko, mo, c0, words_halo, small,
@@ -331,38 +387,40 @@
         coef, right = coefs[:n, : 5 * n], get_small(coefs, 1)
         theta = small[5 * n : 6 * n, :1]
         around = rows([words_halo[:n], halo_lanes((q_a, q_f, q_b), n, 3 * n), words_halo[n:]])
-        c_halo = halo_lanes((h_a, h_f, h_b), 0, n) + mm(coef, around)
+        c_halo = halo_lanes((h_a, h_f, h_b), 0, n) + mm3(coef, around)
         put_sources(xs, 0, c_local[...])
         put_sources(xs, c_local.shape[1] // xs.shape[2], c_halo)
         apply_pair(xs, cols, w_high, w_low, res.at[0], res.at[1])
-        image = res[0] - theta * res[1] - mm(lanes([right, -theta * right]), rows([ko[...], mo[...]]))
+        image = res[0] - theta * res[1] - mm3(lanes([right, -theta * right]), rows([ko[...], mo[...]]))
         image_out[...] = image
         p_out[...] = c_local[...] + c0[...] - relax * inv_d[...] * image
         send_tiles(iface, outgoing, 0, p_out)
 
-    def k_e(
-        cols, p, h_a, h_f, h_b, image2, v, t, c0, small, w_high, w_low, inv_d, p_out, grams, xs, res
+    def k_e0(image2, p, tests_high, tests_low, part):
+        right = rows([image2[...], p[...], jnp.zeros((MAT - 2 * n, p.shape[1]), F32)])
+        both = nt3(tests_high[...], tests_low[...], right) * scale
+        lane, _ = lane_row((n, MAT))
+        part[...] = jnp.where(lane < n, both[:n], both[n:])
+
+    def k_e1(
+        cols, p, h_a, h_f, h_b, c0, small, part, tests_high, tests_low, w_high, w_low, inv_d, p_out, grams, xs, res
     ):
-        image, fresh = half(
-            cols, p[...], halo_lanes((h_a, h_f, h_b), 0, n), small, c0, w_high, w_low, inv_d, xs, res
+        fresh, added = half(
+            cols, p[...], halo_lanes((h_a, h_f, h_b), 0, n), small, c0, w_high, w_low, inv_d,
+            tests_high, tests_low, xs, res,
         )
         p_out[...] = fresh
-        right = rows([image2[...], image, p[...], fresh, jnp.zeros((MAT - 4 * n, p.shape[1]), F32)])
-        both = nt(rows([t[...], v[...]]), right) * scale
         lane, _ = lane_row((n, MAT))
-        fill_blocks(grams, fold(jnp.where(lane < 2 * n, both[:n], both[n:])))
-
-    def k_f(red, p, v, words, small, words_grams, out):
-        g_left, g_a, g_p, g_fresh = (value[:, :n] for value in blocks_of(unfold(total(red)), n)[:4])
+        both = jnp.where(lane < 2 * n, part[...], pltpu.roll(added, 2 * n, 1))
+        fill_blocks(grams, fold(jnp.where(lane < 4 * n, both, 0.0)))
+
+    def k_f(red, p, v, words, small, small_b, words_grams, out):
+        g_left, g_p, g_a, g_fresh = (value[:, :n] for value in blocks_of(unfold(total(red)), n)[:4])
         g_kf, g_mf, g_h1, g_h2 = (get_small(words_grams, k) for k in range(4))
-        coef, right = solve(small, g_left, g_kf, g_mf, g_a, g_p, g_h1, g_h2, g_fresh)
-        out[...] = p[...] + mm(lanes([coef, -right]), rows([words[...], v[...]]))
-
-    return k_a, k_b0, k_b1, k_c, k_d0, k_d1, k_e, k_f
-
-
-def ordered(first, second):
-    return lax.optimization_barrier((first, second))
+        coef, right = solve(small, small_b, g_left, g_kf, g_mf, g_p, g_h1, g_h2, g_a, g_fresh)
+        out[...] = p[...] + mm3(lanes([coef, -right]), rows([words[...], v[...]]))
+
+    return k_a, k_b0, k_b1, k_c0, k_c1, k_d0, k_d1, k_e0, k_e1, k_f
 
 
 def shards(basis, k_tiles, m_tiles, tile_part, tile_slot, iface):
@@ -382,7 +440,7 @@
     def reduced(blocks_out):
         return lax.all_to_all(blocks_out, "parts", 0, 0, tiled=True)
 
-    k_a, k_b0, k_b1, k_c, k_d0, k_d1, k_e, k_f = make_kernels(n, scale)
+    k_a, k_b0, k_b1, k_c0, k_c1, k_d0, k_d1, k_e0, k_e1, k_f = make_kernels(n, scale)
     sources = tiles + 3 * count
     xs = lambda m: pltpu.VMEM((sources, 2 * m, width), BF16)
     vec = ((n, local), F32)
@@ -406,14 +464,15 @@
         + [pltpu.SemaphoreType.DMA((2, tiles + 1))],
     )(*(in_hbm(value) for value in (tile_part, tile_slot, k_tiles, m_tiles)))
     w = (w_high, w_low, inv_d)
+    packed = ((parts, n // 2 + 1, 1, MAT), F32)
     kb, mb, u, outgoing, grams = call(
-        k_a, [vec, vec, vecs(2), out(2 * n), grams16], [SM, SM] + [VM] * 7, [xs(n)]
+        k_a, [vec, vec, vecs(2), out(2 * n), packed], [SM, SM] + [VM] * 7, [xs(n)]
     )(cols, iface, basis, *h0, *w)
-    red, outgoing = ordered(reduced(grams), outgoing)
+    red = reduced(grams)
     h1 = halo(outgoing)
-    v, t, ko, mo, c0, words, small, theta = call(
-        k_b0, [vec] * 5 + [vecs(5), mats(9), ((1, n), F32)], [VM] * 5
-    )(red, basis, kb, mb, u)
+    ko, mo, c0, words, small, theta = call(
+        k_b0, [vec] * 3 + [vecs(5), mats(9), ((1, n), F32)], [VM] * 4
+    )(red, kb, mb, u)
     p1, image0, words, words_halo, kf, outgoing = call(
         k_b1,
         [vec, vec, vecs(5), ((3 * n, 3 * count * width), F32), vecs(2), out(3 * n)],
@@ -421,19 +480,26 @@
         [xs(2 * n), pltpu.VMEM((2, 2 * n, local), F32)],
     )(cols, iface, *h1, *w, ko, mo, c0, words, small)
     h2 = halo(outgoing)
-    p2, outgoing, grams = call(k_c, [vec, out(n), grams16], [SM, SM] + [VM] * 14, [xs(n), res])(
-        cols, iface, p1, *h2, image0, v, t, c0, words, kf, small, *w
-    )
-    red, outgoing = ordered(reduced(grams), outgoing)
+    v, tests_high, tests_low, small_b, part = call(
+        k_c0, [vec] + [((2 * n, local), BF16)] * 2 + [mats(2), mats(1)], [VM] * 7
+    )(small, basis, mb, image0, kf, p1, words)
+    tests = (tests_high, tests_low)
+    p2, outgoing, grams = call(k_c1, [vec, out(n), grams16], [SM, SM] + [VM] * 12, [xs(n), res])(
+        cols, iface, p1, *h2, c0, small, part, *tests, *w
+    )
+    red = reduced(grams)
     h3 = halo(outgoing)
-    c2, words_grams, coefs = call(k_d0, [vec, mats(4), mats(2)], [VM] * 4)(red, p2, words, small)
+    c2, words_grams, coefs = call(k_d0, [vec, mats(4), mats(2)], [VM] * 5)(
+        red, p2, words, small, small_b
+    )
     p3, image2, outgoing = call(k_d1, [vec, vec, out(n)], [SM, SM] + [VM] * 16, [xs(n), res])(
         cols, iface, c2, coefs, *h3, *h2, ko, mo, c0, words_halo, small, *w
     )
     h4 = halo(outgoing)
-    p4, grams = call(k_e, [vec, grams8], [SM] + [VM] * 12, [xs(n), res])(cols, p3, *h4, image2, v, t, c0, small, *w)
+    (part,) = call(k_e0, [mats(1)], [VM] * 4)(image2, p3, *tests)
+    p4, grams = call(k_e1, [vec, grams8], [SM] + [VM] * 12, [xs(n), res])(cols, p3, *h4, c0, small, part, *tests, *w)
     red = reduced(grams)
-    (correct,) = call(k_f, [vec], [VM] * 6)(red, p4, v, words, small, words_grams)
+    (correct,) = call(k_f, [vec], [VM] * 7)(red, p4, v, words, small, small_b, words_grams)
     return (correct, theta.reshape(-1))
 
 

time: 89.3 us -> 89.9 us (level)
  blocking collectives: 36.4 us -> 10.4 us
  local copies, waits for them, and re-layouts: 0.01 us -> 12.4 us
  starting transfers between devices: 15 us -> 26.1 us
  waiting for transfers between devices: 16.6 us -> 19.4 us
    all_to_all x3 -> x1, blocking collectives: 36.4 us -> 10.4 us  [reduced(): return lax.all_to_all(blocks_out, 'parts', 0, 0, tiled=True)]
    unnamed x4 -> x56, local copies, waits for them, and re-layouts: 0.01 us -> 12.4 us
    all_to_all x0 -> x2, waiting for transfers between devices: none -> 9.35 us  [reduced(): return lax.all_to_all(blocks_out, 'parts', 0, 0, tiled=True)]
    ppermute x15, waiting for transfers between devices: 16.6 us -> 10.1 us  [halo(): lax.ppermute(outgoing, 'parts', pairs)]
    ppermute x15, starting transfers between devices: 15 us -> 20.8 us  [halo(): lax.ppermute(outgoing, 'parts', pairs)]
    all_to_all x0 -> x2, starting transfers between devices: none -> 5.35 us  [reduced(): return lax.all_to_all(blocks_out, 'parts', 0, 0, tiled=True)]
    pallas_call x6 -> x8, Pallas kernels: 11.1 us -> 10.6 us  [the longest x1 2.77 us: shards(): call(k_a, [vec, vec, vecs(2), out(2 * n), packed], [SM, SM] + [VM] * 7, [...]
  transfers between devices with their start and end apart: 15 -> 17, of which waited for: 5 -> 7; matrix products, arithmetic and copies ran while one was open for 0% -> 0% of each run, Pallas kernels for 8% -> 7%
where the time goes in v3:
time: 89.9 us; the launch traced here: 89.2 us
  starting transfers between devices  26.1 us (29%)
  Pallas kernels  19.8 us (22%)
  waiting for transfers between devices  19.4 us (22%)
  local copies, waits for them, and re-layouts  12.4 us (14%)
  blocking collectives  10.4 us (12%)
  between operations  0.91 us (1%)
    ppermute x15, starting transfers between devices, halo(): lax.ppermute(outgoing, 'parts', pairs)  20.8 us
    unnamed x56, local copies, waits for them, and re-layouts  12.4 us
    all_to_all x1, blocking collectives, reduced(): return lax.all_to_all(blocks_out, 'parts', 0, 0, tiled=True)  10.4 us
    ppermute x15, waiting for transfers between devices, halo(): lax.ppermute(outgoing, 'parts', pairs)  10.1 us
    all_to_all x2, waiting for transfers between devices, reduced(): return lax.all_to_all(blocks_out, 'parts', 0, 0, tiled=True)  9.35 us
    all_to_all x2, starting transfers between devices, reduced(): return lax.all_to_all(blocks_out, 'parts', 0, 0, tiled=True)  5.35 us
    pallas_call x1, Pallas kernels, shards(): call(make_prep(count), [((tiles, blocks * width, 2 * width), BF16)] * 2 +...  3.94 us
    pallas_call x1, Pallas kernels, shards(): call(k_a, [vec, vec, vecs(2), out(2 * n), packed], [SM, SM] + [VM] * 7, [...  2.77 us
  transfers between devices with their start and end apart: 17, of which 7 were waited for; matrix products, arithmetic and copies ran while one was open for 0% of the time, Pallas kernels for 7%

profile of v3, /device:TPU:0, one launch (start us, length us, event | category | flops | bytes accessed | tf_op | source)
XLA Modules:
  0.0 89.2 jit_solution(7193934976328917798)
XLA Ops:
  0.6 1.4 %shard_map.78 = f32[2,16,128]{2,1,0:T(8,128)S(1)} custom-call(s32[2]{0:T(128)} %iface.7, f32[16,1024]{1,0:T(8,128)} %basis.5), custom_call_target="tpu_custom_call" | custom-call | tf_op jit(solution)/shard_map/pallas_call | solution.py:454
  2.0 0.0 copy-start.5
  2.0 0.0 copy-start.24
  2.1 6.5 %collective-permute-start.2 = (f32[2,16,128]{2,1,0:T(8,128)S(1)}, f32[2,16,128]{2,1,0:T(8,128)S(1)}, u32[]{:S(2)}, u32[]{:S(2)}) collective-permute-start(f32[2,16,128]{2,1,0:T(8,128)S(1)} %shard_map.78), channel_id=1, source_target_pairs={{0,31},{1,2},{2,1},{3,4},{4,3},{5,6},{6,5},{7,8},{8,7},{9,10},{10,... | collective-permute-start | bytes 49160 | tf_op jit(solution)/shard_map/ppermute | solution.py:438
  8.6 0.0 collective-permute-start.1
  8.6 0.0 collective-permute-start
  8.6 3.9 %shard_map.77 = (bf16[8,640,256]{2,1,0:T(8,128)(2,1)S(1)}, bf16[8,640,256]{2,1,0:T(8,128)(2,1)S(1)}, f32[1,1024]{1,0:T(1,128)S(1)}, s32[8,5]{1,0:T(8,128)S(1)}) custom-call(s32[8,5]{1,0:T(8,128)} %part_hbm.1, s32[8,5]{1,0:T(8,128)} %slot_hbm.1, f32[8,5,128,128]{3,2,1,0:T(8,128)} %k_hbm.1, f32[8,5,128,128]{3,2,1,0:T(8,128)} %m_hbm.1), custom_call_target="tpu_custom_call" | custom-call | tf_op jit(solution)/shard_map/pallas_call | solution.py:458
  12.5 0.0 collective-permute-done.2.h_b
  12.6 0.7 collective-permute-done.1.h_f
  13.2 0.0 collective-permute-done.h_a
  13.2 2.8 %shard_map.79 = (f32[16,1024]{1,0:T(8,128)S(1)}, f32[16,1024]{1,0:T(8,128)S(1)}, f32[32,1024]{1,0:T(8,128)S(1)}, f32[2,32,128]{2,1,0:T(8,128)S(1)}, f32[32,9,1,128]{3,2,1,0:T(1,128)}) custom-call(s32[8,5]{1,0:T(8,128)S(1)} %get-tuple-element.39.cols, s32[2]{0:T(128)S(1)} %copy-done.24, f32[16,1024]{1,0:T(8,128)S(1)} %copy-done.5, ...), custom_call_target="tpu_custom_call" | custom-call | tf_op jit(solution)/shard_map/pallas_call | solution.py:468
  16.0 2.8 %all-to-all-start = ((f32[32,9,1,128]{3,2,1,0:T(1,128)}), f32[32,9,1,128]{3,2,1,0:T(1,128)S(1)}, u32[]{:S(2)}, u32[]{:S(2)}) async-start(f32[32,9,1,128]{3,2,1,0:T(1,128)} %get-tuple-element.44), calls=%async_computation | async-start | bytes 294912 | tf_op jit(solution)/shard_map/all_to_all | solution.py:441
  18.8 5.3 %collective-permute-start.5 = (f32[2,32,128]{2,1,0:T(8,128)S(1)}, f32[2,32,128]{2,1,0:T(8,128)S(1)}, u32[]{:S(2)}, u32[]{:S(2)}) collective-permute-start(f32[2,32,128]{2,1,0:T(8,128)S(1)} %get-tuple-element.43), channel_id=1, source_target_pairs={{0,31},{1,2},{2,1},{3,4},{4,3},{5,6},{6,5},{7,8},{8,7},{9,10},{10,... | collective-permute-start | bytes 98312 | tf_op jit(solution)/shard_map/ppermute | solution.py:438
  24.0 0.0 collective-permute-start.4
  24.1 0.0 collective-permute-start.3
  24.1 3.2 %all-to-all-done.red = f32[32,9,1,128]{3,2,1,0:T(1,128)S(1)} async-done(((f32[32,9,1,128]{3,2,1,0:T(1,128)}), f32[32,9,1,128]{3,2,1,0:T(1,128)S(1)}, u32[]{:S(2)}, u32[]{:S(2)}) %all-to-all-start) | async-done | bytes 147488 | tf_op jit(solution)/shard_map/all_to_all | solution.py:441
  27.3 1.4 %shard_map.80 = (f32[16,1024]{1,0:T(8,128)S(1)}, f32[16,1024]{1,0:T(8,128)S(1)}, f32[16,1024]{1,0:T(8,128)S(1)}, f32[80,1024]{1,0:T(8,128)S(1)}, f32[144,128]{1,0:T(8,128)S(1)}, /*index=5*/f32[1,16]{1,0:T(1,128)}) custom-call(f32[32,9,1,128]{3,2,1,0:T(1,128)S(1)} %all-to-all-done.red, f32[16,1024]{1,0:T(8,128)S(1)} %get-tuple-element.45.kb, ...), custom_call_target="tpu_custom_call" | custom-call | tf_op jit(solution)/shard_map/pallas_call | solution.py:473
  28.6 0.0 collective-permute-done.5.h_b
  28.6 0.2 collective-permute-done.4.h_f
  28.9 0.0 collective-permute-done.3.h_a
  28.9 1.7 %copy-done.1 = bf16[8,640,256]{2,1,0:T(8,128)(2,1)S(1)} copy-done((bf16[8,640,256]{2,1,0:T(8,128)(2,1)S(1)}, bf16[8,640,256]{2,1,0:T(8,128)(2,1)}, u32[]{:S(2)}) %copy-start.1) | copy-done | bytes 2621464
  30.6 1.9 %shard_map.81 = (f32[16,1024]{1,0:T(8,128)S(1)}, f32[16,1024]{1,0:T(8,128)S(1)}, f32[80,1024]{1,0:T(8,128)S(1)}, f32[48,768]{1,0:T(8,128)S(1)}, f32[32,1024]{1,0:T(8,128)S(1)}, /*index=5*/f32[2,48,128]{2,1,0:T(8,128)S(1)}) custom-call(s32[8,5]{1,0:T(8,128)S(1)} %get-tuple-element.39.cols, s32[2]{0:T(128)S(1)} %copy-done.24, ...), custom_call_target="tpu_custom_call" | custom-call | tf_op jit(solution)/shard_map/pallas_call | solution.py:476
  32.5 2.2 %collective-permute-start.8 = (f32[2,48,128]{2,1,0:T(8,128)S(1)}, f32[2,48,128]{2,1,0:T(8,128)S(1)}, u32[]{:S(2)}, u32[]{:S(2)}) collective-permute-start(f32[2,48,128]{2,1,0:T(8,128)S(1)} %get-tuple-element.54), channel_id=1, source_target_pairs={{0,31},{1,2},{2,1},{3,4},{4,3},{5,6},{6,5},{7,8},{8,7},{9,10},{10,... | collective-permute-start | bytes 147464 | tf_op jit(solution)/shard_map/ppermute | solution.py:438
  34.7 0.0 collective-permute-start.7
  34.7 0.0 collective-permute-start.6
  34.7 0.5 shard_map.82
  35.2 0.0 copy-start.17
  35.2 0.6 copy-done.17
  35.8 3.9 %collective-permute-done.8.h_b.q_b = f32[2,48,128]{2,1,0:T(8,128)S(1)} collective-permute-done((f32[2,48,128]{2,1,0:T(8,128)S(1)}, f32[2,48,128]{2,1,0:T(8,128)S(1)}, u32[]{:S(2)}, u32[]{:S(2)}) %collective-permute-start.8) | collective-permute-done | bytes 49184 | tf_op jit(solution)/shard_map/ppermute | solution.py:438
  39.8 0.2 collective-permute-done.7.h_f.q_f
  40.0 0.0 collective-permute-done.6.h_a.q_a
  40.0 1.7 %shard_map.83 = (f32[16,1024]{1,0:T(8,128)S(1)}, f32[2,16,128]{2,1,0:T(8,128)S(1)}, f32[32,16,128]{2,1,0:T(8,128)S(1)}) custom-call(s32[8,5]{1,0:T(8,128)S(1)} %get-tuple-element.39.cols, s32[2]{0:T(128)S(1)} %copy-done.25, f32[16,1024]{1,0:T(8,128)S(1)} %get-tuple-element.53.p, f32[2,48,128]{2,1,0:T(8,128)S(1)} %collective-permute-done.6.h_a.q_a, ...), custom_call_target="tpu_custom_call" | custom-call | tf_op jit(solution)/shard_map/pallas_call | solution.py:487
  41.8 0.7 copy-done.8
  42.5 0.6 copy-done.19
  43.1 0.6 copy-done.27
  43.7 2.6 %all-to-all-start.1 = ((f32[32,16,128]{2,1,0:T(8,128)}), f32[32,16,128]{2,1,0:T(8,128)S(1)}, u32[]{:S(2)}, u32[]{:S(2)}) async-start(f32[32,16,128]{2,1,0:T(8,128)} %copy-done.8), calls=%async_computation.1 | async-start | bytes 524288 | tf_op jit(solution)/shard_map/all_to_all | solution.py:441
  46.3 5.3 %collective-permute-start.11 = (f32[2,16,128]{2,1,0:T(8,128)}, f32[2,16,128]{2,1,0:T(8,128)}, u32[]{:S(2)}, u32[]{:S(2)}) collective-permute-start(f32[2,16,128]{2,1,0:T(8,128)} %copy-done.27), channel_id=1, source_target_pairs={{0,31},{1,2},{2,1},{3,4},{4,3},{5,6},{6,5},{7,8},{8,7},{9,10},{10,... | collective-permute-start | bytes 49160 | tf_op jit(solution)/shard_map/ppermute | solution.py:438
  51.6 0.0 collective-permute-start.10
  51.6 0.0 collective-permute-start.9
  51.6 6.1 %all-to-all-done.1.red = f32[32,16,128]{2,1,0:T(8,128)S(1)} async-done(((f32[32,16,128]{2,1,0:T(8,128)}), f32[32,16,128]{2,1,0:T(8,128)S(1)}, u32[]{:S(2)}, u32[]{:S(2)}) %all-to-all-start.1) | async-done | bytes 262176 | tf_op jit(solution)/shard_map/all_to_all | solution.py:441
  57.7 0.8 copy-done.20
  58.5 0.7 copy-done.22
  59.3 0.7 shard_map.84
  59.9 0.0 collective-permute-done.11.h_b
  59.9 0.0 collective-permute-done.10.h_f
  59.9 0.0 collective-permute-done.9.h_a
  60.0 1.7 %copy-done.3 = bf16[8,640,256]{2,1,0:T(8,128)(2,1)S(1)} copy-done((bf16[8,640,256]{2,1,0:T(8,128)(2,1)S(1)}, bf16[8,640,256]{2,1,0:T(8,128)(2,1)}, u32[]{:S(2)}) %copy-start.3) | copy-done | bytes 2621464
  61.7 0.8 copy-done.7
  62.5 0.8 copy-done.10
  63.3 0.8 copy-done.12
  64.1 0.8 copy-done.14
  64.9 0.9 %copy-done.16 = f32[48,768]{1,0:T(8,128)S(1)} copy-done((f32[48,768]{1,0:T(8,128)S(1)}, f32[48,768]{1,0:T(8,128)}, u32[]{:S(2)}) %copy-start.16) | copy-done | bytes 147480
  65.8 0.7 copy-done.26
  66.5 2.0 %shard_map.85 = (f32[16,1024]{1,0:T(8,128)S(1)}, f32[16,1024]{1,0:T(8,128)S(1)}, f32[2,16,128]{2,1,0:T(8,128)S(1)}) custom-call(s32[8,5]{1,0:T(8,128)S(1)} %get-tuple-element.39.cols, s32[2]{0:T(128)S(1)} %copy-done.26, f32[16,1024]{1,0:T(8,128)S(1)} %get-tuple-element.64.c_local, f32[32,128]{1,0:T(8,128)S(1)} %get-tuple-element.65.coefs, ...), custom_call_target="tpu_custom_call" | custom-call | tf_op jit(solution)/shard_map/pallas_call | solution.py:495
  68.5 1.1 %collective-permute-start.14 = (f32[2,16,128]{2,1,0:T(8,128)S(1)}, f32[2,16,128]{2,1,0:T(8,128)S(1)}, u32[]{:S(2)}, u32[]{:S(2)}) collective-permute-start(f32[2,16,128]{2,1,0:T(8,128)S(1)} %get-tuple-element.69), channel_id=1, source_target_pairs={{0,31},{1,2},{2,1},{3,4},{4,3},{5,6},{6,5},{7,8},{8,7},{9,10},{10,... | collective-permute-start | bytes 49160 | tf_op jit(solution)/shard_map/ppermute | solution.py:438
  69.6 0.4 collective-permute-start.13
  70.0 0.0 collective-permute-start.12
  70.0 0.2 shard_map.86.part
  70.3 5.0 %collective-permute-done.14.h_b = f32[2,16,128]{2,1,0:T(8,128)S(1)} collective-permute-done((f32[2,16,128]{2,1,0:T(8,128)S(1)}, f32[2,16,128]{2,1,0:T(8,128)S(1)}, u32[]{:S(2)}, u32[]{:S(2)}) %collective-permute-start.14) | collective-permute-done | bytes 16416 | tf_op jit(solution)/shard_map/ppermute | solution.py:438
  75.3 0.0 collective-permute-done.13.h_f
  75.3 0.0 collective-permute-done.12.h_a
  75.3 1.8 %shard_map.87 = (f32[16,1024]{1,0:T(8,128)S(1)}, f32[32,8,128]{2,1,0:T(8,128)S(1)}) custom-call(s32[8,5]{1,0:T(8,128)S(1)} %get-tuple-element.39.cols, f32[16,1024]{1,0:T(8,128)S(1)} %get-tuple-element.68.p, f32[2,16,128]{2,1,0:T(8,128)S(1)} %collective-permute-done.12.h_a, f32[2,16,128]{2,1,0:T(8,128)S(1)} %collective-permute-done.13.h_f, ...), custom_call_target="tpu_custom_call" | custom-call | tf_op jit(solution)/shard_map/pallas_call | solution.py:500
  77.1 10.4 %all_to_all.15.red = f32[32,8,128]{2,1,0:T(8,128)S(1)} all-to-all(f32[32,8,128]{2,1,0:T(8,128)S(1)} %get-tuple-element.71), channel_id=1, replica_groups=mesh['parts'=32] {'parts'}, dimensions={0} | all-to-all | bytes 262144 | tf_op jit(solution)/shard_map/all_to_all | solution.py:441
  87.6 1.6 %shard_map.88 = f32[16,1024]{1,0:T(8,128)} custom-call(f32[32,8,128]{2,1,0:T(8,128)S(1)} %all_to_all.15.red, f32[16,1024]{1,0:T(8,128)S(1)} %get-tuple-element.72.p, f32[16,1024]{1,0:T(8,128)S(1)} %copy-done.18, f32[80,1024]{1,0:T(8,128)S(1)} %get-tuple-element.57.words, f32[144,128]{1,0:T(8,128)S(1)} %get-tuple-element.52.small, f32[32,128]{1,0:T(8,128)S(1)} %copy-done.23, ...), custom_call_target="tpu_custom_call" | custom-call | tf_op jit(solution)/shard_map/pallas_call | solution.py:502
  (39 shorter events, 0.1 us)
Async XLA Ops:
  2.0 11.2 %copy-start.5 = (f32[16,1024]{1,0:T(8,128)S(1)}, f32[16,1024]{1,0:T(8,128)}, u32[]{:S(2)}) copy-start(f32[16,1024]{1,0:T(8,128)} %basis.5) | copy-start | bytes 196612
  2.0 11.2 %copy-start.24 = (s32[2]{0:T(128)S(1)}, s32[2]{0:T(128)}, u32[]{:S(2)}) copy-start(s32[2]{0:T(128)} %iface.7) | copy-start | bytes 28
  2.1 10.5 %collective-permute-start.2 = (f32[2,16,128]{2,1,0:T(8,128)S(1)}, f32[2,16,128]{2,1,0:T(8,128)S(1)}, u32[]{:S(2)}, u32[]{:S(2)}) collective-permute-start(f32[2,16,128]{2,1,0:T(8,128)S(1)} %shard_map.78), channel_id=1, source_target_pairs={{0,31},{1,2},{2,1},{3,4},{4,3},{5,6},{6,5},{7,8},{8,7},{9,10},{10,... | collective-permute-start | bytes 49160 | tf_op jit(solution)/shard_map/ppermute | solution.py:438
  8.6 4.6 %collective-permute-start.1 = (f32[2,16,128]{2,1,0:T(8,128)S(1)}, f32[2,16,128]{2,1,0:T(8,128)S(1)}, u32[]{:S(2)}, u32[]{:S(2)}) collective-permute-start(f32[2,16,128]{2,1,0:T(8,128)S(1)} %shard_map.78), channel_id=1, source_target_pairs={{0,16},{1,17},{2,18},{3,19},{4,20},{5,21},{6,22},{7,23},{8,24},{9,... | collective-permute-start | bytes 49160 | tf_op jit(solution)/shard_map/ppermute | solution.py:438
  8.6 4.6 %collective-permute-start = (f32[2,16,128]{2,1,0:T(8,128)S(1)}, f32[2,16,128]{2,1,0:T(8,128)S(1)}, u32[]{:S(2)}, u32[]{:S(2)}) collective-permute-start(f32[2,16,128]{2,1,0:T(8,128)S(1)} %shard_map.78), channel_id=1, source_target_pairs={{0,1},{1,0},{2,3},{3,2},{4,5},{5,4},{6,7},{7,6},{8,9},{9,8},{10,11... | collective-permute-start | bytes 49160 | tf_op jit(solution)/shard_map/ppermute | solution.py:438
  12.5 3.5 %copy-start = (bf16[8,640,256]{2,1,0:T(8,128)(2,1)}, bf16[8,640,256]{2,1,0:T(8,128)(2,1)S(1)}, u32[]{:S(2)}) copy-start(bf16[8,640,256]{2,1,0:T(8,128)(2,1)S(1)} %get-tuple-element.41.w_low) | copy-start | bytes 7864324
  16.0 11.3 %all-to-all-start = ((f32[32,9,1,128]{3,2,1,0:T(1,128)}), f32[32,9,1,128]{3,2,1,0:T(1,128)S(1)}, u32[]{:S(2)}, u32[]{:S(2)}) async-start(f32[32,9,1,128]{3,2,1,0:T(1,128)} %get-tuple-element.44), calls=%async_computation | async-start | bytes 294912 | tf_op jit(solution)/shard_map/all_to_all | solution.py:441
  18.8 9.9 %collective-permute-start.5 = (f32[2,32,128]{2,1,0:T(8,128)S(1)}, f32[2,32,128]{2,1,0:T(8,128)S(1)}, u32[]{:S(2)}, u32[]{:S(2)}) collective-permute-start(f32[2,32,128]{2,1,0:T(8,128)S(1)} %get-tuple-element.43), channel_id=1, source_target_pairs={{0,31},{1,2},{2,1},{3,4},{4,3},{5,6},{6,5},{7,8},{8,7},{9,10},{10,... | collective-permute-start | bytes 98312 | tf_op jit(solution)/shard_map/ppermute | solution.py:438
  24.0 4.8 %collective-permute-start.4 = (f32[2,32,128]{2,1,0:T(8,128)S(1)}, f32[2,32,128]{2,1,0:T(8,128)S(1)}, u32[]{:S(2)}, u32[]{:S(2)}) collective-permute-start(f32[2,32,128]{2,1,0:T(8,128)S(1)} %get-tuple-element.43), channel_id=1, source_target_pairs={{0,16},{1,17},{2,18},{3,19},{4,20},{5,21},{6,22},{7,23},{8,24},{9,... | collective-permute-start | bytes 98312 | tf_op jit(solution)/shard_map/ppermute | solution.py:438
  24.1 4.8 %collective-permute-start.3 = (f32[2,32,128]{2,1,0:T(8,128)S(1)}, f32[2,32,128]{2,1,0:T(8,128)S(1)}, u32[]{:S(2)}, u32[]{:S(2)}) collective-permute-start(f32[2,32,128]{2,1,0:T(8,128)S(1)} %get-tuple-element.43), channel_id=1, source_target_pairs={{0,1},{1,0},{2,3},{3,2},{4,5},{5,4},{6,7},{7,6},{8,9},{9,8},{10,11... | collective-permute-start | bytes 98312 | tf_op jit(solution)/shard_map/ppermute | solution.py:438
  28.6 3.9 %copy-start.6 = (f32[16,1024]{1,0:T(8,128)}, f32[16,1024]{1,0:T(8,128)S(1)}, u32[]{:S(2)}) copy-start(f32[16,1024]{1,0:T(8,128)S(1)} %get-tuple-element.49.mo) | copy-start | bytes 196612
  28.9 1.7 %copy-start.1 = (bf16[8,640,256]{2,1,0:T(8,128)(2,1)S(1)}, bf16[8,640,256]{2,1,0:T(8,128)(2,1)}, u32[]{:S(2)}) copy-start(bf16[8,640,256]{2,1,0:T(8,128)(2,1)} %copy-done) | copy-start | bytes 7864324
  30.6 9.4 %copy-start.2 = (bf16[8,640,256]{2,1,0:T(8,128)(2,1)S(1)}, bf16[8,640,256]{2,1,0:T(8,128)(2,1)}, u32[]{:S(2)}) copy-start(bf16[8,640,256]{2,1,0:T(8,128)(2,1)} %copy-done) | copy-start | bytes 7864324
  30.6 9.4 %copy-start.25 = (s32[2]{0:T(128)S(1)}, s32[2]{0:T(128)}, u32[]{:S(2)}) copy-start(s32[2]{0:T(128)} %iface.7) | copy-start | bytes 28
  32.5 9.2 %copy-start.15 = (f32[48,768]{1,0:T(8,128)}, f32[48,768]{1,0:T(8,128)S(1)}, u32[]{:S(2)}) copy-start(f32[48,768]{1,0:T(8,128)S(1)} %get-tuple-element.67.words_halo) | copy-start | bytes 442372
  32.5 7.3 %collective-permute-start.8 = (f32[2,48,128]{2,1,0:T(8,128)S(1)}, f32[2,48,128]{2,1,0:T(8,128)S(1)}, u32[]{:S(2)}, u32[]{:S(2)}) collective-permute-start(f32[2,48,128]{2,1,0:T(8,128)S(1)} %get-tuple-element.54), channel_id=1, source_target_pairs={{0,31},{1,2},{2,1},{3,4},{4,3},{5,6},{6,5},{7,8},{8,7},{9,10},{10,... | collective-permute-start | bytes 147464 | tf_op jit(solution)/shard_map/ppermute | solution.py:438
  34.7 5.3 %collective-permute-start.7 = (f32[2,48,128]{2,1,0:T(8,128)S(1)}, f32[2,48,128]{2,1,0:T(8,128)S(1)}, u32[]{:S(2)}, u32[]{:S(2)}) collective-permute-start(f32[2,48,128]{2,1,0:T(8,128)S(1)} %get-tuple-element.54), channel_id=1, source_target_pairs={{0,16},{1,17},{2,18},{3,19},{4,20},{5,21},{6,22},{7,23},{8,24},{9,... | collective-permute-start | bytes 147464 | tf_op jit(solution)/shard_map/ppermute | solution.py:438
  34.7 5.3 %collective-permute-start.6 = (f32[2,48,128]{2,1,0:T(8,128)S(1)}, f32[2,48,128]{2,1,0:T(8,128)S(1)}, u32[]{:S(2)}, u32[]{:S(2)}) collective-permute-start(f32[2,48,128]{2,1,0:T(8,128)S(1)} %get-tuple-element.54), channel_id=1, source_target_pairs={{0,1},{1,0},{2,3},{3,2},{4,5},{5,4},{6,7},{7,6},{8,9},{9,8},{10,11... | collective-permute-start | bytes 147464 | tf_op jit(solution)/shard_map/ppermute | solution.py:438
  35.2 0.6 copy-start.17
  35.8 5.9 %copy-start.21 = (f32[32,128]{1,0:T(8,128)}, f32[32,128]{1,0:T(8,128)S(1)}, u32[]{:S(2)}) copy-start(f32[32,128]{1,0:T(8,128)S(1)} %get-tuple-element.63.small_b) | copy-start | bytes 49156
  39.8 2.0 %copy-start.9 = (f32[2,48,128]{2,1,0:T(8,128)}, f32[2,48,128]{2,1,0:T(8,128)S(1)}, u32[]{:S(2)}) copy-start(f32[2,48,128]{2,1,0:T(8,128)S(1)} %collective-permute-done.8.h_b.q_b) | copy-start | bytes 147460
  40.0 1.8 %copy-start.11 = (f32[2,48,128]{2,1,0:T(8,128)}, f32[2,48,128]{2,1,0:T(8,128)S(1)}, u32[]{:S(2)}) copy-start(f32[2,48,128]{2,1,0:T(8,128)S(1)} %collective-permute-done.7.h_f.q_f) | copy-start | bytes 147460
  40.0 1.8 %copy-start.13 = (f32[2,48,128]{2,1,0:T(8,128)}, f32[2,48,128]{2,1,0:T(8,128)S(1)}, u32[]{:S(2)}) copy-start(f32[2,48,128]{2,1,0:T(8,128)S(1)} %collective-permute-done.6.h_a.q_a) | copy-start | bytes 147460
  41.8 0.7 copy-start.8
  42.5 0.6 copy-start.19
  43.1 0.6 copy-start.27
  43.7 14.0 %all-to-all-start.1 = ((f32[32,16,128]{2,1,0:T(8,128)}), f32[32,16,128]{2,1,0:T(8,128)S(1)}, u32[]{:S(2)}, u32[]{:S(2)}) async-start(f32[32,16,128]{2,1,0:T(8,128)} %copy-done.8), calls=%async_computation.1 | async-start | bytes 524288 | tf_op jit(solution)/shard_map/all_to_all | solution.py:441
  46.3 13.6 %collective-permute-start.11 = (f32[2,16,128]{2,1,0:T(8,128)}, f32[2,16,128]{2,1,0:T(8,128)}, u32[]{:S(2)}, u32[]{:S(2)}) collective-permute-start(f32[2,16,128]{2,1,0:T(8,128)} %copy-done.27), channel_id=1, source_target_pairs={{0,31},{1,2},{2,1},{3,4},{4,3},{5,6},{6,5},{7,8},{8,7},{9,10},{10,... | collective-permute-start | bytes 49160 | tf_op jit(solution)/shard_map/ppermute | solution.py:438
  51.6 8.4 %collective-permute-start.10 = (f32[2,16,128]{2,1,0:T(8,128)}, f32[2,16,128]{2,1,0:T(8,128)}, u32[]{:S(2)}, u32[]{:S(2)}) collective-permute-start(f32[2,16,128]{2,1,0:T(8,128)} %copy-done.27), channel_id=1, source_target_pairs={{0,16},{1,17},{2,18},{3,19},{4,20},{5,21},{6,22},{7,23},{8,24},{9,... | collective-permute-start | bytes 49160 | tf_op jit(solution)/shard_map/ppermute | solution.py:438
  51.6 8.4 %collective-permute-start.9 = (f32[2,16,128]{2,1,0:T(8,128)}, f32[2,16,128]{2,1,0:T(8,128)}, u32[]{:S(2)}, u32[]{:S(2)}) collective-permute-start(f32[2,16,128]{2,1,0:T(8,128)} %copy-done.27), channel_id=1, source_target_pairs={{0,1},{1,0},{2,3},{3,2},{4,5},{5,4},{6,7},{7,6},{8,9},{9,8},{10,11... | collective-permute-start | bytes 49160 | tf_op jit(solution)/shard_map/ppermute | solution.py:438
  57.7 0.8 copy-start.20
  58.5 0.7 copy-start.22
  60.0 1.7 %copy-start.3 = (bf16[8,640,256]{2,1,0:T(8,128)(2,1)S(1)}, bf16[8,640,256]{2,1,0:T(8,128)(2,1)}, u32[]{:S(2)}) copy-start(bf16[8,640,256]{2,1,0:T(8,128)(2,1)} %copy-done) | copy-start | bytes 7864324
  61.7 0.8 copy-start.7
  62.5 0.8 copy-start.10
  63.3 0.8 copy-start.12
  64.1 0.8 copy-start.14
  64.9 0.9 %copy-start.16 = (f32[48,768]{1,0:T(8,128)S(1)}, f32[48,768]{1,0:T(8,128)}, u32[]{:S(2)}) copy-start(f32[48,768]{1,0:T(8,128)} %copy-done.15) | copy-start | bytes 442372
  65.8 0.7 copy-start.26
  66.5 8.8 %copy-start.4 = (bf16[8,640,256]{2,1,0:T(8,128)(2,1)S(1)}, bf16[8,640,256]{2,1,0:T(8,128)(2,1)}, u32[]{:S(2)}) copy-start(bf16[8,640,256]{2,1,0:T(8,128)(2,1)} %copy-done) | copy-start | bytes 7864324
  68.5 6.8 %collective-permute-start.14 = (f32[2,16,128]{2,1,0:T(8,128)S(1)}, f32[2,16,128]{2,1,0:T(8,128)S(1)}, u32[]{:S(2)}, u32[]{:S(2)}) collective-permute-start(f32[2,16,128]{2,1,0:T(8,128)S(1)} %get-tuple-element.69), channel_id=1, source_target_pairs={{0,31},{1,2},{2,1},{3,4},{4,3},{5,6},{6,5},{7,8},{8,7},{9,10},{10,... | collective-permute-start | bytes 49160 | tf_op jit(solution)/shard_map/ppermute | solution.py:438
  69.6 5.7 %collective-permute-start.13 = (f32[2,16,128]{2,1,0:T(8,128)S(1)}, f32[2,16,128]{2,1,0:T(8,128)S(1)}, u32[]{:S(2)}, u32[]{:S(2)}) collective-permute-start(f32[2,16,128]{2,1,0:T(8,128)S(1)} %get-tuple-element.69), channel_id=1, source_target_pairs={{0,16},{1,17},{2,18},{3,19},{4,20},{5,21},{6,22},{7,23},{8,24},{9,... | collective-permute-start | bytes 49160 | tf_op jit(solution)/shard_map/ppermute | solution.py:438
  70.0 5.3 %collective-permute-start.12 = (f32[2,16,128]{2,1,0:T(8,128)S(1)}, f32[2,16,128]{2,1,0:T(8,128)S(1)}, u32[]{:S(2)}, u32[]{:S(2)}) collective-permute-start(f32[2,16,128]{2,1,0:T(8,128)S(1)} %get-tuple-element.69), channel_id=1, source_target_pairs={{0,1},{1,0},{2,3},{3,2},{4,5},{5,4},{6,7},{7,6},{8,9},{9,8},{10,11... | collective-permute-start | bytes 49160 | tf_op jit(solution)/shard_map/ppermute | solution.py:438
  70.2 17.3 %copy-start.18 = (f32[16,1024]{1,0:T(8,128)S(1)}, f32[16,1024]{1,0:T(8,128)}, u32[]{:S(2)}) copy-start(f32[16,1024]{1,0:T(8,128)} %copy-done.17) | copy-start | bytes 196612
  70.3 17.3 %copy-start.23 = (f32[32,128]{1,0:T(8,128)S(1)}, f32[32,128]{1,0:T(8,128)}, u32[]{:S(2)}) copy-start(f32[32,128]{1,0:T(8,128)} %copy-done.21) | copy-start | bytes 49156

commit v4 on v3

--- a/solution.py
+++ b/solution.py
@@ -56,10 +56,10 @@
 
 def nt3(high, low, right):
     dims = (((1,), (1,)), ((), ()))
-    rh, rl = split(right)
     n = high.shape[0]
-    both = lax.dot_general(jnp.concatenate([high, low], axis=0), rh, dims, preferred_element_type=F32)
-    return both[:n] + both[n:] + lax.dot_general(high, rl, dims, preferred_element_type=F32)
+    left = jnp.concatenate([high, low], axis=0)
+    both = sum(lax.dot_general(left, part, dims, preferred_element_type=F32) for part in split(right))
+    return both[:n] + both[n:]
 
 
 def rows(parts):
@@ -146,19 +146,16 @@
     return jnp.sum(jnp.where(lane == row, a, 0.0), axis=1, keepdims=True)
 
 
-def k_first(iface_hbm, basis, outgoing, iface, sems):
-    copy = pltpu.make_async_copy(iface_hbm, iface, sems.at[0])
-    copy.start()
-    copy.wait()
-    width = outgoing.shape[2]
-    copies = []
-    for slot in range(outgoing.shape[0]):
-        start = pl.multiple_of(iface[slot] * width, width)
-        copy = pltpu.make_async_copy(basis.at[:, pl.ds(start, width)], outgoing.at[slot], sems.at[slot])
+def k_first(iface_hbm, basis_hbm, outgoing, iface, basis, sems):
+    copies = [
+        pltpu.make_async_copy(iface_hbm, iface, sems.at[0]),
+        pltpu.make_async_copy(basis_hbm, basis, sems.at[1]),
+    ]
+    for copy in copies:
         copy.start()
-        copies.append(copy)
     for copy in copies:
         copy.wait()
+    send_tiles(iface, outgoing, 0, basis)
 
 
 def make_prep(count):
@@ -224,6 +221,30 @@
     return rows([jnp.where(keep, value, 0.0), jnp.where(keep, pltpu.roll(value, MAT // 2, 1), 0.0)])
 
 
+def pack_rows(value):
+    lane, row = lane_row(value.shape)
+    m = value.shape[0] // 2
+    n = MAT // m
+    shift = n
+    while shift < MAT:
+        value = value + pltpu.roll(value, shift, 1)
+        shift *= 2
+    value = jnp.where(lane // n == row % m, value, 0.0)
+    return [jnp.sum(value[k * m : (k + 1) * m], axis=0, keepdims=True) for k in range(2)]
+
+
+def unpack_rows(pair, m):
+    value = rows([jnp.broadcast_to(part, (m, MAT)) for part in pair])
+    lane, row = lane_row(value.shape)
+    n = MAT // m
+    value = jnp.where(lane // n == row % m, value, 0.0)
+    shift = n
+    while shift < MAT:
+        value = value + pltpu.roll(value, shift, 1)
+        shift *= 2
+    return value
+
+
 def make_kernels(n, scale):
     def put_small(ref, k, value):
         ref[k * n : (k + 1) * n] = jnp.broadcast_to(value, (n, MAT)) if value.shape[1] == 1 else lanes(
@@ -242,7 +263,7 @@
         u[n:] = mb[...] * d
         send_tiles(iface, outgoing, 0, u)
         right = rows([basis[...], u[...], kb[...], mb[...], jnp.zeros((MAT - 5 * n, basis.shape[1]), F32)])
-        both = nt(rows([basis[...], mb[...]]), right) * scale
+        both = nt3(*split(rows([basis[...], mb[...]])), right) * scale
         lane, row = lane_row((n, MAT))
         chosen = jnp.where(lane < 3 * n, both[:n], both[n:])
         mass = pltpu.roll(chosen, MAT - 4 * n, 1)
@@ -317,8 +338,10 @@
         high, low = split(rows([mm3(lc, mb[...]), v]))
         tests_high[...] = high
         tests_low[...] = low
-        put_small(small_b, 0, nt(mm(lv, get_small(small, 1)), lc))
-        put_small(small_b, 1, nt(mm(lc, get_small(small, 4)), lv))
+        mass = nt(mm(lv, get_small(small, 1)), lc)
+        ef = nt(mm(lc, get_small(small, 4)), lv)
+        for k, value in enumerate((mass, ef, mm(ef, get_small(small, 0)), mm(ef, mass))):
+            put_small(small_b, k, value)
         right = rows([image0[...], kf[...], p[...], words[n : 3 * n], jnp.zeros((2 * n, p.shape[1]), F32)])
         both = nt3(high, low, right) * scale
         lane, _ = lane_row((n, MAT))
@@ -337,7 +360,7 @@
         return fresh, jnp.where(lane < n, both[:n], both[n:])
 
     def k_c1(
-        cols, iface, p, h_a, h_f, h_b, c0, small, part, tests_high, tests_low, w_high, w_low, inv_d,
+        cols, iface, p, h_a, h_f, h_b, c0, small, part, pair, tests_high, tests_low, w_high, w_low, inv_d,
         p_out, outgoing, grams, xs, res,
     ):
         fresh, added = half(
@@ -346,20 +369,26 @@
         )
         p_out[...] = fresh
         send_tiles(iface, outgoing, 0, p_out)
+        chip = part[...] + pair[...]
+        chip = jnp.where(lax.axis_index("parts") % 2 == 0, chip, pltpu.roll(chip, MAT - 3 * n, 1))
         lane, _ = lane_row((n, MAT))
-        fill_blocks(grams, jnp.where(lane < 6 * n, part[...], pltpu.roll(added, 6 * n, 1)))
-
-    def solve(small, small_b, g_left, g_kf, g_mf, g_p, g_h1, g_h2, g_a, g_fresh):
-        cross, e1, e2 = (get_small(small, k) for k in (0, 2, 3))
-        mass, ef = (get_small(small_b, k) for k in range(2))
+        first = jnp.where(lane < 3 * n, chip, pltpu.roll(added, 3 * n, 1))
+        packed = fold(jnp.where(lane < 4 * n, first, 0.0))
+        fifth = pack_rows(jnp.where(lane < n, pltpu.roll(added, MAT - n, 1), 0.0))
+        for device in range(grams.shape[0]):
+            grams[device, : n // 2, 0, :] = packed
+            for k in range(2):
+                grams[device, n // 2 + k] = fifth[k]
+
+    def solve(small, small_b, kf_test, mf_test, g_left, g_p, g_a):
+        cross, mass, ef = get_small(small, 0), get_small(small_b, 0), get_small(small_b, 1)
         theta = small[5 * n : 6 * n, :1]
         right = g_p + relax * mm(g_left, ef)
-        left = (
-            g_a
-            + mm(lanes([relax * g_left, -relax * theta * g_left]), rows([g_kf, g_mf]))
-            + mm(lanes([-right, theta * right]), rows([cross, mass]))
+        left = g_a + mm(
+            lanes([relax * g_left, -relax * theta * g_left, -g_p, theta * g_p]),
+            rows([kf_test, mf_test, cross, mass]),
         )
-        coef = lanes(
+        return lanes(
             [
                 relax * (g_left + left),
                 -relax * relax * g_left,
@@ -368,17 +397,30 @@
                 -relax * theta * right,
             ]
         )
-        after = g_fresh + mm(coef, rows([ef, g_h1, g_h2, e1, e2]))
-        return coef, after
-
-    def k_d0(red, p, words, small, small_b, c_out, words_grams, coefs):
-        g = [value[:, :n] for value in blocks_of(total(red), n)]
-        coef, right = solve(small, small_b, *g)
-        for k, index in enumerate((1, 2, 4, 5)):
-            put_small(words_grams, k, g[index])
+
+    def k_d0(red, p, words, small, small_b, c_out, tests_out, onto_v, coefs):
+        half_n = n // 2
+        sums = [red[device, :half_n, 0, :] for device in range(2)]
+        fifth = [red[0, half_n + k] + red[1, half_n + k] for k in range(2)]
+        for device in range(2, red.shape[0]):
+            sums[device % 2] = sums[device % 2] + red[device, :half_n, 0, :]
+            for k in range(2):
+                fifth[k] = fifth[k] + red[device, half_n + k]
+        lane, _ = lane_row((n, MAT))
+        whole = jnp.where(lane < 4 * n, unfold(sums[0]), jnp.where(lane < 5 * n, unpack_rows(fifth, half_n), 0.0))
+        g_left, g_kf, g_mf, g_a, g_fresh = (value[:, :n] for value in blocks_of(whole, n)[:5])
+        g_p, g_h1, g_h2, g_a_odd = (value[:, :n] for value in blocks_of(unfold(sums[1]), n)[:4])
+        g_a = g_a + g_a_odd
+        kf_test, mf_test = g_kf - get_small(small_b, 2), g_mf - get_small(small_b, 3)
+        coef = solve(small, small_b, kf_test, mf_test, g_left, g_p, g_a)
+        c_out[...] = p[...] + mm3(coef, words[...])
+        put_small(tests_out, 0, kf_test)
+        put_small(tests_out, 1, mf_test)
+        onto = (get_small(small_b, 1), g_h1, g_h2, get_small(small, 2), get_small(small, 3))
+        for k, value in enumerate(onto):
+            put_small(onto_v, k, value)
         coefs[:n] = lanes([coef, jnp.zeros((n, MAT - 5 * n), F32)])
-        put_small(coefs, 1, right)
-        c_out[...] = p[...] + mm3(coef, words[...])
+        put_small(coefs, 1, g_fresh + mm(coef, rows(list(onto))))
 
     def k_d1(
         cols, iface, c_local, coefs, h_a, h_f, h_b, q_a, q_f, q_b, ko, mo, c0, words_halo, small,
@@ -396,11 +438,13 @@
         p_out[...] = c_local[...] + c0[...] - relax * inv_d[...] * image
         send_tiles(iface, outgoing, 0, p_out)
 
-    def k_e0(image2, p, tests_high, tests_low, part):
+    def k_e0(image2, p, tests_high, tests_low, v, words, onto_v, part, last_high, last_low):
         right = rows([image2[...], p[...], jnp.zeros((MAT - 2 * n, p.shape[1]), F32)])
         both = nt3(tests_high[...], tests_low[...], right) * scale
         lane, _ = lane_row((n, MAT))
         part[...] = jnp.where(lane < n, both[:n], both[n:])
+        free = words[...] - mm3(onto_v[:, :n], v[...])
+        last_high[...], last_low[...] = split(rows([free, v[...]]))
 
     def k_e1(
         cols, p, h_a, h_f, h_b, c0, small, part, tests_high, tests_low, w_high, w_low, inv_d, p_out, grams, xs, res
@@ -414,11 +458,13 @@
         both = jnp.where(lane < 2 * n, part[...], pltpu.roll(added, 2 * n, 1))
         fill_blocks(grams, fold(jnp.where(lane < 4 * n, both, 0.0)))
 
-    def k_f(red, p, v, words, small, small_b, words_grams, out):
+    def k_f(red, p, small, small_b, tests_in, last_high, last_low, out):
         g_left, g_p, g_a, g_fresh = (value[:, :n] for value in blocks_of(unfold(total(red)), n)[:4])
-        g_kf, g_mf, g_h1, g_h2 = (get_small(words_grams, k) for k in range(4))
-        coef, right = solve(small, small_b, g_left, g_kf, g_mf, g_p, g_h1, g_h2, g_a, g_fresh)
-        out[...] = p[...] + mm3(lanes([coef, -right]), rows([words[...], v[...]]))
+        coef = solve(small, small_b, get_small(tests_in, 0), get_small(tests_in, 1), g_left, g_p, g_a)
+        high, low = split(lanes([coef, -g_fresh]))
+        both = jnp.dot(rows([high, low]), last_high[...], preferred_element_type=F32)
+        low = jnp.dot(high, last_low[...], preferred_element_type=F32)
+        out[...] = p[...] + both[:n] + both[n:] + low
 
     return k_a, k_b0, k_b1, k_c0, k_c1, k_d0, k_d1, k_e0, k_e1, k_f
 
@@ -447,12 +493,14 @@
     vecs = lambda m: ((m * n, local), F32)
     mats = lambda m: ((m * n, MAT), F32)
     out = lambda m: ((count, m, width), F32)
-    grams16 = ((parts, n, MAT), F32)
     grams8 = ((parts, n // 2, MAT), F32)
     res = pltpu.VMEM((2, n, local), F32)
 
     (outgoing,) = call(
-        k_first, [out(n)], [HBM, HBM], [pltpu.SMEM((count,), jnp.int32), pltpu.SemaphoreType.DMA((count,))]
+        k_first,
+        [out(n)],
+        [HBM, HBM],
+        [pltpu.SMEM((count,), jnp.int32), pltpu.VMEM((n, local), F32), pltpu.SemaphoreType.DMA((2,))],
     )(in_hbm(iface), in_hbm(basis))
     h0 = halo(outgoing)
     w_high, w_low, inv_d, cols = call(
@@ -481,25 +529,27 @@
     )(cols, iface, *h1, *w, ko, mo, c0, words, small)
     h2 = halo(outgoing)
     v, tests_high, tests_low, small_b, part = call(
-        k_c0, [vec] + [((2 * n, local), BF16)] * 2 + [mats(2), mats(1)], [VM] * 7
+        k_c0, [vec] + [((2 * n, local), BF16)] * 2 + [mats(4), mats(1)], [VM] * 7
     )(small, basis, mb, image0, kf, p1, words)
     tests = (tests_high, tests_low)
-    p2, outgoing, grams = call(k_c1, [vec, out(n), grams16], [SM, SM] + [VM] * 12, [xs(n), res])(
-        cols, iface, p1, *h2, c0, small, part, *tests, *w
+    pair = lax.ppermute(part, "parts", chip)
+    packed = ((parts, n // 2 + 2, 1, MAT), F32)
+    p2, outgoing, grams = call(k_c1, [vec, out(n), packed], [SM, SM] + [VM] * 13, [xs(n), res])(
+        cols, iface, p1, *h2, c0, small, part, pair, *tests, *w
     )
     red = reduced(grams)
     h3 = halo(outgoing)
-    c2, words_grams, coefs = call(k_d0, [vec, mats(4), mats(2)], [VM] * 5)(
+    c2, word_tests, onto_v, coefs = call(k_d0, [vec, mats(2), mats(5), mats(2)], [VM] * 5)(
         red, p2, words, small, small_b
     )
     p3, image2, outgoing = call(k_d1, [vec, vec, out(n)], [SM, SM] + [VM] * 16, [xs(n), res])(
         cols, iface, c2, coefs, *h3, *h2, ko, mo, c0, words_halo, small, *w
     )
     h4 = halo(outgoing)
-    (part,) = call(k_e0, [mats(1)], [VM] * 4)(image2, p3, *tests)
+    part, *last = call(k_e0, [mats(1)] + [((6 * n, local), BF16)] * 2, [VM] * 7)(image2, p3, *tests, v, words, onto_v)
     p4, grams = call(k_e1, [vec, grams8], [SM] + [VM] * 12, [xs(n), res])(cols, p3, *h4, c0, small, part, *tests, *w)
     red = reduced(grams)
-    (correct,) = call(k_f, [vec], [VM] * 7)(red, p4, v, words, small, small_b, words_grams)
+    (correct,) = call(k_f, [vec], [VM] * 7)(red, p4, small, small_b, word_tests, *last)
     return (correct, theta.reshape(-1))
 
 

time: 89.9 us -> 84.8 us (0.943)
  waiting for transfers between devices: 19.4 us -> 15.7 us
  local copies, waits for them, and re-layouts: 12.4 us -> 10.2 us
  starting transfers between devices: 26.1 us -> 27.3 us
    all_to_all x2, waiting for transfers between devices: 9.35 us -> 6.59 us  [reduced(): return lax.all_to_all(blocks_out, 'parts', 0, 0, tiled=True)]
    unnamed x56 -> x50, local copies, waits for them, and re-layouts: 12.4 us -> 10.2 us
    ppermute x15, waiting for transfers between devices: 10.1 us -> 8.28 us  [halo(): lax.ppermute(outgoing, 'parts', pairs)]
  transfers between devices with their start and end apart: 17 -> 18, of which waited for: 7 -> 8; matrix products, arithmetic and copies ran while one was open for 0% -> 0% of each run, Pallas kernels for 7% -> 8%
where the time goes in v4:
time: 84.8 us; the launch traced here: 84.2 us
  starting transfers between devices  27.3 us (32%)
  Pallas kernels  19.6 us (23%)
  waiting for transfers between devices  15.7 us (19%)
  blocking collectives  10.4 us (12%)
  local copies, waits for them, and re-layouts  10.2 us (12%)
  between operations  0.9 us (1%)
    ppermute x15, starting transfers between devices, halo(): lax.ppermute(outgoing, 'parts', pairs)  21.4 us
    all_to_all x1, blocking collectives, reduced(): return lax.all_to_all(blocks_out, 'parts', 0, 0, tiled=True)  10.4 us
    unnamed x50, local copies, waits for them, and re-layouts  10.2 us
    ppermute x15, waiting for transfers between devices, halo(): lax.ppermute(outgoing, 'parts', pairs)  8.28 us
    all_to_all x2, waiting for transfers between devices, reduced(): return lax.all_to_all(blocks_out, 'parts', 0, 0, tiled=True)  6.59 us
    all_to_all x2, starting transfers between devices, reduced(): return lax.all_to_all(blocks_out, 'parts', 0, 0, tiled=True)  5.34 us
    pallas_call x1, Pallas kernels, shards(): call(make_prep(count), [((tiles, blocks * width, 2 * width), BF16)] * 2 +...  3.94 us
    pallas_call x1, Pallas kernels, shards(): call(k_a, [vec, vec, vecs(2), out(2 * n), packed], [SM, SM] + [VM] * 7, [...  2.66 us
  transfers between devices with their start and end apart: 18, of which 8 were waited for; matrix products, arithmetic and copies ran while one was open for 0% of the time, Pallas kernels for 8%

profile of v4, /device:TPU:0, one launch (start us, length us, event | category | flops | bytes accessed | tf_op | source)
XLA Modules:
  0.0 84.2 jit_solution(7896284776966417039)
XLA Ops:
  0.6 0.9 %shard_map.78 = f32[2,16,128]{2,1,0:T(8,128)S(1)} custom-call(s32[2]{0:T(128)} %iface.7, f32[16,1024]{1,0:T(8,128)} %basis.3), custom_call_target="tpu_custom_call" | custom-call | tf_op jit(solution)/shard_map/pallas_call | solution.py:499
  1.5 0.0 copy-start.5
  1.5 0.0 copy-start.21
  1.5 6.5 %collective-permute-start.2 = (f32[2,16,128]{2,1,0:T(8,128)S(1)}, f32[2,16,128]{2,1,0:T(8,128)S(1)}, u32[]{:S(2)}, u32[]{:S(2)}) collective-permute-start(f32[2,16,128]{2,1,0:T(8,128)S(1)} %shard_map.78), channel_id=1, source_target_pairs={{0,31},{1,2},{2,1},{3,4},{4,3},{5,6},{6,5},{7,8},{8,7},{9,10},{10,... | collective-permute-start | bytes 49160 | tf_op jit(solution)/shard_map/ppermute | solution.py:484
  8.0 0.0 collective-permute-start.1
  8.0 0.0 collective-permute-start
  8.0 3.9 %shard_map.77 = (bf16[8,640,256]{2,1,0:T(8,128)(2,1)S(1)}, bf16[8,640,256]{2,1,0:T(8,128)(2,1)S(1)}, f32[1,1024]{1,0:T(1,128)S(1)}, s32[8,5]{1,0:T(8,128)S(1)}) custom-call(s32[8,5]{1,0:T(8,128)} %part_hbm.1, s32[8,5]{1,0:T(8,128)} %slot_hbm.1, f32[8,5,128,128]{3,2,1,0:T(8,128)} %k_hbm.1, f32[8,5,128,128]{3,2,1,0:T(8,128)} %m_hbm.1), custom_call_target="tpu_custom_call" | custom-call | tf_op jit(solution)/shard_map/pallas_call | solution.py:506
  11.9 0.0 copy-start
  12.0 0.0 collective-permute-done.2.h_b
  12.0 0.7 collective-permute-done.1.h_f
  12.6 0.0 collective-permute-done.h_a
  12.6 2.7 %shard_map.79 = (f32[16,1024]{1,0:T(8,128)S(1)}, f32[16,1024]{1,0:T(8,128)S(1)}, f32[32,1024]{1,0:T(8,128)S(1)}, f32[2,32,128]{2,1,0:T(8,128)S(1)}, f32[32,9,1,128]{3,2,1,0:T(1,128)}) custom-call(s32[8,5]{1,0:T(8,128)S(1)} %get-tuple-element.43.cols, s32[2]{0:T(128)S(1)} %copy-done.21, f32[16,1024]{1,0:T(8,128)S(1)} %copy-done.5, ...), custom_call_target="tpu_custom_call" | custom-call | tf_op jit(solution)/shard_map/pallas_call | solution.py:516
  15.3 0.0 copy-done
  15.3 2.8 %all-to-all-start = ((f32[32,9,1,128]{3,2,1,0:T(1,128)}), f32[32,9,1,128]{3,2,1,0:T(1,128)S(1)}, u32[]{:S(2)}, u32[]{:S(2)}) async-start(f32[32,9,1,128]{3,2,1,0:T(1,128)} %get-tuple-element.48), calls=%async_computation | async-start | bytes 294912 | tf_op jit(solution)/shard_map/all_to_all | solution.py:487
  18.1 5.3 %collective-permute-start.5 = (f32[2,32,128]{2,1,0:T(8,128)S(1)}, f32[2,32,128]{2,1,0:T(8,128)S(1)}, u32[]{:S(2)}, u32[]{:S(2)}) collective-permute-start(f32[2,32,128]{2,1,0:T(8,128)S(1)} %get-tuple-element.47), channel_id=1, source_target_pairs={{0,31},{1,2},{2,1},{3,4},{4,3},{5,6},{6,5},{7,8},{8,7},{9,10},{10,... | collective-permute-start | bytes 98312 | tf_op jit(solution)/shard_map/ppermute | solution.py:484
  23.3 0.0 collective-permute-start.4
  23.3 0.0 collective-permute-start.3
  23.3 3.2 %all-to-all-done.red = f32[32,9,1,128]{3,2,1,0:T(1,128)S(1)} async-done(((f32[32,9,1,128]{3,2,1,0:T(1,128)}), f32[32,9,1,128]{3,2,1,0:T(1,128)S(1)}, u32[]{:S(2)}, u32[]{:S(2)}) %all-to-all-start) | async-done | bytes 147488 | tf_op jit(solution)/shard_map/all_to_all | solution.py:487
  26.6 1.4 %shard_map.80 = (f32[16,1024]{1,0:T(8,128)S(1)}, f32[16,1024]{1,0:T(8,128)S(1)}, f32[16,1024]{1,0:T(8,128)S(1)}, f32[80,1024]{1,0:T(8,128)S(1)}, f32[144,128]{1,0:T(8,128)S(1)}, /*index=5*/f32[1,16]{1,0:T(1,128)}) custom-call(f32[32,9,1,128]{3,2,1,0:T(1,128)S(1)} %all-to-all-done.red, f32[16,1024]{1,0:T(8,128)S(1)} %get-tuple-element.49.kb, ...), custom_call_target="tpu_custom_call" | custom-call | tf_op jit(solution)/shard_map/pallas_call | solution.py:521
  27.9 0.0 collective-permute-done.5.h_b
  27.9 0.2 collective-permute-done.4.h_f
  28.2 0.0 collective-permute-done.3.h_a
  28.2 1.7 %copy-done.1 = bf16[8,640,256]{2,1,0:T(8,128)(2,1)S(1)} copy-done((bf16[8,640,256]{2,1,0:T(8,128)(2,1)S(1)}, bf16[8,640,256]{2,1,0:T(8,128)(2,1)}, u32[]{:S(2)}) %copy-start.1) | copy-done | bytes 2621464
  29.9 1.9 %shard_map.81 = (f32[16,1024]{1,0:T(8,128)S(1)}, f32[16,1024]{1,0:T(8,128)S(1)}, f32[80,1024]{1,0:T(8,128)S(1)}, f32[48,768]{1,0:T(8,128)S(1)}, f32[32,1024]{1,0:T(8,128)S(1)}, /*index=5*/f32[2,48,128]{2,1,0:T(8,128)S(1)}) custom-call(s32[8,5]{1,0:T(8,128)S(1)} %get-tuple-element.43.cols, s32[2]{0:T(128)S(1)} %copy-done.21, ...), custom_call_target="tpu_custom_call" | custom-call | tf_op jit(solution)/shard_map/pallas_call | solution.py:524
  31.8 2.2 %collective-permute-start.8 = (f32[2,48,128]{2,1,0:T(8,128)S(1)}, f32[2,48,128]{2,1,0:T(8,128)S(1)}, u32[]{:S(2)}, u32[]{:S(2)}) collective-permute-start(f32[2,48,128]{2,1,0:T(8,128)S(1)} %get-tuple-element.58), channel_id=1, source_target_pairs={{0,31},{1,2},{2,1},{3,4},{4,3},{5,6},{6,5},{7,8},{8,7},{9,10},{10,... | collective-permute-start | bytes 147464 | tf_op jit(solution)/shard_map/ppermute | solution.py:484
  34.0 0.0 collective-permute-start.7
  34.0 0.0 collective-permute-start.6
  34.0 0.7 shard_map.82
  34.7 0.6 collective-permute-start.9
  35.3 0.8 collective-permute-done.9.pair
  36.1 3.0 %collective-permute-done.8.h_b.q_b = f32[2,48,128]{2,1,0:T(8,128)S(1)} collective-permute-done((f32[2,48,128]{2,1,0:T(8,128)S(1)}, f32[2,48,128]{2,1,0:T(8,128)S(1)}, u32[]{:S(2)}, u32[]{:S(2)}) %collective-permute-start.8) | collective-permute-done | bytes 49184 | tf_op jit(solution)/shard_map/ppermute | solution.py:484
  39.1 0.2 collective-permute-done.7.h_f.q_f
  39.2 0.0 collective-permute-done.6.h_a.q_a
  39.3 2.1 %shard_map.83 = (f32[16,1024]{1,0:T(8,128)S(1)}, f32[2,16,128]{2,1,0:T(8,128)S(1)}, f32[32,10,1,128]{3,2,1,0:T(1,128)S(1)}) custom-call(s32[8,5]{1,0:T(8,128)S(1)} %get-tuple-element.43.cols, s32[2]{0:T(128)S(1)} %copy-done.22, f32[16,1024]{1,0:T(8,128)S(1)} %get-tuple-element.57.p, f32[2,48,128]{2,1,0:T(8,128)S(1)} %collective-permute-done.6.h_a.q_a, ...), custom_call_target="tpu_custom_call" | custom-call | tf_op jit(solution)/shard_map/pallas_call | solution.py:537
  41.4 0.7 copy-done.14
  42.1 0.6 copy-done.19
  42.7 0.6 copy-done.24
  43.3 2.6 %all-to-all-start.1 = ((f32[32,10,1,128]{3,2,1,0:T(1,128)}), f32[32,10,1,128]{3,2,1,0:T(1,128)S(1)}, u32[]{:S(2)}, u32[]{:S(2)}) async-start(f32[32,10,1,128]{3,2,1,0:T(1,128)} %copy-done.14), calls=%async_computation.1 | async-start | bytes 327680 | tf_op jit(solution)/shard_map/all_to_all | solution.py:487
  45.9 5.3 %collective-permute-start.12 = (f32[2,16,128]{2,1,0:T(8,128)}, f32[2,16,128]{2,1,0:T(8,128)}, u32[]{:S(2)}, u32[]{:S(2)}) collective-permute-start(f32[2,16,128]{2,1,0:T(8,128)} %copy-done.24), channel_id=1, source_target_pairs={{0,31},{1,2},{2,1},{3,4},{4,3},{5,6},{6,5},{7,8},{8,7},{9,10},{10,... | collective-permute-start | bytes 49160 | tf_op jit(solution)/shard_map/ppermute | solution.py:484
  51.1 0.0 collective-permute-start.11
  51.1 0.0 collective-permute-start.10
  51.1 3.4 %all-to-all-done.1.red = f32[32,10,1,128]{3,2,1,0:T(1,128)S(1)} async-done(((f32[32,10,1,128]{3,2,1,0:T(1,128)}), f32[32,10,1,128]{3,2,1,0:T(1,128)S(1)}, u32[]{:S(2)}, u32[]{:S(2)}) %all-to-all-start.1) | async-done | bytes 163872 | tf_op jit(solution)/shard_map/all_to_all | solution.py:487
  54.5 0.8 copy-done.20
  55.4 0.7 shard_map.84
  56.1 0.0 collective-permute-done.12.h_b
  56.1 0.0 collective-permute-done.11.h_f
  56.1 0.0 collective-permute-done.10.h_a
  56.1 1.7 %copy-done.3 = bf16[8,640,256]{2,1,0:T(8,128)(2,1)S(1)} copy-done((bf16[8,640,256]{2,1,0:T(8,128)(2,1)S(1)}, bf16[8,640,256]{2,1,0:T(8,128)(2,1)}, u32[]{:S(2)}) %copy-start.3) | copy-done | bytes 2621464
  57.9 0.8 copy-done.9
  58.7 0.8 copy-done.11
  59.5 0.8 copy-done.13
  60.3 0.9 %copy-done.16 = f32[48,768]{1,0:T(8,128)S(1)} copy-done((f32[48,768]{1,0:T(8,128)S(1)}, f32[48,768]{1,0:T(8,128)}, u32[]{:S(2)}) %copy-start.16) | copy-done | bytes 147480
  61.2 0.7 copy-done.23
  61.8 2.0 %shard_map.85 = (f32[16,1024]{1,0:T(8,128)S(1)}, f32[16,1024]{1,0:T(8,128)S(1)}, f32[2,16,128]{2,1,0:T(8,128)S(1)}) custom-call(s32[8,5]{1,0:T(8,128)S(1)} %get-tuple-element.43.cols, s32[2]{0:T(128)S(1)} %copy-done.23, f32[16,1024]{1,0:T(8,128)S(1)} %get-tuple-element.68.c_local, f32[32,128]{1,0:T(8,128)S(1)} %get-tuple-element.69.coefs, ...), custom_call_target="tpu_custom_call" | custom-call | tf_op jit(solution)/shard_map/pallas_call | solution.py:545
  63.8 2.2 %collective-permute-start.15 = (f32[2,16,128]{2,1,0:T(8,128)S(1)}, f32[2,16,128]{2,1,0:T(8,128)S(1)}, u32[]{:S(2)}, u32[]{:S(2)}) collective-permute-start(f32[2,16,128]{2,1,0:T(8,128)S(1)} %get-tuple-element.73), channel_id=1, source_target_pairs={{0,31},{1,2},{2,1},{3,4},{4,3},{5,6},{6,5},{7,8},{8,7},{9,10},{10,... | collective-permute-start | bytes 49160 | tf_op jit(solution)/shard_map/ppermute | solution.py:484
  66.0 0.1 collective-permute-start.14
  66.0 0.0 collective-permute-start.13
  66.0 0.4 shard_map.86
  66.4 4.2 %collective-permute-done.15.h_b = f32[2,16,128]{2,1,0:T(8,128)S(1)} collective-permute-done((f32[2,16,128]{2,1,0:T(8,128)S(1)}, f32[2,16,128]{2,1,0:T(8,128)S(1)}, u32[]{:S(2)}, u32[]{:S(2)}) %collective-permute-start.15) | collective-permute-done | bytes 16416 | tf_op jit(solution)/shard_map/ppermute | solution.py:484
  70.7 0.0 collective-permute-done.14.h_f
  70.7 0.0 collective-permute-done.13.h_a
  70.7 1.9 %shard_map.87 = (f32[16,1024]{1,0:T(8,128)S(1)}, f32[32,8,128]{2,1,0:T(8,128)S(1)}) custom-call(s32[8,5]{1,0:T(8,128)S(1)} %get-tuple-element.43.cols, f32[16,1024]{1,0:T(8,128)S(1)} %get-tuple-element.72.p, f32[2,16,128]{2,1,0:T(8,128)S(1)} %collective-permute-done.13.h_a, f32[2,16,128]{2,1,0:T(8,128)S(1)} %collective-permute-done.14.h_f, ...), custom_call_target="tpu_custom_call" | custom-call | tf_op jit(solution)/shard_map/pallas_call | solution.py:550
  72.6 10.4 %all_to_all.15.red = f32[32,8,128]{2,1,0:T(8,128)S(1)} all-to-all(f32[32,8,128]{2,1,0:T(8,128)S(1)} %get-tuple-element.78), channel_id=1, replica_groups=mesh['parts'=32] {'parts'}, dimensions={0} | all-to-all | bytes 262144 | tf_op jit(solution)/shard_map/all_to_all | solution.py:487
  83.0 1.2 %shard_map.88 = f32[16,1024]{1,0:T(8,128)} custom-call(f32[32,8,128]{2,1,0:T(8,128)S(1)} %all_to_all.15.red, f32[16,1024]{1,0:T(8,128)S(1)} %get-tuple-element.79.p, f32[144,128]{1,0:T(8,128)S(1)} %get-tuple-element.56.small, f32[64,128]{1,0:T(8,128)S(1)} %get-tuple-element.67.small_b, f32[32,128]{1,0:T(8,128)S(1)} %get-tuple-element.80.tests_in, ...), custom_call_target="tpu_custom_call" | custom-call | tf_op jit(solution)/shard_map/pallas_call | solution.py:552
  (35 shorter events, 0.1 us)
Async XLA Ops:
  1.5 11.1 %copy-start.5 = (f32[16,1024]{1,0:T(8,128)S(1)}, f32[16,1024]{1,0:T(8,128)}, u32[]{:S(2)}) copy-start(f32[16,1024]{1,0:T(8,128)} %basis.3) | copy-start | bytes 196612
  1.5 11.1 %copy-start.21 = (s32[2]{0:T(128)S(1)}, s32[2]{0:T(128)}, u32[]{:S(2)}) copy-start(s32[2]{0:T(128)} %iface.7) | copy-start | bytes 28
  1.5 10.4 %collective-permute-start.2 = (f32[2,16,128]{2,1,0:T(8,128)S(1)}, f32[2,16,128]{2,1,0:T(8,128)S(1)}, u32[]{:S(2)}, u32[]{:S(2)}) collective-permute-start(f32[2,16,128]{2,1,0:T(8,128)S(1)} %shard_map.78), channel_id=1, source_target_pairs={{0,31},{1,2},{2,1},{3,4},{4,3},{5,6},{6,5},{7,8},{8,7},{9,10},{10,... | collective-permute-start | bytes 49160 | tf_op jit(solution)/shard_map/ppermute | solution.py:484
  8.0 4.6 %collective-permute-start.1 = (f32[2,16,128]{2,1,0:T(8,128)S(1)}, f32[2,16,128]{2,1,0:T(8,128)S(1)}, u32[]{:S(2)}, u32[]{:S(2)}) collective-permute-start(f32[2,16,128]{2,1,0:T(8,128)S(1)} %shard_map.78), channel_id=1, source_target_pairs={{0,16},{1,17},{2,18},{3,19},{4,20},{5,21},{6,22},{7,23},{8,24},{9,... | collective-permute-start | bytes 49160 | tf_op jit(solution)/shard_map/ppermute | solution.py:484
  8.0 4.6 %collective-permute-start = (f32[2,16,128]{2,1,0:T(8,128)S(1)}, f32[2,16,128]{2,1,0:T(8,128)S(1)}, u32[]{:S(2)}, u32[]{:S(2)}) collective-permute-start(f32[2,16,128]{2,1,0:T(8,128)S(1)} %shard_map.78), channel_id=1, source_target_pairs={{0,1},{1,0},{2,3},{3,2},{4,5},{5,4},{6,7},{7,6},{8,9},{9,8},{10,11... | collective-permute-start | bytes 49160 | tf_op jit(solution)/shard_map/ppermute | solution.py:484
  11.9 3.4 %copy-start = (bf16[8,640,256]{2,1,0:T(8,128)(2,1)}, bf16[8,640,256]{2,1,0:T(8,128)(2,1)S(1)}, u32[]{:S(2)}) copy-start(bf16[8,640,256]{2,1,0:T(8,128)(2,1)S(1)} %get-tuple-element.45.w_low) | copy-start | bytes 7864324
  15.3 12.9 %copy-start.6 = (f32[16,1024]{1,0:T(8,128)}, f32[16,1024]{1,0:T(8,128)S(1)}, u32[]{:S(2)}) copy-start(f32[16,1024]{1,0:T(8,128)S(1)} %get-tuple-element.50.mb) | copy-start | bytes 196612
  15.3 11.3 %all-to-all-start = ((f32[32,9,1,128]{3,2,1,0:T(1,128)}), f32[32,9,1,128]{3,2,1,0:T(1,128)S(1)}, u32[]{:S(2)}, u32[]{:S(2)}) async-start(f32[32,9,1,128]{3,2,1,0:T(1,128)} %get-tuple-element.48), calls=%async_computation | async-start | bytes 294912 | tf_op jit(solution)/shard_map/all_to_all | solution.py:487
  18.1 9.9 %collective-permute-start.5 = (f32[2,32,128]{2,1,0:T(8,128)S(1)}, f32[2,32,128]{2,1,0:T(8,128)S(1)}, u32[]{:S(2)}, u32[]{:S(2)}) collective-permute-start(f32[2,32,128]{2,1,0:T(8,128)S(1)} %get-tuple-element.47), channel_id=1, source_target_pairs={{0,31},{1,2},{2,1},{3,4},{4,3},{5,6},{6,5},{7,8},{8,7},{9,10},{10,... | collective-permute-start | bytes 98312 | tf_op jit(solution)/shard_map/ppermute | solution.py:484
  23.3 4.8 %collective-permute-start.4 = (f32[2,32,128]{2,1,0:T(8,128)S(1)}, f32[2,32,128]{2,1,0:T(8,128)S(1)}, u32[]{:S(2)}, u32[]{:S(2)}) collective-permute-start(f32[2,32,128]{2,1,0:T(8,128)S(1)} %get-tuple-element.47), channel_id=1, source_target_pairs={{0,16},{1,17},{2,18},{3,19},{4,20},{5,21},{6,22},{7,23},{8,24},{9,... | collective-permute-start | bytes 98312 | tf_op jit(solution)/shard_map/ppermute | solution.py:484
  23.3 4.8 %collective-permute-start.3 = (f32[2,32,128]{2,1,0:T(8,128)S(1)}, f32[2,32,128]{2,1,0:T(8,128)S(1)}, u32[]{:S(2)}, u32[]{:S(2)}) collective-permute-start(f32[2,32,128]{2,1,0:T(8,128)S(1)} %get-tuple-element.47), channel_id=1, source_target_pairs={{0,1},{1,0},{2,3},{3,2},{4,5},{5,4},{6,7},{7,6},{8,9},{9,8},{10,11... | collective-permute-start | bytes 98312 | tf_op jit(solution)/shard_map/ppermute | solution.py:484
  28.2 1.7 %copy-start.1 = (bf16[8,640,256]{2,1,0:T(8,128)(2,1)S(1)}, bf16[8,640,256]{2,1,0:T(8,128)(2,1)}, u32[]{:S(2)}) copy-start(bf16[8,640,256]{2,1,0:T(8,128)(2,1)} %copy-done) | copy-start | bytes 7864324
  29.9 4.1 %copy-start.7 = (f32[16,1024]{1,0:T(8,128)S(1)}, f32[16,1024]{1,0:T(8,128)}, u32[]{:S(2)}) copy-start(f32[16,1024]{1,0:T(8,128)} %copy-done.6) | copy-start | bytes 196612
  29.9 9.3 %copy-start.2 = (bf16[8,640,256]{2,1,0:T(8,128)(2,1)S(1)}, bf16[8,640,256]{2,1,0:T(8,128)(2,1)}, u32[]{:S(2)}) copy-start(bf16[8,640,256]{2,1,0:T(8,128)(2,1)} %copy-done) | copy-start | bytes 7864324
  29.9 9.3 %copy-start.22 = (s32[2]{0:T(128)S(1)}, s32[2]{0:T(128)}, u32[]{:S(2)}) copy-start(s32[2]{0:T(128)} %iface.7) | copy-start | bytes 28
  31.8 9.6 %copy-start.15 = (f32[48,768]{1,0:T(8,128)}, f32[48,768]{1,0:T(8,128)S(1)}, u32[]{:S(2)}) copy-start(f32[48,768]{1,0:T(8,128)S(1)} %get-tuple-element.71.words_halo) | copy-start | bytes 442372
  31.8 7.3 %collective-permute-start.8 = (f32[2,48,128]{2,1,0:T(8,128)S(1)}, f32[2,48,128]{2,1,0:T(8,128)S(1)}, u32[]{:S(2)}, u32[]{:S(2)}) collective-permute-start(f32[2,48,128]{2,1,0:T(8,128)S(1)} %get-tuple-element.58), channel_id=1, source_target_pairs={{0,31},{1,2},{2,1},{3,4},{4,3},{5,6},{6,5},{7,8},{8,7},{9,10},{10,... | collective-permute-start | bytes 147464 | tf_op jit(solution)/shard_map/ppermute | solution.py:484
  34.0 5.2 %collective-permute-start.7 = (f32[2,48,128]{2,1,0:T(8,128)S(1)}, f32[2,48,128]{2,1,0:T(8,128)S(1)}, u32[]{:S(2)}, u32[]{:S(2)}) collective-permute-start(f32[2,48,128]{2,1,0:T(8,128)S(1)} %get-tuple-element.58), channel_id=1, source_target_pairs={{0,16},{1,17},{2,18},{3,19},{4,20},{5,21},{6,22},{7,23},{8,24},{9,... | collective-permute-start | bytes 147464 | tf_op jit(solution)/shard_map/ppermute | solution.py:484
  34.0 5.2 %collective-permute-start.6 = (f32[2,48,128]{2,1,0:T(8,128)S(1)}, f32[2,48,128]{2,1,0:T(8,128)S(1)}, u32[]{:S(2)}, u32[]{:S(2)}) collective-permute-start(f32[2,48,128]{2,1,0:T(8,128)S(1)} %get-tuple-element.58), channel_id=1, source_target_pairs={{0,1},{1,0},{2,3},{3,2},{4,5},{5,4},{6,7},{7,6},{8,9},{9,8},{10,11... | collective-permute-start | bytes 147464 | tf_op jit(solution)/shard_map/ppermute | solution.py:484
  34.7 6.7 %copy-start.17 = (f32[16,1024]{1,0:T(8,128)}, f32[16,1024]{1,0:T(8,128)S(1)}, u32[]{:S(2)}) copy-start(f32[16,1024]{1,0:T(8,128)S(1)} %get-tuple-element.75.v) | copy-start | bytes 196612
  34.7 1.4 %collective-permute-start.9 = (f32[16,128]{1,0:T(8,128)S(1)}, f32[16,128]{1,0:T(8,128)S(1)}, u32[]{:S(2)}, u32[]{:S(2)}) collective-permute-start(f32[16,128]{1,0:T(8,128)S(1)} %get-tuple-element.62.part), channel_id=1, source_target_pairs={{0,1},{1,0},{2,3},{3,2},{4,5},{5,4},{6,7},{7,6},{8,9},{9,8},{10,11... | collective-permute-start | bytes 24584 | tf_op jit(solution)/shard_map/ppermute | solution.py:535
  39.1 2.3 %copy-start.8 = (f32[2,48,128]{2,1,0:T(8,128)}, f32[2,48,128]{2,1,0:T(8,128)S(1)}, u32[]{:S(2)}) copy-start(f32[2,48,128]{2,1,0:T(8,128)S(1)} %collective-permute-done.8.h_b.q_b) | copy-start | bytes 147460
  39.2 2.1 %copy-start.10 = (f32[2,48,128]{2,1,0:T(8,128)}, f32[2,48,128]{2,1,0:T(8,128)S(1)}, u32[]{:S(2)}) copy-start(f32[2,48,128]{2,1,0:T(8,128)S(1)} %collective-permute-done.7.h_f.q_f) | copy-start | bytes 147460
  39.2 2.2 %copy-start.12 = (f32[2,48,128]{2,1,0:T(8,128)}, f32[2,48,128]{2,1,0:T(8,128)S(1)}, u32[]{:S(2)}) copy-start(f32[2,48,128]{2,1,0:T(8,128)S(1)} %collective-permute-done.6.h_a.q_a) | copy-start | bytes 147460
  41.4 0.7 copy-start.14
  42.1 0.6 copy-start.19
  42.7 0.6 copy-start.24
  43.3 11.2 %all-to-all-start.1 = ((f32[32,10,1,128]{3,2,1,0:T(1,128)}), f32[32,10,1,128]{3,2,1,0:T(1,128)S(1)}, u32[]{:S(2)}, u32[]{:S(2)}) async-start(f32[32,10,1,128]{3,2,1,0:T(1,128)} %copy-done.14), calls=%async_computation.1 | async-start | bytes 327680 | tf_op jit(solution)/shard_map/all_to_all | solution.py:487
  45.9 10.2 %collective-permute-start.12 = (f32[2,16,128]{2,1,0:T(8,128)}, f32[2,16,128]{2,1,0:T(8,128)}, u32[]{:S(2)}, u32[]{:S(2)}) collective-permute-start(f32[2,16,128]{2,1,0:T(8,128)} %copy-done.24), channel_id=1, source_target_pairs={{0,31},{1,2},{2,1},{3,4},{4,3},{5,6},{6,5},{7,8},{8,7},{9,10},{10,... | collective-permute-start | bytes 49160 | tf_op jit(solution)/shard_map/ppermute | solution.py:484
  51.1 5.0 %collective-permute-start.11 = (f32[2,16,128]{2,1,0:T(8,128)}, f32[2,16,128]{2,1,0:T(8,128)}, u32[]{:S(2)}, u32[]{:S(2)}) collective-permute-start(f32[2,16,128]{2,1,0:T(8,128)} %copy-done.24), channel_id=1, source_target_pairs={{0,16},{1,17},{2,18},{3,19},{4,20},{5,21},{6,22},{7,23},{8,24},{9,... | collective-permute-start | bytes 49160 | tf_op jit(solution)/shard_map/ppermute | solution.py:484
  51.1 5.0 %collective-permute-start.10 = (f32[2,16,128]{2,1,0:T(8,128)}, f32[2,16,128]{2,1,0:T(8,128)}, u32[]{:S(2)}, u32[]{:S(2)}) collective-permute-start(f32[2,16,128]{2,1,0:T(8,128)} %copy-done.24), channel_id=1, source_target_pairs={{0,1},{1,0},{2,3},{3,2},{4,5},{5,4},{6,7},{7,6},{8,9},{9,8},{10,11... | collective-permute-start | bytes 49160 | tf_op jit(solution)/shard_map/ppermute | solution.py:484
  54.5 0.8 copy-start.20
  56.1 1.7 %copy-start.3 = (bf16[8,640,256]{2,1,0:T(8,128)(2,1)S(1)}, bf16[8,640,256]{2,1,0:T(8,128)(2,1)}, u32[]{:S(2)}) copy-start(bf16[8,640,256]{2,1,0:T(8,128)(2,1)} %copy-done) | copy-start | bytes 7864324
  57.9 0.8 copy-start.9
  58.7 0.8 copy-start.11
  59.5 0.8 copy-start.13
  60.3 0.9 %copy-start.16 = (f32[48,768]{1,0:T(8,128)S(1)}, f32[48,768]{1,0:T(8,128)}, u32[]{:S(2)}) copy-start(f32[48,768]{1,0:T(8,128)} %copy-done.15) | copy-start | bytes 442372
  61.2 0.7 copy-start.23
  61.8 4.2 %copy-start.18 = (f32[16,1024]{1,0:T(8,128)S(1)}, f32[16,1024]{1,0:T(8,128)}, u32[]{:S(2)}) copy-start(f32[16,1024]{1,0:T(8,128)} %copy-done.17) | copy-start | bytes 196612
  61.8 8.9 %copy-start.4 = (bf16[8,640,256]{2,1,0:T(8,128)(2,1)S(1)}, bf16[8,640,256]{2,1,0:T(8,128)(2,1)}, u32[]{:S(2)}) copy-start(bf16[8,640,256]{2,1,0:T(8,128)(2,1)} %copy-done) | copy-start | bytes 7864324
  63.8 6.9 %collective-permute-start.15 = (f32[2,16,128]{2,1,0:T(8,128)S(1)}, f32[2,16,128]{2,1,0:T(8,128)S(1)}, u32[]{:S(2)}, u32[]{:S(2)}) collective-permute-start(f32[2,16,128]{2,1,0:T(8,128)S(1)} %get-tuple-element.73), channel_id=1, source_target_pairs={{0,31},{1,2},{2,1},{3,4},{4,3},{5,6},{6,5},{7,8},{8,7},{9,10},{10,... | collective-permute-start | bytes 49160 | tf_op jit(solution)/shard_map/ppermute | solution.py:484
  66.0 4.7 %collective-permute-start.14 = (f32[2,16,128]{2,1,0:T(8,128)S(1)}, f32[2,16,128]{2,1,0:T(8,128)S(1)}, u32[]{:S(2)}, u32[]{:S(2)}) collective-permute-start(f32[2,16,128]{2,1,0:T(8,128)S(1)} %get-tuple-element.73), channel_id=1, source_target_pairs={{0,16},{1,17},{2,18},{3,19},{4,20},{5,21},{6,22},{7,23},{8,24},{9,... | collective-permute-start | bytes 49160 | tf_op jit(solution)/shard_map/ppermute | solution.py:484
  66.0 4.7 %collective-permute-start.13 = (f32[2,16,128]{2,1,0:T(8,128)S(1)}, f32[2,16,128]{2,1,0:T(8,128)S(1)}, u32[]{:S(2)}, u32[]{:S(2)}) collective-permute-start(f32[2,16,128]{2,1,0:T(8,128)S(1)} %get-tuple-element.73), channel_id=1, source_target_pairs={{0,1},{1,0},{2,3},{3,2},{4,5},{5,4},{6,7},{7,6},{8,9},{9,8},{10,11... | collective-permute-start | bytes 49160 | tf_op jit(solution)/shard_map/ppermute | solution.py:484

commit v5 on v4

--- a/solution.py
+++ b/solution.py
@@ -11,7 +11,6 @@
 F32 = jnp.float32
 BF16 = jnp.bfloat16
 VM = pl.BlockSpec(memory_space=pltpu.VMEM)
-SM = pl.BlockSpec(memory_space=pltpu.SMEM)
 HBM = pl.BlockSpec(memory_space=pltpu.MemorySpace.HBM)
 MAT = 128
 
@@ -93,6 +92,20 @@
         result = both[:n] + both[n:] + low
         k_out[:, i * width : (i + 1) * width] = result[:, :width]
         m_out[:, i * width : (i + 1) * width] = result[:, width:]
+
+
+def apply_iface(xs, cols, w_high, w_low, tile):
+    n = xs.shape[1] // 2
+    width = xs.shape[2]
+    lhs = lanes([xs[cols[tile, b]] for b in range(cols.shape[1])])
+    both = jnp.dot(lhs, w_high[tile], preferred_element_type=F32)
+    low = jnp.dot(lhs[:n], w_low[tile], preferred_element_type=F32)
+    result = both[:n] + both[n:] + low
+    return result[:, :width], result[:, width:]
+
+
+def lanes_of(tile, width):
+    return pl.ds(pl.multiple_of(tile * width, width), width)
 
 
 def send_tiles(iface, outgoing, at, ref):
@@ -305,8 +318,7 @@
         theta_out[...] = jnp.sum(jnp.where(lane == row, theta, 0.0), axis=0, keepdims=True)[:, :n]
 
     def k_b1(
-        cols, iface, h_a, h_f, h_b, w_high, w_low, inv_d, ko, mo, c0, words_in, small,
-        p_out, image_out, words, words_halo, kf_out, outgoing, xs, res,
+        cols, iface, h_a, h_f, h_b, w_high, w_low, inv_d, ko, mo, c0, words_in, small, words_halo, outgoing, xs
     ):
         lv, lc, right = (get_small(small, k) for k in (6, 7, 8))
         theta = small[5 * n : 6 * n, :1]
@@ -315,9 +327,25 @@
         g2, f1 = both[:n], both[n:]
         put_sources(xs, 0, rows([c0[...], words_in[:n]]))
         put_sources(xs, c0.shape[1] // xs.shape[2], rows([-relax * (g1 - theta * g2), f1]))
-        apply_pair(xs, cols, w_high, w_low, res.at[0], res.at[1])
         for k, value in ((0, f1), (1, g1), (2, g2)):
             words_halo[k * n : (k + 1) * n] = value
+        coef = lanes([right, -theta * right])
+        for slot in range(outgoing.shape[0]):
+            tile = iface[slot]
+            at = lanes_of(tile, xs.shape[2])
+            k_tile, m_tile = apply_iface(xs, cols, w_high, w_low, tile)
+            d = inv_d[:, at]
+            image = k_tile[:n] - theta * m_tile[:n] - mm3(coef, rows([ko[:, at], mo[:, at]]))
+            outgoing[slot, :n] = 2.0 * c0[:, at] - relax * d * image
+            outgoing[slot, n : 2 * n] = k_tile[n:] * d
+            outgoing[slot, 2 * n :] = m_tile[n:] * d
+
+    def k_b2(
+        cols, xs, w_high, w_low, inv_d, ko, mo, c0, words_in, small, p_out, image_out, words, kf_out, res
+    ):
+        right = get_small(small, 8)
+        theta = small[5 * n : 6 * n, :1]
+        apply_pair(xs, cols, w_high, w_low, res.at[0], res.at[1])
         d = inv_d[...]
         image = res[0, :n] - theta * res[1, :n] - mm3(lanes([right, -theta * right]), rows([ko[...], mo[...]]))
         image_out[...] = image
@@ -328,8 +356,6 @@
         words[2 * n : 3 * n] = res[1, n:] * d
         words[3 * n :] = words_in[3 * n :]
         p_out[...] = 2.0 * c0[...] - relax * d * image
-        send_tiles(iface, outgoing, 0, p_out)
-        send_tiles(iface, outgoing, n, words.at[n : 3 * n])
 
     def k_c0(small, basis, mb, image0, kf, p, words, v_out, tests_high, tests_low, small_b, part):
         lv, lc = get_small(small, 6), get_small(small, 7)
@@ -424,7 +450,7 @@
 
     def k_d1(
         cols, iface, c_local, coefs, h_a, h_f, h_b, q_a, q_f, q_b, ko, mo, c0, words_halo, small,
-        w_high, w_low, inv_d, p_out, image_out, outgoing, xs, res,
+        w_high, w_low, inv_d, outgoing, xs,
     ):
         coef, right = coefs[:n, : 5 * n], get_small(coefs, 1)
         theta = small[5 * n : 6 * n, :1]
@@ -432,11 +458,21 @@
         c_halo = halo_lanes((h_a, h_f, h_b), 0, n) + mm3(coef, around)
         put_sources(xs, 0, c_local[...])
         put_sources(xs, c_local.shape[1] // xs.shape[2], c_halo)
+        onto = lanes([right, -theta * right])
+        for slot in range(outgoing.shape[0]):
+            tile = iface[slot]
+            at = lanes_of(tile, xs.shape[2])
+            k_tile, m_tile = apply_iface(xs, cols, w_high, w_low, tile)
+            image = k_tile - theta * m_tile - mm3(onto, rows([ko[:, at], mo[:, at]]))
+            outgoing[slot] = c_local[:, at] + c0[:, at] - relax * inv_d[:, at] * image
+
+    def k_d2(cols, xs, c_local, coefs, ko, mo, c0, small, w_high, w_low, inv_d, p_out, image_out, res):
+        right = get_small(coefs, 1)
+        theta = small[5 * n : 6 * n, :1]
         apply_pair(xs, cols, w_high, w_low, res.at[0], res.at[1])
         image = res[0] - theta * res[1] - mm3(lanes([right, -theta * right]), rows([ko[...], mo[...]]))
         image_out[...] = image
         p_out[...] = c_local[...] + c0[...] - relax * inv_d[...] * image
-        send_tiles(iface, outgoing, 0, p_out)
 
     def k_e0(image2, p, tests_high, tests_low, v, words, onto_v, part, last_high, last_low):
         right = rows([image2[...], p[...], jnp.zeros((MAT - 2 * n, p.shape[1]), F32)])
@@ -466,7 +502,7 @@
         low = jnp.dot(high, last_low[...], preferred_element_type=F32)
         out[...] = p[...] + both[:n] + both[n:] + low
 
-    return k_a, k_b0, k_b1, k_c0, k_c1, k_d0, k_d1, k_e0, k_e1, k_f
+    return k_a, k_b0, k_b1, k_b2, k_c0, k_c1, k_d0, k_d1, k_d2, k_e0, k_e1, k_f
 
 
 def shards(basis, k_tiles, m_tiles, tile_part, tile_slot, iface):
@@ -486,7 +522,7 @@
     def reduced(blocks_out):
         return lax.all_to_all(blocks_out, "parts", 0, 0, tiled=True)
 
-    k_a, k_b0, k_b1, k_c0, k_c1, k_d0, k_d1, k_e0, k_e1, k_f = make_kernels(n, scale)
+    k_a, k_b0, k_b1, k_b2, k_c0, k_c1, k_d0, k_d1, k_d2, k_e0, k_e1, k_f = make_kernels(n, scale)
     sources = tiles + 3 * count
     xs = lambda m: pltpu.VMEM((sources, 2 * m, width), BF16)
     vec = ((n, local), F32)
@@ -500,7 +536,7 @@
         k_first,
         [out(n)],
         [HBM, HBM],
-        [pltpu.SMEM((count,), jnp.int32), pltpu.VMEM((n, local), F32), pltpu.SemaphoreType.DMA((2,))],
+        [pltpu.VMEM((count,), jnp.int32), pltpu.VMEM((n, local), F32), pltpu.SemaphoreType.DMA((2,))],
     )(in_hbm(iface), in_hbm(basis))
     h0 = halo(outgoing)
     w_high, w_low, inv_d, cols = call(
@@ -514,27 +550,28 @@
     w = (w_high, w_low, inv_d)
     packed = ((parts, n // 2 + 1, 1, MAT), F32)
     kb, mb, u, outgoing, grams = call(
-        k_a, [vec, vec, vecs(2), out(2 * n), packed], [SM, SM] + [VM] * 7, [xs(n)]
+        k_a, [vec, vec, vecs(2), out(2 * n), packed], [VM, VM] + [VM] * 7, [xs(n)]
     )(cols, iface, basis, *h0, *w)
     red = reduced(grams)
     h1 = halo(outgoing)
     ko, mo, c0, words, small, theta = call(
         k_b0, [vec] * 3 + [vecs(5), mats(9), ((1, n), F32)], [VM] * 4
     )(red, kb, mb, u)
-    p1, image0, words, words_halo, kf, outgoing = call(
-        k_b1,
-        [vec, vec, vecs(5), ((3 * n, 3 * count * width), F32), vecs(2), out(3 * n)],
-        [SM, SM] + [VM] * 11,
-        [xs(2 * n), pltpu.VMEM((2, 2 * n, local), F32)],
+    sources_of = lambda m: ((sources, 2 * m, width), BF16)
+    words_halo, outgoing, source = call(
+        k_b1, [((3 * n, 3 * count * width), F32), out(3 * n), sources_of(2 * n)], [VM, VM] + [VM] * 11
     )(cols, iface, *h1, *w, ko, mo, c0, words, small)
     h2 = halo(outgoing)
+    p1, image0, words, kf = call(
+        k_b2, [vec, vec, vecs(5), vecs(2)], [VM] + [VM] * 9, [pltpu.VMEM((2, 2 * n, local), F32)]
+    )(cols, source, *w, ko, mo, c0, words, small)
     v, tests_high, tests_low, small_b, part = call(
         k_c0, [vec] + [((2 * n, local), BF16)] * 2 + [mats(4), mats(1)], [VM] * 7
     )(small, basis, mb, image0, kf, p1, words)
     tests = (tests_high, tests_low)
     pair = lax.ppermute(part, "parts", chip)
     packed = ((parts, n // 2 + 2, 1, MAT), F32)
-    p2, outgoing, grams = call(k_c1, [vec, out(n), packed], [SM, SM] + [VM] * 13, [xs(n), res])(
+    p2, outgoing, grams = call(k_c1, [vec, out(n), packed], [VM, VM] + [VM] * 13, [xs(n), res])(
         cols, iface, p1, *h2, c0, small, part, pair, *tests, *w
     )
     red = reduced(grams)
@@ -542,12 +579,13 @@
     c2, word_tests, onto_v, coefs = call(k_d0, [vec, mats(2), mats(5), mats(2)], [VM] * 5)(
         red, p2, words, small, small_b
     )
-    p3, image2, outgoing = call(k_d1, [vec, vec, out(n)], [SM, SM] + [VM] * 16, [xs(n), res])(
+    outgoing, source = call(k_d1, [out(n), sources_of(n)], [VM, VM] + [VM] * 16)(
         cols, iface, c2, coefs, *h3, *h2, ko, mo, c0, words_halo, small, *w
     )
     h4 = halo(outgoing)
+    p3, image2 = call(k_d2, [vec, vec], [VM] + [VM] * 10, [res])(cols, source, c2, coefs, ko, mo, c0, small, *w)
     part, *last = call(k_e0, [mats(1)] + [((6 * n, local), BF16)] * 2, [VM] * 7)(image2, p3, *tests, v, words, onto_v)
-    p4, grams = call(k_e1, [vec, grams8], [SM] + [VM] * 12, [xs(n), res])(cols, p3, *h4, c0, small, part, *tests, *w)
+    p4, grams = call(k_e1, [vec, grams8], [VM] + [VM] * 12, [xs(n), res])(cols, p3, *h4, c0, small, part, *tests, *w)
     red = reduced(grams)
     (correct,) = call(k_f, [vec], [VM] * 7)(red, p4, small, small_b, word_tests, *last)
     return (correct, theta.reshape(-1))

time: 84.8 us -> 81.9 us (0.966)
  waiting for transfers between devices: 15.7 us -> 13.1 us
  Pallas kernels: 19.6 us -> 18.2 us
  local copies, waits for them, and re-layouts: 10.2 us -> 11.5 us
    ppermute x15, waiting for transfers between devices: 8.28 us -> 5.67 us  [halo(): lax.ppermute(outgoing, 'parts', pairs)]
    pallas_call x6 -> x8, Pallas kernels: 11.3 us -> 9.83 us  [the longest x1 2.18 us: shards(): call(k_a, [vec, vec, vecs(2), out(2 * n), packed], [VM, VM] + [VM] * 7, [...]
    unnamed x50 -> x44, local copies, waits for them, and re-layouts: 10.2 us -> 11.5 us
  transfers between devices with their start and end apart: 18 -> 18, of which waited for: 8 -> 8; matrix products, arithmetic and copies ran while one was open for 0% -> 0% of each run, Pallas kernels for 8% -> 11%
where the time goes in v5:
time: 81.9 us; the launch traced here: 81.3 us
  starting transfers between devices  27.2 us (33%)
  Pallas kernels  18.2 us (22%)
  waiting for transfers between devices  13.1 us (16%)
  local copies, waits for them, and re-layouts  11.5 us (14%)
  blocking collectives  10.4 us (13%)
  between operations  0.91 us (1%)
    ppermute x15, starting transfers between devices, halo(): lax.ppermute(outgoing, 'parts', pairs)  21.3 us
    unnamed x44, local copies, waits for them, and re-layouts  11.5 us
    all_to_all x1, blocking collectives, reduced(): return lax.all_to_all(blocks_out, 'parts', 0, 0, tiled=True)  10.4 us
    all_to_all x2, waiting for transfers between devices, reduced(): return lax.all_to_all(blocks_out, 'parts', 0, 0, tiled=True)  6.59 us
    ppermute x15, waiting for transfers between devices, halo(): lax.ppermute(outgoing, 'parts', pairs)  5.67 us
    all_to_all x2, starting transfers between devices, reduced(): return lax.all_to_all(blocks_out, 'parts', 0, 0, tiled=True)  5.41 us
    pallas_call x1, Pallas kernels, shards(): call(make_prep(count), [((tiles, blocks * width, 2 * width), BF16)] * 2 +...  3.94 us
    pallas_call x1, Pallas kernels, shards(): call(k_a, [vec, vec, vecs(2), out(2 * n), packed], [VM, VM] + [VM] * 7, [...  2.18 us
  transfers between devices with their start and end apart: 18, of which 8 were waited for; matrix products, arithmetic and copies ran while one was open for 0% of the time, Pallas kernels for 11%

profile of v5, /device:TPU:0, one launch (start us, length us, event | category | flops | bytes accessed | tf_op | source)
XLA Modules:
  0.0 81.3 jit_solution(15651892537732870461)
XLA Ops:
  0.6 1.0 %shard_map.78 = f32[2,16,128]{2,1,0:T(8,128)S(1)} custom-call(s32[2]{0:T(128)} %iface.7, f32[16,1024]{1,0:T(8,128)} %basis.3), custom_call_target="tpu_custom_call" | custom-call | tf_op jit(solution)/shard_map/pallas_call | solution.py:535
  1.6 0.0 copy-start.5
  1.6 0.0 copy-start.19
  1.6 6.5 %collective-permute-start.2 = (f32[2,16,128]{2,1,0:T(8,128)S(1)}, f32[2,16,128]{2,1,0:T(8,128)S(1)}, u32[]{:S(2)}, u32[]{:S(2)}) collective-permute-start(f32[2,16,128]{2,1,0:T(8,128)S(1)} %shard_map.78), channel_id=1, source_target_pairs={{0,31},{1,2},{2,1},{3,4},{4,3},{5,6},{6,5},{7,8},{8,7},{9,10},{10,... | collective-permute-start | bytes 49160 | tf_op jit(solution)/shard_map/ppermute | solution.py:520
  8.1 0.0 collective-permute-start.1
  8.1 0.0 collective-permute-start
  8.1 3.9 %shard_map.77 = (bf16[8,640,256]{2,1,0:T(8,128)(2,1)S(1)}, bf16[8,640,256]{2,1,0:T(8,128)(2,1)S(1)}, f32[1,1024]{1,0:T(1,128)S(1)}, s32[8,5]{1,0:T(8,128)S(1)}) custom-call(s32[8,5]{1,0:T(8,128)} %part_hbm.1, s32[8,5]{1,0:T(8,128)} %slot_hbm.1, f32[8,5,128,128]{3,2,1,0:T(8,128)} %k_hbm.1, f32[8,5,128,128]{3,2,1,0:T(8,128)} %m_hbm.1), custom_call_target="tpu_custom_call" | custom-call | tf_op jit(solution)/shard_map/pallas_call | solution.py:542
  12.1 0.0 collective-permute-done.2.h_b
  12.1 0.7 collective-permute-done.1.h_f
  12.7 0.0 collective-permute-done.h_a
  12.8 2.2 %shard_map.79 = (f32[16,1024]{1,0:T(8,128)S(1)}, f32[16,1024]{1,0:T(8,128)S(1)}, f32[32,1024]{1,0:T(8,128)S(1)}, f32[2,32,128]{2,1,0:T(8,128)S(1)}, f32[32,9,1,128]{3,2,1,0:T(1,128)}) custom-call(s32[8,5]{1,0:T(8,128)S(1)} %get-tuple-element.45.cols, s32[2]{0:T(128)S(1)} %copy-done.19, f32[16,1024]{1,0:T(8,128)S(1)} %copy-done.5, ...), custom_call_target="tpu_custom_call" | custom-call | tf_op jit(solution)/shard_map/pallas_call | solution.py:552
  14.9 2.8 %all-to-all-start = ((f32[32,9,1,128]{3,2,1,0:T(1,128)}), f32[32,9,1,128]{3,2,1,0:T(1,128)S(1)}, u32[]{:S(2)}, u32[]{:S(2)}) async-start(f32[32,9,1,128]{3,2,1,0:T(1,128)} %get-tuple-element.50), calls=%async_computation | async-start | bytes 294912 | tf_op jit(solution)/shard_map/all_to_all | solution.py:523
  17.7 5.3 %collective-permute-start.5 = (f32[2,32,128]{2,1,0:T(8,128)S(1)}, f32[2,32,128]{2,1,0:T(8,128)S(1)}, u32[]{:S(2)}, u32[]{:S(2)}) collective-permute-start(f32[2,32,128]{2,1,0:T(8,128)S(1)} %get-tuple-element.49), channel_id=1, source_target_pairs={{0,31},{1,2},{2,1},{3,4},{4,3},{5,6},{6,5},{7,8},{8,7},{9,10},{10,... | collective-permute-start | bytes 98312 | tf_op jit(solution)/shard_map/ppermute | solution.py:520
  23.0 0.0 collective-permute-start.4
  23.0 0.0 collective-permute-start.3
  23.0 3.2 %all-to-all-done.red = f32[32,9,1,128]{3,2,1,0:T(1,128)S(1)} async-done(((f32[32,9,1,128]{3,2,1,0:T(1,128)}), f32[32,9,1,128]{3,2,1,0:T(1,128)S(1)}, u32[]{:S(2)}, u32[]{:S(2)}) %all-to-all-start) | async-done | bytes 147488 | tf_op jit(solution)/shard_map/all_to_all | solution.py:523
  26.2 1.4 %shard_map.80 = (f32[16,1024]{1,0:T(8,128)S(1)}, f32[16,1024]{1,0:T(8,128)S(1)}, f32[16,1024]{1,0:T(8,128)S(1)}, f32[80,1024]{1,0:T(8,128)S(1)}, f32[144,128]{1,0:T(8,128)S(1)}, /*index=5*/f32[1,16]{1,0:T(1,128)}) custom-call(f32[32,9,1,128]{3,2,1,0:T(1,128)S(1)} %all-to-all-done.red, f32[16,1024]{1,0:T(8,128)S(1)} %get-tuple-element.51.kb, ...), custom_call_target="tpu_custom_call" | custom-call | tf_op jit(solution)/shard_map/pallas_call | solution.py:557
  27.6 0.0 collective-permute-done.5.h_b
  27.6 0.2 collective-permute-done.4.h_f
  27.8 0.0 collective-permute-done.3.h_a
  27.8 1.7 %copy-done.1 = bf16[8,640,256]{2,1,0:T(8,128)(2,1)S(1)} copy-done((bf16[8,640,256]{2,1,0:T(8,128)(2,1)S(1)}, bf16[8,640,256]{2,1,0:T(8,128)(2,1)}, u32[]{:S(2)}) %copy-start.1) | copy-done | bytes 2621464
  29.5 0.5 shard_map.81
  30.1 0.6 copy-done.13
  30.7 2.1 %collective-permute-start.8 = (f32[2,48,128]{2,1,0:T(8,128)S(1)}, f32[2,48,128]{2,1,0:T(8,128)S(1)}, u32[]{:S(2)}, u32[]{:S(2)}) collective-permute-start(f32[2,48,128]{2,1,0:T(8,128)S(1)} %get-tuple-element.61), channel_id=1, source_target_pairs={{0,31},{1,2},{2,1},{3,4},{4,3},{5,6},{6,5},{7,8},{8,7},{9,10},{10,... | collective-permute-start | bytes 147464 | tf_op jit(solution)/shard_map/ppermute | solution.py:520
  32.8 0.0 collective-permute-start.7
  32.8 0.0 collective-permute-start.6
  32.9 1.1 %shard_map.82 = (f32[16,1024]{1,0:T(8,128)S(1)}, f32[16,1024]{1,0:T(8,128)S(1)}, f32[80,1024]{1,0:T(8,128)S(1)}, f32[32,1024]{1,0:T(8,128)S(1)}) custom-call(s32[8,5]{1,0:T(8,128)S(1)} %get-tuple-element.45.cols, bf16[14,64,128]{2,1,0:T(8,128)(2,1)S(1)} %get-tuple-element.59.xs, bf16[8,640,256]{2,1,0:T(8,128)(2,1)S(1)} %get-tuple-element.46.w_high, ...), custom_call_target="tpu_custom_call" | custom-call | tf_op jit(solution)/shard_map/pallas_call | solution.py:565
  33.9 0.7 shard_map.83
  34.6 0.6 copy-done.15
  35.3 0.5 collective-permute-start.9
  35.8 0.8 %collective-permute-done.9.pair = f32[16,128]{1,0:T(8,128)S(1)} collective-permute-done((f32[16,128]{1,0:T(8,128)S(1)}, f32[16,128]{1,0:T(8,128)S(1)}, u32[]{:S(2)}, u32[]{:S(2)}) %collective-permute-start.9) | collective-permute-done | bytes 8224 | tf_op jit(solution)/shard_map/ppermute | solution.py:572
  36.6 1.3 %collective-permute-done.8.h_b.q_b = f32[2,48,128]{2,1,0:T(8,128)S(1)} collective-permute-done((f32[2,48,128]{2,1,0:T(8,128)S(1)}, f32[2,48,128]{2,1,0:T(8,128)S(1)}, u32[]{:S(2)}, u32[]{:S(2)}) %collective-permute-start.8) | collective-permute-done | bytes 49184 | tf_op jit(solution)/shard_map/ppermute | solution.py:520
  37.9 0.1 collective-permute-done.7.h_f.q_f
  38.1 0.0 collective-permute-done.6.h_a.q_a
  38.1 1.6 %shard_map.84 = (f32[16,1024]{1,0:T(8,128)S(1)}, f32[2,16,128]{2,1,0:T(8,128)S(1)}, f32[32,10,1,128]{3,2,1,0:T(1,128)S(1)}) custom-call(s32[8,5]{1,0:T(8,128)S(1)} %get-tuple-element.45.cols, s32[2]{0:T(128)S(1)} %copy-done.19, f32[16,1024]{1,0:T(8,128)S(1)} %get-tuple-element.60.p, f32[2,48,128]{2,1,0:T(8,128)S(1)} %collective-permute-done.6.h_a.q_a, ...), custom_call_target="tpu_custom_call" | custom-call | tf_op jit(solution)/shard_map/pallas_call | solution.py:574
  39.7 0.6 copy-done.12
  40.4 0.6 copy-done.17
  41.0 0.6 copy-done.21
  41.6 2.6 %all-to-all-start.1 = ((f32[32,10,1,128]{3,2,1,0:T(1,128)}), f32[32,10,1,128]{3,2,1,0:T(1,128)S(1)}, u32[]{:S(2)}, u32[]{:S(2)}) async-start(f32[32,10,1,128]{3,2,1,0:T(1,128)} %copy-done.12), calls=%async_computation.1 | async-start | bytes 327680 | tf_op jit(solution)/shard_map/all_to_all | solution.py:523
  44.2 5.3 %collective-permute-start.12 = (f32[2,16,128]{2,1,0:T(8,128)}, f32[2,16,128]{2,1,0:T(8,128)}, u32[]{:S(2)}, u32[]{:S(2)}) collective-permute-start(f32[2,16,128]{2,1,0:T(8,128)} %copy-done.21), channel_id=1, source_target_pairs={{0,31},{1,2},{2,1},{3,4},{4,3},{5,6},{6,5},{7,8},{8,7},{9,10},{10,... | collective-permute-start | bytes 49160 | tf_op jit(solution)/shard_map/ppermute | solution.py:520
  49.5 0.0 collective-permute-start.11
  49.5 0.0 collective-permute-start.10
  49.5 3.4 %all-to-all-done.1.red = f32[32,10,1,128]{3,2,1,0:T(1,128)S(1)} async-done(((f32[32,10,1,128]{3,2,1,0:T(1,128)}), f32[32,10,1,128]{3,2,1,0:T(1,128)S(1)}, u32[]{:S(2)}, u32[]{:S(2)}) %all-to-all-start.1) | async-done | bytes 163872 | tf_op jit(solution)/shard_map/all_to_all | solution.py:523
  52.9 0.8 %copy-done.18 = f32[16,1024]{1,0:T(8,128)S(1)} copy-done((f32[16,1024]{1,0:T(8,128)S(1)}, f32[16,1024]{1,0:T(8,128)}, u32[]{:S(2)}) %copy-start.18) | copy-done | bytes 65560
  53.7 0.7 shard_map.85
  54.5 0.0 collective-permute-done.11.h_f
  54.5 0.0 collective-permute-done.10.h_a
  54.5 1.7 %copy-done.3 = bf16[8,640,256]{2,1,0:T(8,128)(2,1)S(1)} copy-done((bf16[8,640,256]{2,1,0:T(8,128)(2,1)S(1)}, bf16[8,640,256]{2,1,0:T(8,128)(2,1)}, u32[]{:S(2)}) %copy-start.3) | copy-done | bytes 2621464
  56.2 0.8 copy-done.7
  57.0 0.8 copy-done.9
  57.8 0.8 copy-done.11
  58.6 0.9 %copy-done.14 = f32[48,768]{1,0:T(8,128)S(1)} copy-done((f32[48,768]{1,0:T(8,128)S(1)}, f32[48,768]{1,0:T(8,128)}, u32[]{:S(2)}) %copy-start.14) | copy-done | bytes 147480
  59.5 0.7 copy-done.20
  60.2 1.2 %shard_map.86 = (f32[2,16,128]{2,1,0:T(8,128)S(1)}, bf16[14,32,128]{2,1,0:T(8,128)(2,1)S(1)}) custom-call(s32[8,5]{1,0:T(8,128)S(1)} %get-tuple-element.45.cols, s32[2]{0:T(128)S(1)} %copy-done.20, f32[16,1024]{1,0:T(8,128)S(1)} %get-tuple-element.71.c_local, f32[32,128]{1,0:T(8,128)S(1)} %get-tuple-element.72.coefs, ...), custom_call_target="tpu_custom_call" | custom-call | tf_op jit(solution)/shard_map/pallas_call | solution.py:582
  61.4 2.1 %collective-permute-start.15 = (f32[2,16,128]{2,1,0:T(8,128)S(1)}, f32[2,16,128]{2,1,0:T(8,128)S(1)}, u32[]{:S(2)}, u32[]{:S(2)}) collective-permute-start(f32[2,16,128]{2,1,0:T(8,128)S(1)} %get-tuple-element.77), channel_id=1, source_target_pairs={{0,31},{1,2},{2,1},{3,4},{4,3},{5,6},{6,5},{7,8},{8,7},{9,10},{10,... | collective-permute-start | bytes 49160 | tf_op jit(solution)/shard_map/ppermute | solution.py:520
  63.6 0.0 collective-permute-start.14
  63.6 0.9 %shard_map.87 = (f32[16,1024]{1,0:T(8,128)S(1)}, f32[16,1024]{1,0:T(8,128)S(1)}) custom-call(s32[8,5]{1,0:T(8,128)S(1)} %get-tuple-element.45.cols, bf16[14,32,128]{2,1,0:T(8,128)(2,1)S(1)} %get-tuple-element.75.xs, f32[16,1024]{1,0:T(8,128)S(1)} %get-tuple-element.71.c_local, f32[32,128]{1,0:T(8,128)S(1)} %get-tuple-element.72.coefs, ...), custom_call_target="tpu_custom_call" | custom-call | tf_op jit(solution)/shard_map/pallas_call | solution.py:586
  64.6 0.4 shard_map.88
  65.0 3.3 %collective-permute-done.15.h_b = f32[2,16,128]{2,1,0:T(8,128)S(1)} collective-permute-done((f32[2,16,128]{2,1,0:T(8,128)S(1)}, f32[2,16,128]{2,1,0:T(8,128)S(1)}, u32[]{:S(2)}, u32[]{:S(2)}) %collective-permute-start.15) | collective-permute-done | bytes 16416 | tf_op jit(solution)/shard_map/ppermute | solution.py:520
  68.3 0.0 collective-permute-done.14.h_f
  68.3 0.0 collective-permute-done.13.h_a
  68.3 1.3 %shard_map.89 = (f32[16,1024]{1,0:T(8,128)S(1)}, f32[32,8,128]{2,1,0:T(8,128)S(1)}) custom-call(s32[8,5]{1,0:T(8,128)S(1)} %get-tuple-element.45.cols, f32[16,1024]{1,0:T(8,128)S(1)} %get-tuple-element.76.p, f32[2,16,128]{2,1,0:T(8,128)S(1)} %collective-permute-done.13.h_a, f32[2,16,128]{2,1,0:T(8,128)S(1)} %collective-permute-done.14.h_f, ...), custom_call_target="tpu_custom_call" | custom-call | tf_op jit(solution)/shard_map/pallas_call | solution.py:588
  69.6 10.4 %all_to_all.15.red = f32[32,8,128]{2,1,0:T(8,128)S(1)} all-to-all(f32[32,8,128]{2,1,0:T(8,128)S(1)} %get-tuple-element.82), channel_id=1, replica_groups=mesh['parts'=32] {'parts'}, dimensions={0} | all-to-all | bytes 262144 | tf_op jit(solution)/shard_map/all_to_all | solution.py:523
  80.1 1.2 %shard_map.90 = f32[16,1024]{1,0:T(8,128)} custom-call(f32[32,8,128]{2,1,0:T(8,128)S(1)} %all_to_all.15.red, f32[16,1024]{1,0:T(8,128)S(1)} %get-tuple-element.83.p, f32[144,128]{1,0:T(8,128)S(1)} %get-tuple-element.58.small, f32[64,128]{1,0:T(8,128)S(1)} %get-tuple-element.70.small_b, f32[32,128]{1,0:T(8,128)S(1)} %get-tuple-element.84.tests_in, ...), custom_call_target="tpu_custom_call" | custom-call | tf_op jit(solution)/shard_map/pallas_call | solution.py:590
  (31 shorter events, 0.1 us)
Async XLA Ops:
  1.6 11.1 %copy-start.5 = (f32[16,1024]{1,0:T(8,128)S(1)}, f32[16,1024]{1,0:T(8,128)}, u32[]{:S(2)}) copy-start(f32[16,1024]{1,0:T(8,128)} %basis.3) | copy-start | bytes 196612
  1.6 11.1 %copy-start.19 = (s32[2]{0:T(128)S(1)}, s32[2]{0:T(128)}, u32[]{:S(2)}) copy-start(s32[2]{0:T(128)} %iface.7) | copy-start | bytes 28
  1.6 10.4 %collective-permute-start.2 = (f32[2,16,128]{2,1,0:T(8,128)S(1)}, f32[2,16,128]{2,1,0:T(8,128)S(1)}, u32[]{:S(2)}, u32[]{:S(2)}) collective-permute-start(f32[2,16,128]{2,1,0:T(8,128)S(1)} %shard_map.78), channel_id=1, source_target_pairs={{0,31},{1,2},{2,1},{3,4},{4,3},{5,6},{6,5},{7,8},{8,7},{9,10},{10,... | collective-permute-start | bytes 49160 | tf_op jit(solution)/shard_map/ppermute | solution.py:520
  8.1 4.6 %collective-permute-start.1 = (f32[2,16,128]{2,1,0:T(8,128)S(1)}, f32[2,16,128]{2,1,0:T(8,128)S(1)}, u32[]{:S(2)}, u32[]{:S(2)}) collective-permute-start(f32[2,16,128]{2,1,0:T(8,128)S(1)} %shard_map.78), channel_id=1, source_target_pairs={{0,16},{1,17},{2,18},{3,19},{4,20},{5,21},{6,22},{7,23},{8,24},{9,... | collective-permute-start | bytes 49160 | tf_op jit(solution)/shard_map/ppermute | solution.py:520
  8.1 4.6 %collective-permute-start = (f32[2,16,128]{2,1,0:T(8,128)S(1)}, f32[2,16,128]{2,1,0:T(8,128)S(1)}, u32[]{:S(2)}, u32[]{:S(2)}) collective-permute-start(f32[2,16,128]{2,1,0:T(8,128)S(1)} %shard_map.78), channel_id=1, source_target_pairs={{0,1},{1,0},{2,3},{3,2},{4,5},{5,4},{6,7},{7,6},{8,9},{9,8},{10,11... | collective-permute-start | bytes 49160 | tf_op jit(solution)/shard_map/ppermute | solution.py:520
  12.1 2.9 %copy-start = (bf16[8,640,256]{2,1,0:T(8,128)(2,1)}, bf16[8,640,256]{2,1,0:T(8,128)(2,1)S(1)}, u32[]{:S(2)}) copy-start(bf16[8,640,256]{2,1,0:T(8,128)(2,1)S(1)} %get-tuple-element.47.w_low) | copy-start | bytes 7864324
  14.9 11.3 %all-to-all-start = ((f32[32,9,1,128]{3,2,1,0:T(1,128)}), f32[32,9,1,128]{3,2,1,0:T(1,128)S(1)}, u32[]{:S(2)}, u32[]{:S(2)}) async-start(f32[32,9,1,128]{3,2,1,0:T(1,128)} %get-tuple-element.50), calls=%async_computation | async-start | bytes 294912 | tf_op jit(solution)/shard_map/all_to_all | solution.py:523
  17.7 9.9 %collective-permute-start.5 = (f32[2,32,128]{2,1,0:T(8,128)S(1)}, f32[2,32,128]{2,1,0:T(8,128)S(1)}, u32[]{:S(2)}, u32[]{:S(2)}) collective-permute-start(f32[2,32,128]{2,1,0:T(8,128)S(1)} %get-tuple-element.49), channel_id=1, source_target_pairs={{0,31},{1,2},{2,1},{3,4},{4,3},{5,6},{6,5},{7,8},{8,7},{9,10},{10,... | collective-permute-start | bytes 98312 | tf_op jit(solution)/shard_map/ppermute | solution.py:520
  23.0 4.8 %collective-permute-start.4 = (f32[2,32,128]{2,1,0:T(8,128)S(1)}, f32[2,32,128]{2,1,0:T(8,128)S(1)}, u32[]{:S(2)}, u32[]{:S(2)}) collective-permute-start(f32[2,32,128]{2,1,0:T(8,128)S(1)} %get-tuple-element.49), channel_id=1, source_target_pairs={{0,16},{1,17},{2,18},{3,19},{4,20},{5,21},{6,22},{7,23},{8,24},{9,... | collective-permute-start | bytes 98312 | tf_op jit(solution)/shard_map/ppermute | solution.py:520
  23.0 4.8 %collective-permute-start.3 = (f32[2,32,128]{2,1,0:T(8,128)S(1)}, f32[2,32,128]{2,1,0:T(8,128)S(1)}, u32[]{:S(2)}, u32[]{:S(2)}) collective-permute-start(f32[2,32,128]{2,1,0:T(8,128)S(1)} %get-tuple-element.49), channel_id=1, source_target_pairs={{0,1},{1,0},{2,3},{3,2},{4,5},{5,4},{6,7},{7,6},{8,9},{9,8},{10,11... | collective-permute-start | bytes 98312 | tf_op jit(solution)/shard_map/ppermute | solution.py:520
  27.8 1.7 %copy-start.1 = (bf16[8,640,256]{2,1,0:T(8,128)(2,1)S(1)}, bf16[8,640,256]{2,1,0:T(8,128)(2,1)}, u32[]{:S(2)}) copy-start(bf16[8,640,256]{2,1,0:T(8,128)(2,1)} %copy-done) | copy-start | bytes 7864324
  30.1 0.7 copy-start.13
  30.7 7.2 %collective-permute-start.8 = (f32[2,48,128]{2,1,0:T(8,128)S(1)}, f32[2,48,128]{2,1,0:T(8,128)S(1)}, u32[]{:S(2)}, u32[]{:S(2)}) collective-permute-start(f32[2,48,128]{2,1,0:T(8,128)S(1)} %get-tuple-element.61), channel_id=1, source_target_pairs={{0,31},{1,2},{2,1},{3,4},{4,3},{5,6},{6,5},{7,8},{8,7},{9,10},{10,... | collective-permute-start | bytes 147464 | tf_op jit(solution)/shard_map/ppermute | solution.py:520
  32.8 5.2 %collective-permute-start.7 = (f32[2,48,128]{2,1,0:T(8,128)S(1)}, f32[2,48,128]{2,1,0:T(8,128)S(1)}, u32[]{:S(2)}, u32[]{:S(2)}) collective-permute-start(f32[2,48,128]{2,1,0:T(8,128)S(1)} %get-tuple-element.61), channel_id=1, source_target_pairs={{0,16},{1,17},{2,18},{3,19},{4,20},{5,21},{6,22},{7,23},{8,24},{9,... | collective-permute-start | bytes 147464 | tf_op jit(solution)/shard_map/ppermute | solution.py:520
  32.8 5.2 %collective-permute-start.6 = (f32[2,48,128]{2,1,0:T(8,128)S(1)}, f32[2,48,128]{2,1,0:T(8,128)S(1)}, u32[]{:S(2)}, u32[]{:S(2)}) collective-permute-start(f32[2,48,128]{2,1,0:T(8,128)S(1)} %get-tuple-element.61), channel_id=1, source_target_pairs={{0,1},{1,0},{2,3},{3,2},{4,5},{5,4},{6,7},{7,6},{8,9},{9,8},{10,11... | collective-permute-start | bytes 147464 | tf_op jit(solution)/shard_map/ppermute | solution.py:520
  32.8 5.2 %copy-start.2 = (bf16[8,640,256]{2,1,0:T(8,128)(2,1)S(1)}, bf16[8,640,256]{2,1,0:T(8,128)(2,1)}, u32[]{:S(2)}) copy-start(bf16[8,640,256]{2,1,0:T(8,128)(2,1)} %copy-done) | copy-start | bytes 7864324
  34.6 0.6 copy-start.15
  35.3 1.3 %collective-permute-start.9 = (f32[16,128]{1,0:T(8,128)S(1)}, f32[16,128]{1,0:T(8,128)S(1)}, u32[]{:S(2)}, u32[]{:S(2)}) collective-permute-start(f32[16,128]{1,0:T(8,128)S(1)} %get-tuple-element.65.part), channel_id=1, source_target_pairs={{0,1},{1,0},{2,3},{3,2},{4,5},{5,4},{6,7},{7,6},{8,9},{9,8},{10,11... | collective-permute-start | bytes 24584 | tf_op jit(solution)/shard_map/ppermute | solution.py:572
  37.9 1.7 %copy-start.6 = (f32[2,48,128]{2,1,0:T(8,128)}, f32[2,48,128]{2,1,0:T(8,128)S(1)}, u32[]{:S(2)}) copy-start(f32[2,48,128]{2,1,0:T(8,128)S(1)} %collective-permute-done.8.h_b.q_b) | copy-start | bytes 147460
  38.1 1.6 %copy-start.8 = (f32[2,48,128]{2,1,0:T(8,128)}, f32[2,48,128]{2,1,0:T(8,128)S(1)}, u32[]{:S(2)}) copy-start(f32[2,48,128]{2,1,0:T(8,128)S(1)} %collective-permute-done.7.h_f.q_f) | copy-start | bytes 147460
  38.1 1.6 %copy-start.10 = (f32[2,48,128]{2,1,0:T(8,128)}, f32[2,48,128]{2,1,0:T(8,128)S(1)}, u32[]{:S(2)}) copy-start(f32[2,48,128]{2,1,0:T(8,128)S(1)} %collective-permute-done.6.h_a.q_a) | copy-start | bytes 147460
  39.7 0.7 copy-start.12
  40.4 0.6 copy-start.17
  41.0 0.6 copy-start.21
  41.6 11.3 %all-to-all-start.1 = ((f32[32,10,1,128]{3,2,1,0:T(1,128)}), f32[32,10,1,128]{3,2,1,0:T(1,128)S(1)}, u32[]{:S(2)}, u32[]{:S(2)}) async-start(f32[32,10,1,128]{3,2,1,0:T(1,128)} %copy-done.12), calls=%async_computation.1 | async-start | bytes 327680 | tf_op jit(solution)/shard_map/all_to_all | solution.py:523
  44.2 10.2 %collective-permute-start.12 = (f32[2,16,128]{2,1,0:T(8,128)}, f32[2,16,128]{2,1,0:T(8,128)}, u32[]{:S(2)}, u32[]{:S(2)}) collective-permute-start(f32[2,16,128]{2,1,0:T(8,128)} %copy-done.21), channel_id=1, source_target_pairs={{0,31},{1,2},{2,1},{3,4},{4,3},{5,6},{6,5},{7,8},{8,7},{9,10},{10,... | collective-permute-start | bytes 49160 | tf_op jit(solution)/shard_map/ppermute | solution.py:520
  49.5 5.0 %collective-permute-start.11 = (f32[2,16,128]{2,1,0:T(8,128)}, f32[2,16,128]{2,1,0:T(8,128)}, u32[]{:S(2)}, u32[]{:S(2)}) collective-permute-start(f32[2,16,128]{2,1,0:T(8,128)} %copy-done.21), channel_id=1, source_target_pairs={{0,16},{1,17},{2,18},{3,19},{4,20},{5,21},{6,22},{7,23},{8,24},{9,... | collective-permute-start | bytes 49160 | tf_op jit(solution)/shard_map/ppermute | solution.py:520
  49.5 5.0 %collective-permute-start.10 = (f32[2,16,128]{2,1,0:T(8,128)}, f32[2,16,128]{2,1,0:T(8,128)}, u32[]{:S(2)}, u32[]{:S(2)}) collective-permute-start(f32[2,16,128]{2,1,0:T(8,128)} %copy-done.21), channel_id=1, source_target_pairs={{0,1},{1,0},{2,3},{3,2},{4,5},{5,4},{6,7},{7,6},{8,9},{9,8},{10,11... | collective-permute-start | bytes 49160 | tf_op jit(solution)/shard_map/ppermute | solution.py:520
  52.9 0.8 %copy-start.18 = (f32[16,1024]{1,0:T(8,128)S(1)}, f32[16,1024]{1,0:T(8,128)}, u32[]{:S(2)}) copy-start(f32[16,1024]{1,0:T(8,128)} %copy-done.17) | copy-start | bytes 196612
  54.5 1.7 %copy-start.3 = (bf16[8,640,256]{2,1,0:T(8,128)(2,1)S(1)}, bf16[8,640,256]{2,1,0:T(8,128)(2,1)}, u32[]{:S(2)}) copy-start(bf16[8,640,256]{2,1,0:T(8,128)(2,1)} %copy-done) | copy-start | bytes 7864324
  56.2 0.8 copy-start.7
  57.0 0.8 copy-start.9
  57.8 0.8 copy-start.11
  58.6 0.9 %copy-start.14 = (f32[48,768]{1,0:T(8,128)S(1)}, f32[48,768]{1,0:T(8,128)}, u32[]{:S(2)}) copy-start(f32[48,768]{1,0:T(8,128)} %copy-done.13) | copy-start | bytes 442372
  59.5 0.7 copy-start.20
  61.4 6.8 %collective-permute-start.15 = (f32[2,16,128]{2,1,0:T(8,128)S(1)}, f32[2,16,128]{2,1,0:T(8,128)S(1)}, u32[]{:S(2)}, u32[]{:S(2)}) collective-permute-start(f32[2,16,128]{2,1,0:T(8,128)S(1)} %get-tuple-element.77), channel_id=1, source_target_pairs={{0,31},{1,2},{2,1},{3,4},{4,3},{5,6},{6,5},{7,8},{8,7},{9,10},{10,... | collective-permute-start | bytes 49160 | tf_op jit(solution)/shard_map/ppermute | solution.py:520
  63.6 4.7 %collective-permute-start.14 = (f32[2,16,128]{2,1,0:T(8,128)S(1)}, f32[2,16,128]{2,1,0:T(8,128)S(1)}, u32[]{:S(2)}, u32[]{:S(2)}) collective-permute-start(f32[2,16,128]{2,1,0:T(8,128)S(1)} %get-tuple-element.77), channel_id=1, source_target_pairs={{0,16},{1,17},{2,18},{3,19},{4,20},{5,21},{6,22},{7,23},{8,24},{9,... | collective-permute-start | bytes 49160 | tf_op jit(solution)/shard_map/ppermute | solution.py:520
  63.6 4.7 %collective-permute-start.13 = (f32[2,16,128]{2,1,0:T(8,128)S(1)}, f32[2,16,128]{2,1,0:T(8,128)S(1)}, u32[]{:S(2)}, u32[]{:S(2)}) collective-permute-start(f32[2,16,128]{2,1,0:T(8,128)S(1)} %get-tuple-element.77), channel_id=1, source_target_pairs={{0,1},{1,0},{2,3},{3,2},{4,5},{5,4},{6,7},{7,6},{8,9},{9,8},{10,11... | collective-permute-start | bytes 49160 | tf_op jit(solution)/shard_map/ppermute | solution.py:520
  63.6 1.0 %copy-start.16 = (f32[16,1024]{1,0:T(8,128)S(1)}, f32[16,1024]{1,0:T(8,128)}, u32[]{:S(2)}) copy-start(f32[16,1024]{1,0:T(8,128)} %copy-done.15) | copy-start | bytes 196612
  63.6 4.7 %copy-start.4 = (bf16[8,640,256]{2,1,0:T(8,128)(2,1)S(1)}, bf16[8,640,256]{2,1,0:T(8,128)(2,1)}, u32[]{:S(2)}) copy-start(bf16[8,640,256]{2,1,0:T(8,128)(2,1)} %copy-done) | copy-start | bytes 7864324

commit v6 on v5

--- a/solution.py
+++ b/solution.py
@@ -94,10 +94,11 @@
         m_out[:, i * width : (i + 1) * width] = result[:, width:]
 
 
-def apply_iface(xs, cols, w_high, w_low, tile):
-    n = xs.shape[1] // 2
+def apply_iface(xs, cols, w_high, w_low, tile, n):
+    low_at = xs.shape[1] // 2
     width = xs.shape[2]
-    lhs = lanes([xs[cols[tile, b]] for b in range(cols.shape[1])])
+    blocks = range(cols.shape[1])
+    lhs = rows([lanes([xs[cols[tile, b], at : at + n] for b in blocks]) for at in (0, low_at)])
     both = jnp.dot(lhs, w_high[tile], preferred_element_type=F32)
     low = jnp.dot(lhs[:n], w_low[tile], preferred_element_type=F32)
     result = both[:n] + both[n:] + low
@@ -300,8 +301,10 @@
         g_mm = jnp.where(lane < n, g_mm, 0.0)
         inv_v, inv_c = inverse_chols(g_bb, g_mm)
         lv, lc = inv_v[:, :n], inv_c[:, :n]
-        cross = nt(mm(lv, g_km[:, :n]), lc)
-        theta = diagonal(cross) * diagonal(inv_c) / diagonal(inv_v)
+        left_cross = mm(lv, g_km[:, :n])
+        cross = nt(left_cross, lc)
+        cross_diag = jnp.sum(left_cross * lc, axis=1, keepdims=True)
+        theta = cross_diag * (diagonal(inv_c) / diagonal(inv_v))
         g1 = mm3(lv, u[:n])
         both = mm3(rows([lv, lc]), u[n:])
         g2, f1 = both[:n], both[n:]
@@ -333,12 +336,9 @@
         for slot in range(outgoing.shape[0]):
             tile = iface[slot]
             at = lanes_of(tile, xs.shape[2])
-            k_tile, m_tile = apply_iface(xs, cols, w_high, w_low, tile)
-            d = inv_d[:, at]
-            image = k_tile[:n] - theta * m_tile[:n] - mm3(coef, rows([ko[:, at], mo[:, at]]))
-            outgoing[slot, :n] = 2.0 * c0[:, at] - relax * d * image
-            outgoing[slot, n : 2 * n] = k_tile[n:] * d
-            outgoing[slot, 2 * n :] = m_tile[n:] * d
+            k_tile, m_tile = apply_iface(xs, cols, w_high, w_low, tile, n)
+            image = k_tile - theta * m_tile - mm3(coef, rows([ko[:, at], mo[:, at]]))
+            outgoing[slot] = 2.0 * c0[:, at] - relax * inv_d[:, at] * image
 
     def k_b2(
         cols, xs, w_high, w_low, inv_d, ko, mo, c0, words_in, small, p_out, image_out, words, kf_out, res
@@ -386,7 +386,7 @@
         return fresh, jnp.where(lane < n, both[:n], both[n:])
 
     def k_c1(
-        cols, iface, p, h_a, h_f, h_b, c0, small, part, pair, tests_high, tests_low, w_high, w_low, inv_d,
+        cols, iface, p, h_a, h_f, h_b, c0, words, small, part, pair, tests_high, tests_low, w_high, w_low, inv_d,
         p_out, outgoing, grams, xs, res,
     ):
         fresh, added = half(
@@ -395,6 +395,7 @@
         )
         p_out[...] = fresh
         send_tiles(iface, outgoing, 0, p_out)
+        send_tiles(iface, outgoing, n, words.at[n : 3 * n])
         chip = part[...] + pair[...]
         chip = jnp.where(lax.axis_index("parts") % 2 == 0, chip, pltpu.roll(chip, MAT - 3 * n, 1))
         lane, _ = lane_row((n, MAT))
@@ -449,12 +450,12 @@
         put_small(coefs, 1, g_fresh + mm(coef, rows(list(onto))))
 
     def k_d1(
-        cols, iface, c_local, coefs, h_a, h_f, h_b, q_a, q_f, q_b, ko, mo, c0, words_halo, small,
+        cols, iface, c_local, coefs, h_a, h_f, h_b, ko, mo, c0, words_halo, small,
         w_high, w_low, inv_d, outgoing, xs,
     ):
         coef, right = coefs[:n, : 5 * n], get_small(coefs, 1)
         theta = small[5 * n : 6 * n, :1]
-        around = rows([words_halo[:n], halo_lanes((q_a, q_f, q_b), n, 3 * n), words_halo[n:]])
+        around = rows([words_halo[:n], halo_lanes((h_a, h_f, h_b), n, 3 * n), words_halo[n:]])
         c_halo = halo_lanes((h_a, h_f, h_b), 0, n) + mm3(coef, around)
         put_sources(xs, 0, c_local[...])
         put_sources(xs, c_local.shape[1] // xs.shape[2], c_halo)
@@ -462,7 +463,7 @@
         for slot in range(outgoing.shape[0]):
             tile = iface[slot]
             at = lanes_of(tile, xs.shape[2])
-            k_tile, m_tile = apply_iface(xs, cols, w_high, w_low, tile)
+            k_tile, m_tile = apply_iface(xs, cols, w_high, w_low, tile, n)
             image = k_tile - theta * m_tile - mm3(onto, rows([ko[:, at], mo[:, at]]))
             outgoing[slot] = c_local[:, at] + c0[:, at] - relax * inv_d[:, at] * image
 
@@ -517,7 +518,10 @@
     far = [(source, (source + half_way) % parts) for source in range(parts)]
 
     def halo(outgoing):
-        return [lax.ppermute(outgoing, "parts", pairs) for pairs in (chip, far, other)]
+        got = []
+        for pairs in (chip, far, other):
+            got.append(lax.ppermute(outgoing, "parts", pairs))
+        return got
 
     def reduced(blocks_out):
         return lax.all_to_all(blocks_out, "parts", 0, 0, tiled=True)
@@ -559,7 +563,7 @@
     )(red, kb, mb, u)
     sources_of = lambda m: ((sources, 2 * m, width), BF16)
     words_halo, outgoing, source = call(
-        k_b1, [((3 * n, 3 * count * width), F32), out(3 * n), sources_of(2 * n)], [VM, VM] + [VM] * 11
+        k_b1, [((3 * n, 3 * count * width), F32), out(n), sources_of(2 * n)], [VM, VM] + [VM] * 11
     )(cols, iface, *h1, *w, ko, mo, c0, words, small)
     h2 = halo(outgoing)
     p1, image0, words, kf = call(
@@ -571,16 +575,16 @@
     tests = (tests_high, tests_low)
     pair = lax.ppermute(part, "parts", chip)
     packed = ((parts, n // 2 + 2, 1, MAT), F32)
-    p2, outgoing, grams = call(k_c1, [vec, out(n), packed], [VM, VM] + [VM] * 13, [xs(n), res])(
-        cols, iface, p1, *h2, c0, small, part, pair, *tests, *w
+    p2, outgoing, grams = call(k_c1, [vec, out(3 * n), packed], [VM, VM] + [VM] * 14, [xs(n), res])(
+        cols, iface, p1, *h2, c0, words, small, part, pair, *tests, *w
     )
     red = reduced(grams)
     h3 = halo(outgoing)
     c2, word_tests, onto_v, coefs = call(k_d0, [vec, mats(2), mats(5), mats(2)], [VM] * 5)(
         red, p2, words, small, small_b
     )
-    outgoing, source = call(k_d1, [out(n), sources_of(n)], [VM, VM] + [VM] * 16)(
-        cols, iface, c2, coefs, *h3, *h2, ko, mo, c0, words_halo, small, *w
+    outgoing, source = call(k_d1, [out(n), sources_of(n)], [VM, VM] + [VM] * 13)(
+        cols, iface, c2, coefs, *h3, ko, mo, c0, words_halo, small, *w
     )
     h4 = halo(outgoing)
     p3, image2 = call(k_d2, [vec, vec], [VM] + [VM] * 10, [res])(cols, source, c2, coefs, ko, mo, c0, small, *w)

time: 81.9 us -> 83.2 us (1.016)
  starting transfers between devices: 27.2 us -> 32.7 us
  local copies, waits for them, and re-layouts: 11.5 us -> 8.47 us
  waiting for transfers between devices: 13.1 us -> 11.6 us
    ppermute x15, starting transfers between devices: 21.3 us -> 26.6 us  [halo(): got.append(lax.ppermute(outgoing, 'parts', pairs))]
    unnamed x44 -> x38, local copies, waits for them, and re-layouts: 11.5 us -> 8.47 us
    ppermute x15, waiting for transfers between devices: 5.67 us -> 4.22 us  [halo(): got.append(lax.ppermute(outgoing, 'parts', pairs))]
  transfers between devices with their start and end apart: 18 -> 18, of which waited for: 8 -> 6; matrix products, arithmetic and copies ran while one was open for 0% -> 0% of each run, Pallas kernels for 11% -> 11%
where the time goes in v6:
time: 83.2 us; the launch traced here: 82.7 us
  starting transfers between devices  32.7 us (39%)
  Pallas kernels  18.3 us (22%)
  waiting for transfers between devices  11.6 us (14%)
  blocking collectives  10.8 us (13%)
  local copies, waits for them, and re-layouts  8.47 us (10%)
  between operations  0.94 us (1%)
    ppermute x15, starting transfers between devices, halo(): got.append(lax.ppermute(outgoing, 'parts', pairs))  26.6 us
    all_to_all x1, blocking collectives, reduced(): return lax.all_to_all(blocks_out, 'parts', 0, 0, tiled=True)  10.8 us
    unnamed x38, local copies, waits for them, and re-layouts  8.47 us
    all_to_all x2, waiting for transfers between devices, reduced(): return lax.all_to_all(blocks_out, 'parts', 0, 0, tiled=True)  6.24 us
    all_to_all x2, starting transfers between devices, reduced(): return lax.all_to_all(blocks_out, 'parts', 0, 0, tiled=True)  6.05 us
    ppermute x15, waiting for transfers between devices, halo(): got.append(lax.ppermute(outgoing, 'parts', pairs))  4.22 us
    pallas_call x1, Pallas kernels, shards(): call(make_prep(count), [((tiles, blocks * width, 2 * width), BF16)] * 2 +...  3.94 us
    pallas_call x1, Pallas kernels, shards(): call(k_a, [vec, vec, vecs(2), out(2 * n), packed], [VM, VM] + [VM] * 7, [...  2.21 us
  transfers between devices with their start and end apart: 18, of which 6 were waited for; matrix products, arithmetic and copies ran while one was open for 0% of the time, Pallas kernels for 11%

profile of v6, /device:TPU:0, one launch (start us, length us, event | category | flops | bytes accessed | tf_op | source)
XLA Modules:
  0.0 82.7 jit_solution(7577679517259720037)
XLA Ops:
  0.6 1.0 %shard_map.78 = f32[2,16,128]{2,1,0:T(8,128)S(1)} custom-call(s32[2]{0:T(128)} %iface.7, f32[16,1024]{1,0:T(8,128)} %basis.3), custom_call_target="tpu_custom_call" | custom-call | tf_op jit(solution)/shard_map/pallas_call | solution.py:539
  1.6 0.0 copy-start.5
  1.6 0.0 copy-start.15
  1.6 0.6 collective-permute-start
  2.2 3.7 %collective-permute-start.1 = (f32[2,16,128]{2,1,0:T(8,128)S(1)}, f32[2,16,128]{2,1,0:T(8,128)S(1)}, u32[]{:S(2)}, u32[]{:S(2)}) collective-permute-start(f32[2,16,128]{2,1,0:T(8,128)S(1)} %shard_map.78), channel_id=1, source_target_pairs={{0,16},{1,17},{2,18},{3,19},{4,20},{5,21},{6,22},{7,23},{8,24},{9,... | collective-permute-start | bytes 49160 | tf_op jit(solution)/shard_map/ppermute | solution.py:523
  5.8 3.0 %collective-permute-start.2 = (f32[2,16,128]{2,1,0:T(8,128)S(1)}, f32[2,16,128]{2,1,0:T(8,128)S(1)}, u32[]{:S(2)}, u32[]{:S(2)}) collective-permute-start(f32[2,16,128]{2,1,0:T(8,128)S(1)} %shard_map.78), channel_id=1, source_target_pairs={{0,31},{1,2},{2,1},{3,4},{4,3},{5,6},{6,5},{7,8},{8,7},{9,10},{10,... | collective-permute-start | bytes 49160 | tf_op jit(solution)/shard_map/ppermute | solution.py:523
  8.8 3.9 %shard_map.77 = (bf16[8,640,256]{2,1,0:T(8,128)(2,1)S(1)}, bf16[8,640,256]{2,1,0:T(8,128)(2,1)S(1)}, f32[1,1024]{1,0:T(1,128)S(1)}, s32[8,5]{1,0:T(8,128)S(1)}) custom-call(s32[8,5]{1,0:T(8,128)} %part_hbm.1, s32[8,5]{1,0:T(8,128)} %slot_hbm.1, f32[8,5,128,128]{3,2,1,0:T(8,128)} %k_hbm.1, f32[8,5,128,128]{3,2,1,0:T(8,128)} %m_hbm.1), custom_call_target="tpu_custom_call" | custom-call | tf_op jit(solution)/shard_map/pallas_call | solution.py:546
  12.8 0.0 collective-permute-done.h_a
  12.8 0.0 collective-permute-done.1.h_f
  12.8 0.0 collective-permute-done.2.h_b
  12.8 2.2 %shard_map.79 = (f32[16,1024]{1,0:T(8,128)S(1)}, f32[16,1024]{1,0:T(8,128)S(1)}, f32[32,1024]{1,0:T(8,128)S(1)}, f32[2,32,128]{2,1,0:T(8,128)S(1)}, f32[32,9,1,128]{3,2,1,0:T(1,128)}) custom-call(s32[8,5]{1,0:T(8,128)S(1)} %get-tuple-element.45.cols, s32[2]{0:T(128)S(1)} %copy-done.15, f32[16,1024]{1,0:T(8,128)S(1)} %copy-done.5, ...), custom_call_target="tpu_custom_call" | custom-call | tf_op jit(solution)/shard_map/pallas_call | solution.py:556
  15.1 3.1 %all-to-all-start = ((f32[32,9,1,128]{3,2,1,0:T(1,128)}), f32[32,9,1,128]{3,2,1,0:T(1,128)S(1)}, u32[]{:S(2)}, u32[]{:S(2)}) async-start(f32[32,9,1,128]{3,2,1,0:T(1,128)} %get-tuple-element.50), calls=%async_computation | async-start | bytes 294912 | tf_op jit(solution)/shard_map/all_to_all | solution.py:527
  18.2 0.3 collective-permute-start.3
  18.5 2.5 %collective-permute-start.4 = (f32[2,32,128]{2,1,0:T(8,128)S(1)}, f32[2,32,128]{2,1,0:T(8,128)S(1)}, u32[]{:S(2)}, u32[]{:S(2)}) collective-permute-start(f32[2,32,128]{2,1,0:T(8,128)S(1)} %get-tuple-element.49), channel_id=1, source_target_pairs={{0,16},{1,17},{2,18},{3,19},{4,20},{5,21},{6,22},{7,23},{8,24},{9,... | collective-permute-start | bytes 98312 | tf_op jit(solution)/shard_map/ppermute | solution.py:523
  21.0 3.0 %collective-permute-start.5 = (f32[2,32,128]{2,1,0:T(8,128)S(1)}, f32[2,32,128]{2,1,0:T(8,128)S(1)}, u32[]{:S(2)}, u32[]{:S(2)}) collective-permute-start(f32[2,32,128]{2,1,0:T(8,128)S(1)} %get-tuple-element.49), channel_id=1, source_target_pairs={{0,31},{1,2},{2,1},{3,4},{4,3},{5,6},{6,5},{7,8},{8,7},{9,10},{10,... | collective-permute-start | bytes 98312 | tf_op jit(solution)/shard_map/ppermute | solution.py:523
  24.0 2.9 %all-to-all-done.red = f32[32,9,1,128]{3,2,1,0:T(1,128)S(1)} async-done(((f32[32,9,1,128]{3,2,1,0:T(1,128)}), f32[32,9,1,128]{3,2,1,0:T(1,128)S(1)}, u32[]{:S(2)}, u32[]{:S(2)}) %all-to-all-start) | async-done | bytes 147488 | tf_op jit(solution)/shard_map/all_to_all | solution.py:527
  26.9 1.4 %shard_map.80 = (f32[16,1024]{1,0:T(8,128)S(1)}, f32[16,1024]{1,0:T(8,128)S(1)}, f32[16,1024]{1,0:T(8,128)S(1)}, f32[80,1024]{1,0:T(8,128)S(1)}, f32[144,128]{1,0:T(8,128)S(1)}, /*index=5*/f32[1,16]{1,0:T(1,128)}) custom-call(f32[32,9,1,128]{3,2,1,0:T(1,128)S(1)} %all-to-all-done.red, f32[16,1024]{1,0:T(8,128)S(1)} %get-tuple-element.51.kb, ...), custom_call_target="tpu_custom_call" | custom-call | tf_op jit(solution)/shard_map/pallas_call | solution.py:561
  28.3 0.0 collective-permute-done.3.h_a
  28.3 0.0 collective-permute-done.4.h_f
  28.3 0.0 collective-permute-done.5.h_b
  28.3 1.7 %copy-done.1 = bf16[8,640,256]{2,1,0:T(8,128)(2,1)S(1)} copy-done((bf16[8,640,256]{2,1,0:T(8,128)(2,1)S(1)}, bf16[8,640,256]{2,1,0:T(8,128)(2,1)}, u32[]{:S(2)}) %copy-start.1) | copy-done | bytes 2621464
  30.1 0.5 shard_map.81
  30.6 0.0 copy-done.6
  30.6 0.0 copy-start.9
  30.6 0.6 copy-done.9
  31.2 0.3 collective-permute-start.6
  31.5 0.8 collective-permute-start.7
  32.3 2.6 %collective-permute-start.8 = (f32[2,16,128]{2,1,0:T(8,128)S(1)}, f32[2,16,128]{2,1,0:T(8,128)S(1)}, u32[]{:S(2)}, u32[]{:S(2)}) collective-permute-start(f32[2,16,128]{2,1,0:T(8,128)S(1)} %get-tuple-element.61), channel_id=1, source_target_pairs={{0,31},{1,2},{2,1},{3,4},{4,3},{5,6},{6,5},{7,8},{8,7},{9,10},{10,... | collective-permute-start | bytes 49160 | tf_op jit(solution)/shard_map/ppermute | solution.py:523
  34.9 1.1 %shard_map.82 = (f32[16,1024]{1,0:T(8,128)S(1)}, f32[16,1024]{1,0:T(8,128)S(1)}, f32[80,1024]{1,0:T(8,128)S(1)}, f32[32,1024]{1,0:T(8,128)S(1)}) custom-call(s32[8,5]{1,0:T(8,128)S(1)} %get-tuple-element.45.cols, bf16[14,64,128]{2,1,0:T(8,128)(2,1)S(1)} %get-tuple-element.59.xs, bf16[8,640,256]{2,1,0:T(8,128)(2,1)S(1)} %get-tuple-element.46.w_high, ...), custom_call_target="tpu_custom_call" | custom-call | tf_op jit(solution)/shard_map/pallas_call | solution.py:569
  36.0 0.7 shard_map.83
  36.7 0.1 collective-permute-start.9
  36.8 1.2 %collective-permute-done.9.pair = f32[16,128]{1,0:T(8,128)S(1)} collective-permute-done((f32[16,128]{1,0:T(8,128)S(1)}, f32[16,128]{1,0:T(8,128)S(1)}, u32[]{:S(2)}, u32[]{:S(2)}) %collective-permute-start.9) | collective-permute-done | bytes 8224 | tf_op jit(solution)/shard_map/ppermute | solution.py:576
  37.9 0.0 collective-permute-done.6.h_a
  37.9 0.0 collective-permute-done.7.h_f
  37.9 1.1 %collective-permute-done.8.h_b = f32[2,16,128]{2,1,0:T(8,128)S(1)} collective-permute-done((f32[2,16,128]{2,1,0:T(8,128)S(1)}, f32[2,16,128]{2,1,0:T(8,128)S(1)}, u32[]{:S(2)}, u32[]{:S(2)}) %collective-permute-start.8) | collective-permute-done | bytes 16416 | tf_op jit(solution)/shard_map/ppermute | solution.py:523
  39.1 1.6 %shard_map.84 = (f32[16,1024]{1,0:T(8,128)S(1)}, f32[2,48,128]{2,1,0:T(8,128)S(1)}, f32[32,10,1,128]{3,2,1,0:T(1,128)S(1)}) custom-call(s32[8,5]{1,0:T(8,128)S(1)} %get-tuple-element.45.cols, s32[2]{0:T(128)S(1)} %copy-done.16, f32[16,1024]{1,0:T(8,128)S(1)} %get-tuple-element.60.p, f32[2,16,128]{2,1,0:T(8,128)S(1)} %collective-permute-done.6.h_a, ...), custom_call_target="tpu_custom_call" | custom-call | tf_op jit(solution)/shard_map/pallas_call | solution.py:578
  40.7 0.7 copy-done.8
  41.4 0.6 copy-done.13
  42.0 0.6 copy-done.18
  42.6 2.9 %all-to-all-start.1 = ((f32[32,10,1,128]{3,2,1,0:T(1,128)}), f32[32,10,1,128]{3,2,1,0:T(1,128)S(1)}, u32[]{:S(2)}, u32[]{:S(2)}) async-start(f32[32,10,1,128]{3,2,1,0:T(1,128)} %copy-done.8), calls=%async_computation.1 | async-start | bytes 327680 | tf_op jit(solution)/shard_map/all_to_all | solution.py:527
  45.5 0.3 collective-permute-start.10
  45.9 2.5 %collective-permute-start.11 = (f32[2,48,128]{2,1,0:T(8,128)}, f32[2,48,128]{2,1,0:T(8,128)}, u32[]{:S(2)}, u32[]{:S(2)}) collective-permute-start(f32[2,48,128]{2,1,0:T(8,128)} %copy-done.18), channel_id=1, source_target_pairs={{0,16},{1,17},{2,18},{3,19},{4,20},{5,21},{6,22},{7,23},{8,24},{9,... | collective-permute-start | bytes 147464 | tf_op jit(solution)/shard_map/ppermute | solution.py:523
  48.4 3.0 %collective-permute-start.12 = (f32[2,48,128]{2,1,0:T(8,128)}, f32[2,48,128]{2,1,0:T(8,128)}, u32[]{:S(2)}, u32[]{:S(2)}) collective-permute-start(f32[2,48,128]{2,1,0:T(8,128)} %copy-done.18), channel_id=1, source_target_pairs={{0,31},{1,2},{2,1},{3,4},{4,3},{5,6},{6,5},{7,8},{8,7},{9,10},{10,... | collective-permute-start | bytes 147464 | tf_op jit(solution)/shard_map/ppermute | solution.py:523
  51.4 3.3 %all-to-all-done.1.red = f32[32,10,1,128]{3,2,1,0:T(1,128)S(1)} async-done(((f32[32,10,1,128]{3,2,1,0:T(1,128)}), f32[32,10,1,128]{3,2,1,0:T(1,128)S(1)}, u32[]{:S(2)}, u32[]{:S(2)}) %all-to-all-start.1) | async-done | bytes 163872 | tf_op jit(solution)/shard_map/all_to_all | solution.py:527
  54.7 0.8 %copy-done.14 = f32[16,1024]{1,0:T(8,128)S(1)} copy-done((f32[16,1024]{1,0:T(8,128)S(1)}, f32[16,1024]{1,0:T(8,128)}, u32[]{:S(2)}) %copy-start.14) | copy-done | bytes 65560
  55.5 0.7 shard_map.85
  56.2 0.0 collective-permute-done.10.h_a
  56.3 0.0 collective-permute-done.11.h_f
  56.3 0.1 collective-permute-done.12.h_b
  56.4 1.7 %copy-done.3 = bf16[8,640,256]{2,1,0:T(8,128)(2,1)S(1)} copy-done((bf16[8,640,256]{2,1,0:T(8,128)(2,1)S(1)}, bf16[8,640,256]{2,1,0:T(8,128)(2,1)}, u32[]{:S(2)}) %copy-start.3) | copy-done | bytes 2621464
  58.1 0.9 %copy-done.10 = f32[48,768]{1,0:T(8,128)S(1)} copy-done((f32[48,768]{1,0:T(8,128)S(1)}, f32[48,768]{1,0:T(8,128)}, u32[]{:S(2)}) %copy-start.10) | copy-done | bytes 147480
  59.0 0.7 copy-done.17
  59.7 1.3 %shard_map.86 = (f32[2,16,128]{2,1,0:T(8,128)S(1)}, bf16[14,32,128]{2,1,0:T(8,128)(2,1)S(1)}) custom-call(s32[8,5]{1,0:T(8,128)S(1)} %get-tuple-element.45.cols, s32[2]{0:T(128)S(1)} %copy-done.17, f32[16,1024]{1,0:T(8,128)S(1)} %get-tuple-element.71.c_local, f32[32,128]{1,0:T(8,128)S(1)} %get-tuple-element.72.coefs, ...), custom_call_target="tpu_custom_call" | custom-call | tf_op jit(solution)/shard_map/pallas_call | solution.py:586
  61.0 0.3 collective-permute-start.13
  61.3 1.4 %collective-permute-start.14 = (f32[2,16,128]{2,1,0:T(8,128)S(1)}, f32[2,16,128]{2,1,0:T(8,128)S(1)}, u32[]{:S(2)}, u32[]{:S(2)}) collective-permute-start(f32[2,16,128]{2,1,0:T(8,128)S(1)} %get-tuple-element.77), channel_id=1, source_target_pairs={{0,16},{1,17},{2,18},{3,19},{4,20},{5,21},{6,22},{7,23},{8,24},{9,... | collective-permute-start | bytes 49160 | tf_op jit(solution)/shard_map/ppermute | solution.py:523
  62.6 2.4 %collective-permute-start.15 = (f32[2,16,128]{2,1,0:T(8,128)S(1)}, f32[2,16,128]{2,1,0:T(8,128)S(1)}, u32[]{:S(2)}, u32[]{:S(2)}) collective-permute-start(f32[2,16,128]{2,1,0:T(8,128)S(1)} %get-tuple-element.77), channel_id=1, source_target_pairs={{0,31},{1,2},{2,1},{3,4},{4,3},{5,6},{6,5},{7,8},{8,7},{9,10},{10,... | collective-permute-start | bytes 49160 | tf_op jit(solution)/shard_map/ppermute | solution.py:523
  65.0 0.9 %shard_map.87 = (f32[16,1024]{1,0:T(8,128)S(1)}, f32[16,1024]{1,0:T(8,128)S(1)}) custom-call(s32[8,5]{1,0:T(8,128)S(1)} %get-tuple-element.45.cols, bf16[14,32,128]{2,1,0:T(8,128)(2,1)S(1)} %get-tuple-element.75.xs, f32[16,1024]{1,0:T(8,128)S(1)} %get-tuple-element.71.c_local, f32[32,128]{1,0:T(8,128)S(1)} %get-tuple-element.72.coefs, ...), custom_call_target="tpu_custom_call" | custom-call | tf_op jit(solution)/shard_map/pallas_call | solution.py:590
  66.0 0.4 shard_map.88
  66.4 0.0 collective-permute-done.13.h_a
  66.4 0.0 collective-permute-done.14.h_f
  66.4 3.0 %collective-permute-done.15.h_b = f32[2,16,128]{2,1,0:T(8,128)S(1)} collective-permute-done((f32[2,16,128]{2,1,0:T(8,128)S(1)}, f32[2,16,128]{2,1,0:T(8,128)S(1)}, u32[]{:S(2)}, u32[]{:S(2)}) %collective-permute-start.15) | collective-permute-done | bytes 16416 | tf_op jit(solution)/shard_map/ppermute | solution.py:523
  69.4 1.3 %shard_map.89 = (f32[16,1024]{1,0:T(8,128)S(1)}, f32[32,8,128]{2,1,0:T(8,128)S(1)}) custom-call(s32[8,5]{1,0:T(8,128)S(1)} %get-tuple-element.45.cols, f32[16,1024]{1,0:T(8,128)S(1)} %get-tuple-element.76.p, f32[2,16,128]{2,1,0:T(8,128)S(1)} %collective-permute-done.13.h_a, f32[2,16,128]{2,1,0:T(8,128)S(1)} %collective-permute-done.14.h_f, ...), custom_call_target="tpu_custom_call" | custom-call | tf_op jit(solution)/shard_map/pallas_call | solution.py:592
  70.7 10.8 %all_to_all.15.red = f32[32,8,128]{2,1,0:T(8,128)S(1)} all-to-all(f32[32,8,128]{2,1,0:T(8,128)S(1)} %get-tuple-element.82), channel_id=1, replica_groups=mesh['parts'=32] {'parts'}, dimensions={0} | all-to-all | bytes 262144 | tf_op jit(solution)/shard_map/all_to_all | solution.py:527
  81.5 1.2 %shard_map.90 = f32[16,1024]{1,0:T(8,128)} custom-call(f32[32,8,128]{2,1,0:T(8,128)S(1)} %all_to_all.15.red, f32[16,1024]{1,0:T(8,128)S(1)} %get-tuple-element.83.p, f32[144,128]{1,0:T(8,128)S(1)} %get-tuple-element.58.small, f32[64,128]{1,0:T(8,128)S(1)} %get-tuple-element.70.small_b, f32[32,128]{1,0:T(8,128)S(1)} %get-tuple-element.84.tests_in, ...), custom_call_target="tpu_custom_call" | custom-call | tf_op jit(solution)/shard_map/pallas_call | solution.py:594
  (25 shorter events, 0.0 us)
Async XLA Ops:
  1.6 11.2 %copy-start.5 = (f32[16,1024]{1,0:T(8,128)S(1)}, f32[16,1024]{1,0:T(8,128)}, u32[]{:S(2)}) copy-start(f32[16,1024]{1,0:T(8,128)} %basis.3) | copy-start | bytes 196612
  1.6 11.2 %copy-start.15 = (s32[2]{0:T(128)S(1)}, s32[2]{0:T(128)}, u32[]{:S(2)}) copy-start(s32[2]{0:T(128)} %iface.7) | copy-start | bytes 28
  1.6 11.2 %collective-permute-start = (f32[2,16,128]{2,1,0:T(8,128)S(1)}, f32[2,16,128]{2,1,0:T(8,128)S(1)}, u32[]{:S(2)}, u32[]{:S(2)}) collective-permute-start(f32[2,16,128]{2,1,0:T(8,128)S(1)} %shard_map.78), channel_id=1, source_target_pairs={{0,1},{1,0},{2,3},{3,2},{4,5},{5,4},{6,7},{7,6},{8,9},{9,8},{10,11... | collective-permute-start | bytes 49160 | tf_op jit(solution)/shard_map/ppermute | solution.py:523
  2.2 10.6 %collective-permute-start.1 = (f32[2,16,128]{2,1,0:T(8,128)S(1)}, f32[2,16,128]{2,1,0:T(8,128)S(1)}, u32[]{:S(2)}, u32[]{:S(2)}) collective-permute-start(f32[2,16,128]{2,1,0:T(8,128)S(1)} %shard_map.78), channel_id=1, source_target_pairs={{0,16},{1,17},{2,18},{3,19},{4,20},{5,21},{6,22},{7,23},{8,24},{9,... | collective-permute-start | bytes 49160 | tf_op jit(solution)/shard_map/ppermute | solution.py:523
  5.8 7.0 %collective-permute-start.2 = (f32[2,16,128]{2,1,0:T(8,128)S(1)}, f32[2,16,128]{2,1,0:T(8,128)S(1)}, u32[]{:S(2)}, u32[]{:S(2)}) collective-permute-start(f32[2,16,128]{2,1,0:T(8,128)S(1)} %shard_map.78), channel_id=1, source_target_pairs={{0,31},{1,2},{2,1},{3,4},{4,3},{5,6},{6,5},{7,8},{8,7},{9,10},{10,... | collective-permute-start | bytes 49160 | tf_op jit(solution)/shard_map/ppermute | solution.py:523
  12.8 2.3 %copy-start = (bf16[8,640,256]{2,1,0:T(8,128)(2,1)}, bf16[8,640,256]{2,1,0:T(8,128)(2,1)S(1)}, u32[]{:S(2)}) copy-start(bf16[8,640,256]{2,1,0:T(8,128)(2,1)S(1)} %get-tuple-element.47.w_low) | copy-start | bytes 7864324
  15.1 15.5 %copy-start.6 = (f32[16,1024]{1,0:T(8,128)}, f32[16,1024]{1,0:T(8,128)S(1)}, u32[]{:S(2)}) copy-start(f32[16,1024]{1,0:T(8,128)S(1)} %get-tuple-element.52.mb) | copy-start | bytes 196612
  15.1 11.9 %all-to-all-start = ((f32[32,9,1,128]{3,2,1,0:T(1,128)}), f32[32,9,1,128]{3,2,1,0:T(1,128)S(1)}, u32[]{:S(2)}, u32[]{:S(2)}) async-start(f32[32,9,1,128]{3,2,1,0:T(1,128)} %get-tuple-element.50), calls=%async_computation | async-start | bytes 294912 | tf_op jit(solution)/shard_map/all_to_all | solution.py:527
  18.2 10.1 %collective-permute-start.3 = (f32[2,32,128]{2,1,0:T(8,128)S(1)}, f32[2,32,128]{2,1,0:T(8,128)S(1)}, u32[]{:S(2)}, u32[]{:S(2)}) collective-permute-start(f32[2,32,128]{2,1,0:T(8,128)S(1)} %get-tuple-element.49), channel_id=1, source_target_pairs={{0,1},{1,0},{2,3},{3,2},{4,5},{5,4},{6,7},{7,6},{8,9},{9,8},{10,11... | collective-permute-start | bytes 98312 | tf_op jit(solution)/shard_map/ppermute | solution.py:523
  18.5 9.8 %collective-permute-start.4 = (f32[2,32,128]{2,1,0:T(8,128)S(1)}, f32[2,32,128]{2,1,0:T(8,128)S(1)}, u32[]{:S(2)}, u32[]{:S(2)}) collective-permute-start(f32[2,32,128]{2,1,0:T(8,128)S(1)} %get-tuple-element.49), channel_id=1, source_target_pairs={{0,16},{1,17},{2,18},{3,19},{4,20},{5,21},{6,22},{7,23},{8,24},{9,... | collective-permute-start | bytes 98312 | tf_op jit(solution)/shard_map/ppermute | solution.py:523
  21.0 7.3 %collective-permute-start.5 = (f32[2,32,128]{2,1,0:T(8,128)S(1)}, f32[2,32,128]{2,1,0:T(8,128)S(1)}, u32[]{:S(2)}, u32[]{:S(2)}) collective-permute-start(f32[2,32,128]{2,1,0:T(8,128)S(1)} %get-tuple-element.49), channel_id=1, source_target_pairs={{0,31},{1,2},{2,1},{3,4},{4,3},{5,6},{6,5},{7,8},{8,7},{9,10},{10,... | collective-permute-start | bytes 98312 | tf_op jit(solution)/shard_map/ppermute | solution.py:523
  28.3 1.7 %copy-start.1 = (bf16[8,640,256]{2,1,0:T(8,128)(2,1)S(1)}, bf16[8,640,256]{2,1,0:T(8,128)(2,1)}, u32[]{:S(2)}) copy-start(bf16[8,640,256]{2,1,0:T(8,128)(2,1)} %copy-done) | copy-start | bytes 7864324
  30.6 0.6 copy-start.9
  31.2 6.7 %collective-permute-start.6 = (f32[2,16,128]{2,1,0:T(8,128)S(1)}, f32[2,16,128]{2,1,0:T(8,128)S(1)}, u32[]{:S(2)}, u32[]{:S(2)}) collective-permute-start(f32[2,16,128]{2,1,0:T(8,128)S(1)} %get-tuple-element.61), channel_id=1, source_target_pairs={{0,1},{1,0},{2,3},{3,2},{4,5},{5,4},{6,7},{7,6},{8,9},{9,8},{10,11... | collective-permute-start | bytes 49160 | tf_op jit(solution)/shard_map/ppermute | solution.py:523
  31.5 6.4 %collective-permute-start.7 = (f32[2,16,128]{2,1,0:T(8,128)S(1)}, f32[2,16,128]{2,1,0:T(8,128)S(1)}, u32[]{:S(2)}, u32[]{:S(2)}) collective-permute-start(f32[2,16,128]{2,1,0:T(8,128)S(1)} %get-tuple-element.61), channel_id=1, source_target_pairs={{0,16},{1,17},{2,18},{3,19},{4,20},{5,21},{6,22},{7,23},{8,24},{9,... | collective-permute-start | bytes 49160 | tf_op jit(solution)/shard_map/ppermute | solution.py:523
  32.3 6.8 %collective-permute-start.8 = (f32[2,16,128]{2,1,0:T(8,128)S(1)}, f32[2,16,128]{2,1,0:T(8,128)S(1)}, u32[]{:S(2)}, u32[]{:S(2)}) collective-permute-start(f32[2,16,128]{2,1,0:T(8,128)S(1)} %get-tuple-element.61), channel_id=1, source_target_pairs={{0,31},{1,2},{2,1},{3,4},{4,3},{5,6},{6,5},{7,8},{8,7},{9,10},{10,... | collective-permute-start | bytes 49160 | tf_op jit(solution)/shard_map/ppermute | solution.py:523
  34.9 1.1 %copy-start.7 = (f32[16,1024]{1,0:T(8,128)S(1)}, f32[16,1024]{1,0:T(8,128)}, u32[]{:S(2)}) copy-start(f32[16,1024]{1,0:T(8,128)} %copy-done.6) | copy-start | bytes 196612
  34.9 4.2 %copy-start.2 = (bf16[8,640,256]{2,1,0:T(8,128)(2,1)S(1)}, bf16[8,640,256]{2,1,0:T(8,128)(2,1)}, u32[]{:S(2)}) copy-start(bf16[8,640,256]{2,1,0:T(8,128)(2,1)} %copy-done) | copy-start | bytes 7864324
  34.9 4.2 %copy-start.16 = (s32[2]{0:T(128)S(1)}, s32[2]{0:T(128)}, u32[]{:S(2)}) copy-start(s32[2]{0:T(128)} %iface.7) | copy-start | bytes 28
  36.7 4.0 %copy-start.11 = (f32[16,1024]{1,0:T(8,128)}, f32[16,1024]{1,0:T(8,128)S(1)}, u32[]{:S(2)}) copy-start(f32[16,1024]{1,0:T(8,128)S(1)} %get-tuple-element.79.v) | copy-start | bytes 196612
  36.7 1.2 %collective-permute-start.9 = (f32[16,128]{1,0:T(8,128)S(1)}, f32[16,128]{1,0:T(8,128)S(1)}, u32[]{:S(2)}, u32[]{:S(2)}) collective-permute-start(f32[16,128]{1,0:T(8,128)S(1)} %get-tuple-element.65.part), channel_id=1, source_target_pairs={{0,1},{1,0},{2,3},{3,2},{4,5},{5,4},{6,7},{7,6},{8,9},{9,8},{10,11... | collective-permute-start | bytes 24584 | tf_op jit(solution)/shard_map/ppermute | solution.py:576
  40.7 0.7 copy-start.8
  41.3 0.6 copy-start.13
  42.0 0.6 copy-start.18
  42.6 12.1 %all-to-all-start.1 = ((f32[32,10,1,128]{3,2,1,0:T(1,128)}), f32[32,10,1,128]{3,2,1,0:T(1,128)S(1)}, u32[]{:S(2)}, u32[]{:S(2)}) async-start(f32[32,10,1,128]{3,2,1,0:T(1,128)} %copy-done.8), calls=%async_computation.1 | async-start | bytes 327680 | tf_op jit(solution)/shard_map/all_to_all | solution.py:527
  45.5 10.7 %collective-permute-start.10 = (f32[2,48,128]{2,1,0:T(8,128)}, f32[2,48,128]{2,1,0:T(8,128)}, u32[]{:S(2)}, u32[]{:S(2)}) collective-permute-start(f32[2,48,128]{2,1,0:T(8,128)} %copy-done.18), channel_id=1, source_target_pairs={{0,1},{1,0},{2,3},{3,2},{4,5},{5,4},{6,7},{7,6},{8,9},{9,8},{10,11... | collective-permute-start | bytes 147464 | tf_op jit(solution)/shard_map/ppermute | solution.py:523
  45.9 10.4 %collective-permute-start.11 = (f32[2,48,128]{2,1,0:T(8,128)}, f32[2,48,128]{2,1,0:T(8,128)}, u32[]{:S(2)}, u32[]{:S(2)}) collective-permute-start(f32[2,48,128]{2,1,0:T(8,128)} %copy-done.18), channel_id=1, source_target_pairs={{0,16},{1,17},{2,18},{3,19},{4,20},{5,21},{6,22},{7,23},{8,24},{9,... | collective-permute-start | bytes 147464 | tf_op jit(solution)/shard_map/ppermute | solution.py:523
  48.4 8.0 %collective-permute-start.12 = (f32[2,48,128]{2,1,0:T(8,128)}, f32[2,48,128]{2,1,0:T(8,128)}, u32[]{:S(2)}, u32[]{:S(2)}) collective-permute-start(f32[2,48,128]{2,1,0:T(8,128)} %copy-done.18), channel_id=1, source_target_pairs={{0,31},{1,2},{2,1},{3,4},{4,3},{5,6},{6,5},{7,8},{8,7},{9,10},{10,... | collective-permute-start | bytes 147464 | tf_op jit(solution)/shard_map/ppermute | solution.py:523
  54.7 0.8 %copy-start.14 = (f32[16,1024]{1,0:T(8,128)S(1)}, f32[16,1024]{1,0:T(8,128)}, u32[]{:S(2)}) copy-start(f32[16,1024]{1,0:T(8,128)} %copy-done.13) | copy-start | bytes 196612
  56.4 1.7 %copy-start.3 = (bf16[8,640,256]{2,1,0:T(8,128)(2,1)S(1)}, bf16[8,640,256]{2,1,0:T(8,128)(2,1)}, u32[]{:S(2)}) copy-start(bf16[8,640,256]{2,1,0:T(8,128)(2,1)} %copy-done) | copy-start | bytes 7864324
  58.1 0.9 %copy-start.10 = (f32[48,768]{1,0:T(8,128)S(1)}, f32[48,768]{1,0:T(8,128)}, u32[]{:S(2)}) copy-start(f32[48,768]{1,0:T(8,128)} %copy-done.9) | copy-start | bytes 442372
  59.0 0.7 copy-start.17
  61.0 5.4 %collective-permute-start.13 = (f32[2,16,128]{2,1,0:T(8,128)S(1)}, f32[2,16,128]{2,1,0:T(8,128)S(1)}, u32[]{:S(2)}, u32[]{:S(2)}) collective-permute-start(f32[2,16,128]{2,1,0:T(8,128)S(1)} %get-tuple-element.77), channel_id=1, source_target_pairs={{0,1},{1,0},{2,3},{3,2},{4,5},{5,4},{6,7},{7,6},{8,9},{9,8},{10,11... | collective-permute-start | bytes 49160 | tf_op jit(solution)/shard_map/ppermute | solution.py:523
  61.3 5.2 %collective-permute-start.14 = (f32[2,16,128]{2,1,0:T(8,128)S(1)}, f32[2,16,128]{2,1,0:T(8,128)S(1)}, u32[]{:S(2)}, u32[]{:S(2)}) collective-permute-start(f32[2,16,128]{2,1,0:T(8,128)S(1)} %get-tuple-element.77), channel_id=1, source_target_pairs={{0,16},{1,17},{2,18},{3,19},{4,20},{5,21},{6,22},{7,23},{8,24},{9,... | collective-permute-start | bytes 49160 | tf_op jit(solution)/shard_map/ppermute | solution.py:523
  62.6 6.8 %collective-permute-start.15 = (f32[2,16,128]{2,1,0:T(8,128)S(1)}, f32[2,16,128]{2,1,0:T(8,128)S(1)}, u32[]{:S(2)}, u32[]{:S(2)}) collective-permute-start(f32[2,16,128]{2,1,0:T(8,128)S(1)} %get-tuple-element.77), channel_id=1, source_target_pairs={{0,31},{1,2},{2,1},{3,4},{4,3},{5,6},{6,5},{7,8},{8,7},{9,10},{10,... | collective-permute-start | bytes 49160 | tf_op jit(solution)/shard_map/ppermute | solution.py:523
  65.0 1.0 %copy-start.12 = (f32[16,1024]{1,0:T(8,128)S(1)}, f32[16,1024]{1,0:T(8,128)}, u32[]{:S(2)}) copy-start(f32[16,1024]{1,0:T(8,128)} %copy-done.11) | copy-start | bytes 196612
  65.0 4.4 %copy-start.4 = (bf16[8,640,256]{2,1,0:T(8,128)(2,1)S(1)}, bf16[8,640,256]{2,1,0:T(8,128)(2,1)}, u32[]{:S(2)}) copy-start(bf16[8,640,256]{2,1,0:T(8,128)(2,1)} %copy-done) | copy-start | bytes 7864324

commit v7 on v6

--- a/solution.py
+++ b/solution.py
@@ -203,7 +203,7 @@
             for which, source in enumerate((k, m)):
                 copies[i][which].wait()
                 for b in range(blocks):
-                    high, low = split(source[i, b].T)
+                    high, low = (part.T for part in split(source[i, b]))
                     w_high[i, b * width : (b + 1) * width, which * width : (which + 1) * width] = high
                     w_low[i, b * width : (b + 1) * width, which * width : (which + 1) * width] = low
             diag = jnp.sum(jnp.where(row == lane, k[i, 0], 0.0), axis=0, keepdims=True)
@@ -276,8 +276,9 @@
         u[:n] = kb[...] * d
         u[n:] = mb[...] * d
         send_tiles(iface, outgoing, 0, u)
-        right = rows([basis[...], u[...], kb[...], mb[...], jnp.zeros((MAT - 5 * n, basis.shape[1]), F32)])
+        right = rows([basis[...], u[...], kb[...], mb[...]])
         both = nt3(*split(rows([basis[...], mb[...]])), right) * scale
+        both = lanes([both, jnp.zeros((2 * n, MAT - 5 * n), F32)])
         lane, row = lane_row((n, MAT))
         chosen = jnp.where(lane < 3 * n, both[:n], both[n:])
         mass = pltpu.roll(chosen, MAT - 4 * n, 1)
@@ -288,7 +289,7 @@
             grams[device, : n // 2, 0, :] = packed
             grams[device, n // 2] = mass_diag
 
-    def k_b0(red, kb, mb, u, ko_out, mo_out, c0_out, words, small, theta_out):
+    def k_b0(red, u, c0_out, words, small, theta_out):
         packed, mass_diag = red[0, : n // 2, 0, :], red[0, n // 2]
         for device in range(1, red.shape[0]):
             packed = packed + red[device, : n // 2, 0, :]
@@ -311,17 +312,15 @@
         for k, value in ((0, f1), (3, g1), (4, g2)):
             words[k * n : (k + 1) * n] = value
         c0_out[...] = -relax * (g1 - theta * g2)
-        ko_out[...] = mm3(lv, kb[...])
-        mo_out[...] = mm3(lv, mb[...])
         e1 = nt(mm(lv, g_u1b[:, :n]), lv)
         e2 = nt(mm(lv, g_u2b[:, :n]), lv)
         right = -relax * (e1 - theta * e2)
-        for k, value in enumerate((cross, g_mm[:, :n], e1, e2, g_u2b[:, :n], theta, lv, lc, right)):
+        for k, value in enumerate((cross, g_mm[:, :n], e1, e2, g_u2b[:, :n], theta, lv, lc, mm(right, lv))):
             put_small(small, k, value)
         theta_out[...] = jnp.sum(jnp.where(lane == row, theta, 0.0), axis=0, keepdims=True)[:, :n]
 
     def k_b1(
-        cols, iface, h_a, h_f, h_b, w_high, w_low, inv_d, ko, mo, c0, words_in, small, words_halo, outgoing, xs
+        cols, iface, h_a, h_f, h_b, w_high, w_low, inv_d, kb, mb, c0, words_in, small, words_halo, outgoing, xs
     ):
         lv, lc, right = (get_small(small, k) for k in (6, 7, 8))
         theta = small[5 * n : 6 * n, :1]
@@ -337,17 +336,17 @@
             tile = iface[slot]
             at = lanes_of(tile, xs.shape[2])
             k_tile, m_tile = apply_iface(xs, cols, w_high, w_low, tile, n)
-            image = k_tile - theta * m_tile - mm3(coef, rows([ko[:, at], mo[:, at]]))
+            image = k_tile - theta * m_tile - mm3(coef, rows([kb[:, at], mb[:, at]]))
             outgoing[slot] = 2.0 * c0[:, at] - relax * inv_d[:, at] * image
 
     def k_b2(
-        cols, xs, w_high, w_low, inv_d, ko, mo, c0, words_in, small, p_out, image_out, words, kf_out, res
+        cols, xs, w_high, w_low, inv_d, kb, mb, c0, words_in, small, p_out, image_out, words, kf_out, res
     ):
         right = get_small(small, 8)
         theta = small[5 * n : 6 * n, :1]
         apply_pair(xs, cols, w_high, w_low, res.at[0], res.at[1])
         d = inv_d[...]
-        image = res[0, :n] - theta * res[1, :n] - mm3(lanes([right, -theta * right]), rows([ko[...], mo[...]]))
+        image = res[0, :n] - theta * res[1, :n] - mm3(lanes([right, -theta * right]), rows([kb[...], mb[...]]))
         image_out[...] = image
         kf_out[:n] = res[0, n:]
         kf_out[n:] = res[1, n:]
@@ -447,10 +446,10 @@
         for k, value in enumerate(onto):
             put_small(onto_v, k, value)
         coefs[:n] = lanes([coef, jnp.zeros((n, MAT - 5 * n), F32)])
-        put_small(coefs, 1, g_fresh + mm(coef, rows(list(onto))))
+        put_small(coefs, 1, mm(g_fresh, get_small(small, 6)) + mm(coef, mm(rows(list(onto)), get_small(small, 6))))
 
     def k_d1(
-        cols, iface, c_local, coefs, h_a, h_f, h_b, ko, mo, c0, words_halo, small,
+        cols, iface, c_local, coefs, h_a, h_f, h_b, kb, mb, c0, words_halo, small,
         w_high, w_low, inv_d, outgoing, xs,
     ):
         coef, right = coefs[:n, : 5 * n], get_small(coefs, 1)
@@ -464,14 +463,14 @@
             tile = iface[slot]
             at = lanes_of(tile, xs.shape[2])
             k_tile, m_tile = apply_iface(xs, cols, w_high, w_low, tile, n)
-            image = k_tile - theta * m_tile - mm3(onto, rows([ko[:, at], mo[:, at]]))
+            image = k_tile - theta * m_tile - mm3(onto, rows([kb[:, at], mb[:, at]]))
             outgoing[slot] = c_local[:, at] + c0[:, at] - relax * inv_d[:, at] * image
 
-    def k_d2(cols, xs, c_local, coefs, ko, mo, c0, small, w_high, w_low, inv_d, p_out, image_out, res):
+    def k_d2(cols, xs, c_local, coefs, kb, mb, c0, small, w_high, w_low, inv_d, p_out, image_out, res):
         right = get_small(coefs, 1)
         theta = small[5 * n : 6 * n, :1]
         apply_pair(xs, cols, w_high, w_low, res.at[0], res.at[1])
-        image = res[0] - theta * res[1] - mm3(lanes([right, -theta * right]), rows([ko[...], mo[...]]))
+        image = res[0] - theta * res[1] - mm3(lanes([right, -theta * right]), rows([kb[...], mb[...]]))
         image_out[...] = image
         p_out[...] = c_local[...] + c0[...] - relax * inv_d[...] * image
 
@@ -558,17 +557,15 @@
     )(cols, iface, basis, *h0, *w)
     red = reduced(grams)
     h1 = halo(outgoing)
-    ko, mo, c0, words, small, theta = call(
-        k_b0, [vec] * 3 + [vecs(5), mats(9), ((1, n), F32)], [VM] * 4
-    )(red, kb, mb, u)
+    c0, words, small, theta = call(k_b0, [vec, vecs(5), mats(9), ((1, n), F32)], [VM] * 2)(red, u)
     sources_of = lambda m: ((sources, 2 * m, width), BF16)
     words_halo, outgoing, source = call(
         k_b1, [((3 * n, 3 * count * width), F32), out(n), sources_of(2 * n)], [VM, VM] + [VM] * 11
-    )(cols, iface, *h1, *w, ko, mo, c0, words, small)
+    )(cols, iface, *h1, *w, kb, mb, c0, words, small)
     h2 = halo(outgoing)
     p1, image0, words, kf = call(
         k_b2, [vec, vec, vecs(5), vecs(2)], [VM] + [VM] * 9, [pltpu.VMEM((2, 2 * n, local), F32)]
-    )(cols, source, *w, ko, mo, c0, words, small)
+    )(cols, source, *w, kb, mb, c0, words, small)
     v, tests_high, tests_low, small_b, part = call(
         k_c0, [vec] + [((2 * n, local), BF16)] * 2 + [mats(4), mats(1)], [VM] * 7
     )(small, basis, mb, image0, kf, p1, words)
@@ -584,10 +581,10 @@
         red, p2, words, small, small_b
     )
     outgoing, source = call(k_d1, [out(n), sources_of(n)], [VM, VM] + [VM] * 13)(
-        cols, iface, c2, coefs, *h3, ko, mo, c0, words_halo, small, *w
+        cols, iface, c2, coefs, *h3, kb, mb, c0, words_halo, small, *w
     )
     h4 = halo(outgoing)
-    p3, image2 = call(k_d2, [vec, vec], [VM] + [VM] * 10, [res])(cols, source, c2, coefs, ko, mo, c0, small, *w)
+    p3, image2 = call(k_d2, [vec, vec], [VM] + [VM] * 10, [res])(cols, source, c2, coefs, kb, mb, c0, small, *w)
     part, *last = call(k_e0, [mats(1)] + [((6 * n, local), BF16)] * 2, [VM] * 7)(image2, p3, *tests, v, words, onto_v)
     p4, grams = call(k_e1, [vec, grams8], [VM] + [VM] * 12, [xs(n), res])(cols, p3, *h4, c0, small, part, *tests, *w)
     red = reduced(grams)

time: 83.2 us -> 83.2 us (level)
    unnamed x38 -> x34, local copies, waits for them, and re-layouts: 8.47 us -> 8.45 us
  transfers between devices with their start and end apart: 18 -> 18, of which waited for: 6 -> 6; matrix products, arithmetic and copies ran while one was open for 0% -> 0% of each run, Pallas kernels for 11% -> 10%
where the time goes in v7:
time: 83.2 us; the launch traced here: 82.7 us
  starting transfers between devices  33 us (40%)
  Pallas kernels  17.8 us (21%)
  waiting for transfers between devices  11.6 us (14%)
  blocking collectives  11 us (13%)
  local copies, waits for them, and re-layouts  8.45 us (10%)
  between operations  0.95 us (1%)
    ppermute x15, starting transfers between devices, halo(): got.append(lax.ppermute(outgoing, 'parts', pairs))  26.6 us
    all_to_all x1, blocking collectives, reduced(): return lax.all_to_all(blocks_out, 'parts', 0, 0, tiled=True)  11 us
    unnamed x34, local copies, waits for them, and re-layouts  8.45 us
    all_to_all x2, starting transfers between devices, reduced(): return lax.all_to_all(blocks_out, 'parts', 0, 0, tiled=True)  6.29 us
    all_to_all x2, waiting for transfers between devices, reduced(): return lax.all_to_all(blocks_out, 'parts', 0, 0, tiled=True)  6.24 us
    ppermute x15, waiting for transfers between devices, halo(): got.append(lax.ppermute(outgoing, 'parts', pairs))  4.2 us
    pallas_call x1, Pallas kernels, shards(): call(make_prep(count), [((tiles, blocks * width, 2 * width), BF16)] * 2 +...  3.47 us
    pallas_call x1, Pallas kernels, shards(): call(k_a, [vec, vec, vecs(2), out(2 * n), packed], [VM, VM] + [VM] * 7, [...  2.16 us
  transfers between devices with their start and end apart: 18, of which 6 were waited for; matrix products, arithmetic and copies ran while one was open for 0% of the time, Pallas kernels for 10%

profile of v7, /device:TPU:0, one launch (start us, length us, event | category | flops | bytes accessed | tf_op | source)
XLA Modules:
  0.0 82.7 jit_solution(2053175630086223898)
XLA Ops:
  0.6 1.0 %shard_map.78 = f32[2,16,128]{2,1,0:T(8,128)S(1)} custom-call(s32[2]{0:T(128)} %iface.7, f32[16,1024]{1,0:T(8,128)} %basis.3), custom_call_target="tpu_custom_call" | custom-call | tf_op jit(solution)/shard_map/pallas_call | solution.py:538
  1.6 0.0 copy-start.5
  1.6 0.0 copy-start.13
  1.6 0.6 collective-permute-start
  2.2 3.7 %collective-permute-start.1 = (f32[2,16,128]{2,1,0:T(8,128)S(1)}, f32[2,16,128]{2,1,0:T(8,128)S(1)}, u32[]{:S(2)}, u32[]{:S(2)}) collective-permute-start(f32[2,16,128]{2,1,0:T(8,128)S(1)} %shard_map.78), channel_id=1, source_target_pairs={{0,16},{1,17},{2,18},{3,19},{4,20},{5,21},{6,22},{7,23},{8,24},{9,... | collective-permute-start | bytes 49160 | tf_op jit(solution)/shard_map/ppermute | solution.py:522
  5.8 3.0 %collective-permute-start.2 = (f32[2,16,128]{2,1,0:T(8,128)S(1)}, f32[2,16,128]{2,1,0:T(8,128)S(1)}, u32[]{:S(2)}, u32[]{:S(2)}) collective-permute-start(f32[2,16,128]{2,1,0:T(8,128)S(1)} %shard_map.78), channel_id=1, source_target_pairs={{0,31},{1,2},{2,1},{3,4},{4,3},{5,6},{6,5},{7,8},{8,7},{9,10},{10,... | collective-permute-start | bytes 49160 | tf_op jit(solution)/shard_map/ppermute | solution.py:522
  8.8 3.5 %shard_map.77 = (bf16[8,640,256]{2,1,0:T(8,128)(2,1)S(1)}, bf16[8,640,256]{2,1,0:T(8,128)(2,1)S(1)}, f32[1,1024]{1,0:T(1,128)S(1)}, s32[8,5]{1,0:T(8,128)S(1)}) custom-call(s32[8,5]{1,0:T(8,128)} %part_hbm.1, s32[8,5]{1,0:T(8,128)} %slot_hbm.1, f32[8,5,128,128]{3,2,1,0:T(8,128)} %k_hbm.1, f32[8,5,128,128]{3,2,1,0:T(8,128)} %m_hbm.1), custom_call_target="tpu_custom_call" | custom-call | tf_op jit(solution)/shard_map/pallas_call | solution.py:545
  12.3 0.0 collective-permute-done.h_a
  12.3 0.0 collective-permute-done.1.h_f
  12.4 0.3 collective-permute-done.2.h_b
  12.6 0.0 copy-done.5
  12.6 2.2 %shard_map.79 = (f32[16,1024]{1,0:T(8,128)S(1)}, f32[16,1024]{1,0:T(8,128)S(1)}, f32[32,1024]{1,0:T(8,128)S(1)}, f32[2,32,128]{2,1,0:T(8,128)S(1)}, f32[32,9,1,128]{3,2,1,0:T(1,128)}) custom-call(s32[8,5]{1,0:T(8,128)S(1)} %get-tuple-element.43.cols, s32[2]{0:T(128)S(1)} %copy-done.13, f32[16,1024]{1,0:T(8,128)S(1)} %copy-done.5, ...), custom_call_target="tpu_custom_call" | custom-call | tf_op jit(solution)/shard_map/pallas_call | solution.py:555
  14.8 3.4 %all-to-all-start = ((f32[32,9,1,128]{3,2,1,0:T(1,128)}), f32[32,9,1,128]{3,2,1,0:T(1,128)S(1)}, u32[]{:S(2)}, u32[]{:S(2)}) async-start(f32[32,9,1,128]{3,2,1,0:T(1,128)} %get-tuple-element.50), calls=%async_computation | async-start | bytes 294912 | tf_op jit(solution)/shard_map/all_to_all | solution.py:526
  18.1 0.3 collective-permute-start.3
  18.5 2.5 %collective-permute-start.4 = (f32[2,32,128]{2,1,0:T(8,128)S(1)}, f32[2,32,128]{2,1,0:T(8,128)S(1)}, u32[]{:S(2)}, u32[]{:S(2)}) collective-permute-start(f32[2,32,128]{2,1,0:T(8,128)S(1)} %get-tuple-element.47), channel_id=1, source_target_pairs={{0,16},{1,17},{2,18},{3,19},{4,20},{5,21},{6,22},{7,23},{8,24},{9,... | collective-permute-start | bytes 98312 | tf_op jit(solution)/shard_map/ppermute | solution.py:522
  21.0 3.0 %collective-permute-start.5 = (f32[2,32,128]{2,1,0:T(8,128)S(1)}, f32[2,32,128]{2,1,0:T(8,128)S(1)}, u32[]{:S(2)}, u32[]{:S(2)}) collective-permute-start(f32[2,32,128]{2,1,0:T(8,128)S(1)} %get-tuple-element.47), channel_id=1, source_target_pairs={{0,31},{1,2},{2,1},{3,4},{4,3},{5,6},{6,5},{7,8},{8,7},{9,10},{10,... | collective-permute-start | bytes 98312 | tf_op jit(solution)/shard_map/ppermute | solution.py:522
  24.0 2.9 %all-to-all-done.red = f32[32,9,1,128]{3,2,1,0:T(1,128)S(1)} async-done(((f32[32,9,1,128]{3,2,1,0:T(1,128)}), f32[32,9,1,128]{3,2,1,0:T(1,128)S(1)}, u32[]{:S(2)}, u32[]{:S(2)}) %all-to-all-start) | async-done | bytes 147488 | tf_op jit(solution)/shard_map/all_to_all | solution.py:526
  26.9 1.2 %shard_map.80 = (f32[16,1024]{1,0:T(8,128)S(1)}, f32[80,1024]{1,0:T(8,128)S(1)}, f32[144,128]{1,0:T(8,128)S(1)}, f32[1,16]{1,0:T(1,128)}) custom-call(f32[32,9,1,128]{3,2,1,0:T(1,128)S(1)} %all-to-all-done.red, f32[32,1024]{1,0:T(8,128)S(1)} %get-tuple-element.51.u), custom_call_target="tpu_custom_call" | custom-call | tf_op jit(solution)/shard_map/pallas_call | solution.py:560
  28.1 0.0 collective-permute-done.3.h_a
  28.1 0.0 collective-permute-done.4.h_f
  28.1 0.0 collective-permute-done.5.h_b
  28.1 1.7 %copy-done.1 = bf16[8,640,256]{2,1,0:T(8,128)(2,1)S(1)} copy-done((bf16[8,640,256]{2,1,0:T(8,128)(2,1)S(1)}, bf16[8,640,256]{2,1,0:T(8,128)(2,1)}, u32[]{:S(2)}) %copy-start.1) | copy-done | bytes 2621464
  29.8 0.5 shard_map.81
  30.4 0.0 copy-start.7
  30.4 0.6 copy-done.7
  31.0 0.3 collective-permute-start.6
  31.3 0.8 collective-permute-start.7
  32.1 2.6 %collective-permute-start.8 = (f32[2,16,128]{2,1,0:T(8,128)S(1)}, f32[2,16,128]{2,1,0:T(8,128)S(1)}, u32[]{:S(2)}, u32[]{:S(2)}) collective-permute-start(f32[2,16,128]{2,1,0:T(8,128)S(1)} %get-tuple-element.57), channel_id=1, source_target_pairs={{0,31},{1,2},{2,1},{3,4},{4,3},{5,6},{6,5},{7,8},{8,7},{9,10},{10,... | collective-permute-start | bytes 49160 | tf_op jit(solution)/shard_map/ppermute | solution.py:522
  34.7 1.1 %shard_map.82 = (f32[16,1024]{1,0:T(8,128)S(1)}, f32[16,1024]{1,0:T(8,128)S(1)}, f32[80,1024]{1,0:T(8,128)S(1)}, f32[32,1024]{1,0:T(8,128)S(1)}) custom-call(s32[8,5]{1,0:T(8,128)S(1)} %get-tuple-element.43.cols, bf16[14,64,128]{2,1,0:T(8,128)(2,1)S(1)} %get-tuple-element.55.xs, bf16[8,640,256]{2,1,0:T(8,128)(2,1)S(1)} %get-tuple-element.44.w_high, ...), custom_call_target="tpu_custom_call" | custom-call | tf_op jit(solution)/shard_map/pallas_call | solution.py:566
  35.8 0.7 shard_map.83
  36.5 0.1 collective-permute-start.9
  36.5 1.2 %collective-permute-done.9.pair = f32[16,128]{1,0:T(8,128)S(1)} collective-permute-done((f32[16,128]{1,0:T(8,128)S(1)}, f32[16,128]{1,0:T(8,128)S(1)}, u32[]{:S(2)}, u32[]{:S(2)}) %collective-permute-start.9) | collective-permute-done | bytes 8224 | tf_op jit(solution)/shard_map/ppermute | solution.py:573
  37.7 0.0 collective-permute-done.6.h_a
  37.7 0.0 collective-permute-done.7.h_f
  37.7 1.1 %collective-permute-done.8.h_b = f32[2,16,128]{2,1,0:T(8,128)S(1)} collective-permute-done((f32[2,16,128]{2,1,0:T(8,128)S(1)}, f32[2,16,128]{2,1,0:T(8,128)S(1)}, u32[]{:S(2)}, u32[]{:S(2)}) %collective-permute-start.8) | collective-permute-done | bytes 16416 | tf_op jit(solution)/shard_map/ppermute | solution.py:522
  38.9 1.6 %shard_map.84 = (f32[16,1024]{1,0:T(8,128)S(1)}, f32[2,48,128]{2,1,0:T(8,128)S(1)}, f32[32,10,1,128]{3,2,1,0:T(1,128)S(1)}) custom-call(s32[8,5]{1,0:T(8,128)S(1)} %get-tuple-element.43.cols, s32[2]{0:T(128)S(1)} %copy-done.14, f32[16,1024]{1,0:T(8,128)S(1)} %get-tuple-element.56.p, f32[2,16,128]{2,1,0:T(8,128)S(1)} %collective-permute-done.6.h_a, ...), custom_call_target="tpu_custom_call" | custom-call | tf_op jit(solution)/shard_map/pallas_call | solution.py:575
  40.5 0.7 copy-done.6
  41.1 0.6 copy-done.11
  41.7 0.6 copy-done.16
  42.4 2.9 %all-to-all-start.1 = ((f32[32,10,1,128]{3,2,1,0:T(1,128)}), f32[32,10,1,128]{3,2,1,0:T(1,128)S(1)}, u32[]{:S(2)}, u32[]{:S(2)}) async-start(f32[32,10,1,128]{3,2,1,0:T(1,128)} %copy-done.6), calls=%async_computation.1 | async-start | bytes 327680 | tf_op jit(solution)/shard_map/all_to_all | solution.py:526
  45.3 0.3 collective-permute-start.10
  45.6 2.5 %collective-permute-start.11 = (f32[2,48,128]{2,1,0:T(8,128)}, f32[2,48,128]{2,1,0:T(8,128)}, u32[]{:S(2)}, u32[]{:S(2)}) collective-permute-start(f32[2,48,128]{2,1,0:T(8,128)} %copy-done.16), channel_id=1, source_target_pairs={{0,16},{1,17},{2,18},{3,19},{4,20},{5,21},{6,22},{7,23},{8,24},{9,... | collective-permute-start | bytes 147464 | tf_op jit(solution)/shard_map/ppermute | solution.py:522
  48.2 3.0 %collective-permute-start.12 = (f32[2,48,128]{2,1,0:T(8,128)}, f32[2,48,128]{2,1,0:T(8,128)}, u32[]{:S(2)}, u32[]{:S(2)}) collective-permute-start(f32[2,48,128]{2,1,0:T(8,128)} %copy-done.16), channel_id=1, source_target_pairs={{0,31},{1,2},{2,1},{3,4},{4,3},{5,6},{6,5},{7,8},{8,7},{9,10},{10,... | collective-permute-start | bytes 147464 | tf_op jit(solution)/shard_map/ppermute | solution.py:522
  51.1 3.3 %all-to-all-done.1.red = f32[32,10,1,128]{3,2,1,0:T(1,128)S(1)} async-done(((f32[32,10,1,128]{3,2,1,0:T(1,128)}), f32[32,10,1,128]{3,2,1,0:T(1,128)S(1)}, u32[]{:S(2)}, u32[]{:S(2)}) %all-to-all-start.1) | async-done | bytes 163872 | tf_op jit(solution)/shard_map/all_to_all | solution.py:526
  54.5 0.8 %copy-done.12 = f32[16,1024]{1,0:T(8,128)S(1)} copy-done((f32[16,1024]{1,0:T(8,128)S(1)}, f32[16,1024]{1,0:T(8,128)}, u32[]{:S(2)}) %copy-start.12) | copy-done | bytes 65560
  55.3 0.9 %shard_map.85 = (f32[16,1024]{1,0:T(8,128)S(1)}, f32[32,128]{1,0:T(8,128)S(1)}, f32[80,128]{1,0:T(8,128)S(1)}, f32[32,128]{1,0:T(8,128)S(1)}) custom-call(f32[32,10,1,128]{3,2,1,0:T(1,128)S(1)} %all-to-all-done.1.red, f32[16,1024]{1,0:T(8,128)S(1)} %copy-done.12, f32[80,1024]{1,0:T(8,128)S(1)} %get-tuple-element.58.words, ...), custom_call_target="tpu_custom_call" | custom-call | tf_op jit(solution)/shard_map/pallas_call | solution.py:580
  56.2 0.0 collective-permute-done.10.h_a
  56.2 0.0 collective-permute-done.11.h_f
  56.2 0.0 collective-permute-done.12.h_b
  56.3 1.7 %copy-done.3 = bf16[8,640,256]{2,1,0:T(8,128)(2,1)S(1)} copy-done((bf16[8,640,256]{2,1,0:T(8,128)(2,1)S(1)}, bf16[8,640,256]{2,1,0:T(8,128)(2,1)}, u32[]{:S(2)}) %copy-start.3) | copy-done | bytes 2621464
  58.0 0.9 %copy-done.8 = f32[48,768]{1,0:T(8,128)S(1)} copy-done((f32[48,768]{1,0:T(8,128)S(1)}, f32[48,768]{1,0:T(8,128)}, u32[]{:S(2)}) %copy-start.8) | copy-done | bytes 147480
  58.9 0.7 copy-done.15
  59.6 1.3 %shard_map.86 = (f32[2,16,128]{2,1,0:T(8,128)S(1)}, bf16[14,32,128]{2,1,0:T(8,128)(2,1)S(1)}) custom-call(s32[8,5]{1,0:T(8,128)S(1)} %get-tuple-element.43.cols, s32[2]{0:T(128)S(1)} %copy-done.15, f32[16,1024]{1,0:T(8,128)S(1)} %get-tuple-element.67.c_local, f32[32,128]{1,0:T(8,128)S(1)} %get-tuple-element.68.coefs, ...), custom_call_target="tpu_custom_call" | custom-call | tf_op jit(solution)/shard_map/pallas_call | solution.py:583
  60.9 0.3 collective-permute-start.13
  61.2 1.2 %collective-permute-start.14 = (f32[2,16,128]{2,1,0:T(8,128)S(1)}, f32[2,16,128]{2,1,0:T(8,128)S(1)}, u32[]{:S(2)}, u32[]{:S(2)}) collective-permute-start(f32[2,16,128]{2,1,0:T(8,128)S(1)} %get-tuple-element.73), channel_id=1, source_target_pairs={{0,16},{1,17},{2,18},{3,19},{4,20},{5,21},{6,22},{7,23},{8,24},{9,... | collective-permute-start | bytes 49160 | tf_op jit(solution)/shard_map/ppermute | solution.py:522
  62.4 2.6 %collective-permute-start.15 = (f32[2,16,128]{2,1,0:T(8,128)S(1)}, f32[2,16,128]{2,1,0:T(8,128)S(1)}, u32[]{:S(2)}, u32[]{:S(2)}) collective-permute-start(f32[2,16,128]{2,1,0:T(8,128)S(1)} %get-tuple-element.73), channel_id=1, source_target_pairs={{0,31},{1,2},{2,1},{3,4},{4,3},{5,6},{6,5},{7,8},{8,7},{9,10},{10,... | collective-permute-start | bytes 49160 | tf_op jit(solution)/shard_map/ppermute | solution.py:522
  65.0 0.9 %shard_map.87 = (f32[16,1024]{1,0:T(8,128)S(1)}, f32[16,1024]{1,0:T(8,128)S(1)}) custom-call(s32[8,5]{1,0:T(8,128)S(1)} %get-tuple-element.43.cols, bf16[14,32,128]{2,1,0:T(8,128)(2,1)S(1)} %get-tuple-element.71.xs, f32[16,1024]{1,0:T(8,128)S(1)} %get-tuple-element.67.c_local, f32[32,128]{1,0:T(8,128)S(1)} %get-tuple-element.68.coefs, ...), custom_call_target="tpu_custom_call" | custom-call | tf_op jit(solution)/shard_map/pallas_call | solution.py:587
  66.0 0.4 shard_map.88
  66.4 0.0 collective-permute-done.13.h_a
  66.4 0.0 collective-permute-done.14.h_f
  66.4 2.8 %collective-permute-done.15.h_b = f32[2,16,128]{2,1,0:T(8,128)S(1)} collective-permute-done((f32[2,16,128]{2,1,0:T(8,128)S(1)}, f32[2,16,128]{2,1,0:T(8,128)S(1)}, u32[]{:S(2)}, u32[]{:S(2)}) %collective-permute-start.15) | collective-permute-done | bytes 16416 | tf_op jit(solution)/shard_map/ppermute | solution.py:522
  69.2 1.3 %shard_map.89 = (f32[16,1024]{1,0:T(8,128)S(1)}, f32[32,8,128]{2,1,0:T(8,128)S(1)}) custom-call(s32[8,5]{1,0:T(8,128)S(1)} %get-tuple-element.43.cols, f32[16,1024]{1,0:T(8,128)S(1)} %get-tuple-element.72.p, f32[2,16,128]{2,1,0:T(8,128)S(1)} %collective-permute-done.13.h_a, f32[2,16,128]{2,1,0:T(8,128)S(1)} %collective-permute-done.14.h_f, ...), custom_call_target="tpu_custom_call" | custom-call | tf_op jit(solution)/shard_map/pallas_call | solution.py:589
  70.5 11.0 %all_to_all.15.red = f32[32,8,128]{2,1,0:T(8,128)S(1)} all-to-all(f32[32,8,128]{2,1,0:T(8,128)S(1)} %get-tuple-element.78), channel_id=1, replica_groups=mesh['parts'=32] {'parts'}, dimensions={0} | all-to-all | bytes 262144 | tf_op jit(solution)/shard_map/all_to_all | solution.py:526
  81.5 1.2 %shard_map.90 = f32[16,1024]{1,0:T(8,128)} custom-call(f32[32,8,128]{2,1,0:T(8,128)S(1)} %all_to_all.15.red, f32[16,1024]{1,0:T(8,128)S(1)} %get-tuple-element.79.p, f32[144,128]{1,0:T(8,128)S(1)} %get-tuple-element.54.small, f32[64,128]{1,0:T(8,128)S(1)} %get-tuple-element.66.small_b, f32[32,128]{1,0:T(8,128)S(1)} %get-tuple-element.80.tests_in, ...), custom_call_target="tpu_custom_call" | custom-call | tf_op jit(solution)/shard_map/pallas_call | solution.py:591
  (21 shorter events, 0.0 us)
Async XLA Ops:
  1.6 11.0 %copy-start.5 = (f32[16,1024]{1,0:T(8,128)S(1)}, f32[16,1024]{1,0:T(8,128)}, u32[]{:S(2)}) copy-start(f32[16,1024]{1,0:T(8,128)} %basis.3) | copy-start | bytes 196612
  1.6 11.0 %copy-start.13 = (s32[2]{0:T(128)S(1)}, s32[2]{0:T(128)}, u32[]{:S(2)}) copy-start(s32[2]{0:T(128)} %iface.7) | copy-start | bytes 28
  1.6 10.7 %collective-permute-start = (f32[2,16,128]{2,1,0:T(8,128)S(1)}, f32[2,16,128]{2,1,0:T(8,128)S(1)}, u32[]{:S(2)}, u32[]{:S(2)}) collective-permute-start(f32[2,16,128]{2,1,0:T(8,128)S(1)} %shard_map.78), channel_id=1, source_target_pairs={{0,1},{1,0},{2,3},{3,2},{4,5},{5,4},{6,7},{7,6},{8,9},{9,8},{10,11... | collective-permute-start | bytes 49160 | tf_op jit(solution)/shard_map/ppermute | solution.py:522
  2.2 10.1 %collective-permute-start.1 = (f32[2,16,128]{2,1,0:T(8,128)S(1)}, f32[2,16,128]{2,1,0:T(8,128)S(1)}, u32[]{:S(2)}, u32[]{:S(2)}) collective-permute-start(f32[2,16,128]{2,1,0:T(8,128)S(1)} %shard_map.78), channel_id=1, source_target_pairs={{0,16},{1,17},{2,18},{3,19},{4,20},{5,21},{6,22},{7,23},{8,24},{9,... | collective-permute-start | bytes 49160 | tf_op jit(solution)/shard_map/ppermute | solution.py:522
  5.8 6.8 %collective-permute-start.2 = (f32[2,16,128]{2,1,0:T(8,128)S(1)}, f32[2,16,128]{2,1,0:T(8,128)S(1)}, u32[]{:S(2)}, u32[]{:S(2)}) collective-permute-start(f32[2,16,128]{2,1,0:T(8,128)S(1)} %shard_map.78), channel_id=1, source_target_pairs={{0,31},{1,2},{2,1},{3,4},{4,3},{5,6},{6,5},{7,8},{8,7},{9,10},{10,... | collective-permute-start | bytes 49160 | tf_op jit(solution)/shard_map/ppermute | solution.py:522
  12.3 2.5 %copy-start = (bf16[8,640,256]{2,1,0:T(8,128)(2,1)}, bf16[8,640,256]{2,1,0:T(8,128)(2,1)S(1)}, u32[]{:S(2)}) copy-start(bf16[8,640,256]{2,1,0:T(8,128)(2,1)S(1)} %get-tuple-element.45.w_low) | copy-start | bytes 7864324
  14.8 12.1 %all-to-all-start = ((f32[32,9,1,128]{3,2,1,0:T(1,128)}), f32[32,9,1,128]{3,2,1,0:T(1,128)S(1)}, u32[]{:S(2)}, u32[]{:S(2)}) async-start(f32[32,9,1,128]{3,2,1,0:T(1,128)} %get-tuple-element.50), calls=%async_computation | async-start | bytes 294912 | tf_op jit(solution)/shard_map/all_to_all | solution.py:526
  18.1 10.0 %collective-permute-start.3 = (f32[2,32,128]{2,1,0:T(8,128)S(1)}, f32[2,32,128]{2,1,0:T(8,128)S(1)}, u32[]{:S(2)}, u32[]{:S(2)}) collective-permute-start(f32[2,32,128]{2,1,0:T(8,128)S(1)} %get-tuple-element.47), channel_id=1, source_target_pairs={{0,1},{1,0},{2,3},{3,2},{4,5},{5,4},{6,7},{7,6},{8,9},{9,8},{10,11... | collective-permute-start | bytes 98312 | tf_op jit(solution)/shard_map/ppermute | solution.py:522
  18.5 9.6 %collective-permute-start.4 = (f32[2,32,128]{2,1,0:T(8,128)S(1)}, f32[2,32,128]{2,1,0:T(8,128)S(1)}, u32[]{:S(2)}, u32[]{:S(2)}) collective-permute-start(f32[2,32,128]{2,1,0:T(8,128)S(1)} %get-tuple-element.47), channel_id=1, source_target_pairs={{0,16},{1,17},{2,18},{3,19},{4,20},{5,21},{6,22},{7,23},{8,24},{9,... | collective-permute-start | bytes 98312 | tf_op jit(solution)/shard_map/ppermute | solution.py:522
  21.0 7.1 %collective-permute-start.5 = (f32[2,32,128]{2,1,0:T(8,128)S(1)}, f32[2,32,128]{2,1,0:T(8,128)S(1)}, u32[]{:S(2)}, u32[]{:S(2)}) collective-permute-start(f32[2,32,128]{2,1,0:T(8,128)S(1)} %get-tuple-element.47), channel_id=1, source_target_pairs={{0,31},{1,2},{2,1},{3,4},{4,3},{5,6},{6,5},{7,8},{8,7},{9,10},{10,... | collective-permute-start | bytes 98312 | tf_op jit(solution)/shard_map/ppermute | solution.py:522
  28.1 1.7 %copy-start.1 = (bf16[8,640,256]{2,1,0:T(8,128)(2,1)S(1)}, bf16[8,640,256]{2,1,0:T(8,128)(2,1)}, u32[]{:S(2)}) copy-start(bf16[8,640,256]{2,1,0:T(8,128)(2,1)} %copy-done) | copy-start | bytes 7864324
  30.4 0.7 copy-start.7
  31.0 6.7 %collective-permute-start.6 = (f32[2,16,128]{2,1,0:T(8,128)S(1)}, f32[2,16,128]{2,1,0:T(8,128)S(1)}, u32[]{:S(2)}, u32[]{:S(2)}) collective-permute-start(f32[2,16,128]{2,1,0:T(8,128)S(1)} %get-tuple-element.57), channel_id=1, source_target_pairs={{0,1},{1,0},{2,3},{3,2},{4,5},{5,4},{6,7},{7,6},{8,9},{9,8},{10,11... | collective-permute-start | bytes 49160 | tf_op jit(solution)/shard_map/ppermute | solution.py:522
  31.3 6.4 %collective-permute-start.7 = (f32[2,16,128]{2,1,0:T(8,128)S(1)}, f32[2,16,128]{2,1,0:T(8,128)S(1)}, u32[]{:S(2)}, u32[]{:S(2)}) collective-permute-start(f32[2,16,128]{2,1,0:T(8,128)S(1)} %get-tuple-element.57), channel_id=1, source_target_pairs={{0,16},{1,17},{2,18},{3,19},{4,20},{5,21},{6,22},{7,23},{8,24},{9,... | collective-permute-start | bytes 49160 | tf_op jit(solution)/shard_map/ppermute | solution.py:522
  32.1 6.8 %collective-permute-start.8 = (f32[2,16,128]{2,1,0:T(8,128)S(1)}, f32[2,16,128]{2,1,0:T(8,128)S(1)}, u32[]{:S(2)}, u32[]{:S(2)}) collective-permute-start(f32[2,16,128]{2,1,0:T(8,128)S(1)} %get-tuple-element.57), channel_id=1, source_target_pairs={{0,31},{1,2},{2,1},{3,4},{4,3},{5,6},{6,5},{7,8},{8,7},{9,10},{10,... | collective-permute-start | bytes 49160 | tf_op jit(solution)/shard_map/ppermute | solution.py:522
  34.7 4.2 %copy-start.2 = (bf16[8,640,256]{2,1,0:T(8,128)(2,1)S(1)}, bf16[8,640,256]{2,1,0:T(8,128)(2,1)}, u32[]{:S(2)}) copy-start(bf16[8,640,256]{2,1,0:T(8,128)(2,1)} %copy-done) | copy-start | bytes 7864324
  34.7 4.2 %copy-start.14 = (s32[2]{0:T(128)S(1)}, s32[2]{0:T(128)}, u32[]{:S(2)}) copy-start(s32[2]{0:T(128)} %iface.7) | copy-start | bytes 28
  36.5 4.0 %copy-start.9 = (f32[16,1024]{1,0:T(8,128)}, f32[16,1024]{1,0:T(8,128)S(1)}, u32[]{:S(2)}) copy-start(f32[16,1024]{1,0:T(8,128)S(1)} %get-tuple-element.75.v) | copy-start | bytes 196612
  36.5 1.2 %collective-permute-start.9 = (f32[16,128]{1,0:T(8,128)S(1)}, f32[16,128]{1,0:T(8,128)S(1)}, u32[]{:S(2)}, u32[]{:S(2)}) collective-permute-start(f32[16,128]{1,0:T(8,128)S(1)} %get-tuple-element.61.part), channel_id=1, source_target_pairs={{0,1},{1,0},{2,3},{3,2},{4,5},{5,4},{6,7},{7,6},{8,9},{9,8},{10,11... | collective-permute-start | bytes 24584 | tf_op jit(solution)/shard_map/ppermute | solution.py:573
  40.4 0.7 copy-start.6
  41.1 0.6 copy-start.11
  41.7 0.6 copy-start.16
  42.4 12.1 %all-to-all-start.1 = ((f32[32,10,1,128]{3,2,1,0:T(1,128)}), f32[32,10,1,128]{3,2,1,0:T(1,128)S(1)}, u32[]{:S(2)}, u32[]{:S(2)}) async-start(f32[32,10,1,128]{3,2,1,0:T(1,128)} %copy-done.6), calls=%async_computation.1 | async-start | bytes 327680 | tf_op jit(solution)/shard_map/all_to_all | solution.py:526
  45.3 10.9 %collective-permute-start.10 = (f32[2,48,128]{2,1,0:T(8,128)}, f32[2,48,128]{2,1,0:T(8,128)}, u32[]{:S(2)}, u32[]{:S(2)}) collective-permute-start(f32[2,48,128]{2,1,0:T(8,128)} %copy-done.16), channel_id=1, source_target_pairs={{0,1},{1,0},{2,3},{3,2},{4,5},{5,4},{6,7},{7,6},{8,9},{9,8},{10,11... | collective-permute-start | bytes 147464 | tf_op jit(solution)/shard_map/ppermute | solution.py:522
  45.6 10.6 %collective-permute-start.11 = (f32[2,48,128]{2,1,0:T(8,128)}, f32[2,48,128]{2,1,0:T(8,128)}, u32[]{:S(2)}, u32[]{:S(2)}) collective-permute-start(f32[2,48,128]{2,1,0:T(8,128)} %copy-done.16), channel_id=1, source_target_pairs={{0,16},{1,17},{2,18},{3,19},{4,20},{5,21},{6,22},{7,23},{8,24},{9,... | collective-permute-start | bytes 147464 | tf_op jit(solution)/shard_map/ppermute | solution.py:522
  48.2 8.1 %collective-permute-start.12 = (f32[2,48,128]{2,1,0:T(8,128)}, f32[2,48,128]{2,1,0:T(8,128)}, u32[]{:S(2)}, u32[]{:S(2)}) collective-permute-start(f32[2,48,128]{2,1,0:T(8,128)} %copy-done.16), channel_id=1, source_target_pairs={{0,31},{1,2},{2,1},{3,4},{4,3},{5,6},{6,5},{7,8},{8,7},{9,10},{10,... | collective-permute-start | bytes 147464 | tf_op jit(solution)/shard_map/ppermute | solution.py:522
  54.5 0.8 %copy-start.12 = (f32[16,1024]{1,0:T(8,128)S(1)}, f32[16,1024]{1,0:T(8,128)}, u32[]{:S(2)}) copy-start(f32[16,1024]{1,0:T(8,128)} %copy-done.11) | copy-start | bytes 196612
  56.3 1.7 %copy-start.3 = (bf16[8,640,256]{2,1,0:T(8,128)(2,1)S(1)}, bf16[8,640,256]{2,1,0:T(8,128)(2,1)}, u32[]{:S(2)}) copy-start(bf16[8,640,256]{2,1,0:T(8,128)(2,1)} %copy-done) | copy-start | bytes 7864324
  58.0 0.9 %copy-start.8 = (f32[48,768]{1,0:T(8,128)S(1)}, f32[48,768]{1,0:T(8,128)}, u32[]{:S(2)}) copy-start(f32[48,768]{1,0:T(8,128)} %copy-done.7) | copy-start | bytes 442372
  58.9 0.7 copy-start.15
  60.9 5.5 %collective-permute-start.13 = (f32[2,16,128]{2,1,0:T(8,128)S(1)}, f32[2,16,128]{2,1,0:T(8,128)S(1)}, u32[]{:S(2)}, u32[]{:S(2)}) collective-permute-start(f32[2,16,128]{2,1,0:T(8,128)S(1)} %get-tuple-element.73), channel_id=1, source_target_pairs={{0,1},{1,0},{2,3},{3,2},{4,5},{5,4},{6,7},{7,6},{8,9},{9,8},{10,11... | collective-permute-start | bytes 49160 | tf_op jit(solution)/shard_map/ppermute | solution.py:522
  61.2 5.2 %collective-permute-start.14 = (f32[2,16,128]{2,1,0:T(8,128)S(1)}, f32[2,16,128]{2,1,0:T(8,128)S(1)}, u32[]{:S(2)}, u32[]{:S(2)}) collective-permute-start(f32[2,16,128]{2,1,0:T(8,128)S(1)} %get-tuple-element.73), channel_id=1, source_target_pairs={{0,16},{1,17},{2,18},{3,19},{4,20},{5,21},{6,22},{7,23},{8,24},{9,... | collective-permute-start | bytes 49160 | tf_op jit(solution)/shard_map/ppermute | solution.py:522
  62.4 6.8 %collective-permute-start.15 = (f32[2,16,128]{2,1,0:T(8,128)S(1)}, f32[2,16,128]{2,1,0:T(8,128)S(1)}, u32[]{:S(2)}, u32[]{:S(2)}) collective-permute-start(f32[2,16,128]{2,1,0:T(8,128)S(1)} %get-tuple-element.73), channel_id=1, source_target_pairs={{0,31},{1,2},{2,1},{3,4},{4,3},{5,6},{6,5},{7,8},{8,7},{9,10},{10,... | collective-permute-start | bytes 49160 | tf_op jit(solution)/shard_map/ppermute | solution.py:522
  65.0 1.0 %copy-start.10 = (f32[16,1024]{1,0:T(8,128)S(1)}, f32[16,1024]{1,0:T(8,128)}, u32[]{:S(2)}) copy-start(f32[16,1024]{1,0:T(8,128)} %copy-done.9) | copy-start | bytes 196612
  65.0 4.2 %copy-start.4 = (bf16[8,640,256]{2,1,0:T(8,128)(2,1)S(1)}, bf16[8,640,256]{2,1,0:T(8,128)(2,1)}, u32[]{:S(2)}) copy-start(bf16[8,640,256]{2,1,0:T(8,128)(2,1)} %copy-done) | copy-start | bytes 7864324

commit v8 on v7

--- a/solution.py
+++ b/solution.py
@@ -410,9 +410,10 @@
         cross, mass, ef = get_small(small, 0), get_small(small_b, 0), get_small(small_b, 1)
         theta = small[5 * n : 6 * n, :1]
         right = g_p + relax * mm(g_left, ef)
-        left = g_a + mm(
-            lanes([relax * g_left, -relax * theta * g_left, -g_p, theta * g_p]),
-            rows([kf_test, mf_test, cross, mass]),
+        left = (
+            g_a
+            + relax * (mm(g_left, kf_test) - theta * mm(g_left, mf_test))
+            - (mm(g_p, cross) - theta * mm(g_p, mass))
         )
         return lanes(
             [

time: 83.2 us -> 83.2 us (level)
  no operation moved by 1% of the time
where the time goes in v8:
time: 83.2 us; the launch traced here: 82.7 us
  starting transfers between devices  33 us (40%)
  Pallas kernels  17.7 us (21%)
  waiting for transfers between devices  11.6 us (14%)
  blocking collectives  11 us (13%)
  local copies, waits for them, and re-layouts  8.45 us (10%)
  between operations  0.95 us (1%)
    ppermute x15, starting transfers between devices, halo(): got.append(lax.ppermute(outgoing, 'parts', pairs))  26.6 us
    all_to_all x1, blocking collectives, reduced(): return lax.all_to_all(blocks_out, 'parts', 0, 0, tiled=True)  11 us
    unnamed x34, local copies, waits for them, and re-layouts  8.45 us
    all_to_all x2, starting transfers between devices, reduced(): return lax.all_to_all(blocks_out, 'parts', 0, 0, tiled=True)  6.29 us
    all_to_all x2, waiting for transfers between devices, reduced(): return lax.all_to_all(blocks_out, 'parts', 0, 0, tiled=True)  6.24 us
    ppermute x15, waiting for transfers between devices, halo(): got.append(lax.ppermute(outgoing, 'parts', pairs))  4.2 us
    pallas_call x1, Pallas kernels, shards(): call(make_prep(count), [((tiles, blocks * width, 2 * width), BF16)] * 2 +...  3.47 us
    pallas_call x1, Pallas kernels, shards(): call(k_a, [vec, vec, vecs(2), out(2 * n), packed], [VM, VM] + [VM] * 7, [...  2.16 us
  transfers between devices with their start and end apart: 18, of which 6 were waited for; matrix products, arithmetic and copies ran while one was open for 0% of the time, Pallas kernels for 10%

profile of v8, /device:TPU:0, one launch (start us, length us, event | category | flops | bytes accessed | tf_op | source)
XLA Modules:
  0.0 82.7 jit_solution(14258116203310143195)
XLA Ops:
  0.6 1.0 %shard_map.78 = f32[2,16,128]{2,1,0:T(8,128)S(1)} custom-call(s32[2]{0:T(128)} %iface.7, f32[16,1024]{1,0:T(8,128)} %basis.3), custom_call_target="tpu_custom_call" | custom-call | tf_op jit(solution)/shard_map/pallas_call | solution.py:539
  1.6 0.0 copy-start.5
  1.6 0.0 copy-start.13
  1.6 0.6 collective-permute-start
  2.2 3.7 %collective-permute-start.1 = (f32[2,16,128]{2,1,0:T(8,128)S(1)}, f32[2,16,128]{2,1,0:T(8,128)S(1)}, u32[]{:S(2)}, u32[]{:S(2)}) collective-permute-start(f32[2,16,128]{2,1,0:T(8,128)S(1)} %shard_map.78), channel_id=1, source_target_pairs={{0,16},{1,17},{2,18},{3,19},{4,20},{5,21},{6,22},{7,23},{8,24},{9,... | collective-permute-start | bytes 49160 | tf_op jit(solution)/shard_map/ppermute | solution.py:523
  5.8 3.0 %collective-permute-start.2 = (f32[2,16,128]{2,1,0:T(8,128)S(1)}, f32[2,16,128]{2,1,0:T(8,128)S(1)}, u32[]{:S(2)}, u32[]{:S(2)}) collective-permute-start(f32[2,16,128]{2,1,0:T(8,128)S(1)} %shard_map.78), channel_id=1, source_target_pairs={{0,31},{1,2},{2,1},{3,4},{4,3},{5,6},{6,5},{7,8},{8,7},{9,10},{10,... | collective-permute-start | bytes 49160 | tf_op jit(solution)/shard_map/ppermute | solution.py:523
  8.8 3.5 %shard_map.77 = (bf16[8,640,256]{2,1,0:T(8,128)(2,1)S(1)}, bf16[8,640,256]{2,1,0:T(8,128)(2,1)S(1)}, f32[1,1024]{1,0:T(1,128)S(1)}, s32[8,5]{1,0:T(8,128)S(1)}) custom-call(s32[8,5]{1,0:T(8,128)} %part_hbm.1, s32[8,5]{1,0:T(8,128)} %slot_hbm.1, f32[8,5,128,128]{3,2,1,0:T(8,128)} %k_hbm.1, f32[8,5,128,128]{3,2,1,0:T(8,128)} %m_hbm.1), custom_call_target="tpu_custom_call" | custom-call | tf_op jit(solution)/shard_map/pallas_call | solution.py:546
  12.3 0.0 collective-permute-done.h_a
  12.3 0.0 collective-permute-done.1.h_f
  12.4 0.3 collective-permute-done.2.h_b
  12.6 0.0 copy-done.5
  12.6 2.2 %shard_map.79 = (f32[16,1024]{1,0:T(8,128)S(1)}, f32[16,1024]{1,0:T(8,128)S(1)}, f32[32,1024]{1,0:T(8,128)S(1)}, f32[2,32,128]{2,1,0:T(8,128)S(1)}, f32[32,9,1,128]{3,2,1,0:T(1,128)}) custom-call(s32[8,5]{1,0:T(8,128)S(1)} %get-tuple-element.43.cols, s32[2]{0:T(128)S(1)} %copy-done.13, f32[16,1024]{1,0:T(8,128)S(1)} %copy-done.5, ...), custom_call_target="tpu_custom_call" | custom-call | tf_op jit(solution)/shard_map/pallas_call | solution.py:556
  14.8 3.4 %all-to-all-start = ((f32[32,9,1,128]{3,2,1,0:T(1,128)}), f32[32,9,1,128]{3,2,1,0:T(1,128)S(1)}, u32[]{:S(2)}, u32[]{:S(2)}) async-start(f32[32,9,1,128]{3,2,1,0:T(1,128)} %get-tuple-element.50), calls=%async_computation | async-start | bytes 294912 | tf_op jit(solution)/shard_map/all_to_all | solution.py:527
  18.1 0.3 collective-permute-start.3
  18.5 2.5 %collective-permute-start.4 = (f32[2,32,128]{2,1,0:T(8,128)S(1)}, f32[2,32,128]{2,1,0:T(8,128)S(1)}, u32[]{:S(2)}, u32[]{:S(2)}) collective-permute-start(f32[2,32,128]{2,1,0:T(8,128)S(1)} %get-tuple-element.47), channel_id=1, source_target_pairs={{0,16},{1,17},{2,18},{3,19},{4,20},{5,21},{6,22},{7,23},{8,24},{9,... | collective-permute-start | bytes 98312 | tf_op jit(solution)/shard_map/ppermute | solution.py:523
  21.0 3.0 %collective-permute-start.5 = (f32[2,32,128]{2,1,0:T(8,128)S(1)}, f32[2,32,128]{2,1,0:T(8,128)S(1)}, u32[]{:S(2)}, u32[]{:S(2)}) collective-permute-start(f32[2,32,128]{2,1,0:T(8,128)S(1)} %get-tuple-element.47), channel_id=1, source_target_pairs={{0,31},{1,2},{2,1},{3,4},{4,3},{5,6},{6,5},{7,8},{8,7},{9,10},{10,... | collective-permute-start | bytes 98312 | tf_op jit(solution)/shard_map/ppermute | solution.py:523
  24.0 2.9 %all-to-all-done.red = f32[32,9,1,128]{3,2,1,0:T(1,128)S(1)} async-done(((f32[32,9,1,128]{3,2,1,0:T(1,128)}), f32[32,9,1,128]{3,2,1,0:T(1,128)S(1)}, u32[]{:S(2)}, u32[]{:S(2)}) %all-to-all-start) | async-done | bytes 147488 | tf_op jit(solution)/shard_map/all_to_all | solution.py:527
  26.9 1.2 %shard_map.80 = (f32[16,1024]{1,0:T(8,128)S(1)}, f32[80,1024]{1,0:T(8,128)S(1)}, f32[144,128]{1,0:T(8,128)S(1)}, f32[1,16]{1,0:T(1,128)}) custom-call(f32[32,9,1,128]{3,2,1,0:T(1,128)S(1)} %all-to-all-done.red, f32[32,1024]{1,0:T(8,128)S(1)} %get-tuple-element.51.u), custom_call_target="tpu_custom_call" | custom-call | tf_op jit(solution)/shard_map/pallas_call | solution.py:561
  28.1 0.0 collective-permute-done.3.h_a
  28.1 0.0 collective-permute-done.4.h_f
  28.1 0.0 collective-permute-done.5.h_b
  28.1 1.7 %copy-done.1 = bf16[8,640,256]{2,1,0:T(8,128)(2,1)S(1)} copy-done((bf16[8,640,256]{2,1,0:T(8,128)(2,1)S(1)}, bf16[8,640,256]{2,1,0:T(8,128)(2,1)}, u32[]{:S(2)}) %copy-start.1) | copy-done | bytes 2621464
  29.8 0.5 shard_map.81
  30.4 0.0 copy-start.7
  30.4 0.6 copy-done.7
  31.0 0.3 collective-permute-start.6
  31.3 0.8 collective-permute-start.7
  32.1 2.6 %collective-permute-start.8 = (f32[2,16,128]{2,1,0:T(8,128)S(1)}, f32[2,16,128]{2,1,0:T(8,128)S(1)}, u32[]{:S(2)}, u32[]{:S(2)}) collective-permute-start(f32[2,16,128]{2,1,0:T(8,128)S(1)} %get-tuple-element.57), channel_id=1, source_target_pairs={{0,31},{1,2},{2,1},{3,4},{4,3},{5,6},{6,5},{7,8},{8,7},{9,10},{10,... | collective-permute-start | bytes 49160 | tf_op jit(solution)/shard_map/ppermute | solution.py:523
  34.7 1.1 %shard_map.82 = (f32[16,1024]{1,0:T(8,128)S(1)}, f32[16,1024]{1,0:T(8,128)S(1)}, f32[80,1024]{1,0:T(8,128)S(1)}, f32[32,1024]{1,0:T(8,128)S(1)}) custom-call(s32[8,5]{1,0:T(8,128)S(1)} %get-tuple-element.43.cols, bf16[14,64,128]{2,1,0:T(8,128)(2,1)S(1)} %get-tuple-element.55.xs, bf16[8,640,256]{2,1,0:T(8,128)(2,1)S(1)} %get-tuple-element.44.w_high, ...), custom_call_target="tpu_custom_call" | custom-call | tf_op jit(solution)/shard_map/pallas_call | solution.py:567
  35.8 0.7 shard_map.83
  36.5 0.1 collective-permute-start.9
  36.5 1.2 %collective-permute-done.9.pair = f32[16,128]{1,0:T(8,128)S(1)} collective-permute-done((f32[16,128]{1,0:T(8,128)S(1)}, f32[16,128]{1,0:T(8,128)S(1)}, u32[]{:S(2)}, u32[]{:S(2)}) %collective-permute-start.9) | collective-permute-done | bytes 8224 | tf_op jit(solution)/shard_map/ppermute | solution.py:574
  37.7 0.0 collective-permute-done.6.h_a
  37.7 0.0 collective-permute-done.7.h_f
  37.7 1.1 %collective-permute-done.8.h_b = f32[2,16,128]{2,1,0:T(8,128)S(1)} collective-permute-done((f32[2,16,128]{2,1,0:T(8,128)S(1)}, f32[2,16,128]{2,1,0:T(8,128)S(1)}, u32[]{:S(2)}, u32[]{:S(2)}) %collective-permute-start.8) | collective-permute-done | bytes 16416 | tf_op jit(solution)/shard_map/ppermute | solution.py:523
  38.9 1.6 %shard_map.84 = (f32[16,1024]{1,0:T(8,128)S(1)}, f32[2,48,128]{2,1,0:T(8,128)S(1)}, f32[32,10,1,128]{3,2,1,0:T(1,128)S(1)}) custom-call(s32[8,5]{1,0:T(8,128)S(1)} %get-tuple-element.43.cols, s32[2]{0:T(128)S(1)} %copy-done.14, f32[16,1024]{1,0:T(8,128)S(1)} %get-tuple-element.56.p, f32[2,16,128]{2,1,0:T(8,128)S(1)} %collective-permute-done.6.h_a, ...), custom_call_target="tpu_custom_call" | custom-call | tf_op jit(solution)/shard_map/pallas_call | solution.py:576
  40.5 0.7 copy-done.6
  41.1 0.6 copy-done.11
  41.7 0.6 copy-done.16
  42.4 2.9 %all-to-all-start.1 = ((f32[32,10,1,128]{3,2,1,0:T(1,128)}), f32[32,10,1,128]{3,2,1,0:T(1,128)S(1)}, u32[]{:S(2)}, u32[]{:S(2)}) async-start(f32[32,10,1,128]{3,2,1,0:T(1,128)} %copy-done.6), calls=%async_computation.1 | async-start | bytes 327680 | tf_op jit(solution)/shard_map/all_to_all | solution.py:527
  45.3 0.3 collective-permute-start.10
  45.6 2.5 %collective-permute-start.11 = (f32[2,48,128]{2,1,0:T(8,128)}, f32[2,48,128]{2,1,0:T(8,128)}, u32[]{:S(2)}, u32[]{:S(2)}) collective-permute-start(f32[2,48,128]{2,1,0:T(8,128)} %copy-done.16), channel_id=1, source_target_pairs={{0,16},{1,17},{2,18},{3,19},{4,20},{5,21},{6,22},{7,23},{8,24},{9,... | collective-permute-start | bytes 147464 | tf_op jit(solution)/shard_map/ppermute | solution.py:523
  48.2 3.0 %collective-permute-start.12 = (f32[2,48,128]{2,1,0:T(8,128)}, f32[2,48,128]{2,1,0:T(8,128)}, u32[]{:S(2)}, u32[]{:S(2)}) collective-permute-start(f32[2,48,128]{2,1,0:T(8,128)} %copy-done.16), channel_id=1, source_target_pairs={{0,31},{1,2},{2,1},{3,4},{4,3},{5,6},{6,5},{7,8},{8,7},{9,10},{10,... | collective-permute-start | bytes 147464 | tf_op jit(solution)/shard_map/ppermute | solution.py:523
  51.1 3.3 %all-to-all-done.1.red = f32[32,10,1,128]{3,2,1,0:T(1,128)S(1)} async-done(((f32[32,10,1,128]{3,2,1,0:T(1,128)}), f32[32,10,1,128]{3,2,1,0:T(1,128)S(1)}, u32[]{:S(2)}, u32[]{:S(2)}) %all-to-all-start.1) | async-done | bytes 163872 | tf_op jit(solution)/shard_map/all_to_all | solution.py:527
  54.5 0.8 %copy-done.12 = f32[16,1024]{1,0:T(8,128)S(1)} copy-done((f32[16,1024]{1,0:T(8,128)S(1)}, f32[16,1024]{1,0:T(8,128)}, u32[]{:S(2)}) %copy-start.12) | copy-done | bytes 65560
  55.3 0.9 %shard_map.85 = (f32[16,1024]{1,0:T(8,128)S(1)}, f32[32,128]{1,0:T(8,128)S(1)}, f32[80,128]{1,0:T(8,128)S(1)}, f32[32,128]{1,0:T(8,128)S(1)}) custom-call(f32[32,10,1,128]{3,2,1,0:T(1,128)S(1)} %all-to-all-done.1.red, f32[16,1024]{1,0:T(8,128)S(1)} %copy-done.12, f32[80,1024]{1,0:T(8,128)S(1)} %get-tuple-element.58.words, ...), custom_call_target="tpu_custom_call" | custom-call | tf_op jit(solution)/shard_map/pallas_call | solution.py:581
  56.2 0.0 collective-permute-done.10.h_a
  56.2 0.0 collective-permute-done.11.h_f
  56.2 0.0 collective-permute-done.12.h_b
  56.3 1.7 %copy-done.3 = bf16[8,640,256]{2,1,0:T(8,128)(2,1)S(1)} copy-done((bf16[8,640,256]{2,1,0:T(8,128)(2,1)S(1)}, bf16[8,640,256]{2,1,0:T(8,128)(2,1)}, u32[]{:S(2)}) %copy-start.3) | copy-done | bytes 2621464
  58.0 0.9 %copy-done.8 = f32[48,768]{1,0:T(8,128)S(1)} copy-done((f32[48,768]{1,0:T(8,128)S(1)}, f32[48,768]{1,0:T(8,128)}, u32[]{:S(2)}) %copy-start.8) | copy-done | bytes 147480
  58.9 0.7 copy-done.15
  59.6 1.3 %shard_map.86 = (f32[2,16,128]{2,1,0:T(8,128)S(1)}, bf16[14,32,128]{2,1,0:T(8,128)(2,1)S(1)}) custom-call(s32[8,5]{1,0:T(8,128)S(1)} %get-tuple-element.43.cols, s32[2]{0:T(128)S(1)} %copy-done.15, f32[16,1024]{1,0:T(8,128)S(1)} %get-tuple-element.67.c_local, f32[32,128]{1,0:T(8,128)S(1)} %get-tuple-element.68.coefs, ...), custom_call_target="tpu_custom_call" | custom-call | tf_op jit(solution)/shard_map/pallas_call | solution.py:584
  60.9 0.3 collective-permute-start.13
  61.2 1.2 %collective-permute-start.14 = (f32[2,16,128]{2,1,0:T(8,128)S(1)}, f32[2,16,128]{2,1,0:T(8,128)S(1)}, u32[]{:S(2)}, u32[]{:S(2)}) collective-permute-start(f32[2,16,128]{2,1,0:T(8,128)S(1)} %get-tuple-element.73), channel_id=1, source_target_pairs={{0,16},{1,17},{2,18},{3,19},{4,20},{5,21},{6,22},{7,23},{8,24},{9,... | collective-permute-start | bytes 49160 | tf_op jit(solution)/shard_map/ppermute | solution.py:523
  62.4 2.6 %collective-permute-start.15 = (f32[2,16,128]{2,1,0:T(8,128)S(1)}, f32[2,16,128]{2,1,0:T(8,128)S(1)}, u32[]{:S(2)}, u32[]{:S(2)}) collective-permute-start(f32[2,16,128]{2,1,0:T(8,128)S(1)} %get-tuple-element.73), channel_id=1, source_target_pairs={{0,31},{1,2},{2,1},{3,4},{4,3},{5,6},{6,5},{7,8},{8,7},{9,10},{10,... | collective-permute-start | bytes 49160 | tf_op jit(solution)/shard_map/ppermute | solution.py:523
  65.0 1.0 %shard_map.87 = (f32[16,1024]{1,0:T(8,128)S(1)}, f32[16,1024]{1,0:T(8,128)S(1)}) custom-call(s32[8,5]{1,0:T(8,128)S(1)} %get-tuple-element.43.cols, bf16[14,32,128]{2,1,0:T(8,128)(2,1)S(1)} %get-tuple-element.71.xs, f32[16,1024]{1,0:T(8,128)S(1)} %get-tuple-element.67.c_local, f32[32,128]{1,0:T(8,128)S(1)} %get-tuple-element.68.coefs, ...), custom_call_target="tpu_custom_call" | custom-call | tf_op jit(solution)/shard_map/pallas_call | solution.py:588
  66.0 0.4 shard_map.88
  66.4 0.0 collective-permute-done.13.h_a
  66.4 0.0 collective-permute-done.14.h_f
  66.4 2.8 %collective-permute-done.15.h_b = f32[2,16,128]{2,1,0:T(8,128)S(1)} collective-permute-done((f32[2,16,128]{2,1,0:T(8,128)S(1)}, f32[2,16,128]{2,1,0:T(8,128)S(1)}, u32[]{:S(2)}, u32[]{:S(2)}) %collective-permute-start.15) | collective-permute-done | bytes 16416 | tf_op jit(solution)/shard_map/ppermute | solution.py:523
  69.2 1.3 %shard_map.89 = (f32[16,1024]{1,0:T(8,128)S(1)}, f32[32,8,128]{2,1,0:T(8,128)S(1)}) custom-call(s32[8,5]{1,0:T(8,128)S(1)} %get-tuple-element.43.cols, f32[16,1024]{1,0:T(8,128)S(1)} %get-tuple-element.72.p, f32[2,16,128]{2,1,0:T(8,128)S(1)} %collective-permute-done.13.h_a, f32[2,16,128]{2,1,0:T(8,128)S(1)} %collective-permute-done.14.h_f, ...), custom_call_target="tpu_custom_call" | custom-call | tf_op jit(solution)/shard_map/pallas_call | solution.py:590
  70.5 11.0 %all_to_all.15.red = f32[32,8,128]{2,1,0:T(8,128)S(1)} all-to-all(f32[32,8,128]{2,1,0:T(8,128)S(1)} %get-tuple-element.78), channel_id=1, replica_groups=mesh['parts'=32] {'parts'}, dimensions={0} | all-to-all | bytes 262144 | tf_op jit(solution)/shard_map/all_to_all | solution.py:527
  81.5 1.2 %shard_map.90 = f32[16,1024]{1,0:T(8,128)} custom-call(f32[32,8,128]{2,1,0:T(8,128)S(1)} %all_to_all.15.red, f32[16,1024]{1,0:T(8,128)S(1)} %get-tuple-element.79.p, f32[144,128]{1,0:T(8,128)S(1)} %get-tuple-element.54.small, f32[64,128]{1,0:T(8,128)S(1)} %get-tuple-element.66.small_b, f32[32,128]{1,0:T(8,128)S(1)} %get-tuple-element.80.tests_in, ...), custom_call_target="tpu_custom_call" | custom-call | tf_op jit(solution)/shard_map/pallas_call | solution.py:592
  (21 shorter events, 0.0 us)
Async XLA Ops:
  1.6 11.0 %copy-start.5 = (f32[16,1024]{1,0:T(8,128)S(1)}, f32[16,1024]{1,0:T(8,128)}, u32[]{:S(2)}) copy-start(f32[16,1024]{1,0:T(8,128)} %basis.3) | copy-start | bytes 196612
  1.6 11.0 %copy-start.13 = (s32[2]{0:T(128)S(1)}, s32[2]{0:T(128)}, u32[]{:S(2)}) copy-start(s32[2]{0:T(128)} %iface.7) | copy-start | bytes 28
  1.6 10.7 %collective-permute-start = (f32[2,16,128]{2,1,0:T(8,128)S(1)}, f32[2,16,128]{2,1,0:T(8,128)S(1)}, u32[]{:S(2)}, u32[]{:S(2)}) collective-permute-start(f32[2,16,128]{2,1,0:T(8,128)S(1)} %shard_map.78), channel_id=1, source_target_pairs={{0,1},{1,0},{2,3},{3,2},{4,5},{5,4},{6,7},{7,6},{8,9},{9,8},{10,11... | collective-permute-start | bytes 49160 | tf_op jit(solution)/shard_map/ppermute | solution.py:523
  2.2 10.1 %collective-permute-start.1 = (f32[2,16,128]{2,1,0:T(8,128)S(1)}, f32[2,16,128]{2,1,0:T(8,128)S(1)}, u32[]{:S(2)}, u32[]{:S(2)}) collective-permute-start(f32[2,16,128]{2,1,0:T(8,128)S(1)} %shard_map.78), channel_id=1, source_target_pairs={{0,16},{1,17},{2,18},{3,19},{4,20},{5,21},{6,22},{7,23},{8,24},{9,... | collective-permute-start | bytes 49160 | tf_op jit(solution)/shard_map/ppermute | solution.py:523
  5.8 6.8 %collective-permute-start.2 = (f32[2,16,128]{2,1,0:T(8,128)S(1)}, f32[2,16,128]{2,1,0:T(8,128)S(1)}, u32[]{:S(2)}, u32[]{:S(2)}) collective-permute-start(f32[2,16,128]{2,1,0:T(8,128)S(1)} %shard_map.78), channel_id=1, source_target_pairs={{0,31},{1,2},{2,1},{3,4},{4,3},{5,6},{6,5},{7,8},{8,7},{9,10},{10,... | collective-permute-start | bytes 49160 | tf_op jit(solution)/shard_map/ppermute | solution.py:523
  12.3 2.5 %copy-start = (bf16[8,640,256]{2,1,0:T(8,128)(2,1)}, bf16[8,640,256]{2,1,0:T(8,128)(2,1)S(1)}, u32[]{:S(2)}) copy-start(bf16[8,640,256]{2,1,0:T(8,128)(2,1)S(1)} %get-tuple-element.45.w_low) | copy-start | bytes 7864324
  14.8 12.1 %all-to-all-start = ((f32[32,9,1,128]{3,2,1,0:T(1,128)}), f32[32,9,1,128]{3,2,1,0:T(1,128)S(1)}, u32[]{:S(2)}, u32[]{:S(2)}) async-start(f32[32,9,1,128]{3,2,1,0:T(1,128)} %get-tuple-element.50), calls=%async_computation | async-start | bytes 294912 | tf_op jit(solution)/shard_map/all_to_all | solution.py:527
  18.1 10.0 %collective-permute-start.3 = (f32[2,32,128]{2,1,0:T(8,128)S(1)}, f32[2,32,128]{2,1,0:T(8,128)S(1)}, u32[]{:S(2)}, u32[]{:S(2)}) collective-permute-start(f32[2,32,128]{2,1,0:T(8,128)S(1)} %get-tuple-element.47), channel_id=1, source_target_pairs={{0,1},{1,0},{2,3},{3,2},{4,5},{5,4},{6,7},{7,6},{8,9},{9,8},{10,11... | collective-permute-start | bytes 98312 | tf_op jit(solution)/shard_map/ppermute | solution.py:523
  18.5 9.6 %collective-permute-start.4 = (f32[2,32,128]{2,1,0:T(8,128)S(1)}, f32[2,32,128]{2,1,0:T(8,128)S(1)}, u32[]{:S(2)}, u32[]{:S(2)}) collective-permute-start(f32[2,32,128]{2,1,0:T(8,128)S(1)} %get-tuple-element.47), channel_id=1, source_target_pairs={{0,16},{1,17},{2,18},{3,19},{4,20},{5,21},{6,22},{7,23},{8,24},{9,... | collective-permute-start | bytes 98312 | tf_op jit(solution)/shard_map/ppermute | solution.py:523
  21.0 7.1 %collective-permute-start.5 = (f32[2,32,128]{2,1,0:T(8,128)S(1)}, f32[2,32,128]{2,1,0:T(8,128)S(1)}, u32[]{:S(2)}, u32[]{:S(2)}) collective-permute-start(f32[2,32,128]{2,1,0:T(8,128)S(1)} %get-tuple-element.47), channel_id=1, source_target_pairs={{0,31},{1,2},{2,1},{3,4},{4,3},{5,6},{6,5},{7,8},{8,7},{9,10},{10,... | collective-permute-start | bytes 98312 | tf_op jit(solution)/shard_map/ppermute | solution.py:523
  28.1 1.7 %copy-start.1 = (bf16[8,640,256]{2,1,0:T(8,128)(2,1)S(1)}, bf16[8,640,256]{2,1,0:T(8,128)(2,1)}, u32[]{:S(2)}) copy-start(bf16[8,640,256]{2,1,0:T(8,128)(2,1)} %copy-done) | copy-start | bytes 7864324
  30.4 0.7 copy-start.7
  31.0 6.7 %collective-permute-start.6 = (f32[2,16,128]{2,1,0:T(8,128)S(1)}, f32[2,16,128]{2,1,0:T(8,128)S(1)}, u32[]{:S(2)}, u32[]{:S(2)}) collective-permute-start(f32[2,16,128]{2,1,0:T(8,128)S(1)} %get-tuple-element.57), channel_id=1, source_target_pairs={{0,1},{1,0},{2,3},{3,2},{4,5},{5,4},{6,7},{7,6},{8,9},{9,8},{10,11... | collective-permute-start | bytes 49160 | tf_op jit(solution)/shard_map/ppermute | solution.py:523
  31.3 6.4 %collective-permute-start.7 = (f32[2,16,128]{2,1,0:T(8,128)S(1)}, f32[2,16,128]{2,1,0:T(8,128)S(1)}, u32[]{:S(2)}, u32[]{:S(2)}) collective-permute-start(f32[2,16,128]{2,1,0:T(8,128)S(1)} %get-tuple-element.57), channel_id=1, source_target_pairs={{0,16},{1,17},{2,18},{3,19},{4,20},{5,21},{6,22},{7,23},{8,24},{9,... | collective-permute-start | bytes 49160 | tf_op jit(solution)/shard_map/ppermute | solution.py:523
  32.1 6.8 %collective-permute-start.8 = (f32[2,16,128]{2,1,0:T(8,128)S(1)}, f32[2,16,128]{2,1,0:T(8,128)S(1)}, u32[]{:S(2)}, u32[]{:S(2)}) collective-permute-start(f32[2,16,128]{2,1,0:T(8,128)S(1)} %get-tuple-element.57), channel_id=1, source_target_pairs={{0,31},{1,2},{2,1},{3,4},{4,3},{5,6},{6,5},{7,8},{8,7},{9,10},{10,... | collective-permute-start | bytes 49160 | tf_op jit(solution)/shard_map/ppermute | solution.py:523
  34.7 4.2 %copy-start.2 = (bf16[8,640,256]{2,1,0:T(8,128)(2,1)S(1)}, bf16[8,640,256]{2,1,0:T(8,128)(2,1)}, u32[]{:S(2)}) copy-start(bf16[8,640,256]{2,1,0:T(8,128)(2,1)} %copy-done) | copy-start | bytes 7864324
  34.7 4.2 %copy-start.14 = (s32[2]{0:T(128)S(1)}, s32[2]{0:T(128)}, u32[]{:S(2)}) copy-start(s32[2]{0:T(128)} %iface.7) | copy-start | bytes 28
  36.5 4.0 %copy-start.9 = (f32[16,1024]{1,0:T(8,128)}, f32[16,1024]{1,0:T(8,128)S(1)}, u32[]{:S(2)}) copy-start(f32[16,1024]{1,0:T(8,128)S(1)} %get-tuple-element.75.v) | copy-start | bytes 196612
  36.5 1.2 %collective-permute-start.9 = (f32[16,128]{1,0:T(8,128)S(1)}, f32[16,128]{1,0:T(8,128)S(1)}, u32[]{:S(2)}, u32[]{:S(2)}) collective-permute-start(f32[16,128]{1,0:T(8,128)S(1)} %get-tuple-element.61.part), channel_id=1, source_target_pairs={{0,1},{1,0},{2,3},{3,2},{4,5},{5,4},{6,7},{7,6},{8,9},{9,8},{10,11... | collective-permute-start | bytes 24584 | tf_op jit(solution)/shard_map/ppermute | solution.py:574
  40.4 0.7 copy-start.6
  41.1 0.6 copy-start.11
  41.7 0.6 copy-start.16
  42.4 12.1 %all-to-all-start.1 = ((f32[32,10,1,128]{3,2,1,0:T(1,128)}), f32[32,10,1,128]{3,2,1,0:T(1,128)S(1)}, u32[]{:S(2)}, u32[]{:S(2)}) async-start(f32[32,10,1,128]{3,2,1,0:T(1,128)} %copy-done.6), calls=%async_computation.1 | async-start | bytes 327680 | tf_op jit(solution)/shard_map/all_to_all | solution.py:527
  45.3 10.9 %collective-permute-start.10 = (f32[2,48,128]{2,1,0:T(8,128)}, f32[2,48,128]{2,1,0:T(8,128)}, u32[]{:S(2)}, u32[]{:S(2)}) collective-permute-start(f32[2,48,128]{2,1,0:T(8,128)} %copy-done.16), channel_id=1, source_target_pairs={{0,1},{1,0},{2,3},{3,2},{4,5},{5,4},{6,7},{7,6},{8,9},{9,8},{10,11... | collective-permute-start | bytes 147464 | tf_op jit(solution)/shard_map/ppermute | solution.py:523
  45.6 10.6 %collective-permute-start.11 = (f32[2,48,128]{2,1,0:T(8,128)}, f32[2,48,128]{2,1,0:T(8,128)}, u32[]{:S(2)}, u32[]{:S(2)}) collective-permute-start(f32[2,48,128]{2,1,0:T(8,128)} %copy-done.16), channel_id=1, source_target_pairs={{0,16},{1,17},{2,18},{3,19},{4,20},{5,21},{6,22},{7,23},{8,24},{9,... | collective-permute-start | bytes 147464 | tf_op jit(solution)/shard_map/ppermute | solution.py:523
  48.2 8.1 %collective-permute-start.12 = (f32[2,48,128]{2,1,0:T(8,128)}, f32[2,48,128]{2,1,0:T(8,128)}, u32[]{:S(2)}, u32[]{:S(2)}) collective-permute-start(f32[2,48,128]{2,1,0:T(8,128)} %copy-done.16), channel_id=1, source_target_pairs={{0,31},{1,2},{2,1},{3,4},{4,3},{5,6},{6,5},{7,8},{8,7},{9,10},{10,... | collective-permute-start | bytes 147464 | tf_op jit(solution)/shard_map/ppermute | solution.py:523
  54.5 0.8 %copy-start.12 = (f32[16,1024]{1,0:T(8,128)S(1)}, f32[16,1024]{1,0:T(8,128)}, u32[]{:S(2)}) copy-start(f32[16,1024]{1,0:T(8,128)} %copy-done.11) | copy-start | bytes 196612
  56.2 1.7 %copy-start.3 = (bf16[8,640,256]{2,1,0:T(8,128)(2,1)S(1)}, bf16[8,640,256]{2,1,0:T(8,128)(2,1)}, u32[]{:S(2)}) copy-start(bf16[8,640,256]{2,1,0:T(8,128)(2,1)} %copy-done) | copy-start | bytes 7864324
  58.0 0.9 %copy-start.8 = (f32[48,768]{1,0:T(8,128)S(1)}, f32[48,768]{1,0:T(8,128)}, u32[]{:S(2)}) copy-start(f32[48,768]{1,0:T(8,128)} %copy-done.7) | copy-start | bytes 442372
  58.9 0.7 copy-start.15
  60.9 5.5 %collective-permute-start.13 = (f32[2,16,128]{2,1,0:T(8,128)S(1)}, f32[2,16,128]{2,1,0:T(8,128)S(1)}, u32[]{:S(2)}, u32[]{:S(2)}) collective-permute-start(f32[2,16,128]{2,1,0:T(8,128)S(1)} %get-tuple-element.73), channel_id=1, source_target_pairs={{0,1},{1,0},{2,3},{3,2},{4,5},{5,4},{6,7},{7,6},{8,9},{9,8},{10,11... | collective-permute-start | bytes 49160 | tf_op jit(solution)/shard_map/ppermute | solution.py:523
  61.2 5.2 %collective-permute-start.14 = (f32[2,16,128]{2,1,0:T(8,128)S(1)}, f32[2,16,128]{2,1,0:T(8,128)S(1)}, u32[]{:S(2)}, u32[]{:S(2)}) collective-permute-start(f32[2,16,128]{2,1,0:T(8,128)S(1)} %get-tuple-element.73), channel_id=1, source_target_pairs={{0,16},{1,17},{2,18},{3,19},{4,20},{5,21},{6,22},{7,23},{8,24},{9,... | collective-permute-start | bytes 49160 | tf_op jit(solution)/shard_map/ppermute | solution.py:523
  62.4 6.8 %collective-permute-start.15 = (f32[2,16,128]{2,1,0:T(8,128)S(1)}, f32[2,16,128]{2,1,0:T(8,128)S(1)}, u32[]{:S(2)}, u32[]{:S(2)}) collective-permute-start(f32[2,16,128]{2,1,0:T(8,128)S(1)} %get-tuple-element.73), channel_id=1, source_target_pairs={{0,31},{1,2},{2,1},{3,4},{4,3},{5,6},{6,5},{7,8},{8,7},{9,10},{10,... | collective-permute-start | bytes 49160 | tf_op jit(solution)/shard_map/ppermute | solution.py:523
  65.0 1.0 %copy-start.10 = (f32[16,1024]{1,0:T(8,128)S(1)}, f32[16,1024]{1,0:T(8,128)}, u32[]{:S(2)}) copy-start(f32[16,1024]{1,0:T(8,128)} %copy-done.9) | copy-start | bytes 196612
  65.0 4.2 %copy-start.4 = (bf16[8,640,256]{2,1,0:T(8,128)(2,1)S(1)}, bf16[8,640,256]{2,1,0:T(8,128)(2,1)}, u32[]{:S(2)}) copy-start(bf16[8,640,256]{2,1,0:T(8,128)(2,1)} %copy-done) | copy-start | bytes 7864324
